TPU v7x, 32 devices: a whole 2x2x4 slice. The times are simulated.
32 devices in a mesh: lat: 8 (over z, y), lon: 4 (over x, core).
Axes of the slice: x: 2, y: 2, z: 4, core: 2. Of those that a mesh axis runs over, the one named last changes fastest.
Arguments:
- right_side: float32 [480, 4, 4096], P('lat', None, 'lon'), may hold values from -6 to 6
- lon_coef: float32 [480], replicated, may hold values from 5 to 500
- lat_coef: float32 [479], replicated, may hold values from 200 to 2000
- level_scale: float32 [4], replicated, may hold values from 0.5 to 4
Outputs:
- solution_grid: float32 [480, 4, 4096], P('lat', None, 'lon')
All inputs are finite; a program needn't handle non-finite values.
Results may differ from a plain program's by a relative error of at most 0.0003.
Values sent between devices are 32-bit elements; how exact they have to be, the bound alone decides.
No kernel may reach another device: no remote copies, remote signals or barrier semaphores. Data moves between devices by JAX's collectives and lax.ppermute only.
A program may use at most 128 MiB of HBM per device.

v0:
```python
import functools
import math

import jax
import jax.numpy as jnp
import numpy as np
from jax import lax
from jax.experimental import pallas as pl
from jax.experimental.pallas import tpu as pltpu
from jax.sharding import PartitionSpec as P

NLON = 4096
OV = 8
N1 = 32
N2 = 128
GROUPS = 16
BLOCK = 8

VMEM = pltpu.VMEM
SMEM = pltpu.SMEM


def numpy_split(table):
    import ml_dtypes

    table = np.asarray(table, np.float32)
    high = table.astype(ml_dtypes.bfloat16)
    low = (table - high.astype(np.float32)).astype(ml_dtypes.bfloat16)
    return high, low


def tables():
    j1 = np.arange(N1)
    j2 = np.arange(N2)
    k2 = np.arange(N2)
    digit = np.arange(GROUPS)
    small = np.zeros((N1, N1))
    small[:GROUPS] = np.cos(2 * np.pi * np.outer(digit, j1) / N1)
    small[GROUPS] = np.cos(np.pi * j1)
    small[GROUPS + 1 :] = -np.sin(2 * np.pi * np.outer(digit[1:], j1) / N1)
    first = np.kron(np.eye(BLOCK), small)
    angle = 2 * np.pi * np.outer(digit, j2) / NLON
    turn_cos = np.cos(angle)
    turn_sin = np.sin(angle)
    phase = 2 * np.pi * (np.outer(j2, k2) % N2) / N2
    cosine, sine = np.cos(phase), np.sin(phase)
    second = np.block([[cosine, -sine], [sine, cosine]])
    special = np.zeros((2 * N2, 2 * N2))
    half = N2 // 2
    special[:N2, : half + 1] = np.cos(2 * np.pi * np.outer(j2, np.arange(half + 1)) / N2)
    special[:N2, half + 1 : N2] = -np.sin(2 * np.pi * np.outer(j2, np.arange(1, half)) / N2)
    odd = 2 * np.pi * np.outer(j2, 1 + 2 * np.arange(half)) / (2 * N2)
    special[N2:, N2 : N2 + half] = np.cos(odd)
    special[N2:, N2 + half :] = -np.sin(odd)
    weight = np.full(2 * N2, 2.0 / NLON)
    weight[0] = 1.0 / NLON
    weight[half] = 1.0 / NLON
    second_back = second.T * (2.0 / NLON)
    special_back = weight[:, None] * special.T
    wave = np.zeros((GROUPS, 2 * N2))
    wave[:, :N2] = digit[:, None] + N1 * k2[None, :]
    wave[:, N2:] = wave[:, :N2]
    lane = np.arange(N2)
    wave[0, :N2] = np.where(lane <= half, N1 * lane, N1 * (lane - half))
    wave[0, N2:] = 16 + N1 * (lane % half)
    eigen = 2.0 - 2.0 * np.cos(2 * np.pi * wave / NLON)
    pair = lambda t: np.concatenate(numpy_split(t), axis=0)
    return dict(
        first=pair(first),
        first_back=pair(first.T),
        second=pair(second),
        second_back=pair(second_back),
        special=pair(special),
        special_back=pair(special_back),
        turn=np.concatenate([turn_cos, turn_sin], axis=0).astype(np.float32),
        eigen=np.stack([eigen[:, :N2], eigen[:, N2:]]).astype(np.float32),
    )


def halves(value):
    high = value.astype(jnp.bfloat16)
    low = (value - high.astype(jnp.float32)).astype(jnp.bfloat16)
    return high, low


def dot(a, b):
    return lax.dot_general(a, b, (((1,), (0,)), ((), ())), preferred_element_type=jnp.float32)


def product_right(value, table_ref):
    size = table_ref.shape[0] // 2
    high, low = halves(value)
    table_high = table_ref[:size, :]
    return dot(high, table_high) + dot(low, table_high) + dot(high, table_ref[size:, :])


def product_left(table_ref, value):
    size = table_ref.shape[0] // 2
    high, low = halves(value)
    both = dot(table_ref[...], high)
    return both[:size] + both[size:] + dot(table_ref[:size, :], low)


def lanes_apart(value, rows):
    real = value[:, :N2].reshape(rows, GROUPS, N2)
    imag = value[:, N2:].reshape(rows, GROUPS, N2)
    return jnp.concatenate([real, imag], axis=1).reshape(rows * 2 * GROUPS, N2)


def lanes_together(value, rows):
    both = value.reshape(rows, 2 * GROUPS, N2)
    return jnp.concatenate([both[:, :GROUPS], both[:, GROUPS:]], axis=2).reshape(rows * GROUPS, 2 * N2)


def load_zeroth(ref, rows):
    return jnp.concatenate(
        [ref[pl.ds(0, rows, stride=2 * GROUPS), :], ref[pl.ds(GROUPS, rows, stride=2 * GROUPS), :]], axis=1
    )


def store_zeroth(ref, rows, value):
    ref[pl.ds(0, rows, stride=2 * GROUPS), :] = value[:, :N2]
    ref[pl.ds(GROUPS, rows, stride=2 * GROUPS), :] = value[:, N2:]


def forward_rows(points_ref, rows, first_ref, turn_ref, second_ref, special_ref, mid_ref, out_ref):
    padded = points_ref.shape[0]
    turn_cos = turn_ref[:GROUPS, :][None]
    turn_sin = turn_ref[GROUPS:, :][None]
    for pair in range(padded // (2 * BLOCK)):
        base = pair * 2 * BLOCK
        left = points_ref[base : base + BLOCK].reshape(BLOCK * N1, N2)
        right = points_ref[base + BLOCK : base + 2 * BLOCK].reshape(BLOCK * N1, N2)
        value = product_left(first_ref, jnp.concatenate([left, right], axis=1))
        for side in range(2):
            digits = value[:, side * N2 : (side + 1) * N2].reshape(BLOCK, N1, N2)
            real, imag = digits[:, :GROUPS], digits[:, GROUPS:]
            turned = jnp.concatenate(
                [real * turn_cos + imag * turn_sin, imag * turn_cos - real * turn_sin], axis=1
            )
            at = (base + side * BLOCK) * N1
            mid_ref[at : at + BLOCK * N1, :] = turned.reshape(BLOCK * N1, N2)
    result = product_right(lanes_together(mid_ref[...], padded), second_ref)
    out_ref[...] = lanes_apart(result, padded)[: rows * N1]
    store_zeroth(out_ref, rows, product_right(load_zeroth(mid_ref, padded), special_ref)[:rows])


def backward_rows(spec_ref, rows, first_ref, turn_ref, second_ref, special_ref, mid_ref, out_ref):
    padded = out_ref.shape[0]
    turn_cos = turn_ref[:GROUPS, :][None]
    turn_sin = turn_ref[GROUPS:, :][None]
    result = product_right(lanes_together(spec_ref[...], rows), second_ref)
    mid_ref[: rows * N1, :] = lanes_apart(result, rows)
    if padded > rows:
        mid_ref[rows * N1 :, :] = jnp.zeros(((padded - rows) * N1, N2), jnp.float32)
    store_zeroth(mid_ref, rows, product_right(load_zeroth(spec_ref, rows), special_ref))
    for pair in range(padded // (2 * BLOCK)):
        base = pair * 2 * BLOCK
        sides = []
        for side in range(2):
            at = (base + side * BLOCK) * N1
            both = mid_ref[at : at + BLOCK * N1, :].reshape(BLOCK, N1, N2)
            real, imag = both[:, :GROUPS], both[:, GROUPS:]
            digits = jnp.concatenate(
                [real * turn_cos - imag * turn_sin, imag * turn_cos + real * turn_sin], axis=1
            )
            sides.append(digits.reshape(BLOCK * N1, N2))
        value = product_left(first_ref, jnp.concatenate(sides, axis=1))
        out_ref[base : base + BLOCK] = value[:, :N2].reshape(BLOCK, N1, N2)
        out_ref[base + BLOCK : base + 2 * BLOCK] = value[:, N2:].reshape(BLOCK, N1, N2)


def factor_kernel(rows, lon_ref, couple_ref, eigen_ref, ratio_ref, inverse_ref, edge_ref):
    eigen = eigen_ref[...]
    groups = eigen.shape[0]
    half = rows // 2
    last = rows + 2 * OV - 1

    def plain(e):
        return 1.0 + lon_ref[e] * eigen

    def put(ref, index, value):
        ref[index * groups : (index + 1) * groups, :] = value

    def chain(start, stop, step, into):
        excess = inverse = None
        for e in range(start, stop + step, step):
            before = couple_ref[e] if step > 0 else couple_ref[e + 1]
            after = couple_ref[e + 1] if step > 0 else couple_ref[e]
            if inverse is None:
                ratio = None
                excess = plain(e) + before
            else:
                ratio = before * inverse
                excess = plain(e) + ratio * excess
            divisor = after + excess
            inverse = 1.0 / divisor
            into(e, ratio, inverse, excess, divisor)

    kept = {}

    def top(e, ratio, inverse, excess, divisor):
        if e == OV - 1:
            put(edge_ref, 0, inverse)
        if e >= OV:
            put(ratio_ref, e - OV, ratio)
            put(inverse_ref, e - OV, inverse)
        if e == OV + half - 1:
            kept["top"] = excess, divisor

    def bottom(e, ratio, inverse, excess, divisor):
        if e == OV + rows:
            put(edge_ref, 1, inverse)
        if e < OV + rows:
            put(ratio_ref, e - OV, ratio)
            put(inverse_ref, e - OV, inverse)
        if e == OV + half:
            kept["bottom"] = excess, divisor

    def next_band(e, ratio, inverse, excess, divisor):
        if ratio is not None:
            put(edge_ref, 7 + e - rows - 1, ratio)
        if e == OV + rows - 1:
            put(edge_ref, 5, inverse)

    def previous_band(e, ratio, inverse, excess, divisor):
        if ratio is not None:
            put(edge_ref, 14 + e - OV, ratio)
        if e == OV:
            put(edge_ref, 6, inverse)

    chain(rows, OV + rows - 1, 1, next_band)
    chain(2 * OV - 1, OV, -1, previous_band)
    chain(0, OV + half - 1, 1, top)
    chain(last, OV + half, -1, bottom)
    excess_top, divisor_top = kept["top"]
    excess_bottom, divisor_bottom = kept["bottom"]
    between = couple_ref[OV + half]
    inverse = 1.0 / (between * (excess_top + excess_bottom) + excess_top * excess_bottom)
    put(edge_ref, 2, divisor_bottom * inverse)
    put(edge_ref, 3, divisor_top * inverse)
    put(edge_ref, 4, between * inverse)


def edge_sums(low_rows, high_rows, edge_ref, groups):
    def edge(index):
        return edge_ref[index * groups : (index + 1) * groups, :]

    top = high_rows(0)
    for i in range(1, OV):
        top = high_rows(i) + edge(7 + i - 1) * top
    bottom = low_rows(OV - 1)
    for i in range(OV - 2, -1, -1):
        bottom = low_rows(i) + edge(14 + i) * bottom
    return top, bottom


def swap_out(parity, up, down, even_ref, odd_ref):
    is_even = parity == 0
    even_ref[...] = jnp.where(is_even, up, down)
    odd_ref[...] = jnp.where(is_even, down, up)


def swap_in(parity, even, odd):
    is_even = parity == 0
    return jnp.where(is_even, odd, even), jnp.where(is_even, even, odd)


def solve_first(rows, groups, right_side_row, from_low, from_high, ratio_ref, inverse_ref, edge_ref, out_ref):
    half = rows // 2

    def at(ref, index):
        return ref[index * groups : (index + 1) * groups, :]

    def put(index, value):
        out_ref[index * groups : (index + 1) * groups, :] = value

    low, high = from_low, from_high
    for i in range(half):
        j = rows - 1 - i
        low = right_side_row(i) + at(ratio_ref, i) * low
        high = right_side_row(j) + at(ratio_ref, j) * high
        put(i, low)
        put(j, high)
    meet(rows, groups, low, high, ratio_ref, inverse_ref, edge_ref, at, lambda i: at(out_ref, i), put)


def meet(rows, groups, low, high, ratio_ref, inverse_ref, edge_ref, at, value, put):
    half = rows // 2
    between = at(edge_ref, 4)
    x_low = at(edge_ref, 2) * low + between * high
    x_high = at(edge_ref, 3) * high + between * low
    put(half - 1, x_low)
    put(half, x_high)
    for i in range(half - 2, -1, -1):
        j = rows - 1 - i
        x_low = value(i) * at(inverse_ref, i) + at(ratio_ref, i + 1) * x_low
        x_high = value(j) * at(inverse_ref, j) + at(ratio_ref, j - 1) * x_high
        put(i, x_low)
        put(j, x_high)


def solve_second(
    rows, groups, couple_low, couple_high, own_top, own_bottom, got_top, got_bottom, sent_top, sent_bottom,
    from_low, from_high, ratio_ref, inverse_ref, edge_ref, first_ref, out_ref, mid_ref,
):
    half = rows // 2

    def at(ref, index):
        return ref[index * groups : (index + 1) * groups, :]

    beyond_low = (got_top + couple_low * own_top) * at(edge_ref, 0)
    beyond_high = (got_bottom + couple_high * own_bottom) * at(edge_ref, 1)
    theirs_low = (sent_bottom + couple_low * from_low) * at(edge_ref, 6)
    theirs_high = (sent_top + couple_high * from_high) * at(edge_ref, 5)
    low = couple_low * (own_top - theirs_low)
    high = couple_high * (own_bottom - theirs_high)
    for i in range(half):
        j = rows - 1 - i
        low = at(ratio_ref, i) * low
        high = at(ratio_ref, j) * high
        if i == 0:
            low = low + couple_low * (from_low - beyond_low)
            high = high + couple_high * (from_high - beyond_high)
        mid_ref[i * groups : (i + 1) * groups, :] = low
        mid_ref[j * groups : (j + 1) * groups, :] = high

    def put(index, value):
        rows_at = slice(index * groups, (index + 1) * groups)
        out_ref[rows_at, :] = first_ref[rows_at, :] + value

    meet(rows, groups, low, high, ratio_ref, inverse_ref, edge_ref, at, lambda i: at(mid_ref, i), put)


def call(body, outs, ins, spaces, scratch, flops, name):
    nbytes = sum(x.size * x.dtype.itemsize for x in ins) + sum(4 * math.prod(s) for s in outs)
    out = pl.pallas_call(
        body,
        out_shape=[jax.ShapeDtypeStruct(s, jnp.float32) for s in outs],
        in_specs=[pl.BlockSpec(memory_space=s) for s in spaces],
        out_specs=[pl.BlockSpec(memory_space=VMEM) for _ in outs],
        scratch_shapes=scratch,
        compiler_params=pltpu.CompilerParams(vmem_limit_bytes=48 << 20),
        cost_estimate=pl.CostEstimate(flops=flops, bytes_accessed=nbytes, transcendentals=0),
        name=name,
    )(*ins)
    return out


def pad_rows(rows):
    return -(-rows // (2 * BLOCK)) * 2 * BLOCK


def swap(value_even, value_odd):
    count = lax.axis_size("lat")
    even = [(i, i ^ 1) for i in range(count) if (i ^ 1) < count]
    odd = [(i, ((i + 1) ^ 1) - 1) for i in range(1, count) if ((i + 1) ^ 1) - 1 < count]
    return lax.ppermute(value_even, "lat", even), lax.ppermute(value_odd, "lat", odd)


def on_device(right_side, lon_coef, lat_coef, level_scale):
    rows, levels, lon_count = right_side.shape
    lon_size = lax.axis_size("lon")
    assert lon_size % levels == 0 and N1 % lon_size == 0 and rows % 2 == 0
    sharers = lon_size // levels
    groups = 2 * GROUPS // sharers
    part_rows = rows // sharers
    digits = N1 // lon_size
    const = {k: jnp.asarray(v) for k, v in tables().items()}
    lon_at = lax.axis_index("lon")
    lat_at = lax.axis_index("lat")
    level = lon_at // sharers
    parity = (lat_at % 2).astype(jnp.int32)
    row_first = lat_at * rows
    extent = rows + 2 * OV
    scale = lax.dynamic_index_in_dim(level_scale, level, 0, False)
    lon_window = scale * lax.dynamic_slice_in_dim(jnp.pad(lon_coef, (OV, OV)), row_first, extent)
    couple = scale * lax.dynamic_slice_in_dim(
        jnp.pad(lat_coef, (OV + 1, OV + 2)), row_first, extent + 1
    )
    eigen = const["eigen"]
    if sharers > 1:
        eigen = lax.dynamic_slice_in_dim(eigen, (lon_at % sharers) * (groups // 2), groups // 2, axis=1)
    eigen = eigen.reshape(groups, N2)
    wide = N2
    block = (rows * groups, wide)
    row = (groups, wide)
    ratio, inverse, edge = call(
        functools.partial(factor_kernel, rows),
        [block, block, (21 * groups, wide)],
        [lon_window, couple, eigen],
        [SMEM, SMEM, VMEM],
        [],
        rows * groups * wide * 20,
        "factor",
    )
    if sharers == 1:
        pieces = exchange_levels(right_side, lon_at)
    else:
        pieces = None
        send = right_side.reshape(sharers, part_rows, levels, lon_count).transpose(2, 0, 1, 3)
        send = send.reshape(lon_size, part_rows, digits, N2)
        got = lax.all_to_all(send, "lon", 0, 0, tiled=True)
        points = got.transpose(1, 0, 2, 3).reshape(part_rows, N1, N2)
    if sharers == 1:
        points = place_pieces(pieces, lon_at, digits)
    padded = pad_rows(part_rows)

    def transform(points_ref, first_ref, turn_ref, second_ref, special_ref, out_ref, full_ref, mid_ref):
        full_ref[:part_rows] = points_ref[...]
        if padded > part_rows:
            full_ref[part_rows:] = jnp.zeros((padded - part_rows, N1, N2), jnp.float32)
        forward_rows(full_ref, part_rows, first_ref, turn_ref, second_ref, special_ref, mid_ref, out_ref)

    (spectral,) = call(
        transform,
        [(part_rows * N1, wide)],
        [points, const["first"], const["turn"], const["second"], const["special"]],
        [VMEM] * 5,
        [pltpu.VMEM((padded, N1, N2), jnp.float32), pltpu.VMEM((padded * N1, wide), jnp.float32)],
        part_rows * NLON * 256 * 4,
        "transform",
    )
    if sharers > 1:
        spectral = to_coefs(spectral, sharers, part_rows, groups)
    parity_arg = parity.reshape(1)

    def edges(parity_ref, spec_ref, edge_ref, top_ref, bottom_ref, even_ref, odd_ref):
        def spec_row(i):
            return spec_ref[i * groups : (i + 1) * groups, :]

        top, bottom = edge_sums(spec_row, lambda i: spec_row(rows - OV + i), edge_ref, groups)
        top_ref[...] = top
        bottom_ref[...] = bottom
        swap_out(parity_ref[0], top, bottom, even_ref, odd_ref)

    sent_top, sent_bottom, even, odd = call(
        edges, [row] * 4, [parity_arg, spectral, edge], [SMEM, VMEM, VMEM], [], groups * wide * 32, "edges"
    )
    even, odd = swap(even, odd)

    def first(parity_ref, spec_ref, even_ref, odd_ref, ratio_ref, inverse_ref, edge_ref, out_ref, e_ref, o_ref):
        low, high = swap_in(parity_ref[0], even_ref[...], odd_ref[...])
        solve_first(
            rows, groups, lambda i: spec_ref[i * groups : (i + 1) * groups, :], low, high,
            ratio_ref, inverse_ref, edge_ref, out_ref,
        )
        swap_out(parity_ref[0], out_ref[(rows - 1) * groups :, :], out_ref[:groups, :], e_ref, o_ref)

    iterate, even2, odd2 = call(
        first, [block, row, row], [parity_arg, spectral, even, odd, ratio, inverse, edge],
        [SMEM] + [VMEM] * 6, [], rows * groups * wide * 8, "first_solve",
    )
    even2, odd2 = swap(even2, odd2)

    def second(
        parity_ref, couple_ref, first_ref, even_ref, odd_ref, even2_ref, odd2_ref, top_ref, bottom_ref,
        ratio_ref, inverse_ref, edge_ref, out_ref, mid_ref,
    ):
        got_top, got_bottom = swap_in(parity_ref[0], even_ref[...], odd_ref[...])
        low, high = swap_in(parity_ref[0], even2_ref[...], odd2_ref[...])
        solve_second(
            rows, groups, couple_ref[OV], couple_ref[OV + rows],
            first_ref[:groups, :], first_ref[(rows - 1) * groups :, :],
            got_top, got_bottom, top_ref[...], bottom_ref[...], low, high,
            ratio_ref, inverse_ref, edge_ref, first_ref, out_ref, mid_ref,
        )

    (iterate,) = call(
        second, [block],
        [parity_arg, couple, iterate, even, odd, even2, odd2, sent_top, sent_bottom, ratio, inverse, edge],
        [SMEM, SMEM] + [VMEM] * 10, [pltpu.VMEM(block, jnp.float32)], rows * groups * wide * 8, "second_solve",
    )
    if sharers > 1:
        iterate = to_rows(iterate, sharers, part_rows, groups)

    def back(spec_ref, first_ref, turn_ref, second_ref, special_ref, out_ref, mid_ref, full_ref):
        backward_rows(spec_ref, part_rows, first_ref, turn_ref, second_ref, special_ref, mid_ref, full_ref)
        out_ref[...] = full_ref[:part_rows]

    (points,) = call(
        back,
        [(part_rows, N1, N2)],
        [iterate, const["first_back"], const["turn"], const["second_back"], const["special_back"]],
        [VMEM] * 5,
        [pltpu.VMEM((padded * N1, wide), jnp.float32), pltpu.VMEM((padded, N1, N2), jnp.float32)],
        part_rows * NLON * 256 * 4,
        "back_transform",
    )
    if sharers == 1:
        return return_levels(points, lon_at, digits, right_side.shape)
    send = points.reshape(part_rows, lon_size, digits, N2).transpose(1, 0, 2, 3)
    got = lax.all_to_all(send, "lon", 0, 0, tiled=True)
    got = got.reshape(levels, sharers, part_rows, lon_count).transpose(1, 2, 0, 3)
    return got.reshape(rows, levels, lon_count)


def exchange_levels(right_side, lon_at):
    rows, levels, lon_count = right_side.shape
    size = levels
    pieces = []
    for mask in range(size):
        piece = lax.dynamic_index_in_dim(right_side, lon_at ^ mask, 1, False)
        piece = piece.reshape(rows, lon_count // N2, N2)
        if mask:
            piece = lax.ppermute(piece, "lon", [(d, d ^ mask) for d in range(size)])
        pieces.append(piece)
    return pieces


def place_pieces(pieces, lon_at, digits):
    stacked = jnp.stack(pieces, axis=1)
    order = lon_at ^ jnp.arange(len(pieces))
    stacked = jnp.take(stacked, order, axis=1)
    return stacked.reshape(stacked.shape[0], N1, N2)


def return_levels(points, lon_at, digits, shape):
    rows, levels, lon_count = shape
    size = levels
    parts = points.reshape(rows, size, digits, N2)
    pieces = []
    for mask in range(size):
        piece = lax.dynamic_index_in_dim(parts, lon_at ^ mask, 1, False)
        if mask:
            piece = lax.ppermute(piece, "lon", [(d, d ^ mask) for d in range(size)])
        pieces.append(piece.reshape(rows, lon_count))
    stacked = jnp.stack(pieces, axis=1)
    return jnp.take(stacked, lon_at ^ jnp.arange(size), axis=1)


def level_groups(sharers):
    size = lax.axis_size("lon")
    return [[first + i for i in range(sharers)] for first in range(0, size, sharers)]


def to_coefs(spectral, sharers, part_rows, groups):
    send = spectral.reshape(part_rows, 2, sharers, groups // 2, N2).transpose(2, 0, 1, 3, 4)
    got = lax.all_to_all(
        send, "lon", 0, 0, tiled=True, axis_index_groups=level_groups(sharers)
    )
    return got.reshape(sharers * part_rows * groups, N2)


def to_rows(values, sharers, part_rows, groups):
    send = values.reshape(sharers, part_rows, 2, groups // 2, N2)
    got = lax.all_to_all(
        send, "lon", 0, 0, tiled=True, axis_index_groups=level_groups(sharers)
    )
    return got.transpose(1, 2, 0, 3, 4).reshape(part_rows * N1, N2)


def solution(mesh):
    return jax.shard_map(
        on_device,
        mesh=mesh,
        in_specs=(P("lat", None, "lon"), P(), P(), P()),
        out_specs=P("lat", None, "lon"),
        check_vma=False,
    )
```

profile of v0, /device:TPU:17, one launch (start us, length us, event | category | flops | bytes accessed | tf_op | source)
XLA Modules:
  0.0 58.1 jit_solution(2555030459880573648)
XLA Ops:
  0.0 4.0 %constant_dynamic-slice_fusion.4 = (f32[60,1,1024]{2,1,0:T(1,128)S(1)}, f32[60,1,1024]{2,1,0:T(1,128)}, f32[60,1,1024]{2,1,0:T(1,128)S(1)}, f32[60,1,1024]{2,1,0:T(1,128)S(1)}) fusion(f32[60,4,1024]{2,1,0:T(4,128)} %param.12, s32[]{:T(128)S(6)} %select_n.64, s32[]{:T(128)S(6)} %select_n.66, s32[]{:T(128)S(6)} %select_n.68, s32[]{:T(128)S(6)} %select_n.67), kind=kLoop, calls=%fused_computation.18 | loop fusion | bytes 1966096 | tf_op jit(solution)/shard_map/jit(dynamic_index_in_dim)/dynamic_slice | solution.py:503
  4.0 0.7 %collective-permute-start = (f32[60,8,128]{2,1,0:T(8,128)}, f32[60,8,128]{2,1,0:T(8,128)S(1)}, u32[]{:S(2)}, u32[]{:S(2)}) collective-permute-start(f32[60,8,128]{2,1,0:T(8,128)} %bitcast.3), channel_id=1, source_target_pairs={{0,1},{1,0},{2,3},{3,2},{4,5},{5,4},{6,7},{7,6},{8,9},{9,8},{10,11... | collective-permute-start | bytes 737288 | tf_op jit(solution)/shard_map/ppermute | solution.py:506
  4.7 1.1 %collective-permute-start.2 = (f32[60,8,128]{2,1,0:T(8,128)S(1)}, f32[60,8,128]{2,1,0:T(8,128)}, u32[]{:S(2)}, u32[]{:S(2)}) collective-permute-start(f32[60,8,128]{2,1,0:T(8,128)S(1)} %bitcast.31), channel_id=1, source_target_pairs={{0,3},{1,2},{2,1},{3,0},{4,7},{5,6},{6,5},{7,4},{8,11},{9,10},{10,... | collective-permute-start | bytes 737288 | tf_op jit(solution)/shard_map/ppermute | solution.py:506
  5.8 0.3 collective-permute-start.1
  6.1 0.0 copy-start.11
  6.1 0.7 %copy-done.11 = f32[4]{0:T(128)S(1)} copy-done((f32[4]{0:T(128)S(1)}, f32[4]{0:T(128)}, u32[]{:S(2)}) %copy-start.11) | copy-done | bytes 40
  6.7 0.6 %dynamic_slice.36 = f32[1]{0:T(128)} dynamic-slice(f32[4]{0:T(128)S(1)} %copy-done.11, s32[]{:T(128)S(6)} %select_n.64), dynamic_slice_sizes={1} | dynamic-slice | bytes 12 | tf_op jit(solution)/shard_map/jit(dynamic_index_in_dim)/dynamic_slice | solution.py:376
  7.4 0.0 copy-done.9
  7.4 0.8 %fusion.couple_ref = f32[77]{0:T(128)S(1)} fusion(s32[]{:T(128)S(6)} %select_n.65, f32[479]{0:T(512)S(1)} %copy-done.9, f32[]{:T(128)} %bitcast.1), kind=kLoop, calls=%fused_computation.20 | loop fusion | flops 77 | bytes 2232 | tf_op jit(solution)/shard_map/mul | solution.py:378
  8.2 0.8 %fusion.1.lon_ref = f32[76]{0:T(128)S(1)} fusion(s32[]{:T(128)S(6)} %select_n.71, f32[480]{0:T(512)S(1)} %copy-done.10, f32[]{:T(128)} %bitcast.1), kind=kLoop, calls=%fused_computation.21 | loop fusion | flops 76 | bytes 2232 | tf_op jit(solution)/shard_map/mul | solution.py:377
  8.9 0.1 broadcast_in_dim.25
  9.0 0.1 broadcast_in_dim.26
  9.1 0.0 copy-done.7
  9.1 1.0 %factor.1 = (f32[1920,128]{1,0:T(8,128)S(1)}, f32[1920,128]{1,0:T(8,128)S(1)}, f32[672,128]{1,0:T(8,128)S(1)}) custom-call(f32[76]{0:T(128)S(1)} %fusion.1.lon_ref, f32[77]{0:T(128)S(1)} %fusion.couple_ref, f32[32,128]{1,0:T(8,128)S(1)} %copy-done.7), custom_call_target="tpu_custom_call" | custom-call | flops 4915200 | bytes 2327140 | tf_op jit(solution)/shard_map/factor/pallas_call | solution.py:337
  10.2 0.0 collective-permute-done
  10.2 0.0 copy-start.8
  10.2 2.8 %collective-permute-done.2 = f32[60,8,128]{2,1,0:T(8,128)} collective-permute-done((f32[60,8,128]{2,1,0:T(8,128)S(1)}, f32[60,8,128]{2,1,0:T(8,128)}, u32[]{:S(2)}, u32[]{:S(2)}) %collective-permute-start.2) | collective-permute-done | bytes 245792 | tf_op jit(solution)/shard_map/ppermute | solution.py:506
  13.0 4.3 %collective-permute-done.1 = f32[60,8,128]{2,1,0:T(8,128)} collective-permute-done((f32[60,8,128]{2,1,0:T(8,128)S(1)}, f32[60,8,128]{2,1,0:T(8,128)}, u32[]{:S(2)}, u32[]{:S(2)}) %collective-permute-start.1) | collective-permute-done | bytes 245792 | tf_op jit(solution)/shard_map/ppermute | solution.py:506
  17.3 0.0 copy-done.8
  17.3 1.2 %pad_maximum_fusion.1 = f32[60,4,8,128]{3,2,1,0:T(8,128)S(1)} fusion(f32[60,1,8,128]{3,2,1,0:T(8,128)} %bitcast.8, f32[60,1,8,128]{3,2,1,0:T(8,128)} %bitcast.6, f32[60,1,8,128]{3,2,1,0:T(8,128)} %bitcast.29, f32[60,1,8,128]{3,2,1,0:T(8,128)S(1)} %bitcast.27), kind=kLoop, calls=%fused_computation.4 | loop fusion | flops 737280 | bytes 1966080 | tf_op jit(solution)/shard_map/stack | solution.py:512
  18.5 1.6 %gather_fusion = f32[4,60,8,128]{3,2,1,0:T(8,128)} fusion(f32[60,4,8,128]{3,2,1,0:T(8,128)S(1)} %pad_maximum_fusion.1, s32[1024]{0:T(1024)S(1)} %pad_clamp_fusion), kind=kCustom, calls=%fused_computation | custom fusion | bytes 1966096 | tf_op jit(solution)/shard_map/jit(_take)/gather | solution.py:514
  20.2 1.5 %bitcast_select_fusion.points_ref = f32[60,32,128]{2,1,0:T(8,128)S(1)} fusion(pred[32]{0:T(512)(128)(4,1)S(1)} %broadcast_in_dim.26, f32[4,60,8,128]{3,2,1,0:T(8,128)} %gather_fusion), kind=kLoop, calls=%fused_computation.5 | loop fusion | flops 245760 | bytes 1966112 | tf_op jit(solution)/shard_map/jit(_take)/select_n | solution.py:514
  21.7 1.1 %transform.1.spec_ref = f32[1920,128]{1,0:T(8,128)S(1)} custom-call(f32[60,32,128]{2,1,0:T(8,128)S(1)} %bitcast_select_fusion.points_ref, bf16[512,256]{1,0:T(8,128)(2,1)S(1)} %copy-done.5, f32[32,128]{1,0:T(8,128)S(1)} %copy-done.6, bf16[512,256]{1,0:T(8,128)(2,1)S(1)} %copy-done.4, bf16[512,256]{1,0:T(8,128)(2,1)S(1)} %copy-done.3), custom_call_target="tpu_custom_call" | custom-call | flops 251658240 | bytes 2768896 | tf_op jit(solution)/shard_map/transform/pallas_call | solution.py:337
  22.8 1.3 %collective-permute-start.3 = (f32[32,128]{1,0:T(8,128)S(1)}, f32[32,128]{1,0:T(8,128)S(1)}, u32[]{:S(2)}, u32[]{:S(2)}) collective-permute-start(f32[32,128]{1,0:T(8,128)S(1)} %get-tuple-element.16), channel_id=1, source_target_pairs={{0,4},{4,0},{8,12},{12,8},{16,20},{20,16},{24,28},{28,24},{1,5},{5... | collective-permute-start | bytes 49160 | tf_op jit(solution)/shard_map/ppermute | solution.py:358
  24.1 2.0 %collective-permute-start.4 = (f32[32,128]{1,0:T(8,128)S(1)}, f32[32,128]{1,0:T(8,128)S(1)}, u32[]{:S(2)}, u32[]{:S(2)}) collective-permute-start(f32[32,128]{1,0:T(8,128)S(1)} %get-tuple-element.17), channel_id=1, source_target_pairs={{4,8},{8,4},{12,16},{16,12},{20,24},{24,20},{5,9},{9,5},{13,17},{1... | collective-permute-start | bytes 49160 | tf_op jit(solution)/shard_map/ppermute | solution.py:358
  26.2 0.0 collective-permute-done.3.even_ref
  26.2 3.3 %collective-permute-done.4.odd_ref = f32[32,128]{1,0:T(8,128)S(1)} collective-permute-done((f32[32,128]{1,0:T(8,128)S(1)}, f32[32,128]{1,0:T(8,128)S(1)}, u32[]{:S(2)}, u32[]{:S(2)}) %collective-permute-start.4) | collective-permute-done | bytes 16416 | tf_op jit(solution)/shard_map/ppermute | solution.py:358
  29.5 0.3 first_solve.1
  29.8 0.3 collective-permute-start.5
  30.1 3.0 %collective-permute-start.6 = (f32[32,128]{1,0:T(8,128)S(1)}, f32[32,128]{1,0:T(8,128)S(1)}, u32[]{:S(2)}, u32[]{:S(2)}) collective-permute-start(f32[32,128]{1,0:T(8,128)S(1)} %get-tuple-element.22), channel_id=1, source_target_pairs={{4,8},{8,4},{12,16},{16,12},{20,24},{24,20},{5,9},{9,5},{13,17},{1... | collective-permute-start | bytes 49160 | tf_op jit(solution)/shard_map/ppermute | solution.py:358
  33.1 0.0 collective-permute-done.5.even2_ref
  33.1 2.4 %collective-permute-done.6.odd2_ref = f32[32,128]{1,0:T(8,128)S(1)} collective-permute-done((f32[32,128]{1,0:T(8,128)S(1)}, f32[32,128]{1,0:T(8,128)S(1)}, u32[]{:S(2)}, u32[]{:S(2)}) %collective-permute-start.6) | collective-permute-done | bytes 16416 | tf_op jit(solution)/shard_map/ppermute | solution.py:358
  35.6 0.9 %second_solve.1.spec_ref = f32[1920,128]{1,0:T(8,128)S(1)} custom-call(s32[1]{0:T(128)} %bitcast.parity_ref, f32[77]{0:T(128)S(1)} %fusion.couple_ref, f32[1920,128]{1,0:T(8,128)S(1)} %get-tuple-element.20.first_ref, f32[32,128]{1,0:T(8,128)S(1)} %collective-permute-done.3.even_ref, f32[32,128]{1,0:T(8,128)S(1)} %collective-permute-done.4.odd_ref, ...), custom_call_target="tpu_custom_call" | custom-call | flops 1966080 | bytes 4374840 | tf_op jit(solution)/shard_map/second_solve/pallas_call | solution.py:337
  36.4 0.1 copy-done
  36.5 0.1 copy-done.1
  36.6 0.1 copy-done.2
  36.7 1.7 %back_transform.1 = f32[60,32,128]{2,1,0:T(8,128)S(1)} custom-call(f32[1920,128]{1,0:T(8,128)S(1)} %second_solve.1.spec_ref, bf16[512,256]{1,0:T(8,128)(2,1)S(1)} %copy-done.2, f32[32,128]{1,0:T(8,128)S(1)} %copy-done.6, bf16[512,256]{1,0:T(8,128)(2,1)S(1)} %copy-done.1, bf16[512,256]{1,0:T(8,128)(2,1)S(1)} %copy-done), custom_call_target="tpu_custom_call" | custom-call | flops 251658240 | bytes 2768896 | tf_op jit(solution)/shard_map/back_transform/pallas_call | solution.py:337
  38.3 0.1 constant_dynamic-slice_fusion
  38.5 5.0 %collective-permute-start.9 = (f32[60,8,128]{2,1,0:T(8,128)S(1)}, f32[60,8,128]{2,1,0:T(8,128)S(1)}, u32[]{:S(2)}, u32[]{:S(2)}) collective-permute-start(f32[60,8,128]{2,1,0:T(8,128)S(1)} %get-tuple-element.26), channel_id=1, source_target_pairs={{0,3},{1,2},{2,1},{3,0},{4,7},{5,6},{6,5},{7,4},{8,11},{9,10},{10,... | collective-permute-start | bytes 737288 | tf_op jit(solution)/shard_map/ppermute | solution.py:526
  43.4 0.3 collective-permute-start.8
  43.7 0.2 collective-permute-start.7
  44.0 6.2 %collective-permute-done.9 = f32[60,8,128]{2,1,0:T(8,128)S(1)} collective-permute-done((f32[60,8,128]{2,1,0:T(8,128)S(1)}, f32[60,8,128]{2,1,0:T(8,128)S(1)}, u32[]{:S(2)}, u32[]{:S(2)}) %collective-permute-start.9) | collective-permute-done | bytes 245792 | tf_op jit(solution)/shard_map/ppermute | solution.py:526
  50.2 5.2 %collective-permute-done.8 = f32[60,8,128]{2,1,0:T(8,128)S(1)} collective-permute-done((f32[60,8,128]{2,1,0:T(8,128)S(1)}, f32[60,8,128]{2,1,0:T(8,128)S(1)}, u32[]{:S(2)}, u32[]{:S(2)}) %collective-permute-start.8) | collective-permute-done | bytes 245792 | tf_op jit(solution)/shard_map/ppermute | solution.py:526
  55.5 0.0 collective-permute-done.7
  55.5 0.1 pad_maximum_fusion
  55.6 0.6 %gather_fusion.1 = f32[4,60,1024]{2,1,0:T(8,128)S(1)} fusion(f32[60,4,1024]{2,0,1:T(8,128)S(1)} %pad_maximum_fusion, s32[1024]{0:T(1024)S(1)} %pad_clamp_fusion), kind=kCustom, calls=%fused_computation.1 | custom fusion | bytes 1966096 | tf_op jit(solution)/shard_map/jit(_take)/gather | solution.py:529
  56.3 0.2 select_bitcast_fusion
  56.5 1.6 %copy.15 = f32[60,4,1024]{2,1,0:T(4,128)} copy(f32[60,4,1024]{2,0,1:T(8,128)S(1)} %select_bitcast_fusion) | data formatting | bytes 1966080 | tf_op jit(solution)/shard_map/jit(_take)/select_n | solution.py:529
  (23 shorter events, 0.3 us)
Async XLA Ops:
  4.0 6.1 %collective-permute-start = (f32[60,8,128]{2,1,0:T(8,128)}, f32[60,8,128]{2,1,0:T(8,128)S(1)}, u32[]{:S(2)}, u32[]{:S(2)}) collective-permute-start(f32[60,8,128]{2,1,0:T(8,128)} %bitcast.3), channel_id=1, source_target_pairs={{0,1},{1,0},{2,3},{3,2},{4,5},{5,4},{6,7},{7,6},{8,9},{9,8},{10,11... | collective-permute-start | bytes 737288 | tf_op jit(solution)/shard_map/ppermute | solution.py:506
  4.7 8.3 %collective-permute-start.2 = (f32[60,8,128]{2,1,0:T(8,128)S(1)}, f32[60,8,128]{2,1,0:T(8,128)}, u32[]{:S(2)}, u32[]{:S(2)}) collective-permute-start(f32[60,8,128]{2,1,0:T(8,128)S(1)} %bitcast.31), channel_id=1, source_target_pairs={{0,3},{1,2},{2,1},{3,0},{4,7},{5,6},{6,5},{7,4},{8,11},{9,10},{10,... | collective-permute-start | bytes 737288 | tf_op jit(solution)/shard_map/ppermute | solution.py:506
  5.8 11.5 %collective-permute-start.1 = (f32[60,8,128]{2,1,0:T(8,128)S(1)}, f32[60,8,128]{2,1,0:T(8,128)}, u32[]{:S(2)}, u32[]{:S(2)}) collective-permute-start(f32[60,8,128]{2,1,0:T(8,128)S(1)} %bitcast.30), channel_id=1, source_target_pairs={{0,2},{1,3},{2,0},{3,1},{4,6},{5,7},{6,4},{7,5},{8,10},{9,11},{10,... | collective-permute-start | bytes 737288 | tf_op jit(solution)/shard_map/ppermute | solution.py:506
  6.1 2.1 %copy-start.10 = (f32[480]{0:T(512)S(1)}, f32[480]{0:T(512)}, u32[]{:S(2)}) copy-start(f32[480]{0:T(512)} %param.13) | copy-start | bytes 5764
  6.1 0.7 %copy-start.11 = (f32[4]{0:T(128)S(1)}, f32[4]{0:T(128)}, u32[]{:S(2)}) copy-start(f32[4]{0:T(128)} %param.15) | copy-start | bytes 52
  6.7 0.7 %copy-start.9 = (f32[479]{0:T(512)S(1)}, f32[479]{0:T(512)}, u32[]{:S(2)}) copy-start(f32[479]{0:T(512)} %param.14) | copy-start | bytes 5752
  7.4 1.7 %copy-start.7 = (f32[32,128]{1,0:T(8,128)S(1)}, f32[32,128]{1,0:T(8,128)}, u32[]{:S(2)}) copy-start(f32[32,128]{1,0:T(8,128)} %constant.123.eigen_ref) | copy-start | bytes 49156
  10.2 7.1 %copy-start.8 = (f32[60,8,128]{2,1,0:T(8,128)}, f32[60,8,128]{2,1,0:T(8,128)S(1)}, u32[]{:S(2)}) copy-start(f32[60,8,128]{2,1,0:T(8,128)S(1)} %collective-permute-done) | copy-start | bytes 737284
  20.2 1.5 %copy-start.3 = (bf16[512,256]{1,0:T(8,128)(2,1)S(1)}, bf16[512,256]{1,0:T(8,128)(2,1)}, u32[]{:S(2)}) copy-start(bf16[512,256]{1,0:T(8,128)(2,1)} %constant.114.clone.special_ref) | copy-start | bytes 786436
  20.2 1.5 %copy-start.4 = (bf16[512,256]{1,0:T(8,128)(2,1)S(1)}, bf16[512,256]{1,0:T(8,128)(2,1)}, u32[]{:S(2)}) copy-start(bf16[512,256]{1,0:T(8,128)(2,1)} %constant.112.clone.second_ref) | copy-start | bytes 786436
  20.2 1.5 %copy-start.5 = (bf16[512,256]{1,0:T(8,128)(2,1)S(1)}, bf16[512,256]{1,0:T(8,128)(2,1)}, u32[]{:S(2)}) copy-start(bf16[512,256]{1,0:T(8,128)(2,1)} %constant.110.clone.first_ref) | copy-start | bytes 786436
  20.2 1.5 %copy-start.6 = (f32[32,128]{1,0:T(8,128)S(1)}, f32[32,128]{1,0:T(8,128)}, u32[]{:S(2)}) copy-start(f32[32,128]{1,0:T(8,128)} %constant.116.clone.turn_ref) | copy-start | bytes 49156
  22.8 3.3 %collective-permute-start.3 = (f32[32,128]{1,0:T(8,128)S(1)}, f32[32,128]{1,0:T(8,128)S(1)}, u32[]{:S(2)}, u32[]{:S(2)}) collective-permute-start(f32[32,128]{1,0:T(8,128)S(1)} %get-tuple-element.16), channel_id=1, source_target_pairs={{0,4},{4,0},{8,12},{12,8},{16,20},{20,16},{24,28},{28,24},{1,5},{5... | collective-permute-start | bytes 49160 | tf_op jit(solution)/shard_map/ppermute | solution.py:358
  24.1 5.4 %collective-permute-start.4 = (f32[32,128]{1,0:T(8,128)S(1)}, f32[32,128]{1,0:T(8,128)S(1)}, u32[]{:S(2)}, u32[]{:S(2)}) collective-permute-start(f32[32,128]{1,0:T(8,128)S(1)} %get-tuple-element.17), channel_id=1, source_target_pairs={{4,8},{8,4},{12,16},{16,12},{20,24},{24,20},{5,9},{9,5},{13,17},{1... | collective-permute-start | bytes 49160 | tf_op jit(solution)/shard_map/ppermute | solution.py:358
  29.8 3.3 %collective-permute-start.5 = (f32[32,128]{1,0:T(8,128)S(1)}, f32[32,128]{1,0:T(8,128)S(1)}, u32[]{:S(2)}, u32[]{:S(2)}) collective-permute-start(f32[32,128]{1,0:T(8,128)S(1)} %get-tuple-element.21), channel_id=1, source_target_pairs={{0,4},{4,0},{8,12},{12,8},{16,20},{20,16},{24,28},{28,24},{1,5},{5... | collective-permute-start | bytes 49160 | tf_op jit(solution)/shard_map/ppermute | solution.py:358
  30.1 5.5 %collective-permute-start.6 = (f32[32,128]{1,0:T(8,128)S(1)}, f32[32,128]{1,0:T(8,128)S(1)}, u32[]{:S(2)}, u32[]{:S(2)}) collective-permute-start(f32[32,128]{1,0:T(8,128)S(1)} %get-tuple-element.22), channel_id=1, source_target_pairs={{4,8},{8,4},{12,16},{16,12},{20,24},{24,20},{5,9},{9,5},{13,17},{1... | collective-permute-start | bytes 49160 | tf_op jit(solution)/shard_map/ppermute | solution.py:358
  35.5 1.0 %copy-start = (bf16[512,256]{1,0:T(8,128)(2,1)S(1)}, bf16[512,256]{1,0:T(8,128)(2,1)}, u32[]{:S(2)}) copy-start(bf16[512,256]{1,0:T(8,128)(2,1)} %constant.115.clone.special_ref) | copy-start | bytes 786436
  35.5 1.0 %copy-start.1 = (bf16[512,256]{1,0:T(8,128)(2,1)S(1)}, bf16[512,256]{1,0:T(8,128)(2,1)}, u32[]{:S(2)}) copy-start(bf16[512,256]{1,0:T(8,128)(2,1)} %constant.113.clone.second_ref) | copy-start | bytes 786436
  35.5 1.1 %copy-start.2 = (bf16[512,256]{1,0:T(8,128)(2,1)S(1)}, bf16[512,256]{1,0:T(8,128)(2,1)}, u32[]{:S(2)}) copy-start(bf16[512,256]{1,0:T(8,128)(2,1)} %constant.111.clone.first_ref) | copy-start | bytes 786436
  38.5 11.7 %collective-permute-start.9 = (f32[60,8,128]{2,1,0:T(8,128)S(1)}, f32[60,8,128]{2,1,0:T(8,128)S(1)}, u32[]{:S(2)}, u32[]{:S(2)}) collective-permute-start(f32[60,8,128]{2,1,0:T(8,128)S(1)} %get-tuple-element.26), channel_id=1, source_target_pairs={{0,3},{1,2},{2,1},{3,0},{4,7},{5,6},{6,5},{7,4},{8,11},{9,10},{10,... | collective-permute-start | bytes 737288 | tf_op jit(solution)/shard_map/ppermute | solution.py:526
  43.4 12.0 %collective-permute-start.8 = (f32[60,8,128]{2,1,0:T(8,128)S(1)}, f32[60,8,128]{2,1,0:T(8,128)S(1)}, u32[]{:S(2)}, u32[]{:S(2)}) collective-permute-start(f32[60,8,128]{2,1,0:T(8,128)S(1)} %get-tuple-element.27), channel_id=1, source_target_pairs={{0,2},{1,3},{2,0},{3,1},{4,6},{5,7},{6,4},{7,5},{8,10},{9,11},{10,... | collective-permute-start | bytes 737288 | tf_op jit(solution)/shard_map/ppermute | solution.py:526
  43.7 11.8 %collective-permute-start.7 = (f32[60,8,128]{2,1,0:T(8,128)S(1)}, f32[60,8,128]{2,1,0:T(8,128)S(1)}, u32[]{:S(2)}, u32[]{:S(2)}) collective-permute-start(f32[60,8,128]{2,1,0:T(8,128)S(1)} %get-tuple-element.28), channel_id=1, source_target_pairs={{0,1},{1,0},{2,3},{3,2},{4,5},{5,4},{6,7},{7,6},{8,9},{9,8},{10,11... | collective-permute-start | bytes 737288 | tf_op jit(solution)/shard_map/ppermute | solution.py:526
where the time goes:
time: 58.4 us; the launch traced here: 58.1 us
  waiting for transfers between devices  24.3 us (42%)
  starting transfers between devices  14.1 us (24%)
  local copies, waits for them, and re-layouts  9.91 us (17%)
  Pallas kernels  4.98 us (9%)
  other arithmetic  4.56 us (8%)
    ppermute x3, waiting for transfers between devices, return_levels(): piece = lax.ppermute(piece, 'lon', [(d, d ^ mask) for d in range(size)])  11.4 us
    ppermute x3, waiting for transfers between devices, exchange_levels(): piece = lax.ppermute(piece, 'lon', [(d, d ^ mask) for d in range(size)])  7.1 us
    ppermute x2, waiting for transfers between devices, swap(): lax.ppermute(value_odd, 'lat', odd)  5.77 us
    ppermute x3, starting transfers between devices, return_levels(): piece = lax.ppermute(piece, 'lon', [(d, d ^ mask) for d in range(size)])  5.44 us
    ppermute x2, starting transfers between devices, swap(): lax.ppermute(value_odd, 'lat', odd)  5.03 us
    pallas_call x6, Pallas kernels, call(): pl.pallas_call(body, out_shape=[jax.ShapeDtypeStruct(s, jnp.float32) for...  4.98 us
    dynamic_slice x1, local copies, waits for them, and re-layouts, exchange_levels(): piece = lax.dynamic_index_in_dim(right_side, lon_at ^ mask, 1, False)  4.02 us
    ppermute x3, starting transfers between devices, exchange_levels(): piece = lax.ppermute(piece, 'lon', [(d, d ^ mask) for d in range(size)])  2.03 us
  transfers between devices with their start and end apart: 10, of which 6 were waited for; matrix products, arithmetic and copies ran while one was open for 4% of the time, Pallas kernels for 2%

commit v1 on v0

--- a/solution.py
+++ b/solution.py
@@ -358,52 +358,220 @@
     return lax.ppermute(value_even, "lat", even), lax.ppermute(value_odd, "lat", odd)
 
 
-def on_device(right_side, lon_coef, lat_coef, level_scale):
-    rows, levels, lon_count = right_side.shape
-    lon_size = lax.axis_size("lon")
-    assert lon_size % levels == 0 and N1 % lon_size == 0 and rows % 2 == 0
-    sharers = lon_size // levels
-    groups = 2 * GROUPS // sharers
-    part_rows = rows // sharers
-    digits = N1 // lon_size
-    const = {k: jnp.asarray(v) for k, v in tables().items()}
-    lon_at = lax.axis_index("lon")
-    lat_at = lax.axis_index("lat")
-    level = lon_at // sharers
-    parity = (lat_at % 2).astype(jnp.int32)
-    row_first = lat_at * rows
+def swap_levels(pieces):
+    size = len(pieces)
+    return [pieces[0]] + [
+        lax.ppermute(pieces[mask], "lon", [(d, d ^ mask) for d in range(size)]) for mask in range(1, size)
+    ]
+
+
+def operator_parts(rows, level, lon_coef, lat_coef, level_scale):
+    row_first = lax.axis_index("lat") * rows
     extent = rows + 2 * OV
     scale = lax.dynamic_index_in_dim(level_scale, level, 0, False)
     lon_window = scale * lax.dynamic_slice_in_dim(jnp.pad(lon_coef, (OV, OV)), row_first, extent)
     couple = scale * lax.dynamic_slice_in_dim(
         jnp.pad(lat_coef, (OV + 1, OV + 2)), row_first, extent + 1
     )
-    eigen = const["eigen"]
-    if sharers > 1:
-        eigen = lax.dynamic_slice_in_dim(eigen, (lon_at % sharers) * (groups // 2), groups // 2, axis=1)
-    eigen = eigen.reshape(groups, N2)
-    wide = N2
-    block = (rows * groups, wide)
-    row = (groups, wide)
-    ratio, inverse, edge = call(
+    return lon_window, couple
+
+
+def factor(rows, groups, lon_window, couple, eigen):
+    block = (rows * groups, N2)
+    return call(
         functools.partial(factor_kernel, rows),
-        [block, block, (21 * groups, wide)],
+        [block, block, (21 * groups, N2)],
         [lon_window, couple, eigen],
         [SMEM, SMEM, VMEM],
         [],
-        rows * groups * wide * 20,
+        rows * groups * N2 * 20,
         "factor",
     )
-    if sharers == 1:
-        pieces = exchange_levels(right_side, lon_at)
-    else:
-        pieces = None
-        send = right_side.reshape(sharers, part_rows, levels, lon_count).transpose(2, 0, 1, 3)
-        send = send.reshape(lon_size, part_rows, digits, N2)
-        got = lax.all_to_all(send, "lon", 0, 0, tiled=True)
-        points = got.transpose(1, 0, 2, 3).reshape(part_rows, N1, N2)
-    if sharers == 1:
-        points = place_pieces(pieces, lon_at, digits)
+
+
+def vmem(*shape):
+    return pltpu.VMEM(shape, jnp.float32)
+
+
+def rows_of(ref, groups, first=0):
+    return lambda i: ref[(i - first) * groups : (i - first + 1) * groups, :]
+
+
+def fill(full_ref, pieces, where, rows):
+    padded = full_ref.shape[0]
+    width = N1 // len(pieces)
+    for mask, piece in enumerate(pieces):
+        at = pl.multiple_of((where ^ mask) * width, width)
+        full_ref[:rows, pl.ds(at, width), :] = piece[...].reshape(rows, width, N2)
+    if padded > rows:
+        full_ref[rows:] = jnp.zeros((padded - rows, N1, N2), jnp.float32)
+
+
+def on_device(right_side, lon_coef, lat_coef, level_scale):
+    const = {k: jnp.asarray(v) for k, v in tables().items()}
+    if lax.axis_size("lon") != right_side.shape[1]:
+        return shared_levels(const, right_side, lon_coef, lat_coef, level_scale)
+    return whole_levels(const, right_side, lon_coef, lat_coef, level_scale)
+
+
+def whole_levels(const, right_side, lon_coef, lat_coef, level_scale):
+    rows, levels, lon_count = right_side.shape
+    digits = N1 // levels
+    groups = 2 * GROUPS
+    lon_at = lax.axis_index("lon").astype(jnp.int32)
+    parity = (lax.axis_index("lat") % 2).astype(jnp.int32)
+    place = jnp.stack([lon_at, parity])
+    lon_window, couple = operator_parts(rows, lon_at, lon_coef, lat_coef, level_scale)
+    ratio, inverse, edge = factor(rows, groups, lon_window, couple, const["eigen"].reshape(groups, N2))
+    block = (rows * groups, N2)
+    row = (groups, N2)
+    ends = 2 * OV
+    inner = rows - ends
+    by_row = right_side.reshape(rows, levels, digits, N2).transpose(0, 2, 1, 3).reshape(-1, N2)
+
+    def pack(place_ref, in_ref, *out_refs):
+        for mask in range(levels):
+            level = place_ref[0] ^ mask
+            end_ref, inner_ref = out_refs[2 * mask : 2 * mask + 2]
+            span = OV * digits
+            end_ref[:span, :] = in_ref[pl.ds(level, span, stride=levels), :]
+            inner_ref[...] = in_ref[pl.ds(level + levels * span, inner * digits, stride=levels), :]
+            end_ref[span:, :] = in_ref[pl.ds(level + levels * (rows - OV) * digits, span, stride=levels), :]
+
+    packed = call(
+        pack, [(ends * digits, N2), (inner * digits, N2)] * levels, [place, by_row], [SMEM, VMEM], [], 0, "pack"
+    )
+    end_pieces = swap_levels(packed[0::2])
+    inner_pieces = swap_levels(packed[1::2])
+    forward = [const["first"], const["turn"], const["second"], const["special"]]
+    pad_ends, pad_inner = pad_rows(ends), pad_rows(inner)
+
+    def ends_body(place_ref, *refs):
+        pieces, refs = refs[:levels], refs[levels:]
+        tables_in, edge_ref = refs[:4], refs[4]
+        spec_ref, top_ref, bottom_ref, even_ref, odd_ref, full_ref, mid_ref = refs[5:]
+        fill(full_ref, pieces, place_ref[0], ends)
+        forward_rows(full_ref, ends, *tables_in, mid_ref, spec_ref)
+        top, bottom = edge_sums(rows_of(spec_ref, groups), rows_of(spec_ref, groups, -OV), edge_ref, groups)
+        top_ref[...] = top
+        bottom_ref[...] = bottom
+        swap_out(place_ref[1], top, bottom, even_ref, odd_ref)
+
+    end_spectral, sent_top, sent_bottom, even, odd = call(
+        ends_body,
+        [(ends * groups, N2)] + [row] * 4,
+        [place, *end_pieces, *forward, edge],
+        [SMEM] + [VMEM] * (levels + 5),
+        [vmem(pad_ends, N1, N2), vmem(pad_ends * N1, N2)],
+        ends * NLON * 256 * 4,
+        "ends",
+    )
+    even, odd = swap(even, odd)
+
+    def inner_body(place_ref, *refs):
+        pieces, refs = refs[:levels], refs[levels:]
+        tables_in, refs = refs[:4], refs[4:]
+        ends_ref, even_ref, odd_ref, ratio_ref, inverse_ref, edge_ref = refs[:6]
+        out_ref, even_out, odd_out, full_ref, mid_ref, spec_ref = refs[6:]
+        fill(full_ref, pieces, place_ref[0], inner)
+        forward_rows(full_ref, inner, *tables_in, mid_ref, spec_ref)
+        low, high = swap_in(place_ref[1], even_ref[...], odd_ref[...])
+
+        def spec_row(i):
+            if i < OV:
+                return rows_of(ends_ref, groups)(i)
+            if i >= rows - OV:
+                return rows_of(ends_ref, groups, rows - ends)(i)
+            return rows_of(spec_ref, groups, OV)(i)
+
+        solve_first(rows, groups, spec_row, low, high, ratio_ref, inverse_ref, edge_ref, out_ref)
+        swap_out(place_ref[1], out_ref[(rows - 1) * groups :, :], out_ref[:groups, :], even_out, odd_out)
+
+    iterate, even2, odd2 = call(
+        inner_body,
+        [block, row, row],
+        [place, *inner_pieces, *forward, end_spectral, even, odd, ratio, inverse, edge],
+        [SMEM] + [VMEM] * (levels + 10),
+        [vmem(pad_inner, N1, N2), vmem(pad_inner * N1, N2), vmem(inner * N1, N2)],
+        inner * NLON * 256 * 4,
+        "inner",
+    )
+    even2, odd2 = swap(even2, odd2)
+    pad_all = pad_rows(rows)
+
+    def second_body(place_ref, couple_ref, *refs):
+        first_ref, even_ref, odd_ref, even2_ref, odd2_ref, top_ref, bottom_ref = refs[:7]
+        ratio_ref, inverse_ref, edge_ref = refs[7:10]
+        tables_in = refs[10:14]
+        out_refs = refs[14 : 14 + levels]
+        sum_ref, mid_ref, full_ref = refs[14 + levels :]
+        second_part(
+            rows, groups, place_ref[1], couple_ref, first_ref, even_ref, odd_ref, even2_ref, odd2_ref,
+            top_ref, bottom_ref, ratio_ref, inverse_ref, edge_ref, sum_ref, mid_ref,
+        )
+        backward_rows(sum_ref, rows, *tables_in, mid_ref, full_ref)
+        for mask in range(levels):
+            at = pl.multiple_of((place_ref[0] ^ mask) * digits, digits)
+            out_refs[mask][...] = full_ref[:rows, pl.ds(at, digits), :].reshape(rows * digits, N2)
+
+    backward = [const["first_back"], const["turn"], const["second_back"], const["special_back"]]
+    pieces = call(
+        second_body,
+        [(rows * digits, N2)] * levels,
+        [place, couple, iterate, even, odd, even2, odd2, sent_top, sent_bottom, ratio, inverse, edge, *backward],
+        [SMEM, SMEM] + [VMEM] * 14,
+        [vmem(*block), vmem(pad_all * N1, N2), vmem(pad_all, N1, N2)],
+        rows * NLON * 256 * 4,
+        "second",
+    )
+    pieces = swap_levels(pieces)
+
+    def unpack(place_ref, *refs):
+        out_ref = refs[levels]
+        for mask in range(levels):
+            out_ref[pl.ds(place_ref[0] ^ mask, rows * digits, stride=levels), :] = refs[mask][...]
+
+    (out,) = call(
+        unpack, [(rows * levels * digits, N2)], [place, *pieces], [SMEM] + [VMEM] * levels, [], 0, "unpack"
+    )
+    return out.reshape(rows, digits, levels, N2).transpose(0, 2, 1, 3).reshape(right_side.shape)
+
+
+def second_part(
+    rows, groups, parity, couple_ref, first_ref, even_ref, odd_ref, even2_ref, odd2_ref, top_ref, bottom_ref,
+    ratio_ref, inverse_ref, edge_ref, out_ref, mid_ref,
+):
+    got_top, got_bottom = swap_in(parity, even_ref[...], odd_ref[...])
+    low, high = swap_in(parity, even2_ref[...], odd2_ref[...])
+    solve_second(
+        rows, groups, couple_ref[OV], couple_ref[OV + rows],
+        first_ref[:groups, :], first_ref[(rows - 1) * groups :, :],
+        got_top, got_bottom, top_ref[...], bottom_ref[...], low, high,
+        ratio_ref, inverse_ref, edge_ref, first_ref, out_ref, mid_ref,
+    )
+
+
+def shared_levels(const, right_side, lon_coef, lat_coef, level_scale):
+    rows, levels, lon_count = right_side.shape
+    lon_size = lax.axis_size("lon")
+    assert lon_size % levels == 0 and GROUPS % (lon_size // levels) == 0 and rows % (lon_size // levels) == 0
+    sharers = lon_size // levels
+    groups = 2 * GROUPS // sharers
+    part_rows = rows // sharers
+    digits = N1 // lon_size
+    lon_at = lax.axis_index("lon")
+    parity = (lax.axis_index("lat") % 2).astype(jnp.int32).reshape(1)
+    lon_window, couple = operator_parts(rows, lon_at // sharers, lon_coef, lat_coef, level_scale)
+    eigen = lax.dynamic_slice_in_dim(
+        const["eigen"], (lon_at % sharers) * (groups // 2), groups // 2, axis=1
+    ).reshape(groups, N2)
+    ratio, inverse, edge = factor(rows, groups, lon_window, couple, eigen)
+    block = (rows * groups, N2)
+    row = (groups, N2)
+    send = right_side.reshape(sharers, part_rows, levels, lon_count).transpose(2, 0, 1, 3)
+    send = send.reshape(lon_size, part_rows, digits, N2)
+    got = lax.all_to_all(send, "lon", 0, 0, tiled=True)
+    points = got.transpose(1, 0, 2, 3).reshape(part_rows, N1, N2)
     padded = pad_rows(part_rows)
 
     def transform(points_ref, first_ref, turn_ref, second_ref, special_ref, out_ref, full_ref, mid_ref):
@@ -414,65 +582,59 @@
 
     (spectral,) = call(
         transform,
-        [(part_rows * N1, wide)],
+        [(part_rows * N1, N2)],
         [points, const["first"], const["turn"], const["second"], const["special"]],
         [VMEM] * 5,
-        [pltpu.VMEM((padded, N1, N2), jnp.float32), pltpu.VMEM((padded * N1, wide), jnp.float32)],
+        [vmem(padded, N1, N2), vmem(padded * N1, N2)],
         part_rows * NLON * 256 * 4,
         "transform",
     )
-    if sharers > 1:
-        spectral = to_coefs(spectral, sharers, part_rows, groups)
-    parity_arg = parity.reshape(1)
+    spectral = to_coefs(spectral, sharers, part_rows, groups)
 
     def edges(parity_ref, spec_ref, edge_ref, top_ref, bottom_ref, even_ref, odd_ref):
-        def spec_row(i):
-            return spec_ref[i * groups : (i + 1) * groups, :]
-
-        top, bottom = edge_sums(spec_row, lambda i: spec_row(rows - OV + i), edge_ref, groups)
+        top, bottom = edge_sums(
+            rows_of(spec_ref, groups), rows_of(spec_ref, groups, OV - rows), edge_ref, groups
+        )
         top_ref[...] = top
         bottom_ref[...] = bottom
         swap_out(parity_ref[0], top, bottom, even_ref, odd_ref)
 
     sent_top, sent_bottom, even, odd = call(
-        edges, [row] * 4, [parity_arg, spectral, edge], [SMEM, VMEM, VMEM], [], groups * wide * 32, "edges"
+        edges, [row] * 4, [parity, spectral, edge], [SMEM, VMEM, VMEM], [], groups * N2 * 32, "edges"
     )
     even, odd = swap(even, odd)
 
     def first(parity_ref, spec_ref, even_ref, odd_ref, ratio_ref, inverse_ref, edge_ref, out_ref, e_ref, o_ref):
         low, high = swap_in(parity_ref[0], even_ref[...], odd_ref[...])
         solve_first(
-            rows, groups, lambda i: spec_ref[i * groups : (i + 1) * groups, :], low, high,
-            ratio_ref, inverse_ref, edge_ref, out_ref,
+            rows, groups, rows_of(spec_ref, groups), low, high, ratio_ref, inverse_ref, edge_ref, out_ref
         )
         swap_out(parity_ref[0], out_ref[(rows - 1) * groups :, :], out_ref[:groups, :], e_ref, o_ref)
 
     iterate, even2, odd2 = call(
-        first, [block, row, row], [parity_arg, spectral, even, odd, ratio, inverse, edge],
-        [SMEM] + [VMEM] * 6, [], rows * groups * wide * 8, "first_solve",
+        first,
+        [block, row, row],
+        [parity, spectral, even, odd, ratio, inverse, edge],
+        [SMEM] + [VMEM] * 6,
+        [],
+        rows * groups * N2 * 8,
+        "first_solve",
     )
     even2, odd2 = swap(even2, odd2)
 
-    def second(
-        parity_ref, couple_ref, first_ref, even_ref, odd_ref, even2_ref, odd2_ref, top_ref, bottom_ref,
-        ratio_ref, inverse_ref, edge_ref, out_ref, mid_ref,
-    ):
-        got_top, got_bottom = swap_in(parity_ref[0], even_ref[...], odd_ref[...])
-        low, high = swap_in(parity_ref[0], even2_ref[...], odd2_ref[...])
-        solve_second(
-            rows, groups, couple_ref[OV], couple_ref[OV + rows],
-            first_ref[:groups, :], first_ref[(rows - 1) * groups :, :],
-            got_top, got_bottom, top_ref[...], bottom_ref[...], low, high,
-            ratio_ref, inverse_ref, edge_ref, first_ref, out_ref, mid_ref,
-        )
+    def second(parity_ref, *refs):
+        second_part(rows, groups, parity_ref[0], *refs)
 
     (iterate,) = call(
-        second, [block],
-        [parity_arg, couple, iterate, even, odd, even2, odd2, sent_top, sent_bottom, ratio, inverse, edge],
-        [SMEM, SMEM] + [VMEM] * 10, [pltpu.VMEM(block, jnp.float32)], rows * groups * wide * 8, "second_solve",
-    )
-    if sharers > 1:
-        iterate = to_rows(iterate, sharers, part_rows, groups)
+        second,
+        [block],
+        [parity, couple, iterate, even, odd, even2, odd2, sent_top, sent_bottom, ratio, inverse, edge],
+        [SMEM, SMEM] + [VMEM] * 10,
+        [vmem(*block)],
+        rows * groups * N2 * 8,
+        "second_solve",
+    )
+    iterate = to_rows(iterate, sharers, part_rows, groups)
 
     def back(spec_ref, first_ref, turn_ref, second_ref, special_ref, out_ref, mid_ref, full_ref):
         backward_rows(spec_ref, part_rows, first_ref, turn_ref, second_ref, special_ref, mid_ref, full_ref)
@@ -483,50 +645,14 @@
         [(part_rows, N1, N2)],
         [iterate, const["first_back"], const["turn"], const["second_back"], const["special_back"]],
         [VMEM] * 5,
-        [pltpu.VMEM((padded * N1, wide), jnp.float32), pltpu.VMEM((padded, N1, N2), jnp.float32)],
+        [vmem(padded * N1, N2), vmem(padded, N1, N2)],
         part_rows * NLON * 256 * 4,
         "back_transform",
     )
-    if sharers == 1:
-        return return_levels(points, lon_at, digits, right_side.shape)
     send = points.reshape(part_rows, lon_size, digits, N2).transpose(1, 0, 2, 3)
     got = lax.all_to_all(send, "lon", 0, 0, tiled=True)
     got = got.reshape(levels, sharers, part_rows, lon_count).transpose(1, 2, 0, 3)
     return got.reshape(rows, levels, lon_count)
-
-
-def exchange_levels(right_side, lon_at):
-    rows, levels, lon_count = right_side.shape
-    size = levels
-    pieces = []
-    for mask in range(size):
-        piece = lax.dynamic_index_in_dim(right_side, lon_at ^ mask, 1, False)
-        piece = piece.reshape(rows, lon_count // N2, N2)
-        if mask:
-            piece = lax.ppermute(piece, "lon", [(d, d ^ mask) for d in range(size)])
-        pieces.append(piece)
-    return pieces
-
-
-def place_pieces(pieces, lon_at, digits):
-    stacked = jnp.stack(pieces, axis=1)
-    order = lon_at ^ jnp.arange(len(pieces))
-    stacked = jnp.take(stacked, order, axis=1)
-    return stacked.reshape(stacked.shape[0], N1, N2)
-
-
-def return_levels(points, lon_at, digits, shape):
-    rows, levels, lon_count = shape
-    size = levels
-    parts = points.reshape(rows, size, digits, N2)
-    pieces = []
-    for mask in range(size):
-        piece = lax.dynamic_index_in_dim(parts, lon_at ^ mask, 1, False)
-        if mask:
-            piece = lax.ppermute(piece, "lon", [(d, d ^ mask) for d in range(size)])
-        pieces.append(piece.reshape(rows, lon_count))
-    stacked = jnp.stack(pieces, axis=1)
-    return jnp.take(stacked, lon_at ^ jnp.arange(size), axis=1)
 
 
 def level_groups(sharers):

time: 58.4 us -> 52 us (0.89)
  local copies, waits for them, and re-layouts: 9.91 us -> 1.93 us
  Pallas kernels: 4.98 us -> 9.15 us
  other arithmetic: 4.56 us -> 1.54 us
  starting transfers between devices: 14.1 us -> 15.7 us
  waiting for transfers between devices: 24.3 us -> 23.3 us
    dynamic_slice x3 -> x1, local copies, waits for them, and re-layouts: 4.8 us -> 0.58 us  [operator_parts(): scale = lax.dynamic_index_in_dim(level_scale, level, 0, False)]
    pallas_call x6, Pallas kernels: 4.98 us -> 9.15 us  [call(): pl.pallas_call(body, out_shape=[jax.ShapeDtypeStruct(s, jnp.float32) for...]
    gather x2 -> x0, local copies, waits for them, and re-layouts: 2.24 us -> none  [the longest x1 1.62 us: place_pieces(): stacked = jnp.take(stacked, order, axis=1)]
    select_n x3 -> x0, other arithmetic: 1.67 us -> none  [the longest x1 1.46 us: place_pieces(): stacked = jnp.take(stacked, order, axis=1)]
    select_n x1 -> x0, local copies, waits for them, and re-layouts: 1.59 us -> none  [return_levels(): return jnp.take(stacked, lon_at ^ jnp.arange(size), axis=1)]
    ppermute x6 -> x9, starting transfers between devices: 7.47 us -> 9.05 us  [swap_levels(): lax.ppermute(pieces[mask], 'lon', [(d, d ^ mask) for d in range(size)])]
    another operation x2 -> x1, other arithmetic: 1.35 us -> 0.07 us  [whole_levels(): place = jnp.stack([lon_at, parity])]
    ppermute x6 -> x9, waiting for transfers between devices: 18.5 us -> 17.6 us  [swap_levels(): lax.ppermute(pieces[mask], 'lon', [(d, d ^ mask) for d in range(size)])]
  transfers between devices with their start and end apart: 10 -> 13, of which waited for: 6 -> 5; matrix products, arithmetic and copies ran while one was open for 4% -> 4% of each run, Pallas kernels for 2% -> 4%
where the time goes in v1:
time: 52 us; the launch traced here: 51.7 us
  waiting for transfers between devices  23.3 us (45%)
  starting transfers between devices  15.7 us (30%)
  Pallas kernels  9.15 us (18%)
  local copies, waits for them, and re-layouts  1.93 us (4%)
  other arithmetic  1.54 us (3%)
    ppermute x9, waiting for transfers between devices, swap_levels(): lax.ppermute(pieces[mask], 'lon', [(d, d ^ mask) for d in range(size)])  17.6 us
    pallas_call x6, Pallas kernels, call(): pl.pallas_call(body, out_shape=[jax.ShapeDtypeStruct(s, jnp.float32) for...  9.15 us
    ppermute x9, starting transfers between devices, swap_levels(): lax.ppermute(pieces[mask], 'lon', [(d, d ^ mask) for d in range(size)])  9.05 us
    ppermute x2, waiting for transfers between devices, swap(): lax.ppermute(value_odd, 'lat', odd)  5.67 us
    ppermute x2, starting transfers between devices, swap(): lax.ppermute(value_odd, 'lat', odd)  5.03 us
    ppermute x2, starting transfers between devices, swap(): lax.ppermute(value_even, 'lat', even)  1.63 us
    unnamed x24, local copies, waits for them, and re-layouts  1.35 us
  transfers between devices with their start and end apart: 13, of which 5 were waited for; matrix products, arithmetic and copies ran while one was open for 4% of the time, Pallas kernels for 4%

profile of v1, /device:TPU:17, one launch (start us, length us, event | category | flops | bytes accessed | tf_op | source)
XLA Modules:
  0.0 51.7 jit_solution(2512714955391594710)
XLA Ops:
  0.0 0.1 pad_add_fusion.place_ref
  0.1 1.2 %copy-done.3 = f32[60,4,1024]{2,1,0:T(4,128)S(1)} copy-done((f32[60,4,1024]{2,1,0:T(4,128)S(1)}, f32[60,4,1024]{2,1,0:T(4,128)}, u32[]{:S(2)}) %copy-start.3) | copy-done | bytes 983064
  1.3 0.7 %pack.1 = (f32[128,128]{1,0:T(8,128)S(1)}, f32[352,128]{1,0:T(8,128)S(1)}, f32[128,128]{1,0:T(8,128)S(1)}, f32[352,128]{1,0:T(8,128)S(1)}, f32[128,128]{1,0:T(8,...) custom-call(s32[2]{0:T(128)S(1)} %pad_add_fusion.place_ref, f32[1920,128]{1,0:T(8,128)S(1)} %bitcast.13), custom_call_target="tpu_custom_call" | custom-call | bytes 1966088 | tf_op jit(solution)/shard_map/pack/pallas_call | solution.py:337
  2.0 0.7 %collective-permute-start.3 = (f32[128,128]{1,0:T(8,128)S(1)}, f32[128,128]{1,0:T(8,128)S(1)}, u32[]{:S(2)}, u32[]{:S(2)}) collective-permute-start(f32[128,128]{1,0:T(8,128)S(1)} %get-tuple-element.33), channel_id=1, source_target_pairs={{0,1},{1,0},{2,3},{3,2},{4,5},{5,4},{6,7},{7,6},{8,9},{9,8},{10,11... | collective-permute-start | bytes 196616 | tf_op jit(solution)/shard_map/ppermute | solution.py:364
  2.7 1.2 %collective-permute-start.4 = (f32[128,128]{1,0:T(8,128)S(1)}, f32[128,128]{1,0:T(8,128)S(1)}, u32[]{:S(2)}, u32[]{:S(2)}) collective-permute-start(f32[128,128]{1,0:T(8,128)S(1)} %get-tuple-element.34), channel_id=1, source_target_pairs={{0,2},{1,3},{2,0},{3,1},{4,6},{5,7},{6,4},{7,5},{8,10},{9,11},{10,... | collective-permute-start | bytes 196616 | tf_op jit(solution)/shard_map/ppermute | solution.py:364
  3.9 0.3 collective-permute-start
  4.3 0.3 collective-permute-start.1
  4.5 1.5 %collective-permute-start.2 = (f32[352,128]{1,0:T(8,128)S(1)}, f32[352,128]{1,0:T(8,128)S(1)}, u32[]{:S(2)}, u32[]{:S(2)}) collective-permute-start(f32[352,128]{1,0:T(8,128)S(1)} %get-tuple-element.31), channel_id=1, source_target_pairs={{0,3},{1,2},{2,1},{3,0},{4,7},{5,6},{6,5},{7,4},{8,11},{9,10},{10,... | collective-permute-start | bytes 540680 | tf_op jit(solution)/shard_map/ppermute | solution.py:364
  6.1 0.0 copy-done.11
  6.1 0.6 %dynamic_slice.10 = f32[1]{0:T(128)} dynamic-slice(f32[4]{0:T(128)S(1)} %copy-done.11, s32[]{:T(128)S(6)} %select_n.18), dynamic_slice_sizes={1} | dynamic-slice | bytes 12 | tf_op jit(solution)/shard_map/jit(dynamic_index_in_dim)/dynamic_slice | solution.py:371
  6.7 0.1 copy-done.9
  6.8 0.7 %fusion.couple_ref = f32[77]{0:T(128)S(1)} fusion(s32[]{:T(128)S(6)} %select_n.19, f32[479]{0:T(512)S(1)} %copy-done.9, f32[]{:T(128)} %bitcast.2), kind=kLoop, calls=%fused_computation.2 | loop fusion | flops 77 | bytes 2232 | tf_op jit(solution)/shard_map/mul | solution.py:373
  7.5 0.0 collective-permute-done.3.refs_1_
  7.5 0.2 collective-permute-start.5
  7.7 0.0 copy-done.10
  7.7 0.7 %fusion.1.lon_ref = f32[76]{0:T(128)S(1)} fusion(s32[]{:T(128)S(6)} %select_n.20, f32[480]{0:T(512)S(1)} %copy-done.10, f32[]{:T(128)} %bitcast.2), kind=kLoop, calls=%fused_computation.3 | loop fusion | flops 76 | bytes 2232 | tf_op jit(solution)/shard_map/mul | solution.py:372
  8.5 0.0 copy-done.8
  8.5 1.0 %factor.1 = (f32[1920,128]{1,0:T(8,128)S(1)}, f32[1920,128]{1,0:T(8,128)S(1)}, f32[672,128]{1,0:T(8,128)S(1)}) custom-call(f32[76]{0:T(128)S(1)} %fusion.1.lon_ref, f32[77]{0:T(128)S(1)} %fusion.couple_ref, f32[32,128]{1,0:T(8,128)S(1)} %copy-done.8), custom_call_target="tpu_custom_call" | custom-call | flops 4915200 | bytes 2327140 | tf_op jit(solution)/shard_map/factor/pallas_call | solution.py:337
  9.5 0.0 collective-permute-done.4.refs_2_
  9.5 6.3 %collective-permute-done.5.refs_3_ = f32[128,128]{1,0:T(8,128)S(1)} collective-permute-done((f32[128,128]{1,0:T(8,128)S(1)}, f32[128,128]{1,0:T(8,128)S(1)}, u32[]{:S(2)}, u32[]{:S(2)}) %collective-permute-start.5) | collective-permute-done | bytes 65568 | tf_op jit(solution)/shard_map/ppermute | solution.py:364
  15.8 0.0 copy-done
  15.8 0.0 copy-done.1
  15.8 0.0 copy-done.2
  15.8 0.0 copy-done.7
  15.8 1.2 %ends.1 = (f32[512,128]{1,0:T(8,128)S(1)}, f32[32,128]{1,0:T(8,128)S(1)}, f32[32,128]{1,0:T(8,128)S(1)}, f32[32,128]{1,0:T(8,128)S(1)}, f32[32,128]{1,0:T(8,128)S(1)}) custom-call(s32[2]{0:T(128)S(1)} %pad_add_fusion.place_ref, f32[128,128]{1,0:T(8,128)S(1)} %get-tuple-element.32.refs_0_, f32[128,128]{1,0:T(8,128)S(1)} %collective-permute-done.3.refs_1_, ...), custom_call_target="tpu_custom_call" | custom-call | flops 67108864 | bytes 1736712 | tf_op jit(solution)/shard_map/ends/pallas_call | solution.py:337
  17.1 1.3 %collective-permute-start.6 = (f32[32,128]{1,0:T(8,128)S(1)}, f32[32,128]{1,0:T(8,128)S(1)}, u32[]{:S(2)}, u32[]{:S(2)}) collective-permute-start(f32[32,128]{1,0:T(8,128)S(1)} %get-tuple-element.38), channel_id=1, source_target_pairs={{0,4},{4,0},{8,12},{12,8},{16,20},{20,16},{24,28},{28,24},{1,5},{5... | collective-permute-start | bytes 49160 | tf_op jit(solution)/shard_map/ppermute | solution.py:358
  18.4 2.0 %collective-permute-start.7 = (f32[32,128]{1,0:T(8,128)S(1)}, f32[32,128]{1,0:T(8,128)S(1)}, u32[]{:S(2)}, u32[]{:S(2)}) collective-permute-start(f32[32,128]{1,0:T(8,128)S(1)} %get-tuple-element.39), channel_id=1, source_target_pairs={{4,8},{8,4},{12,16},{16,12},{20,24},{24,20},{5,9},{9,5},{13,17},{1... | collective-permute-start | bytes 49160 | tf_op jit(solution)/shard_map/ppermute | solution.py:358
  20.4 0.0 collective-permute-done.6.refs_9_.refs_1_
  20.4 3.3 %collective-permute-done.7.refs_10_.refs_2_ = f32[32,128]{1,0:T(8,128)S(1)} collective-permute-done((f32[32,128]{1,0:T(8,128)S(1)}, f32[32,128]{1,0:T(8,128)S(1)}, u32[]{:S(2)}, u32[]{:S(2)}) %collective-permute-start.7) | collective-permute-done | bytes 16416 | tf_op jit(solution)/shard_map/ppermute | solution.py:358
  23.8 0.0 collective-permute-done.refs_1_
  23.8 0.0 collective-permute-done.1.refs_2_
  23.8 0.0 collective-permute-done.2.refs_3_
  23.8 0.0 copy-start.4
  23.8 0.0 copy-start.5
  23.8 0.0 copy-start.6
  23.8 2.0 %inner.1 = (f32[1920,128]{1,0:T(8,128)S(1)}, f32[32,128]{1,0:T(8,128)S(1)}, f32[32,128]{1,0:T(8,128)S(1)}) custom-call(s32[2]{0:T(128)S(1)} %pad_add_fusion.place_ref, f32[352,128]{1,0:T(8,128)S(1)} %get-tuple-element.28.refs_0_, f32[352,128]{1,0:T(8,128)S(1)} %collective-permute-done.refs_1_, f32[352,128]{1,0:T(8,128)S(1)} %collective-permute-done.1.refs_2_, ...), custom_call_target="tpu_custom_call" | custom-call | flops 184549376 | bytes 5144584 | tf_op jit(solution)/shard_map/inner/pallas_call | solution.py:337
  25.9 0.3 collective-permute-start.8
  26.2 3.0 %collective-permute-start.9 = (f32[32,128]{1,0:T(8,128)S(1)}, f32[32,128]{1,0:T(8,128)S(1)}, u32[]{:S(2)}, u32[]{:S(2)}) collective-permute-start(f32[32,128]{1,0:T(8,128)S(1)} %get-tuple-element.44), channel_id=1, source_target_pairs={{4,8},{8,4},{12,16},{16,12},{20,24},{24,20},{5,9},{9,5},{13,17},{1... | collective-permute-start | bytes 49160 | tf_op jit(solution)/shard_map/ppermute | solution.py:358
  29.2 0.0 collective-permute-done.8.refs_3_
  29.2 2.3 %collective-permute-done.9.refs_4_ = f32[32,128]{1,0:T(8,128)S(1)} collective-permute-done((f32[32,128]{1,0:T(8,128)S(1)}, f32[32,128]{1,0:T(8,128)S(1)}, u32[]{:S(2)}, u32[]{:S(2)}) %collective-permute-start.9) | collective-permute-done | bytes 16416 | tf_op jit(solution)/shard_map/ppermute | solution.py:358
  31.6 2.6 %second.1 = (f32[480,128]{1,0:T(8,128)S(1)}, f32[480,128]{1,0:T(8,128)S(1)}, f32[480,128]{1,0:T(8,128)S(1)}, f32[480,128]{1,0:T(8,128)S(1)}) custom-call(s32[2]{0:T(128)S(1)} %pad_add_fusion.place_ref, f32[77]{0:T(128)S(1)} %fusion.couple_ref, f32[1920,128]{1,0:T(8,128)S(1)} %get-tuple-element.42.refs_0_, ...), custom_call_target="tpu_custom_call" | custom-call | flops 251658240 | bytes 5177660 | tf_op jit(solution)/shard_map/second/pallas_call | solution.py:337
  34.1 3.0 %collective-permute-start.10 = (f32[480,128]{1,0:T(8,128)S(1)}, f32[480,128]{1,0:T(8,128)S(1)}, u32[]{:S(2)}, u32[]{:S(2)}) collective-permute-start(f32[480,128]{1,0:T(8,128)S(1)} %get-tuple-element.48), channel_id=1, source_target_pairs={{0,1},{1,0},{2,3},{3,2},{4,5},{5,4},{6,7},{7,6},{8,9},{9,8},{10,11... | collective-permute-start | bytes 737288 | tf_op jit(solution)/shard_map/ppermute | solution.py:364
  37.1 1.2 %collective-permute-start.11 = (f32[480,128]{1,0:T(8,128)S(1)}, f32[480,128]{1,0:T(8,128)S(1)}, u32[]{:S(2)}, u32[]{:S(2)}) collective-permute-start(f32[480,128]{1,0:T(8,128)S(1)} %get-tuple-element.49), channel_id=1, source_target_pairs={{0,2},{1,3},{2,0},{3,1},{4,6},{5,7},{6,4},{7,5},{8,10},{9,11},{10,... | collective-permute-start | bytes 737288 | tf_op jit(solution)/shard_map/ppermute | solution.py:364
  38.3 0.5 collective-permute-start.12
  38.9 0.0 collective-permute-done.10.refs_1_
  38.9 5.8 %collective-permute-done.11.refs_2_ = f32[480,128]{1,0:T(8,128)S(1)} collective-permute-done((f32[480,128]{1,0:T(8,128)S(1)}, f32[480,128]{1,0:T(8,128)S(1)}, u32[]{:S(2)}, u32[]{:S(2)}) %collective-permute-start.11) | collective-permute-done | bytes 245792 | tf_op jit(solution)/shard_map/ppermute | solution.py:364
  44.7 5.4 %collective-permute-done.12.refs_3_ = f32[480,128]{1,0:T(8,128)S(1)} collective-permute-done((f32[480,128]{1,0:T(8,128)S(1)}, f32[480,128]{1,0:T(8,128)S(1)}, u32[]{:S(2)}, u32[]{:S(2)}) %collective-permute-start.12) | collective-permute-done | bytes 245792 | tf_op jit(solution)/shard_map/ppermute | solution.py:364
  50.1 1.6 %unpack.1 = f32[1920,128]{1,0:T(8,128)} custom-call(s32[2]{0:T(128)S(1)} %pad_add_fusion.place_ref, f32[480,128]{1,0:T(8,128)S(1)} %get-tuple-element.47.refs_0_, f32[480,128]{1,0:T(8,128)S(1)} %collective-permute-done.10.refs_1_, f32[480,128]{1,0:T(8,128)S(1)} %collective-permute-done.11.refs_2_, f32[480,128]{1,0:T(8,128)S(1)} %collective-permute-done.12.refs_3_), custom_call_target="tpu_custom_call" | custom-call | bytes 1966088 | tf_op jit(solution)/shard_map/unpack/pallas_call | solution.py:337
  (12 shorter events, 0.0 us)
Async XLA Ops:
  0.1 1.2 %copy-start.3 = (f32[60,4,1024]{2,1,0:T(4,128)S(1)}, f32[60,4,1024]{2,1,0:T(4,128)}, u32[]{:S(2)}) copy-start(f32[60,4,1024]{2,1,0:T(4,128)} %param.12) | copy-start | bytes 2949124
  1.3 4.8 %copy-start.11 = (f32[4]{0:T(128)S(1)}, f32[4]{0:T(128)}, u32[]{:S(2)}) copy-start(f32[4]{0:T(128)} %param.15) | copy-start | bytes 52
  1.3 14.5 %copy-start = (bf16[512,256]{1,0:T(8,128)(2,1)S(1)}, bf16[512,256]{1,0:T(8,128)(2,1)}, u32[]{:S(2)}) copy-start(bf16[512,256]{1,0:T(8,128)(2,1)} %constant.56.clone.refs_7_) | copy-start | bytes 786436
  1.3 14.6 %copy-start.1 = (bf16[512,256]{1,0:T(8,128)(2,1)S(1)}, bf16[512,256]{1,0:T(8,128)(2,1)}, u32[]{:S(2)}) copy-start(bf16[512,256]{1,0:T(8,128)(2,1)} %constant.54.clone.refs_6_) | copy-start | bytes 786436
  1.3 14.6 %copy-start.2 = (bf16[512,256]{1,0:T(8,128)(2,1)S(1)}, bf16[512,256]{1,0:T(8,128)(2,1)}, u32[]{:S(2)}) copy-start(bf16[512,256]{1,0:T(8,128)(2,1)} %constant.52.clone.refs_4_) | copy-start | bytes 786436
  2.0 5.5 %collective-permute-start.3 = (f32[128,128]{1,0:T(8,128)S(1)}, f32[128,128]{1,0:T(8,128)S(1)}, u32[]{:S(2)}, u32[]{:S(2)}) collective-permute-start(f32[128,128]{1,0:T(8,128)S(1)} %get-tuple-element.33), channel_id=1, source_target_pairs={{0,1},{1,0},{2,3},{3,2},{4,5},{5,4},{6,7},{7,6},{8,9},{9,8},{10,11... | collective-permute-start | bytes 196616 | tf_op jit(solution)/shard_map/ppermute | solution.py:364
  2.7 6.8 %collective-permute-start.4 = (f32[128,128]{1,0:T(8,128)S(1)}, f32[128,128]{1,0:T(8,128)S(1)}, u32[]{:S(2)}, u32[]{:S(2)}) collective-permute-start(f32[128,128]{1,0:T(8,128)S(1)} %get-tuple-element.34), channel_id=1, source_target_pairs={{0,2},{1,3},{2,0},{3,1},{4,6},{5,7},{6,4},{7,5},{8,10},{9,11},{10,... | collective-permute-start | bytes 196616 | tf_op jit(solution)/shard_map/ppermute | solution.py:364
  3.9 19.9 %collective-permute-start = (f32[352,128]{1,0:T(8,128)S(1)}, f32[352,128]{1,0:T(8,128)S(1)}, u32[]{:S(2)}, u32[]{:S(2)}) collective-permute-start(f32[352,128]{1,0:T(8,128)S(1)} %get-tuple-element.29), channel_id=1, source_target_pairs={{0,1},{1,0},{2,3},{3,2},{4,5},{5,4},{6,7},{7,6},{8,9},{9,8},{10,11... | collective-permute-start | bytes 540680 | tf_op jit(solution)/shard_map/ppermute | solution.py:364
  4.3 4.2 %copy-start.8 = (f32[32,128]{1,0:T(8,128)S(1)}, f32[32,128]{1,0:T(8,128)}, u32[]{:S(2)}) copy-start(f32[32,128]{1,0:T(8,128)} %constant.65.eigen_ref) | copy-start | bytes 49156
  4.3 19.5 %collective-permute-start.1 = (f32[352,128]{1,0:T(8,128)S(1)}, f32[352,128]{1,0:T(8,128)S(1)}, u32[]{:S(2)}, u32[]{:S(2)}) collective-permute-start(f32[352,128]{1,0:T(8,128)S(1)} %get-tuple-element.30), channel_id=1, source_target_pairs={{0,2},{1,3},{2,0},{3,1},{4,6},{5,7},{6,4},{7,5},{8,10},{9,11},{10,... | collective-permute-start | bytes 540680 | tf_op jit(solution)/shard_map/ppermute | solution.py:364
  4.5 19.3 %collective-permute-start.2 = (f32[352,128]{1,0:T(8,128)S(1)}, f32[352,128]{1,0:T(8,128)S(1)}, u32[]{:S(2)}, u32[]{:S(2)}) collective-permute-start(f32[352,128]{1,0:T(8,128)S(1)} %get-tuple-element.31), channel_id=1, source_target_pairs={{0,3},{1,2},{2,1},{3,0},{4,7},{5,6},{6,5},{7,4},{8,11},{9,10},{10,... | collective-permute-start | bytes 540680 | tf_op jit(solution)/shard_map/ppermute | solution.py:364
  6.1 0.7 %copy-start.9 = (f32[479]{0:T(512)S(1)}, f32[479]{0:T(512)}, u32[]{:S(2)}) copy-start(f32[479]{0:T(512)} %param.14) | copy-start | bytes 5752
  6.8 1.0 %copy-start.10 = (f32[480]{0:T(512)S(1)}, f32[480]{0:T(512)}, u32[]{:S(2)}) copy-start(f32[480]{0:T(512)} %param.13) | copy-start | bytes 5764
  7.5 8.3 %copy-start.7 = (f32[32,128]{1,0:T(8,128)S(1)}, f32[32,128]{1,0:T(8,128)}, u32[]{:S(2)}) copy-start(f32[32,128]{1,0:T(8,128)} %constant.58.clone.refs_5_.refs_11_) | copy-start | bytes 49156
  7.5 8.3 %collective-permute-start.5 = (f32[128,128]{1,0:T(8,128)S(1)}, f32[128,128]{1,0:T(8,128)S(1)}, u32[]{:S(2)}, u32[]{:S(2)}) collective-permute-start(f32[128,128]{1,0:T(8,128)S(1)} %get-tuple-element.35), channel_id=1, source_target_pairs={{0,3},{1,2},{2,1},{3,0},{4,7},{5,6},{6,5},{7,4},{8,11},{9,10},{10,... | collective-permute-start | bytes 196616 | tf_op jit(solution)/shard_map/ppermute | solution.py:364
  17.1 3.4 %collective-permute-start.6 = (f32[32,128]{1,0:T(8,128)S(1)}, f32[32,128]{1,0:T(8,128)S(1)}, u32[]{:S(2)}, u32[]{:S(2)}) collective-permute-start(f32[32,128]{1,0:T(8,128)S(1)} %get-tuple-element.38), channel_id=1, source_target_pairs={{0,4},{4,0},{8,12},{12,8},{16,20},{20,16},{24,28},{28,24},{1,5},{5... | collective-permute-start | bytes 49160 | tf_op jit(solution)/shard_map/ppermute | solution.py:358
  18.4 5.4 %collective-permute-start.7 = (f32[32,128]{1,0:T(8,128)S(1)}, f32[32,128]{1,0:T(8,128)S(1)}, u32[]{:S(2)}, u32[]{:S(2)}) collective-permute-start(f32[32,128]{1,0:T(8,128)S(1)} %get-tuple-element.39), channel_id=1, source_target_pairs={{4,8},{8,4},{12,16},{16,12},{20,24},{24,20},{5,9},{9,5},{13,17},{1... | collective-permute-start | bytes 49160 | tf_op jit(solution)/shard_map/ppermute | solution.py:358
  23.8 7.7 %copy-start.4 = (bf16[512,256]{1,0:T(8,128)(2,1)S(1)}, bf16[512,256]{1,0:T(8,128)(2,1)}, u32[]{:S(2)}) copy-start(bf16[512,256]{1,0:T(8,128)(2,1)} %constant.57.clone.refs_13_) | copy-start | bytes 786436
  23.8 7.7 %copy-start.5 = (bf16[512,256]{1,0:T(8,128)(2,1)S(1)}, bf16[512,256]{1,0:T(8,128)(2,1)}, u32[]{:S(2)}) copy-start(bf16[512,256]{1,0:T(8,128)(2,1)} %constant.55.clone.refs_12_) | copy-start | bytes 786436
  23.8 7.7 %copy-start.6 = (bf16[512,256]{1,0:T(8,128)(2,1)S(1)}, bf16[512,256]{1,0:T(8,128)(2,1)}, u32[]{:S(2)}) copy-start(bf16[512,256]{1,0:T(8,128)(2,1)} %constant.53.clone.refs_10_) | copy-start | bytes 786436
  25.9 3.3 %collective-permute-start.8 = (f32[32,128]{1,0:T(8,128)S(1)}, f32[32,128]{1,0:T(8,128)S(1)}, u32[]{:S(2)}, u32[]{:S(2)}) collective-permute-start(f32[32,128]{1,0:T(8,128)S(1)} %get-tuple-element.43), channel_id=1, source_target_pairs={{0,4},{4,0},{8,12},{12,8},{16,20},{20,16},{24,28},{28,24},{1,5},{5... | collective-permute-start | bytes 49160 | tf_op jit(solution)/shard_map/ppermute | solution.py:358
  26.2 5.4 %collective-permute-start.9 = (f32[32,128]{1,0:T(8,128)S(1)}, f32[32,128]{1,0:T(8,128)S(1)}, u32[]{:S(2)}, u32[]{:S(2)}) collective-permute-start(f32[32,128]{1,0:T(8,128)S(1)} %get-tuple-element.44), channel_id=1, source_target_pairs={{4,8},{8,4},{12,16},{16,12},{20,24},{24,20},{5,9},{9,5},{13,17},{1... | collective-permute-start | bytes 49160 | tf_op jit(solution)/shard_map/ppermute | solution.py:358
  34.1 4.7 %collective-permute-start.10 = (f32[480,128]{1,0:T(8,128)S(1)}, f32[480,128]{1,0:T(8,128)S(1)}, u32[]{:S(2)}, u32[]{:S(2)}) collective-permute-start(f32[480,128]{1,0:T(8,128)S(1)} %get-tuple-element.48), channel_id=1, source_target_pairs={{0,1},{1,0},{2,3},{3,2},{4,5},{5,4},{6,7},{7,6},{8,9},{9,8},{10,11... | collective-permute-start | bytes 737288 | tf_op jit(solution)/shard_map/ppermute | solution.py:364
  37.1 7.5 %collective-permute-start.11 = (f32[480,128]{1,0:T(8,128)S(1)}, f32[480,128]{1,0:T(8,128)S(1)}, u32[]{:S(2)}, u32[]{:S(2)}) collective-permute-start(f32[480,128]{1,0:T(8,128)S(1)} %get-tuple-element.49), channel_id=1, source_target_pairs={{0,2},{1,3},{2,0},{3,1},{4,6},{5,7},{6,4},{7,5},{8,10},{9,11},{10,... | collective-permute-start | bytes 737288 | tf_op jit(solution)/shard_map/ppermute | solution.py:364
  38.3 11.8 %collective-permute-start.12 = (f32[480,128]{1,0:T(8,128)S(1)}, f32[480,128]{1,0:T(8,128)S(1)}, u32[]{:S(2)}, u32[]{:S(2)}) collective-permute-start(f32[480,128]{1,0:T(8,128)S(1)} %get-tuple-element.50), channel_id=1, source_target_pairs={{0,3},{1,2},{2,1},{3,0},{4,7},{5,6},{6,5},{7,4},{8,11},{9,10},{10,... | collective-permute-start | bytes 737288 | tf_op jit(solution)/shard_map/ppermute | solution.py:364

commit v2 on v1

--- a/solution.py
+++ b/solution.py
@@ -29,7 +29,7 @@
     return high, low
 
 
-def tables():
+def tables(levels):
     j1 = np.arange(N1)
     j2 = np.arange(N2)
     k2 = np.arange(N2)
@@ -65,7 +65,10 @@
     wave[0, N2:] = 16 + N1 * (lane % half)
     eigen = 2.0 - 2.0 * np.cos(2 * np.pi * wave / NLON)
     pair = lambda t: np.concatenate(numpy_split(t), axis=0)
+    width = N1 // levels
+    part = [pair(np.kron(np.eye(BLOCK), small.T[at : at + width])) for at in range(0, N1, width)]
     return dict(
+        first_back_part=np.concatenate(part, axis=0),
         first=pair(first),
         first_back=pair(first.T),
         second=pair(second),
@@ -145,27 +148,35 @@
     store_zeroth(out_ref, rows, product_right(load_zeroth(mid_ref, padded), special_ref)[:rows])
 
 
-def backward_rows(spec_ref, rows, first_ref, turn_ref, second_ref, special_ref, mid_ref, out_ref):
-    padded = out_ref.shape[0]
-    turn_cos = turn_ref[:GROUPS, :][None]
-    turn_sin = turn_ref[GROUPS:, :][None]
+def spectral_back(spec_ref, rows, padded, second_ref, special_ref, mid_ref):
     result = product_right(lanes_together(spec_ref[...], rows), second_ref)
     mid_ref[: rows * N1, :] = lanes_apart(result, rows)
     if padded > rows:
-        mid_ref[rows * N1 :, :] = jnp.zeros(((padded - rows) * N1, N2), jnp.float32)
+        mid_ref[rows * N1 : padded * N1, :] = jnp.zeros(((padded - rows) * N1, N2), jnp.float32)
     store_zeroth(mid_ref, rows, product_right(load_zeroth(spec_ref, rows), special_ref))
+
+
+def digits_back(mid_ref, pair, turn_ref, first_ref):
+    turn_cos = turn_ref[:GROUPS, :][None]
+    turn_sin = turn_ref[GROUPS:, :][None]
+    sides = []
+    for side in range(2):
+        at = (2 * pair + side) * BLOCK * N1
+        both = mid_ref[at : at + BLOCK * N1, :].reshape(BLOCK, N1, N2)
+        real, imag = both[:, :GROUPS], both[:, GROUPS:]
+        turned = jnp.concatenate(
+            [real * turn_cos - imag * turn_sin, imag * turn_cos + real * turn_sin], axis=1
+        )
+        sides.append(turned.reshape(BLOCK * N1, N2))
+    return product_left(first_ref, jnp.concatenate(sides, axis=1))
+
+
+def backward_rows(spec_ref, rows, first_ref, turn_ref, second_ref, special_ref, mid_ref, out_ref):
+    padded = out_ref.shape[0]
+    spectral_back(spec_ref, rows, padded, second_ref, special_ref, mid_ref)
     for pair in range(padded // (2 * BLOCK)):
         base = pair * 2 * BLOCK
-        sides = []
-        for side in range(2):
-            at = (base + side * BLOCK) * N1
-            both = mid_ref[at : at + BLOCK * N1, :].reshape(BLOCK, N1, N2)
-            real, imag = both[:, :GROUPS], both[:, GROUPS:]
-            digits = jnp.concatenate(
-                [real * turn_cos - imag * turn_sin, imag * turn_cos + real * turn_sin], axis=1
-            )
-            sides.append(digits.reshape(BLOCK * N1, N2))
-        value = product_left(first_ref, jnp.concatenate(sides, axis=1))
+        value = digits_back(mid_ref, pair, turn_ref, first_ref)
         out_ref[base : base + BLOCK] = value[:, :N2].reshape(BLOCK, N1, N2)
         out_ref[base + BLOCK : base + 2 * BLOCK] = value[:, N2:].reshape(BLOCK, N1, N2)
 
@@ -300,6 +311,24 @@
         put(j, x_high)
 
 
+def sigmas(
+    couple_low, couple_high, own_top, own_bottom, got_top, got_bottom, sent_top, sent_bottom, from_low, from_high,
+    ratio_first, ratio_last, edge_ref,
+):
+    groups = own_top.shape[0]
+
+    def edge(index):
+        return edge_ref[index * groups : (index + 1) * groups, :]
+
+    beyond_low = (got_top + couple_low * own_top) * edge(0)
+    beyond_high = (got_bottom + couple_high * own_bottom) * edge(1)
+    theirs_low = (sent_bottom + couple_low * from_low) * edge(6)
+    theirs_high = (sent_top + couple_high * from_high) * edge(5)
+    low = ratio_first * (couple_low * (own_top - theirs_low)) + couple_low * (from_low - beyond_low)
+    high = ratio_last * (couple_high * (own_bottom - theirs_high)) + couple_high * (from_high - beyond_high)
+    return low, high
+
+
 def solve_second(
     rows, groups, couple_low, couple_high, own_top, own_bottom, got_top, got_bottom, sent_top, sent_bottom,
     from_low, from_high, ratio_ref, inverse_ref, edge_ref, first_ref, out_ref, mid_ref,
@@ -309,19 +338,15 @@
     def at(ref, index):
         return ref[index * groups : (index + 1) * groups, :]
 
-    beyond_low = (got_top + couple_low * own_top) * at(edge_ref, 0)
-    beyond_high = (got_bottom + couple_high * own_bottom) * at(edge_ref, 1)
-    theirs_low = (sent_bottom + couple_low * from_low) * at(edge_ref, 6)
-    theirs_high = (sent_top + couple_high * from_high) * at(edge_ref, 5)
-    low = couple_low * (own_top - theirs_low)
-    high = couple_high * (own_bottom - theirs_high)
+    low, high = sigmas(
+        couple_low, couple_high, own_top, own_bottom, got_top, got_bottom, sent_top, sent_bottom,
+        from_low, from_high, at(ratio_ref, 0), at(ratio_ref, rows - 1), edge_ref,
+    )
     for i in range(half):
         j = rows - 1 - i
-        low = at(ratio_ref, i) * low
-        high = at(ratio_ref, j) * high
-        if i == 0:
-            low = low + couple_low * (from_low - beyond_low)
-            high = high + couple_high * (from_high - beyond_high)
+        if i:
+            low = at(ratio_ref, i) * low
+            high = at(ratio_ref, j) * high
         mid_ref[i * groups : (i + 1) * groups, :] = low
         mid_ref[j * groups : (j + 1) * groups, :] = high
 
@@ -332,13 +357,14 @@
     meet(rows, groups, low, high, ratio_ref, inverse_ref, edge_ref, at, lambda i: at(mid_ref, i), put)
 
 
-def call(body, outs, ins, spaces, scratch, flops, name):
+def call(body, outs, ins, spaces, scratch, flops, name, out_spaces=None, aliases=None):
     nbytes = sum(x.size * x.dtype.itemsize for x in ins) + sum(4 * math.prod(s) for s in outs)
     out = pl.pallas_call(
         body,
         out_shape=[jax.ShapeDtypeStruct(s, jnp.float32) for s in outs],
         in_specs=[pl.BlockSpec(memory_space=s) for s in spaces],
-        out_specs=[pl.BlockSpec(memory_space=VMEM) for _ in outs],
+        out_specs=[pl.BlockSpec(memory_space=s) for s in out_spaces or [VMEM] * len(outs)],
+        input_output_aliases=aliases or {},
         scratch_shapes=scratch,
         compiler_params=pltpu.CompilerParams(vmem_limit_bytes=48 << 20),
         cost_estimate=pl.CostEstimate(flops=flops, bytes_accessed=nbytes, transcendentals=0),
@@ -358,22 +384,20 @@
     return lax.ppermute(value_even, "lat", even), lax.ppermute(value_odd, "lat", odd)
 
 
+def send_level(piece, mask, size):
+    return lax.ppermute(piece, "lon", [(d, d ^ mask) for d in range(size)])
+
+
 def swap_levels(pieces):
-    size = len(pieces)
-    return [pieces[0]] + [
-        lax.ppermute(pieces[mask], "lon", [(d, d ^ mask) for d in range(size)]) for mask in range(1, size)
-    ]
-
-
-def operator_parts(rows, level, lon_coef, lat_coef, level_scale):
+    return [pieces[0]] + [send_level(pieces[mask], mask, len(pieces)) for mask in range(1, len(pieces))]
+
+
+def operator_parts(rows, lon_coef, lat_coef, level_scale):
     row_first = lax.axis_index("lat") * rows
     extent = rows + 2 * OV
-    scale = lax.dynamic_index_in_dim(level_scale, level, 0, False)
-    lon_window = scale * lax.dynamic_slice_in_dim(jnp.pad(lon_coef, (OV, OV)), row_first, extent)
-    couple = scale * lax.dynamic_slice_in_dim(
-        jnp.pad(lat_coef, (OV + 1, OV + 2)), row_first, extent + 1
-    )
-    return lon_window, couple
+    lon_window = lax.dynamic_slice_in_dim(jnp.pad(lon_coef, (OV, OV)), row_first, extent)
+    couple = lax.dynamic_slice_in_dim(jnp.pad(lat_coef, (OV + 1, OV + 2)), row_first, extent + 1)
+    return level_scale[:, None] * lon_window[None], level_scale[:, None] * couple[None]
 
 
 def factor(rows, groups, lon_window, couple, eigen):
@@ -397,21 +421,90 @@
     return lambda i: ref[(i - first) * groups : (i - first + 1) * groups, :]
 
 
-def fill(full_ref, pieces, where, rows):
-    padded = full_ref.shape[0]
-    width = N1 // len(pieces)
-    for mask, piece in enumerate(pieces):
-        at = pl.multiple_of((where ^ mask) * width, width)
-        full_ref[:rows, pl.ds(at, width), :] = piece[...].reshape(rows, width, N2)
-    if padded > rows:
-        full_ref[rows:] = jnp.zeros((padded - rows, N1, N2), jnp.float32)
-
-
 def on_device(right_side, lon_coef, lat_coef, level_scale):
-    const = {k: jnp.asarray(v) for k, v in tables().items()}
+    const = {k: jnp.asarray(v) for k, v in tables(right_side.shape[1]).items()}
     if lax.axis_size("lon") != right_side.shape[1]:
         return shared_levels(const, right_side, lon_coef, lat_coef, level_scale)
     return whole_levels(const, right_side, lon_coef, lat_coef, level_scale)
+
+
+def early_rows(rows):
+    return rows // 2 + 2
+
+
+def influence_kernel(rows, early, levels, lon_ref, couple_ref, eigen_ref, phi_ref, psi_ref, ratio_ref, value_ref):
+    eigen = eigen_ref[...]
+    groups = eigen.shape[0]
+    half = rows // 2
+    span = early * groups
+
+    def at(ref, index):
+        return ref[index * groups : (index + 1) * groups, :]
+
+    def put(ref, index, value):
+        ref[index * groups : (index + 1) * groups, :] = value
+
+    def one_level(level, carry):
+        def plain(e):
+            return 1.0 + lon_ref[level, e] * eigen
+
+        low = high = None
+        low_inverse = high_inverse = low_value = high_value = None
+        for i in range(-OV, half):
+            j = rows - 1 - i
+            e, f = i + OV, j + OV
+            if low is None:
+                low = plain(e) + couple_ref[level, e]
+                high = plain(f) + couple_ref[level, f + 1]
+            else:
+                low_ratio = couple_ref[level, e] * low_inverse
+                high_ratio = couple_ref[level, f + 1] * high_inverse
+                low = plain(e) + low_ratio * low
+                high = plain(f) + high_ratio * high
+            low_divisor = couple_ref[level, e + 1] + low
+            high_divisor = couple_ref[level, f] + high
+            low_inverse = 1.0 / low_divisor
+            high_inverse = 1.0 / high_divisor
+            if i == 0:
+                low_value = high_value = jnp.ones_like(eigen)
+            elif i > 0:
+                low_value = low_ratio * low_value
+                high_value = high_ratio * high_value
+            if i >= 0:
+                put(ratio_ref, i, low_ratio)
+                put(value_ref, i, low_value * low_inverse)
+                if j < early:
+                    put(ratio_ref, j, high_ratio)
+                    put(value_ref, j, high_value * high_inverse)
+        between = couple_ref[level, OV + half]
+        inverse = 1.0 / (between * (low + high) + low * high)
+
+        def place(ref, index, value):
+            ref[pl.ds(pl.multiple_of(level * span + index * groups, groups), groups), :] = value
+
+        phi = high_divisor * inverse * low_value
+        psi = between * inverse * high_value
+        phi_down = between * inverse * low_value
+        psi_down = low_divisor * inverse * high_value
+        place(phi_ref, half - 1, phi)
+        place(psi_ref, half - 1, psi)
+        for i in range(half - 2, -1, -1):
+            ratio = at(ratio_ref, i + 1)
+            phi = at(value_ref, i) + ratio * phi
+            psi = ratio * psi
+            place(phi_ref, i, phi)
+            place(psi_ref, i, psi)
+        place(phi_ref, half, phi_down)
+        place(psi_ref, half, psi_down)
+        for j in range(half + 1, early):
+            ratio = at(ratio_ref, j - 1)
+            phi_down = ratio * phi_down
+            psi_down = at(value_ref, j) + ratio * psi_down
+            place(phi_ref, j, phi_down)
+            place(psi_ref, j, psi_down)
+        return carry
+
+    lax.fori_loop(0, levels, one_level, 0)
 
 
 def whole_levels(const, right_side, lon_coef, lat_coef, level_scale):
@@ -421,28 +514,76 @@
     lon_at = lax.axis_index("lon").astype(jnp.int32)
     parity = (lax.axis_index("lat") % 2).astype(jnp.int32)
     place = jnp.stack([lon_at, parity])
-    lon_window, couple = operator_parts(rows, lon_at, lon_coef, lat_coef, level_scale)
-    ratio, inverse, edge = factor(rows, groups, lon_window, couple, const["eigen"].reshape(groups, N2))
-    block = (rows * groups, N2)
+    half = rows // 2
+    early = early_rows(rows)
+    late = rows - early
+    eigen = const["eigen"].reshape(groups, N2)
+    lon_all, couple_all = operator_parts(rows, lon_coef, lat_coef, level_scale)
+    lon_window = lax.dynamic_index_in_dim(lon_all, lon_at, 0, False)
+    couple = lax.dynamic_index_in_dim(couple_all, lon_at, 0, False)
+    ratio, inverse, edge = factor(rows, groups, lon_window, couple, eigen)
+    phi, psi = call(
+        functools.partial(influence_kernel, rows, early, levels),
+        [(levels * early * groups, N2)] * 2,
+        [lon_all, couple_all, eigen],
+        [SMEM, SMEM, VMEM],
+        [vmem(early * groups, N2), vmem(early * groups, N2)],
+        levels * rows * groups * N2 * 20,
+        "influence",
+    )
     row = (groups, N2)
     ends = 2 * OV
     inner = rows - ends
+    span = OV * digits
     by_row = right_side.reshape(rows, levels, digits, N2).transpose(0, 2, 1, 3).reshape(-1, N2)
 
-    def pack(place_ref, in_ref, *out_refs):
-        for mask in range(levels):
+    far = list(range(2, levels))
+
+    def pack_ends(place_ref, in_ref, *refs):
+        out_refs, (low_ref, high_ref, sems) = refs[:-3], refs[-3:]
+        low = pltpu.make_async_copy(in_ref.at[pl.ds(0, levels * span), :], low_ref, sems.at[0])
+        high = pltpu.make_async_copy(
+            in_ref.at[pl.ds(levels * (rows - OV) * digits, levels * span), :], high_ref, sems.at[1]
+        )
+        low.start()
+        high.start()
+        low.wait()
+        high.wait()
+        for out_ref, mask in zip(out_refs, [0] + far):
             level = place_ref[0] ^ mask
-            end_ref, inner_ref = out_refs[2 * mask : 2 * mask + 2]
-            span = OV * digits
-            end_ref[:span, :] = in_ref[pl.ds(level, span, stride=levels), :]
-            inner_ref[...] = in_ref[pl.ds(level + levels * span, inner * digits, stride=levels), :]
-            end_ref[span:, :] = in_ref[pl.ds(level + levels * (rows - OV) * digits, span, stride=levels), :]
+            out_ref[:span, :] = low_ref[pl.ds(level, span, stride=levels), :]
+            out_ref[span:, :] = high_ref[pl.ds(level, span, stride=levels), :]
+
+    end_packed = call(
+        pack_ends,
+        [(ends * digits, N2)] * (1 + len(far)),
+        [place, by_row],
+        [SMEM, pltpu.HBM],
+        [vmem(levels * span, N2), vmem(levels * span, N2), pltpu.SemaphoreType.DMA((2,))],
+        0,
+        "pack_ends",
+    )
+
+    def pack(place_ref, in_ref, after_ref, *out_refs):
+        del after_ref
+        for mask, out_ref in enumerate(out_refs):
+            level = place_ref[0] ^ mask
+            skip = 0 if mask == 1 else span
+            out_ref[...] = in_ref[pl.ds(level + levels * skip, out_ref.shape[0], stride=levels), :]
 
     packed = call(
-        pack, [(ends * digits, N2), (inner * digits, N2)] * levels, [place, by_row], [SMEM, VMEM], [], 0, "pack"
-    )
-    end_pieces = swap_levels(packed[0::2])
-    inner_pieces = swap_levels(packed[1::2])
+        pack,
+        [((rows if mask == 1 else inner) * digits, N2) for mask in range(levels)],
+        [place, by_row, end_packed[0]],
+        [SMEM, VMEM, pl.ANY],
+        [],
+        0,
+        "pack",
+    )
+    end_pieces = [end_packed[0], None] + [send_level(p, m, levels) for p, m in zip(end_packed[1:], far)]
+    near = send_level(packed[1], 1, levels)
+    end_pieces[1] = near
+    inner_pieces = [packed[0], near] + [send_level(packed[m], m, levels) for m in far]
     forward = [const["first"], const["turn"], const["second"], const["special"]]
     pad_ends, pad_inner = pad_rows(ends), pad_rows(inner)
 
@@ -450,7 +591,11 @@
         pieces, refs = refs[:levels], refs[levels:]
         tables_in, edge_ref = refs[:4], refs[4]
         spec_ref, top_ref, bottom_ref, even_ref, odd_ref, full_ref, mid_ref = refs[5:]
-        fill(full_ref, pieces, place_ref[0], ends)
+        for mask, piece in enumerate(pieces):
+            at = pl.multiple_of((place_ref[0] ^ mask) * digits, digits)
+            last = piece.shape[0] - span
+            full_ref[:OV, pl.ds(at, digits), :] = piece[:span, :].reshape(OV, digits, N2)
+            full_ref[OV:ends, pl.ds(at, digits), :] = piece[last:, :].reshape(OV, digits, N2)
         forward_rows(full_ref, ends, *tables_in, mid_ref, spec_ref)
         top, bottom = edge_sums(rows_of(spec_ref, groups), rows_of(spec_ref, groups, -OV), edge_ref, groups)
         top_ref[...] = top
@@ -467,13 +612,29 @@
         "ends",
     )
     even, odd = swap(even, odd)
+    backward = [const["first_back"], const["turn"], const["second_back"], const["special_back"]]
+    pad_early, pad_late = pad_rows(early), pad_rows(late)
+
+    def spread(place_ref, full_ref, count, out_refs):
+        for mask, out_ref in enumerate(out_refs):
+            at = pl.multiple_of((place_ref[0] ^ mask) * digits, digits)
+            out_ref[: count * digits, :] = full_ref[:count, pl.ds(at, digits), :].reshape(count * digits, N2)
 
     def inner_body(place_ref, *refs):
-        pieces, refs = refs[:levels], refs[levels:]
-        tables_in, refs = refs[:4], refs[4:]
+        pieces, refs = refs[:levels], refs[levels + 1 :]
+        tables_in, back_in, refs = refs[:4], refs[4:7], refs[7:]
         ends_ref, even_ref, odd_ref, ratio_ref, inverse_ref, edge_ref = refs[:6]
-        out_ref, even_out, odd_out, full_ref, mid_ref, spec_ref = refs[6:]
-        fill(full_ref, pieces, place_ref[0], inner)
+        late_ref, top_ref, even_out, odd_out = refs[6:10]
+        early_refs, refs = refs[10 : 10 + levels], refs[10 + levels :]
+        full_ref, mid_ref, spec_ref, sum_ref, back_full_ref, back_mid_ref = refs
+        for mask, piece in enumerate(pieces):
+            at = pl.multiple_of((place_ref[0] ^ mask) * digits, digits)
+            skip = span if mask == 1 else 0
+            full_ref[:inner, pl.ds(at, digits), :] = piece[skip : skip + inner * digits, :].reshape(
+                inner, digits, N2
+            )
+        if pad_inner > inner:
+            full_ref[inner:] = jnp.zeros((pad_inner - inner, N1, N2), jnp.float32)
         forward_rows(full_ref, inner, *tables_in, mid_ref, spec_ref)
         low, high = swap_in(place_ref[1], even_ref[...], odd_ref[...])
 
@@ -484,55 +645,156 @@
                 return rows_of(ends_ref, groups, rows - ends)(i)
             return rows_of(spec_ref, groups, OV)(i)
 
-        solve_first(rows, groups, spec_row, low, high, ratio_ref, inverse_ref, edge_ref, out_ref)
-        swap_out(place_ref[1], out_ref[(rows - 1) * groups :, :], out_ref[:groups, :], even_out, odd_out)
-
-    iterate, even2, odd2 = call(
+        solve_first(rows, groups, spec_row, low, high, ratio_ref, inverse_ref, edge_ref, sum_ref)
+        top = sum_ref[:groups, :]
+        top_ref[...] = top
+        late_ref[...] = sum_ref[early * groups :, :]
+        swap_out(place_ref[1], sum_ref[(rows - 1) * groups :, :], top, even_out, odd_out)
+        early_sum = sum_ref.at[pl.ds(0, early * groups), :]
+        backward_rows(early_sum, early, back_in[0], tables_in[1], back_in[1], back_in[2], back_mid_ref, back_full_ref)
+        spread(place_ref, back_full_ref, early, early_refs)
+
+    late_first, own_top, even2, odd2, *early_pieces = call(
         inner_body,
-        [block, row, row],
-        [place, *inner_pieces, *forward, end_spectral, even, odd, ratio, inverse, edge],
-        [SMEM] + [VMEM] * (levels + 10),
-        [vmem(pad_inner, N1, N2), vmem(pad_inner * N1, N2), vmem(inner * N1, N2)],
-        inner * NLON * 256 * 4,
+        [(late * groups, N2), row, row, row] + [(early * digits, N2)] * levels,
+        [
+            place, *inner_pieces, phi, *forward, backward[0], backward[2], backward[3],
+            end_spectral, even, odd, ratio, inverse, edge,
+        ],
+        [SMEM] + [VMEM] * levels + [pl.ANY] + [VMEM] * 13,
+        [
+            vmem(pad_inner, N1, N2), vmem(pad_inner * N1, N2), vmem(inner * N1, N2), vmem(rows * groups, N2),
+            vmem(pad_early, N1, N2), vmem(pad_early * N1, N2),
+        ],
+        (inner + early) * NLON * 256 * 4,
         "inner",
     )
+    early_pieces = swap_levels(early_pieces)
     even2, odd2 = swap(even2, odd2)
-    pad_all = pad_rows(rows)
 
     def second_body(place_ref, couple_ref, *refs):
-        first_ref, even_ref, odd_ref, even2_ref, odd2_ref, top_ref, bottom_ref = refs[:7]
-        ratio_ref, inverse_ref, edge_ref = refs[7:10]
-        tables_in = refs[10:14]
-        out_refs = refs[14 : 14 + levels]
-        sum_ref, mid_ref, full_ref = refs[14 + levels :]
-        second_part(
-            rows, groups, place_ref[1], couple_ref, first_ref, even_ref, odd_ref, even2_ref, odd2_ref,
-            top_ref, bottom_ref, ratio_ref, inverse_ref, edge_ref, sum_ref, mid_ref,
+        first_ref, own_top_ref, even_ref, odd_ref, even2_ref, odd2_ref, top_ref, bottom_ref = refs[:8]
+        ratio_ref, inverse_ref, edge_ref = refs[8:11]
+        tables_in, refs = refs[11:15], refs[15 + len(far) :]
+        sigma_ref, late_refs = refs[0], refs[1 : 1 + levels]
+        sum_ref, mid_ref, full_ref = refs[1 + levels :]
+        got_top, got_bottom = swap_in(place_ref[1], even_ref[...], odd_ref[...])
+        from_low, from_high = swap_in(place_ref[1], even2_ref[...], odd2_ref[...])
+        low, high = sigmas(
+            couple_ref[OV], couple_ref[OV + rows], own_top_ref[...], first_ref[(late - 1) * groups :, :],
+            got_top, got_bottom, top_ref[...], bottom_ref[...], from_low, from_high,
+            ratio_ref[:groups, :], ratio_ref[(rows - 1) * groups :, :], edge_ref,
         )
-        backward_rows(sum_ref, rows, *tables_in, mid_ref, full_ref)
+        sigma_ref[:groups, :] = low
+        sigma_ref[groups:, :] = high
+        late_refs[1][late * digits : late * digits + groups, :] = low
+        late_refs[1][late * digits + groups :, :] = high
+
+        def at(ref, index):
+            return ref[index * groups : (index + 1) * groups, :]
+
+        for i in range(half):
+            j = rows - 1 - i
+            if i:
+                low = at(ratio_ref, i) * low
+                high = at(ratio_ref, j) * high
+            mid_ref[(j - half) * groups : (j - half + 1) * groups, :] = high
+        x_high = at(edge_ref, 3) * high + at(edge_ref, 4) * low
+        for j in range(half, rows):
+            if j > half:
+                x_high = at(mid_ref, j - half) * at(inverse_ref, j) + at(ratio_ref, j - 1) * x_high
+            if j >= early:
+                here = slice((j - early) * groups, (j - early + 1) * groups)
+                sum_ref[here, :] = first_ref[here, :] + x_high
+        backward_rows(sum_ref, late, *tables_in, mid_ref, full_ref)
+        spread(place_ref, full_ref, late, late_refs)
+
+    sigma, *late_pieces = call(
+        second_body,
+        [(2 * groups, N2)]
+        + [(late * digits + (2 * groups if mask == 1 else 0), N2) for mask in range(levels)],
+        [
+            place, couple, late_first, own_top, even, odd, even2, odd2, sent_top, sent_bottom,
+            ratio, inverse, edge, *backward, *early_pieces[2:],
+        ],
+        [SMEM, SMEM] + [VMEM] * 15 + [pl.ANY] * len(far),
+        [vmem(late * groups, N2), vmem(max(pad_late, half) * N1, N2), vmem(pad_late, N1, N2)],
+        late * NLON * 256 * 4,
+        "second",
+    )
+    late_pieces = swap_levels(late_pieces)
+    sigma_pieces = [sigma, late_pieces[1]] + [send_level(sigma, mask, levels) for mask in far]
+    total = rows * levels * digits
+    early_total = early * levels * digits
+    part = const["first_back_part"]
+
+    def correct(place_ref, *refs):
+        pieces, sigma_refs, refs = refs[:levels], refs[levels : 2 * levels], refs[2 * levels :]
+        phi_ref, psi_ref, part_ref, turn_ref, second_ref, special_ref = refs[:6]
+        out_ref, sum_ref, mid_ref, done_ref, sem = refs[6:]
+        part_rows = part_ref.shape[0] // levels
+        mine = part_ref.at[pl.ds(pl.multiple_of(place_ref[0] * part_rows, part_rows), part_rows), :]
+        size = early * groups
         for mask in range(levels):
-            at = pl.multiple_of((place_ref[0] ^ mask) * digits, digits)
-            out_refs[mask][...] = full_ref[:rows, pl.ds(at, digits), :].reshape(rows * digits, N2)
-
-    backward = [const["first_back"], const["turn"], const["second_back"], const["special_back"]]
-    pieces = call(
-        second_body,
-        [(rows * digits, N2)] * levels,
-        [place, couple, iterate, even, odd, even2, odd2, sent_top, sent_bottom, ratio, inverse, edge, *backward],
-        [SMEM, SMEM] + [VMEM] * 14,
-        [vmem(*block), vmem(pad_all * N1, N2), vmem(pad_all, N1, N2)],
-        rows * NLON * 256 * 4,
-        "second",
-    )
-    pieces = swap_levels(pieces)
+            level = place_ref[0] ^ mask
+            last = sigma_refs[mask].shape[0]
+            low = sigma_refs[mask][last - 2 * groups : last - groups, :]
+            high = sigma_refs[mask][last - groups :, :]
+            first = pl.multiple_of(level * size, size)
+            phi_all = phi_ref[pl.ds(first, size), :].reshape(early, groups, N2)
+            psi_all = psi_ref[pl.ds(first, size), :].reshape(early, groups, N2)
+            sum_ref[...] = (phi_all * low[None] + psi_all * high[None]).reshape(size, N2)
+            spectral_back(sum_ref, early, pad_early, second_ref, special_ref, mid_ref)
+            for pair in range(pad_early // (2 * BLOCK)):
+                value = digits_back(mid_ref, pair, turn_ref, mine)
+                for side in range(2):
+                    begin = (2 * pair + side) * BLOCK
+                    count = min(BLOCK, early - begin)
+                    if count <= 0:
+                        continue
+                    lines = count * digits
+                    whole = pieces[mask][begin * digits : begin * digits + lines, :]
+                    done_ref[pl.ds(level + begin * digits * levels, lines, stride=levels), :] = (
+                        whole + value[:lines, side * N2 : (side + 1) * N2]
+                    )
+        copy = pltpu.make_async_copy(done_ref, out_ref.at[pl.ds(0, early_total), :], sem)
+        copy.start()
+        copy.wait()
+
+    (out,) = call(
+        correct,
+        [(total, N2)],
+        [place, *early_pieces, *sigma_pieces, phi, psi, part, const["turn"], backward[2], backward[3]],
+        [SMEM] + [VMEM] * (2 * levels + 6),
+        [
+            vmem(early * groups, N2), vmem(pad_early * N1, N2), vmem(early_total, N2), pltpu.SemaphoreType.DMA,
+        ],
+        levels * early * NLON * 256 * 3,
+        "correct",
+        out_spaces=[pl.ANY],
+    )
 
     def unpack(place_ref, *refs):
-        out_ref = refs[levels]
+        pieces = refs[:levels]
+        out_ref, done_ref, sem = refs[levels + 1 :]
         for mask in range(levels):
-            out_ref[pl.ds(place_ref[0] ^ mask, rows * digits, stride=levels), :] = refs[mask][...]
+            done_ref[pl.ds(place_ref[0] ^ mask, late * digits, stride=levels), :] = pieces[mask][: late * digits, :]
+        copy = pltpu.make_async_copy(
+            done_ref, out_ref.at[pl.ds(early_total, total - early_total), :], sem
+        )
+        copy.start()
+        copy.wait()
 
     (out,) = call(
-        unpack, [(rows * levels * digits, N2)], [place, *pieces], [SMEM] + [VMEM] * levels, [], 0, "unpack"
+        unpack,
+        [(total, N2)],
+        [place, *late_pieces, out],
+        [SMEM] + [VMEM] * levels + [pl.ANY],
+        [vmem(total - early_total, N2), pltpu.SemaphoreType.DMA],
+        0,
+        "unpack",
+        out_spaces=[pl.ANY],
+        aliases={levels + 1: 0},
     )
     return out.reshape(rows, digits, levels, N2).transpose(0, 2, 1, 3).reshape(right_side.shape)
 
@@ -561,7 +823,9 @@
     digits = N1 // lon_size
     lon_at = lax.axis_index("lon")
     parity = (lax.axis_index("lat") % 2).astype(jnp.int32).reshape(1)
-    lon_window, couple = operator_parts(rows, lon_at // sharers, lon_coef, lat_coef, level_scale)
+    lon_window, couple = operator_parts(rows, lon_coef, lat_coef, level_scale)
+    lon_window = lax.dynamic_index_in_dim(lon_window, lon_at // sharers, 0, False)
+    couple = lax.dynamic_index_in_dim(couple, lon_at // sharers, 0, False)
     eigen = lax.dynamic_slice_in_dim(
         const["eigen"], (lon_at % sharers) * (groups // 2), groups // 2, axis=1
     ).reshape(groups, N2)

time: 52 us -> 48.2 us (0.927)
  waiting for transfers between devices: 23.3 us -> 8.52 us
  Pallas kernels: 9.15 us -> 16.9 us
  starting transfers between devices: 15.7 us -> 19 us
  other arithmetic: 1.54 us -> 0.22 us
  local copies, waits for them, and re-layouts: 1.93 us -> 2.79 us
    ppermute x9 -> x13, waiting for transfers between devices: 17.6 us -> 5.2 us  [send_level(): return lax.ppermute(piece, 'lon', [(d, d ^ mask) for d in range(size)])]
    pallas_call x6 -> x9, Pallas kernels: 9.15 us -> 16.9 us  [call(): pl.pallas_call(body, out_shape=[jax.ShapeDtypeStruct(s, jnp.float32) for...]
    ppermute x9 -> x13, starting transfers between devices: 9.05 us -> 11.5 us  [send_level(): return lax.ppermute(piece, 'lon', [(d, d ^ mask) for d in range(size)])]
    ppermute x2, waiting for transfers between devices: 5.67 us -> 3.32 us  [swap(): lax.ppermute(value_odd, 'lat', odd)]
    ppermute x2, starting transfers between devices: 1.63 us -> 3.55 us  [swap(): lax.ppermute(value_even, 'lat', even)]
    mul x2, other arithmetic: 1.47 us -> 0.14 us  [the longest x1 0.07 us: operator_parts(): level_scale[:, None] * lon_window[None]]
    unnamed x24 -> x30, local copies, waits for them, and re-layouts: 1.35 us -> 2.63 us
    ppermute x2, starting transfers between devices: 5.03 us -> 3.92 us  [swap(): lax.ppermute(value_odd, 'lat', odd)]
  transfers between devices with their start and end apart: 13 -> 17, of which waited for: 5 -> 2; matrix products, arithmetic and copies ran while one was open for 4% -> 1% of each run, Pallas kernels for 4% -> 24%
where the time goes in v2:
time: 48.2 us; the launch traced here: 47.6 us
  starting transfers between devices  19 us (39%)
  Pallas kernels  16.9 us (35%)
  waiting for transfers between devices  8.52 us (18%)
  local copies, waits for them, and re-layouts  2.79 us (6%)
    pallas_call x9, Pallas kernels, call(): pl.pallas_call(body, out_shape=[jax.ShapeDtypeStruct(s, jnp.float32) for...  16.9 us
    ppermute x13, starting transfers between devices, send_level(): return lax.ppermute(piece, 'lon', [(d, d ^ mask) for d in range(size)])  11.5 us
    ppermute x13, waiting for transfers between devices, send_level(): return lax.ppermute(piece, 'lon', [(d, d ^ mask) for d in range(size)])  5.2 us
    ppermute x2, starting transfers between devices, swap(): lax.ppermute(value_odd, 'lat', odd)  3.92 us
    ppermute x2, starting transfers between devices, swap(): lax.ppermute(value_even, 'lat', even)  3.55 us
    ppermute x2, waiting for transfers between devices, swap(): lax.ppermute(value_odd, 'lat', odd)  3.32 us
    unnamed x30, local copies, waits for them, and re-layouts  2.63 us
  transfers between devices with their start and end apart: 17, of which 2 were waited for; matrix products, arithmetic and copies ran while one was open for 1% of the time, Pallas kernels for 24%

profile of v2, /device:TPU:17, one launch (start us, length us, event | category | flops | bytes accessed | tf_op | source)
XLA Modules:
  0.0 47.6 jit_solution(16801977733162460812)
XLA Ops:
  0.0 0.1 pad_add_fusion.place_ref
  0.1 1.2 %copy-done.2 = f32[60,4,1024]{2,1,0:T(4,128)S(1)} copy-done((f32[60,4,1024]{2,1,0:T(4,128)S(1)}, f32[60,4,1024]{2,1,0:T(4,128)}, u32[]{:S(2)}) %copy-start.2) | copy-done | bytes 983064
  1.3 0.0 copy-start.4
  1.3 0.0 copy-start.5
  1.4 0.9 %pack_ends.1 = (f32[128,128]{1,0:T(8,128)S(1)}, f32[128,128]{1,0:T(8,128)S(1)}, f32[128,128]{1,0:T(8,128)S(1)}) custom-call(s32[2]{0:T(128)S(1)} %pad_add_fusion.place_ref, f32[1920,128]{1,0:T(8,128)S(1)} %bitcast.16), custom_call_target="tpu_custom_call" | custom-call | bytes 1179656 | tf_op jit(solution)/shard_map/pack_ends/pallas_call | solution.py:362
  2.3 1.3 %collective-permute-start.3 = (f32[128,128]{1,0:T(8,128)S(1)}, f32[128,128]{1,0:T(8,128)S(1)}, u32[]{:S(2)}, u32[]{:S(2)}) collective-permute-start(f32[128,128]{1,0:T(8,128)S(1)} %get-tuple-element.41), channel_id=1, source_target_pairs={{0,2},{1,3},{2,0},{3,1},{4,6},{5,7},{6,4},{7,5},{8,10},{9,11},{10,... | collective-permute-start | bytes 196616 | tf_op jit(solution)/shard_map/ppermute | solution.py:388
  3.6 1.1 %collective-permute-start.4 = (f32[128,128]{1,0:T(8,128)S(1)}, f32[128,128]{1,0:T(8,128)S(1)}, u32[]{:S(2)}, u32[]{:S(2)}) collective-permute-start(f32[128,128]{1,0:T(8,128)S(1)} %get-tuple-element.42), channel_id=1, source_target_pairs={{0,3},{1,2},{2,1},{3,0},{4,7},{5,6},{6,5},{7,4},{8,11},{9,10},{10,... | collective-permute-start | bytes 196616 | tf_op jit(solution)/shard_map/ppermute | solution.py:388
  4.7 0.6 %pack.1 = (f32[352,128]{1,0:T(8,128)S(1)}, f32[480,128]{1,0:T(8,128)S(1)}, f32[352,128]{1,0:T(8,128)S(1)}, f32[352,128]{1,0:T(8,128)S(1)}) custom-call(s32[2]{0:T(128)S(1)} %pad_add_fusion.place_ref, f32[1920,128]{1,0:T(8,128)S(1)} %bitcast.17, f32[128,128]{1,0:T(8,128)S(1)} %get-tuple-element.35.after_ref.refs_0_), custom_call_target="tpu_custom_call" | custom-call | bytes 1835016 | tf_op jit(solution)/shard_map/pack/pallas_call | solution.py:362
  5.3 1.3 %collective-permute-start.1 = (f32[352,128]{1,0:T(8,128)S(1)}, f32[352,128]{1,0:T(8,128)S(1)}, u32[]{:S(2)}, u32[]{:S(2)}) collective-permute-start(f32[352,128]{1,0:T(8,128)S(1)} %get-tuple-element.38), channel_id=1, source_target_pairs={{0,2},{1,3},{2,0},{3,1},{4,6},{5,7},{6,4},{7,5},{8,10},{9,11},{10,... | collective-permute-start | bytes 540680 | tf_op jit(solution)/shard_map/ppermute | solution.py:388
  6.6 0.3 collective-permute-start.2
  6.9 0.4 collective-permute-start
  7.2 0.1 pad_dynamic-slice_fusion.1
  7.3 0.1 pad_dynamic-slice_fusion
  7.4 0.1 broadcast_multiply_fusion.lon_ref
  7.5 0.1 broadcast_multiply_fusion.1.couple_ref
  7.6 1.0 %factor.1 = (f32[1920,128]{1,0:T(8,128)S(1)}, f32[1920,128]{1,0:T(8,128)S(1)}, f32[672,128]{1,0:T(8,128)S(1)}) custom-call(f32[76]{0:T(128)S(1)} %dynamic-slice_bitcast_fusion.lon_ref, f32[77]{0:T(128)S(1)} %dynamic-slice_bitcast_fusion.1.couple_ref, f32[32,128]{1,0:T(8,128)S(1)} %copy-done.11), custom_call_target="tpu_custom_call" | custom-call | flops 4915200 | bytes 2327140 | tf_op jit(solution)/shard_map/factor/pallas_call | solution.py:362
  8.6 0.0 collective-permute-done.3.refs_2_
  8.6 0.0 collective-permute-done.4.refs_3_
  8.6 0.0 collective-permute-done.refs_1_
  8.7 1.2 %ends.1 = (f32[512,128]{1,0:T(8,128)S(1)}, f32[32,128]{1,0:T(8,128)S(1)}, f32[32,128]{1,0:T(8,128)S(1)}, f32[32,128]{1,0:T(8,128)S(1)}, f32[32,128]{1,0:T(8,128)S(1)}) custom-call(s32[2]{0:T(128)S(1)} %pad_add_fusion.place_ref, f32[128,128]{1,0:T(8,128)S(1)} %get-tuple-element.35.after_ref.refs_0_, f32[480,128]{1,0:T(8,128)S(1)} %collective-permute-done.refs_1_, ...), custom_call_target="tpu_custom_call" | custom-call | flops 67108864 | bytes 1916936 | tf_op jit(solution)/shard_map/ends/pallas_call | solution.py:362
  9.9 1.3 %collective-permute-start.5 = (f32[32,128]{1,0:T(8,128)S(1)}, f32[32,128]{1,0:T(8,128)S(1)}, u32[]{:S(2)}, u32[]{:S(2)}) collective-permute-start(f32[32,128]{1,0:T(8,128)S(1)} %get-tuple-element.45), channel_id=1, source_target_pairs={{0,4},{4,0},{8,12},{12,8},{16,20},{20,16},{24,28},{28,24},{1,5},{5... | collective-permute-start | bytes 49160 | tf_op jit(solution)/shard_map/ppermute | solution.py:384
  11.2 2.0 %collective-permute-start.6 = (f32[32,128]{1,0:T(8,128)S(1)}, f32[32,128]{1,0:T(8,128)S(1)}, u32[]{:S(2)}, u32[]{:S(2)}) collective-permute-start(f32[32,128]{1,0:T(8,128)S(1)} %get-tuple-element.46), channel_id=1, source_target_pairs={{4,8},{8,4},{12,16},{16,12},{20,24},{24,20},{5,9},{9,5},{13,17},{1... | collective-permute-start | bytes 49160 | tf_op jit(solution)/shard_map/ppermute | solution.py:384
  13.2 2.7 %influence.1 = (f32[4096,128]{1,0:T(8,128)S(1)}, f32[4096,128]{1,0:T(8,128)S(1)}) custom-call(f32[4,76]{1,0:T(4,128)S(1)} %broadcast_multiply_fusion.lon_ref, f32[4,77]{1,0:T(4,128)S(1)} %broadcast_multiply_fusion.1.couple_ref, f32[32,128]{1,0:T(8,128)S(1)} %copy-done.11), custom_call_target="tpu_custom_call" | custom-call | flops 19660800 | bytes 4213136 | tf_op jit(solution)/shard_map/influence/pallas_call | solution.py:362
  15.9 1.4 %copy-done = f32[4096,128]{1,0:T(8,128)} copy-done((f32[4096,128]{1,0:T(8,128)}, f32[4096,128]{1,0:T(8,128)S(1)}, u32[]{:S(2)}) %copy-start) | copy-done | bytes 2097176
  17.3 0.0 collective-permute-done.1.refs_2_
  17.3 0.0 collective-permute-done.2.refs_3_
  17.3 0.0 collective-permute-done.6.refs_14_.refs_3_
  17.3 3.1 %inner.1 = (f32[896,128]{1,0:T(8,128)S(1)}, f32[32,128]{1,0:T(8,128)S(1)}, f32[32,128]{1,0:T(8,128)S(1)}, f32[32,128]{1,0:T(8,128)S(1)}, f32[256,128]{1,0:T(8,12...) custom-call(s32[2]{0:T(128)S(1)} %pad_add_fusion.place_ref, ...), custom_call_target="tpu_custom_call" | custom-call | flops 318767104 | bytes 8110088 | tf_op jit(solution)/shard_map/inner/pallas_call | solution.py:362
  20.4 0.0 copy-start.10
  20.5 1.3 %collective-permute-start.9 = (f32[256,128]{1,0:T(8,128)S(1)}, f32[256,128]{1,0:T(8,128)S(1)}, u32[]{:S(2)}, u32[]{:S(2)}) collective-permute-start(f32[256,128]{1,0:T(8,128)S(1)} %get-tuple-element.55), channel_id=1, source_target_pairs={{0,2},{1,3},{2,0},{3,1},{4,6},{5,7},{6,4},{7,5},{8,10},{9,11},{10,... | collective-permute-start | bytes 393224 | tf_op jit(solution)/shard_map/ppermute | solution.py:388
  21.8 1.2 %collective-permute-start.10 = (f32[256,128]{1,0:T(8,128)S(1)}, f32[256,128]{1,0:T(8,128)S(1)}, u32[]{:S(2)}, u32[]{:S(2)}) collective-permute-start(f32[256,128]{1,0:T(8,128)S(1)} %get-tuple-element.56), channel_id=1, source_target_pairs={{0,3},{1,2},{2,1},{3,0},{4,7},{5,6},{6,5},{7,4},{8,11},{9,10},{10,... | collective-permute-start | bytes 393224 | tf_op jit(solution)/shard_map/ppermute | solution.py:388
  23.0 2.2 %collective-permute-start.7 = (f32[32,128]{1,0:T(8,128)S(1)}, f32[32,128]{1,0:T(8,128)S(1)}, u32[]{:S(2)}, u32[]{:S(2)}) collective-permute-start(f32[32,128]{1,0:T(8,128)S(1)} %get-tuple-element.51), channel_id=1, source_target_pairs={{0,4},{4,0},{8,12},{12,8},{16,20},{20,16},{24,28},{28,24},{1,5},{5... | collective-permute-start | bytes 49160 | tf_op jit(solution)/shard_map/ppermute | solution.py:384
  25.2 1.9 %collective-permute-start.8 = (f32[32,128]{1,0:T(8,128)S(1)}, f32[32,128]{1,0:T(8,128)S(1)}, u32[]{:S(2)}, u32[]{:S(2)}) collective-permute-start(f32[32,128]{1,0:T(8,128)S(1)} %get-tuple-element.52), channel_id=1, source_target_pairs={{4,8},{8,4},{12,16},{16,12},{20,24},{24,20},{5,9},{9,5},{13,17},{1... | collective-permute-start | bytes 49160 | tf_op jit(solution)/shard_map/ppermute | solution.py:384
  27.2 0.1 collective-permute-start.14
  27.3 3.3 %collective-permute-done.8.refs_5_ = f32[32,128]{1,0:T(8,128)S(1)} collective-permute-done((f32[32,128]{1,0:T(8,128)S(1)}, f32[32,128]{1,0:T(8,128)S(1)}, u32[]{:S(2)}, u32[]{:S(2)}) %collective-permute-start.8) | collective-permute-done | bytes 16416 | tf_op jit(solution)/shard_map/ppermute | solution.py:384
  30.6 1.7 %second.1 = (f32[64,128]{1,0:T(8,128)S(1)}, f32[224,128]{1,0:T(8,128)S(1)}, f32[288,128]{1,0:T(8,128)S(1)}, f32[224,128]{1,0:T(8,128)S(1)}, f32[224,128]{1,0:T(8,128)S(1)}) custom-call(s32[2]{0:T(128)S(1)} %pad_add_fusion.place_ref, f32[77]{0:T(128)S(1)} %dynamic-slice_bitcast_fusion.1.couple_ref, f32[896,128]{1,0:T(8,128)S(1)} %get-tuple-element.49.refs_0_, ...), custom_call_target="tpu_custom_call" | custom-call | flops 117440512 | bytes 4473148 | tf_op jit(solution)/shard_map/second/pallas_call | solution.py:362
  32.3 1.3 %collective-permute-start.11 = (f32[288,128]{1,0:T(8,128)S(1)}, f32[288,128]{1,0:T(8,128)S(1)}, u32[]{:S(2)}, u32[]{:S(2)}) collective-permute-start(f32[288,128]{1,0:T(8,128)S(1)} %get-tuple-element.58), channel_id=1, source_target_pairs={{0,1},{1,0},{2,3},{3,2},{4,5},{5,4},{6,7},{7,6},{8,9},{9,8},{10,11... | collective-permute-start | bytes 442376 | tf_op jit(solution)/shard_map/ppermute | solution.py:388
  33.6 1.0 %collective-permute-start.12 = (f32[224,128]{1,0:T(8,128)S(1)}, f32[224,128]{1,0:T(8,128)S(1)}, u32[]{:S(2)}, u32[]{:S(2)}) collective-permute-start(f32[224,128]{1,0:T(8,128)S(1)} %get-tuple-element.59), channel_id=1, source_target_pairs={{0,2},{1,3},{2,0},{3,1},{4,6},{5,7},{6,4},{7,5},{8,10},{9,11},{10,... | collective-permute-start | bytes 344072 | tf_op jit(solution)/shard_map/ppermute | solution.py:388
  34.5 0.8 %collective-permute-start.13 = (f32[224,128]{1,0:T(8,128)S(1)}, f32[224,128]{1,0:T(8,128)S(1)}, u32[]{:S(2)}, u32[]{:S(2)}) collective-permute-start(f32[224,128]{1,0:T(8,128)S(1)} %get-tuple-element.60), channel_id=1, source_target_pairs={{0,3},{1,2},{2,1},{3,0},{4,7},{5,6},{6,5},{7,4},{8,11},{9,10},{10,... | collective-permute-start | bytes 344072 | tf_op jit(solution)/shard_map/ppermute | solution.py:388
  35.3 1.0 %collective-permute-start.16 = (f32[64,128]{1,0:T(8,128)S(1)}, f32[64,128]{1,0:T(8,128)S(1)}, u32[]{:S(2)}, u32[]{:S(2)}) collective-permute-start(f32[64,128]{1,0:T(8,128)S(1)} %get-tuple-element.63.refs_4_), channel_id=1, source_target_pairs={{0,3},{1,2},{2,1},{3,0},{4,7},{5,6},{6,5},{7,4},{8,11},{9,10},{10,... | collective-permute-start | bytes 98312 | tf_op jit(solution)/shard_map/ppermute | solution.py:388
  36.3 0.5 %collective-permute-start.15 = (f32[64,128]{1,0:T(8,128)S(1)}, f32[64,128]{1,0:T(8,128)S(1)}, u32[]{:S(2)}, u32[]{:S(2)}) collective-permute-start(f32[64,128]{1,0:T(8,128)S(1)} %get-tuple-element.63.refs_4_), channel_id=1, source_target_pairs={{0,2},{1,3},{2,0},{3,1},{4,6},{5,7},{6,4},{7,5},{8,10},{9,11},{10,... | collective-permute-start | bytes 98312 | tf_op jit(solution)/shard_map/ppermute | solution.py:388
  36.8 5.2 %collective-permute-done.16.refs_7_ = f32[64,128]{1,0:T(8,128)S(1)} collective-permute-done((f32[64,128]{1,0:T(8,128)S(1)}, f32[64,128]{1,0:T(8,128)S(1)}, u32[]{:S(2)}, u32[]{:S(2)}) %collective-permute-start.16) | collective-permute-done | bytes 32800 | tf_op jit(solution)/shard_map/ppermute | solution.py:388
  42.0 0.0 collective-permute-done.15.refs_6_
  42.0 0.0 collective-permute-done.11.refs_5_.refs_1_
  42.0 4.2 %correct.1.refs_4_ = f32[1920,128]{1,0:T(8,128)} custom-call(s32[2]{0:T(128)S(1)} %pad_add_fusion.place_ref, f32[256,128]{1,0:T(8,128)S(1)} %get-tuple-element.61.refs_0_, f32[256,128]{1,0:T(8,128)S(1)} %collective-permute-done.14.refs_1_, f32[256,128]{1,0:T(8,128)S(1)} %collective-permute-done.9.refs_15_.refs_2_, ...), custom_call_target="tpu_custom_call" | custom-call | flops 402653184 | bytes 6750216 | tf_op jit(solution)/shard_map/correct/pallas_call | solution.py:362
  46.2 0.0 collective-permute-done.12.refs_2_
  46.3 0.0 collective-permute-done.13.refs_3_
  46.3 1.4 %unpack.1 = f32[1920,128]{1,0:T(8,128)} custom-call(s32[2]{0:T(128)S(1)} %pad_add_fusion.place_ref, f32[224,128]{1,0:T(8,128)S(1)} %get-tuple-element.57.refs_0_, f32[288,128]{1,0:T(8,128)S(1)} %collective-permute-done.11.refs_5_.refs_1_, f32[224,128]{1,0:T(8,128)S(1)} %collective-permute-done.12.refs_2_, ...), custom_call_target="tpu_custom_call", output_to_operand_aliasing={{}: (5, {})} | custom-call | bytes 2457608 | tf_op jit(solution)/shard_map/unpack/pallas_call | solution.py:362
  (32 shorter events, 0.1 us)
Async XLA Ops:
  0.0 7.6 %copy-start.11 = (f32[32,128]{1,0:T(8,128)S(1)}, f32[32,128]{1,0:T(8,128)}, u32[]{:S(2)}) copy-start(f32[32,128]{1,0:T(8,128)} %constant.72.eigen_ref) | copy-start | bytes 49156
  0.0 8.6 %copy-start.9 = (f32[32,128]{1,0:T(8,128)S(1)}, f32[32,128]{1,0:T(8,128)}, u32[]{:S(2)}) copy-start(f32[32,128]{1,0:T(8,128)} %constant.65.clone.refs_5_.refs_6_.refs_12_.refs_11_) | copy-start | bytes 49156
  0.0 7.2 %copy-start.12 = (f32[479]{0:T(512)S(1)}, f32[479]{0:T(512)}, u32[]{:S(2)}) copy-start(f32[479]{0:T(512)} %param.15) | copy-start | bytes 5752
  0.0 7.3 %copy-start.13 = (f32[480]{0:T(512)S(1)}, f32[480]{0:T(512)}, u32[]{:S(2)}) copy-start(f32[480]{0:T(512)} %param.14) | copy-start | bytes 5764
  0.0 7.4 %copy-start.14 = (f32[4]{0:T(128)S(1)}, f32[4]{0:T(128)}, u32[]{:S(2)}) copy-start(f32[4]{0:T(128)} %param.16) | copy-start | bytes 52
  0.1 1.2 %copy-start.2 = (f32[60,4,1024]{2,1,0:T(4,128)S(1)}, f32[60,4,1024]{2,1,0:T(4,128)}, u32[]{:S(2)}) copy-start(f32[60,4,1024]{2,1,0:T(4,128)} %param.13) | copy-start | bytes 2949124
  1.3 7.3 %copy-start.6 = (bf16[512,256]{1,0:T(8,128)(2,1)S(1)}, bf16[512,256]{1,0:T(8,128)(2,1)}, u32[]{:S(2)}) copy-start(bf16[512,256]{1,0:T(8,128)(2,1)} %constant.63.clone.refs_7_.refs_8_) | copy-start | bytes 786436
  1.3 7.3 %copy-start.7 = (bf16[512,256]{1,0:T(8,128)(2,1)S(1)}, bf16[512,256]{1,0:T(8,128)(2,1)}, u32[]{:S(2)}) copy-start(bf16[512,256]{1,0:T(8,128)(2,1)} %constant.61.clone.refs_6_.refs_7_) | copy-start | bytes 786436
  1.3 7.3 %copy-start.8 = (bf16[512,256]{1,0:T(8,128)(2,1)S(1)}, bf16[512,256]{1,0:T(8,128)(2,1)}, u32[]{:S(2)}) copy-start(bf16[512,256]{1,0:T(8,128)(2,1)} %constant.59.clone.refs_4_.refs_5_) | copy-start | bytes 786436
  1.3 16.0 %copy-start.3 = (bf16[512,256]{1,0:T(8,128)(2,1)S(1)}, bf16[512,256]{1,0:T(8,128)(2,1)}, u32[]{:S(2)}) copy-start(bf16[512,256]{1,0:T(8,128)(2,1)} %constant.64.clone.refs_11_.refs_14_.refs_13_) | copy-start | bytes 786436
  1.3 16.0 %copy-start.4 = (bf16[512,256]{1,0:T(8,128)(2,1)S(1)}, bf16[512,256]{1,0:T(8,128)(2,1)}, u32[]{:S(2)}) copy-start(bf16[512,256]{1,0:T(8,128)(2,1)} %constant.62.clone.refs_10_.refs_13_.refs_12_) | copy-start | bytes 786436
  1.3 16.0 %copy-start.5 = (bf16[512,256]{1,0:T(8,128)(2,1)S(1)}, bf16[512,256]{1,0:T(8,128)(2,1)}, u32[]{:S(2)}) copy-start(bf16[512,256]{1,0:T(8,128)(2,1)} %constant.60.clone.refs_9_.refs_11_) | copy-start | bytes 786436
  2.3 6.3 %collective-permute-start.3 = (f32[128,128]{1,0:T(8,128)S(1)}, f32[128,128]{1,0:T(8,128)S(1)}, u32[]{:S(2)}, u32[]{:S(2)}) collective-permute-start(f32[128,128]{1,0:T(8,128)S(1)} %get-tuple-element.41), channel_id=1, source_target_pairs={{0,2},{1,3},{2,0},{3,1},{4,6},{5,7},{6,4},{7,5},{8,10},{9,11},{10,... | collective-permute-start | bytes 196616 | tf_op jit(solution)/shard_map/ppermute | solution.py:388
  3.6 5.1 %collective-permute-start.4 = (f32[128,128]{1,0:T(8,128)S(1)}, f32[128,128]{1,0:T(8,128)S(1)}, u32[]{:S(2)}, u32[]{:S(2)}) collective-permute-start(f32[128,128]{1,0:T(8,128)S(1)} %get-tuple-element.42), channel_id=1, source_target_pairs={{0,3},{1,2},{2,1},{3,0},{4,7},{5,6},{6,5},{7,4},{8,11},{9,10},{10,... | collective-permute-start | bytes 196616 | tf_op jit(solution)/shard_map/ppermute | solution.py:388
  5.3 12.0 %collective-permute-start.1 = (f32[352,128]{1,0:T(8,128)S(1)}, f32[352,128]{1,0:T(8,128)S(1)}, u32[]{:S(2)}, u32[]{:S(2)}) collective-permute-start(f32[352,128]{1,0:T(8,128)S(1)} %get-tuple-element.38), channel_id=1, source_target_pairs={{0,2},{1,3},{2,0},{3,1},{4,6},{5,7},{6,4},{7,5},{8,10},{9,11},{10,... | collective-permute-start | bytes 540680 | tf_op jit(solution)/shard_map/ppermute | solution.py:388
  6.6 10.7 %collective-permute-start.2 = (f32[352,128]{1,0:T(8,128)S(1)}, f32[352,128]{1,0:T(8,128)S(1)}, u32[]{:S(2)}, u32[]{:S(2)}) collective-permute-start(f32[352,128]{1,0:T(8,128)S(1)} %get-tuple-element.39), channel_id=1, source_target_pairs={{0,3},{1,2},{2,1},{3,0},{4,7},{5,6},{6,5},{7,4},{8,11},{9,10},{10,... | collective-permute-start | bytes 540680 | tf_op jit(solution)/shard_map/ppermute | solution.py:388
  6.9 1.7 %collective-permute-start = (f32[480,128]{1,0:T(8,128)S(1)}, f32[480,128]{1,0:T(8,128)S(1)}, u32[]{:S(2)}, u32[]{:S(2)}) collective-permute-start(f32[480,128]{1,0:T(8,128)S(1)} %get-tuple-element.37), channel_id=1, source_target_pairs={{0,1},{1,0},{2,3},{3,2},{4,5},{5,4},{6,7},{7,6},{8,9},{9,8},{10,11... | collective-permute-start | bytes 737288 | tf_op jit(solution)/shard_map/ppermute | solution.py:388
  9.9 7.4 %collective-permute-start.5 = (f32[32,128]{1,0:T(8,128)S(1)}, f32[32,128]{1,0:T(8,128)S(1)}, u32[]{:S(2)}, u32[]{:S(2)}) collective-permute-start(f32[32,128]{1,0:T(8,128)S(1)} %get-tuple-element.45), channel_id=1, source_target_pairs={{0,4},{4,0},{8,12},{12,8},{16,20},{20,16},{24,28},{28,24},{1,5},{5... | collective-permute-start | bytes 49160 | tf_op jit(solution)/shard_map/ppermute | solution.py:384
  11.2 6.1 %collective-permute-start.6 = (f32[32,128]{1,0:T(8,128)S(1)}, f32[32,128]{1,0:T(8,128)S(1)}, u32[]{:S(2)}, u32[]{:S(2)}) collective-permute-start(f32[32,128]{1,0:T(8,128)S(1)} %get-tuple-element.46), channel_id=1, source_target_pairs={{4,8},{8,4},{12,16},{16,12},{20,24},{24,20},{5,9},{9,5},{13,17},{1... | collective-permute-start | bytes 49160 | tf_op jit(solution)/shard_map/ppermute | solution.py:384
  15.9 1.4 %copy-start = (f32[4096,128]{1,0:T(8,128)}, f32[4096,128]{1,0:T(8,128)S(1)}, u32[]{:S(2)}) copy-start(f32[4096,128]{1,0:T(8,128)S(1)} %get-tuple-element.40.refs_4_.refs_8_) | copy-start | bytes 6291460
  20.4 21.6 %copy-start.1 = (f32[4096,128]{1,0:T(8,128)S(1)}, f32[4096,128]{1,0:T(8,128)}, u32[]{:S(2)}) copy-start(f32[4096,128]{1,0:T(8,128)} %copy-done) | copy-start | bytes 6291460
  20.4 21.6 %copy-start.10 = (bf16[512,256]{1,0:T(8,128)(2,1)S(1)}, bf16[512,256]{1,0:T(8,128)(2,1)}, u32[]{:S(2)}) copy-start(bf16[512,256]{1,0:T(8,128)(2,1)} %constant.58.clone.refs_10_) | copy-start | bytes 786436
  20.5 10.2 %collective-permute-start.9 = (f32[256,128]{1,0:T(8,128)S(1)}, f32[256,128]{1,0:T(8,128)S(1)}, u32[]{:S(2)}, u32[]{:S(2)}) collective-permute-start(f32[256,128]{1,0:T(8,128)S(1)} %get-tuple-element.55), channel_id=1, source_target_pairs={{0,2},{1,3},{2,0},{3,1},{4,6},{5,7},{6,4},{7,5},{8,10},{9,11},{10,... | collective-permute-start | bytes 393224 | tf_op jit(solution)/shard_map/ppermute | solution.py:388
  21.8 8.9 %collective-permute-start.10 = (f32[256,128]{1,0:T(8,128)S(1)}, f32[256,128]{1,0:T(8,128)S(1)}, u32[]{:S(2)}, u32[]{:S(2)}) collective-permute-start(f32[256,128]{1,0:T(8,128)S(1)} %get-tuple-element.56), channel_id=1, source_target_pairs={{0,3},{1,2},{2,1},{3,0},{4,7},{5,6},{6,5},{7,4},{8,11},{9,10},{10,... | collective-permute-start | bytes 393224 | tf_op jit(solution)/shard_map/ppermute | solution.py:388
  23.0 4.3 %collective-permute-start.7 = (f32[32,128]{1,0:T(8,128)S(1)}, f32[32,128]{1,0:T(8,128)S(1)}, u32[]{:S(2)}, u32[]{:S(2)}) collective-permute-start(f32[32,128]{1,0:T(8,128)S(1)} %get-tuple-element.51), channel_id=1, source_target_pairs={{0,4},{4,0},{8,12},{12,8},{16,20},{20,16},{24,28},{28,24},{1,5},{5... | collective-permute-start | bytes 49160 | tf_op jit(solution)/shard_map/ppermute | solution.py:384
  25.2 5.4 %collective-permute-start.8 = (f32[32,128]{1,0:T(8,128)S(1)}, f32[32,128]{1,0:T(8,128)S(1)}, u32[]{:S(2)}, u32[]{:S(2)}) collective-permute-start(f32[32,128]{1,0:T(8,128)S(1)} %get-tuple-element.52), channel_id=1, source_target_pairs={{4,8},{8,4},{12,16},{16,12},{20,24},{24,20},{5,9},{9,5},{13,17},{1... | collective-permute-start | bytes 49160 | tf_op jit(solution)/shard_map/ppermute | solution.py:384
  27.2 9.1 %collective-permute-start.14 = (f32[256,128]{1,0:T(8,128)S(1)}, f32[256,128]{1,0:T(8,128)S(1)}, u32[]{:S(2)}, u32[]{:S(2)}) collective-permute-start(f32[256,128]{1,0:T(8,128)S(1)} %get-tuple-element.62), channel_id=1, source_target_pairs={{0,1},{1,0},{2,3},{3,2},{4,5},{5,4},{6,7},{7,6},{8,9},{9,8},{10,11... | collective-permute-start | bytes 393224 | tf_op jit(solution)/shard_map/ppermute | solution.py:388
  32.3 9.7 %collective-permute-start.11 = (f32[288,128]{1,0:T(8,128)S(1)}, f32[288,128]{1,0:T(8,128)S(1)}, u32[]{:S(2)}, u32[]{:S(2)}) collective-permute-start(f32[288,128]{1,0:T(8,128)S(1)} %get-tuple-element.58), channel_id=1, source_target_pairs={{0,1},{1,0},{2,3},{3,2},{4,5},{5,4},{6,7},{7,6},{8,9},{9,8},{10,11... | collective-permute-start | bytes 442376 | tf_op jit(solution)/shard_map/ppermute | solution.py:388
  33.6 12.7 %collective-permute-start.12 = (f32[224,128]{1,0:T(8,128)S(1)}, f32[224,128]{1,0:T(8,128)S(1)}, u32[]{:S(2)}, u32[]{:S(2)}) collective-permute-start(f32[224,128]{1,0:T(8,128)S(1)} %get-tuple-element.59), channel_id=1, source_target_pairs={{0,2},{1,3},{2,0},{3,1},{4,6},{5,7},{6,4},{7,5},{8,10},{9,11},{10,... | collective-permute-start | bytes 344072 | tf_op jit(solution)/shard_map/ppermute | solution.py:388
  34.5 11.7 %collective-permute-start.13 = (f32[224,128]{1,0:T(8,128)S(1)}, f32[224,128]{1,0:T(8,128)S(1)}, u32[]{:S(2)}, u32[]{:S(2)}) collective-permute-start(f32[224,128]{1,0:T(8,128)S(1)} %get-tuple-element.60), channel_id=1, source_target_pairs={{0,3},{1,2},{2,1},{3,0},{4,7},{5,6},{6,5},{7,4},{8,11},{9,10},{10,... | collective-permute-start | bytes 344072 | tf_op jit(solution)/shard_map/ppermute | solution.py:388
  35.3 6.7 %collective-permute-start.16 = (f32[64,128]{1,0:T(8,128)S(1)}, f32[64,128]{1,0:T(8,128)S(1)}, u32[]{:S(2)}, u32[]{:S(2)}) collective-permute-start(f32[64,128]{1,0:T(8,128)S(1)} %get-tuple-element.63.refs_4_), channel_id=1, source_target_pairs={{0,3},{1,2},{2,1},{3,0},{4,7},{5,6},{6,5},{7,4},{8,11},{9,10},{10,... | collective-permute-start | bytes 98312 | tf_op jit(solution)/shard_map/ppermute | solution.py:388
  36.3 5.7 %collective-permute-start.15 = (f32[64,128]{1,0:T(8,128)S(1)}, f32[64,128]{1,0:T(8,128)S(1)}, u32[]{:S(2)}, u32[]{:S(2)}) collective-permute-start(f32[64,128]{1,0:T(8,128)S(1)} %get-tuple-element.63.refs_4_), channel_id=1, source_target_pairs={{0,2},{1,3},{2,0},{3,1},{4,6},{5,7},{6,4},{7,5},{8,10},{9,11},{10,... | collective-permute-start | bytes 98312 | tf_op jit(solution)/shard_map/ppermute | solution.py:388

commit v3 on v2

--- a/solution.py
+++ b/solution.py
@@ -253,16 +253,13 @@
     put(edge_ref, 4, between * inverse)
 
 
-def edge_sums(low_rows, high_rows, edge_ref, groups):
-    def edge(index):
-        return edge_ref[index * groups : (index + 1) * groups, :]
-
+def edge_sums(low_rows, high_rows, next_ratio, previous_ratio):
     top = high_rows(0)
     for i in range(1, OV):
-        top = high_rows(i) + edge(7 + i - 1) * top
+        top = high_rows(i) + next_ratio(i - 1) * top
     bottom = low_rows(OV - 1)
     for i in range(OV - 2, -1, -1):
-        bottom = low_rows(i) + edge(14 + i) * bottom
+        bottom = low_rows(i) + previous_ratio(i) * bottom
     return top, bottom
 
 
@@ -313,7 +310,7 @@
 
 def sigmas(
     couple_low, couple_high, own_top, own_bottom, got_top, got_bottom, sent_top, sent_bottom, from_low, from_high,
-    ratio_first, ratio_last, edge_ref,
+    ratio_first, ratio_last, edge_ref, next_inverse, previous_inverse,
 ):
     groups = own_top.shape[0]
 
@@ -322,8 +319,8 @@
 
     beyond_low = (got_top + couple_low * own_top) * edge(0)
     beyond_high = (got_bottom + couple_high * own_bottom) * edge(1)
-    theirs_low = (sent_bottom + couple_low * from_low) * edge(6)
-    theirs_high = (sent_top + couple_high * from_high) * edge(5)
+    theirs_low = (sent_bottom + couple_low * from_low) * previous_inverse
+    theirs_high = (sent_top + couple_high * from_high) * next_inverse
     low = ratio_first * (couple_low * (own_top - theirs_low)) + couple_low * (from_low - beyond_low)
     high = ratio_last * (couple_high * (own_bottom - theirs_high)) + couple_high * (from_high - beyond_high)
     return low, high
@@ -340,7 +337,7 @@
 
     low, high = sigmas(
         couple_low, couple_high, own_top, own_bottom, got_top, got_bottom, sent_top, sent_bottom,
-        from_low, from_high, at(ratio_ref, 0), at(ratio_ref, rows - 1), edge_ref,
+        from_low, from_high, at(ratio_ref, 0), at(ratio_ref, rows - 1), edge_ref, at(edge_ref, 5), at(edge_ref, 6),
     )
     for i in range(half):
         j = rows - 1 - i
@@ -357,7 +354,7 @@
     meet(rows, groups, low, high, ratio_ref, inverse_ref, edge_ref, at, lambda i: at(mid_ref, i), put)
 
 
-def call(body, outs, ins, spaces, scratch, flops, name, out_spaces=None, aliases=None):
+def call(body, outs, ins, spaces, scratch, flops, name, out_spaces=None, aliases=None, limit=48):
     nbytes = sum(x.size * x.dtype.itemsize for x in ins) + sum(4 * math.prod(s) for s in outs)
     out = pl.pallas_call(
         body,
@@ -366,7 +363,7 @@
         out_specs=[pl.BlockSpec(memory_space=s) for s in out_spaces or [VMEM] * len(outs)],
         input_output_aliases=aliases or {},
         scratch_shapes=scratch,
-        compiler_params=pltpu.CompilerParams(vmem_limit_bytes=48 << 20),
+        compiler_params=pltpu.CompilerParams(vmem_limit_bytes=limit << 20),
         cost_estimate=pl.CostEstimate(flops=flops, bytes_accessed=nbytes, transcendentals=0),
         name=name,
     )(*ins)
@@ -432,79 +429,153 @@
     return rows // 2 + 2
 
 
-def influence_kernel(rows, early, levels, lon_ref, couple_ref, eigen_ref, phi_ref, psi_ref, ratio_ref, value_ref):
+def edge_kernel(rows, level_ref, lon_ref, couple_ref, eigen_ref, out_ref):
     eigen = eigen_ref[...]
     groups = eigen.shape[0]
+    level = level_ref[0]
+    low = high = low_inverse = high_inverse = None
+    for i in range(OV):
+        e, f = rows + i, 2 * OV - 1 - i
+        if i == 0:
+            low = 1.0 + lon_ref[level, e] * eigen + couple_ref[level, e]
+            high = 1.0 + lon_ref[level, f] * eigen + couple_ref[level, f + 1]
+        else:
+            low_ratio = couple_ref[level, e] * low_inverse
+            high_ratio = couple_ref[level, f + 1] * high_inverse
+            out_ref[(i - 1) * groups : i * groups, :] = low_ratio
+            out_ref[(OV + i - 1) * groups : (OV + i) * groups, :] = high_ratio
+            low = 1.0 + lon_ref[level, e] * eigen + low_ratio * low
+            high = 1.0 + lon_ref[level, f] * eigen + high_ratio * high
+        low_inverse = 1.0 / (couple_ref[level, e + 1] + low)
+        high_inverse = 1.0 / (couple_ref[level, f] + high)
+    out_ref[(OV - 1) * groups : OV * groups, :] = low_inverse
+    out_ref[(2 * OV - 1) * groups :, :] = high_inverse
+
+
+def level_response(rows, early, level, lon_ref, couple_ref, eigen, put_ratio, put_inverse, keep, tables):
     half = rows // 2
-    span = early * groups
-
-    def at(ref, index):
-        return ref[index * groups : (index + 1) * groups, :]
-
-    def put(ref, index, value):
-        ref[index * groups : (index + 1) * groups, :] = value
-
-    def one_level(level, carry):
-        def plain(e):
-            return 1.0 + lon_ref[level, e] * eigen
-
-        low = high = None
-        low_inverse = high_inverse = low_value = high_value = None
-        for i in range(-OV, half):
-            j = rows - 1 - i
-            e, f = i + OV, j + OV
-            if low is None:
-                low = plain(e) + couple_ref[level, e]
-                high = plain(f) + couple_ref[level, f + 1]
-            else:
-                low_ratio = couple_ref[level, e] * low_inverse
-                high_ratio = couple_ref[level, f + 1] * high_inverse
-                low = plain(e) + low_ratio * low
-                high = plain(f) + high_ratio * high
-            low_divisor = couple_ref[level, e + 1] + low
-            high_divisor = couple_ref[level, f] + high
-            low_inverse = 1.0 / low_divisor
-            high_inverse = 1.0 / high_divisor
-            if i == 0:
-                low_value = high_value = jnp.ones_like(eigen)
-            elif i > 0:
-                low_value = low_ratio * low_value
-                high_value = high_ratio * high_value
-            if i >= 0:
-                put(ratio_ref, i, low_ratio)
-                put(value_ref, i, low_value * low_inverse)
-                if j < early:
-                    put(ratio_ref, j, high_ratio)
-                    put(value_ref, j, high_value * high_inverse)
-        between = couple_ref[level, OV + half]
-        inverse = 1.0 / (between * (low + high) + low * high)
-
-        def place(ref, index, value):
-            ref[pl.ds(pl.multiple_of(level * span + index * groups, groups), groups), :] = value
-
-        phi = high_divisor * inverse * low_value
-        psi = between * inverse * high_value
-        phi_down = between * inverse * low_value
-        psi_down = low_divisor * inverse * high_value
-        place(phi_ref, half - 1, phi)
-        place(psi_ref, half - 1, psi)
-        for i in range(half - 2, -1, -1):
-            ratio = at(ratio_ref, i + 1)
-            phi = at(value_ref, i) + ratio * phi
-            psi = ratio * psi
-            place(phi_ref, i, phi)
-            place(psi_ref, i, psi)
-        place(phi_ref, half, phi_down)
-        place(psi_ref, half, psi_down)
-        for j in range(half + 1, early):
-            ratio = at(ratio_ref, j - 1)
-            phi_down = ratio * phi_down
-            psi_down = at(value_ref, j) + ratio * psi_down
-            place(phi_ref, j, phi_down)
-            place(psi_ref, j, psi_down)
+    ratio_at, value_at, put_value, put_phi, put_psi = tables
+
+    def plain(e):
+        return 1.0 + lon_ref[level, e] * eigen
+
+    low = high = None
+    low_inverse = high_inverse = low_value = high_value = None
+    for i in range(-OV, half):
+        j = rows - 1 - i
+        e, f = i + OV, j + OV
+        if low is None:
+            low = plain(e) + couple_ref[level, e]
+            high = plain(f) + couple_ref[level, f + 1]
+        else:
+            low_ratio = couple_ref[level, e] * low_inverse
+            high_ratio = couple_ref[level, f + 1] * high_inverse
+            low = plain(e) + low_ratio * low
+            high = plain(f) + high_ratio * high
+        low_divisor = couple_ref[level, e + 1] + low
+        high_divisor = couple_ref[level, f] + high
+        low_inverse = 1.0 / low_divisor
+        high_inverse = 1.0 / high_divisor
+        if i == -1:
+            keep(0, low_inverse)
+            keep(1, high_inverse)
+        if i == 0:
+            low_value = high_value = jnp.ones_like(eigen)
+        elif i > 0:
+            low_value = low_ratio * low_value
+            high_value = high_ratio * high_value
+        if i >= 0:
+            put_ratio(i, low_ratio)
+            put_ratio(j, high_ratio)
+            put_inverse(i, low_inverse)
+            put_inverse(j, high_inverse)
+            put_value(i, low_value * low_inverse)
+            if j < early:
+                put_value(j, high_value * high_inverse)
+    between = couple_ref[level, OV + half]
+    inverse = 1.0 / (between * (low + high) + low * high)
+    across = between * inverse
+    high_inverse = high_divisor * inverse
+    low_inverse = low_divisor * inverse
+    keep(2, high_inverse)
+    keep(3, low_inverse)
+    keep(4, across)
+    phi = high_inverse * low_value
+    psi = across * high_value
+    phi_down = across * low_value
+    psi_down = low_inverse * high_value
+    put_phi(half - 1, phi)
+    put_psi(half - 1, psi)
+    for i in range(half - 2, -1, -1):
+        ratio = ratio_at(i + 1)
+        phi = value_at(i) + ratio * phi
+        psi = ratio * psi
+        put_phi(i, phi)
+        put_psi(i, psi)
+    put_phi(half, phi_down)
+    put_psi(half, psi_down)
+    for j in range(half + 1, early):
+        ratio = ratio_at(j - 1)
+        phi_down = ratio * phi_down
+        psi_down = value_at(j) + ratio * psi_down
+        put_phi(j, phi_down)
+        put_psi(j, psi_down)
+
+
+def getter(ref, groups):
+    return lambda index: ref[index * groups : (index + 1) * groups, :]
+
+
+def putter(ref, groups, first=0):
+    def put(index, value):
+        at = first + index * groups
+        ref[pl.ds(at if isinstance(at, int) else pl.multiple_of(at, groups), groups), :] = value
+
+    return put
+
+
+def own_kernel(
+    rows, early, place_ref, lon_ref, couple_ref, eigen_ref, ratio_ref, inverse_ref, edge_ref, phi_ref, psi_ref, value_ref
+):
+    groups = eigen_ref.shape[0]
+    level_response(
+        rows, early, place_ref[0], lon_ref, couple_ref, eigen_ref[...], putter(ratio_ref, groups),
+        putter(inverse_ref, groups), putter(edge_ref, groups),
+        (
+            getter(ratio_ref, groups), getter(value_ref, groups), putter(value_ref, groups),
+            putter(phi_ref, groups), putter(psi_ref, groups),
+        ),
+    )
+
+
+def partners_kernel(
+    rows, early, levels, place_ref, lon_ref, couple_ref, eigen_ref, after_ref, phi_ref, psi_ref, kept_ref, value_ref
+):
+    del after_ref
+    eigen = eigen_ref[...]
+    groups = eigen.shape[0]
+
+    def partner(mask, carry):
+        def nothing(index, value):
+            pass
+
+        put_kept = putter(kept_ref, groups)
+
+        def put_ratio(index, value):
+            if index < early:
+                put_kept(index, value)
+
+        first = (mask - 1) * (early * groups)
+        level_response(
+            rows, early, place_ref[0] ^ mask, lon_ref, couple_ref, eigen, put_ratio, nothing, nothing,
+            (
+                getter(kept_ref, groups), getter(value_ref, groups), putter(value_ref, groups),
+                putter(phi_ref, groups, first), putter(psi_ref, groups, first),
+            ),
+        )
         return carry
 
-    lax.fori_loop(0, levels, one_level, 0)
+    lax.fori_loop(1, levels, partner, 0)
 
 
 def whole_levels(const, right_side, lon_coef, lat_coef, level_scale):
@@ -519,17 +590,25 @@
     late = rows - early
     eigen = const["eigen"].reshape(groups, N2)
     lon_all, couple_all = operator_parts(rows, lon_coef, lat_coef, level_scale)
-    lon_window = lax.dynamic_index_in_dim(lon_all, lon_at, 0, False)
-    couple = lax.dynamic_index_in_dim(couple_all, lon_at, 0, False)
-    ratio, inverse, edge = factor(rows, groups, lon_window, couple, eigen)
-    phi, psi = call(
-        functools.partial(influence_kernel, rows, early, levels),
-        [(levels * early * groups, N2)] * 2,
-        [lon_all, couple_all, eigen],
-        [SMEM, SMEM, VMEM],
-        [vmem(early * groups, N2), vmem(early * groups, N2)],
-        levels * rows * groups * N2 * 20,
-        "influence",
+    (around,) = call(
+        functools.partial(edge_kernel, rows),
+        [(2 * OV * groups, N2)],
+        [place, lon_all, couple_all, eigen],
+        [SMEM, SMEM, SMEM, VMEM],
+        [],
+        16 * groups * N2 * 20,
+        "edge",
+    )
+    block = (rows * groups, N2)
+    early_block = (early * groups, N2)
+    ratio, inverse, edge, phi, psi = call(
+        functools.partial(own_kernel, rows, early),
+        [block, block, (5 * groups, N2), early_block, early_block],
+        [place, lon_all, couple_all, eigen],
+        [SMEM, SMEM, SMEM, VMEM],
+        [vmem(*early_block)],
+        rows * groups * N2 * 20,
+        "own",
     )
     row = (groups, N2)
     ends = 2 * OV
@@ -562,6 +641,7 @@
         [vmem(levels * span, N2), vmem(levels * span, N2), pltpu.SemaphoreType.DMA((2,))],
         0,
         "pack_ends",
+        limit=58,
     )
 
     def pack(place_ref, in_ref, after_ref, *out_refs):
@@ -597,7 +677,10 @@
             full_ref[:OV, pl.ds(at, digits), :] = piece[:span, :].reshape(OV, digits, N2)
             full_ref[OV:ends, pl.ds(at, digits), :] = piece[last:, :].reshape(OV, digits, N2)
         forward_rows(full_ref, ends, *tables_in, mid_ref, spec_ref)
-        top, bottom = edge_sums(rows_of(spec_ref, groups), rows_of(spec_ref, groups, -OV), edge_ref, groups)
+        top, bottom = edge_sums(
+            rows_of(spec_ref, groups), rows_of(spec_ref, groups, -OV),
+            rows_of(edge_ref, groups), lambda i: edge_ref[(2 * OV - 2 - i) * groups : (2 * OV - 1 - i) * groups, :],
+        )
         top_ref[...] = top
         bottom_ref[...] = bottom
         swap_out(place_ref[1], top, bottom, even_ref, odd_ref)
@@ -605,7 +688,7 @@
     end_spectral, sent_top, sent_bottom, even, odd = call(
         ends_body,
         [(ends * groups, N2)] + [row] * 4,
-        [place, *end_pieces, *forward, edge],
+        [place, *end_pieces, *forward, around],
         [SMEM] + [VMEM] * (levels + 5),
         [vmem(pad_ends, N1, N2), vmem(pad_ends * N1, N2)],
         ends * NLON * 256 * 4,
@@ -621,7 +704,7 @@
             out_ref[: count * digits, :] = full_ref[:count, pl.ds(at, digits), :].reshape(count * digits, N2)
 
     def inner_body(place_ref, *refs):
-        pieces, refs = refs[:levels], refs[levels + 1 :]
+        pieces, refs = refs[:levels], refs[levels:]
         tables_in, back_in, refs = refs[:4], refs[4:7], refs[7:]
         ends_ref, even_ref, odd_ref, ratio_ref, inverse_ref, edge_ref = refs[:6]
         late_ref, top_ref, even_out, odd_out = refs[6:10]
@@ -658,10 +741,10 @@
         inner_body,
         [(late * groups, N2), row, row, row] + [(early * digits, N2)] * levels,
         [
-            place, *inner_pieces, phi, *forward, backward[0], backward[2], backward[3],
+            place, *inner_pieces, *forward, backward[0], backward[2], backward[3],
             end_spectral, even, odd, ratio, inverse, edge,
         ],
-        [SMEM] + [VMEM] * levels + [pl.ANY] + [VMEM] * 13,
+        [SMEM] + [VMEM] * (levels + 13),
         [
             vmem(pad_inner, N1, N2), vmem(pad_inner * N1, N2), vmem(inner * N1, N2), vmem(rows * groups, N2),
             vmem(pad_early, N1, N2), vmem(pad_early * N1, N2),
@@ -672,23 +755,51 @@
     early_pieces = swap_levels(early_pieces)
     even2, odd2 = swap(even2, odd2)
 
-    def second_body(place_ref, couple_ref, *refs):
+    def sigma_body(place_ref, couple_ref, *refs):
         first_ref, own_top_ref, even_ref, odd_ref, even2_ref, odd2_ref, top_ref, bottom_ref = refs[:8]
-        ratio_ref, inverse_ref, edge_ref = refs[8:11]
-        tables_in, refs = refs[11:15], refs[15 + len(far) :]
-        sigma_ref, late_refs = refs[0], refs[1 : 1 + levels]
-        sum_ref, mid_ref, full_ref = refs[1 + levels :]
+        ratio_ref, edge_ref, around_ref = refs[8:11]
+        sigma_ref = refs[-1]
+        level = place_ref[0]
         got_top, got_bottom = swap_in(place_ref[1], even_ref[...], odd_ref[...])
         from_low, from_high = swap_in(place_ref[1], even2_ref[...], odd2_ref[...])
         low, high = sigmas(
-            couple_ref[OV], couple_ref[OV + rows], own_top_ref[...], first_ref[(late - 1) * groups :, :],
+            couple_ref[level, OV], couple_ref[level, OV + rows], own_top_ref[...], first_ref[(late - 1) * groups :, :],
             got_top, got_bottom, top_ref[...], bottom_ref[...], from_low, from_high,
             ratio_ref[:groups, :], ratio_ref[(rows - 1) * groups :, :], edge_ref,
+            around_ref[(OV - 1) * groups : OV * groups, :], around_ref[(2 * OV - 1) * groups :, :],
         )
         sigma_ref[:groups, :] = low
         sigma_ref[groups:, :] = high
-        late_refs[1][late * digits : late * digits + groups, :] = low
-        late_refs[1][late * digits + groups :, :] = high
+
+    (sigma,) = call(
+        sigma_body,
+        [(2 * groups, N2)],
+        [
+            place, couple_all, late_first, own_top, even, odd, even2, odd2, sent_top, sent_bottom, ratio, edge, around,
+            *early_pieces[1:],
+        ],
+        [SMEM, SMEM] + [VMEM] * 11 + [pl.ANY] * (levels - 1),
+        [],
+        groups * N2 * 40,
+        "sigma",
+    )
+    far_sigma = [send_level(sigma, mask, levels) for mask in far]
+    phi_others, psi_others = call(
+        functools.partial(partners_kernel, rows, early, levels),
+        [((levels - 1) * early * groups, N2)] * 2,
+        [place, lon_all, couple_all, eigen, sigma],
+        [SMEM, SMEM, SMEM, VMEM, pl.ANY],
+        [vmem(*early_block), vmem(*early_block)],
+        (levels - 1) * rows * groups * N2 * 20,
+        "partners",
+    )
+
+    def second_body(place_ref, *refs):
+        sigma_ref, first_ref, ratio_ref, inverse_ref, edge_ref = refs[:5]
+        tables_in, refs = refs[5:9], refs[9:]
+        late_refs = refs[:levels]
+        sum_ref, mid_ref, full_ref = refs[levels:]
+        low, high = sigma_ref[:groups, :], sigma_ref[groups:, :]
 
         def at(ref, index):
             return ref[index * groups : (index + 1) * groups, :]
@@ -708,30 +819,27 @@
                 sum_ref[here, :] = first_ref[here, :] + x_high
         backward_rows(sum_ref, late, *tables_in, mid_ref, full_ref)
         spread(place_ref, full_ref, late, late_refs)
-
-    sigma, *late_pieces = call(
+        late_refs[1][late * digits :, :] = sigma_ref[...]
+
+    late_pieces = call(
         second_body,
-        [(2 * groups, N2)]
-        + [(late * digits + (2 * groups if mask == 1 else 0), N2) for mask in range(levels)],
-        [
-            place, couple, late_first, own_top, even, odd, even2, odd2, sent_top, sent_bottom,
-            ratio, inverse, edge, *backward, *early_pieces[2:],
-        ],
-        [SMEM, SMEM] + [VMEM] * 15 + [pl.ANY] * len(far),
+        [(late * digits + (2 * groups if mask == 1 else 0), N2) for mask in range(levels)],
+        [place, sigma, late_first, ratio, inverse, edge, *backward],
+        [SMEM] + [VMEM] * 9,
         [vmem(late * groups, N2), vmem(max(pad_late, half) * N1, N2), vmem(pad_late, N1, N2)],
         late * NLON * 256 * 4,
         "second",
     )
     late_pieces = swap_levels(late_pieces)
-    sigma_pieces = [sigma, late_pieces[1]] + [send_level(sigma, mask, levels) for mask in far]
+    sigma_pieces = [sigma, late_pieces[1], *far_sigma]
     total = rows * levels * digits
     early_total = early * levels * digits
     part = const["first_back_part"]
 
     def correct(place_ref, *refs):
         pieces, sigma_refs, refs = refs[:levels], refs[levels : 2 * levels], refs[2 * levels :]
-        phi_ref, psi_ref, part_ref, turn_ref, second_ref, special_ref = refs[:6]
-        out_ref, sum_ref, mid_ref, done_ref, sem = refs[6:]
+        phi_ref, psi_ref, phi_others_ref, psi_others_ref, part_ref, turn_ref, second_ref, special_ref = refs[:8]
+        out_ref, sum_ref, mid_ref, done_ref, sem = refs[8:]
         part_rows = part_ref.shape[0] // levels
         mine = part_ref.at[pl.ds(pl.multiple_of(place_ref[0] * part_rows, part_rows), part_rows), :]
         size = early * groups
@@ -740,9 +848,11 @@
             last = sigma_refs[mask].shape[0]
             low = sigma_refs[mask][last - 2 * groups : last - groups, :]
             high = sigma_refs[mask][last - groups :, :]
-            first = pl.multiple_of(level * size, size)
-            phi_all = phi_ref[pl.ds(first, size), :].reshape(early, groups, N2)
-            psi_all = psi_ref[pl.ds(first, size), :].reshape(early, groups, N2)
+            first = (mask - 1) * size
+            phi_all = phi_others_ref[first : first + size, :] if mask else phi_ref[...]
+            psi_all = psi_others_ref[first : first + size, :] if mask else psi_ref[...]
+            phi_all = phi_all.reshape(early, groups, N2)
+            psi_all = psi_all.reshape(early, groups, N2)
             sum_ref[...] = (phi_all * low[None] + psi_all * high[None]).reshape(size, N2)
             spectral_back(sum_ref, early, pad_early, second_ref, special_ref, mid_ref)
             for pair in range(pad_early // (2 * BLOCK)):
@@ -764,33 +874,41 @@
     (out,) = call(
         correct,
         [(total, N2)],
-        [place, *early_pieces, *sigma_pieces, phi, psi, part, const["turn"], backward[2], backward[3]],
-        [SMEM] + [VMEM] * (2 * levels + 6),
+        [place, *early_pieces, *sigma_pieces, phi, psi, phi_others, psi_others, part, const["turn"], *backward[2:]],
+        [SMEM] + [VMEM] * (2 * levels + 8),
         [
             vmem(early * groups, N2), vmem(pad_early * N1, N2), vmem(early_total, N2), pltpu.SemaphoreType.DMA,
         ],
-        levels * early * NLON * 256 * 3,
+        levels * early * NLON * 256 * 40,
         "correct",
         out_spaces=[pl.ANY],
     )
 
+    chunks = 4
+
     def unpack(place_ref, *refs):
         pieces = refs[:levels]
-        out_ref, done_ref, sem = refs[levels + 1 :]
-        for mask in range(levels):
-            done_ref[pl.ds(place_ref[0] ^ mask, late * digits, stride=levels), :] = pieces[mask][: late * digits, :]
-        copy = pltpu.make_async_copy(
-            done_ref, out_ref.at[pl.ds(early_total, total - early_total), :], sem
-        )
-        copy.start()
-        copy.wait()
+        out_ref, done_ref, sems = refs[levels + 1 :]
+        lines = late * digits // chunks
+        copies = []
+        for chunk in range(chunks):
+            for mask in range(levels):
+                first = (place_ref[0] ^ mask) + chunk * lines * levels
+                done_ref[pl.ds(first, lines, stride=levels), :] = pieces[mask][chunk * lines : (chunk + 1) * lines, :]
+            here = pl.ds(chunk * lines * levels, lines * levels)
+            there = pl.ds(early_total + chunk * lines * levels, lines * levels)
+            copy = pltpu.make_async_copy(done_ref.at[here, :], out_ref.at[there, :], sems.at[chunk])
+            copy.start()
+            copies.append(copy)
+        for copy in copies:
+            copy.wait()
 
     (out,) = call(
         unpack,
         [(total, N2)],
         [place, *late_pieces, out],
         [SMEM] + [VMEM] * levels + [pl.ANY],
-        [vmem(total - early_total, N2), pltpu.SemaphoreType.DMA],
+        [vmem(total - early_total, N2), pltpu.SemaphoreType.DMA((chunks,))],
         0,
         "unpack",
         out_spaces=[pl.ANY],
@@ -857,7 +975,8 @@
 
     def edges(parity_ref, spec_ref, edge_ref, top_ref, bottom_ref, even_ref, odd_ref):
         top, bottom = edge_sums(
-            rows_of(spec_ref, groups), rows_of(spec_ref, groups, OV - rows), edge_ref, groups
+            rows_of(spec_ref, groups), rows_of(spec_ref, groups, OV - rows),
+            rows_of(edge_ref, groups, -7), rows_of(edge_ref, groups, -14),
         )
         top_ref[...] = top
         bottom_ref[...] = bottom

time: 48.2 us -> 52 us (1.079)
  local copies, waits for them, and re-layouts: 2.79 us -> 6.53 us
  waiting for transfers between devices: 8.52 us -> 4.87 us
  Pallas kernels: 16.9 us -> 19.1 us
  other arithmetic: 0.22 us -> 2 us
    ppermute x13, waiting for transfers between devices: 5.2 us -> 1.06 us  [send_level(): return lax.ppermute(piece, 'lon', [(d, d ^ mask) for d in range(size)])]
    unnamed x30, local copies, waits for them, and re-layouts: 2.63 us -> 5.01 us
    pallas_call x9 -> x11, Pallas kernels: 16.9 us -> 19.1 us  [call(): pl.pallas_call(body, out_shape=[jax.ShapeDtypeStruct(s, jnp.float32) for...]
    ppermute x2, starting transfers between devices: 3.55 us -> 1.53 us  [swap(): lax.ppermute(value_even, 'lat', even)]
    ppermute x2, starting transfers between devices: 3.92 us -> 5.04 us  [swap(): lax.ppermute(value_odd, 'lat', odd)]
    dynamic_slice x1, local copies, waits for them, and re-layouts: 0.08 us -> 0.76 us  [operator_parts(): lax.dynamic_slice_in_dim(jnp.pad(lat_coef, (OV + 1, OV + 2)), row_first,...]
    dynamic_slice x1, local copies, waits for them, and re-layouts: 0.08 us -> 0.76 us  [operator_parts(): lax.dynamic_slice_in_dim(jnp.pad(lon_coef, (OV, OV)), row_first, extent)]
    mul x1, other arithmetic: 0.07 us -> 0.72 us  [operator_parts(): level_scale[:, None] * couple[None]]
  transfers between devices with their start and end apart: 17 -> 17, of which waited for: 2 -> 3; matrix products, arithmetic and copies ran while one was open for 1% -> 6% of each run, Pallas kernels for 24% -> 20%
where the time goes in v3:
time: 52 us; the launch traced here: 51.4 us
  Pallas kernels  19.1 us (37%)
  starting transfers between devices  18.7 us (36%)
  local copies, waits for them, and re-layouts  6.53 us (13%)
  waiting for transfers between devices  4.87 us (9%)
  other arithmetic  2 us (4%)
    pallas_call x11, Pallas kernels, call(): pl.pallas_call(body, out_shape=[jax.ShapeDtypeStruct(s, jnp.float32) for...  19.1 us
    ppermute x13, starting transfers between devices, send_level(): return lax.ppermute(piece, 'lon', [(d, d ^ mask) for d in range(size)])  12.1 us
    ppermute x2, starting transfers between devices, swap(): lax.ppermute(value_odd, 'lat', odd)  5.04 us
    unnamed x30, local copies, waits for them, and re-layouts  5.01 us
    ppermute x2, waiting for transfers between devices, swap(): lax.ppermute(value_odd, 'lat', odd)  3.8 us
    ppermute x2, starting transfers between devices, swap(): lax.ppermute(value_even, 'lat', even)  1.53 us
    ppermute x13, waiting for transfers between devices, send_level(): return lax.ppermute(piece, 'lon', [(d, d ^ mask) for d in range(size)])  1.06 us
  transfers between devices with their start and end apart: 17, of which 3 were waited for; matrix products, arithmetic and copies ran while one was open for 6% of the time, Pallas kernels for 20%

profile of v3, /device:TPU:17, one launch (start us, length us, event | category | flops | bytes accessed | tf_op | source)
XLA Modules:
  0.0 51.4 jit_solution(17166851410981902050)
XLA Ops:
  0.0 0.0 copy-start.3
  0.0 0.6 %pad_add_fusion.place_ref.level_ref = s32[2]{0:T(128)} fusion(s32[1]{0:T(128)} %bitcast.1, s32[1]{0:T(128)} %bitcast), kind=kLoop, calls=%fused_computation.4 | loop fusion | flops 2 | bytes 16 | tf_op jit(solution)/shard_map/stack | solution.py:587
  0.6 2.3 %pack_ends.1 = (f32[128,128]{1,0:T(8,128)}, f32[128,128]{1,0:T(8,128)}, f32[128,128]{1,0:T(8,128)}) custom-call(s32[2]{0:T(128)} %pad_add_fusion.place_ref.level_ref, f32[1920,128]{1,0:T(8,128)} %bitcast.12), custom_call_target="tpu_custom_call" | custom-call | bytes 1179656 | tf_op jit(solution)/shard_map/pack_ends/pallas_call | solution.py:359
  2.9 0.0 copy-start.5
  3.0 0.0 copy-start.6
  3.0 1.3 %collective-permute-start.3 = (f32[128,128]{1,0:T(8,128)}, f32[128,128]{1,0:T(8,128)S(1)}, u32[]{:S(2)}, u32[]{:S(2)}) collective-permute-start(f32[128,128]{1,0:T(8,128)} %get-tuple-element.41), channel_id=1, source_target_pairs={{0,2},{1,3},{2,0},{3,1},{4,6},{5,7},{6,4},{7,5},{8,10},{9,11},{10,... | collective-permute-start | bytes 196616 | tf_op jit(solution)/shard_map/ppermute | solution.py:385
  4.2 1.1 %collective-permute-start.4 = (f32[128,128]{1,0:T(8,128)}, f32[128,128]{1,0:T(8,128)S(1)}, u32[]{:S(2)}, u32[]{:S(2)}) collective-permute-start(f32[128,128]{1,0:T(8,128)} %get-tuple-element.42), channel_id=1, source_target_pairs={{0,3},{1,2},{2,1},{3,0},{4,7},{5,6},{6,5},{7,4},{8,11},{9,10},{10,... | collective-permute-start | bytes 196616 | tf_op jit(solution)/shard_map/ppermute | solution.py:385
  5.4 0.8 %copy-done.7 = f32[128,128]{1,0:T(8,128)S(1)} copy-done((f32[128,128]{1,0:T(8,128)S(1)}, f32[128,128]{1,0:T(8,128)}, u32[]{:S(2)}) %copy-start.7) | copy-done | bytes 65560
  6.2 0.6 %copy-done.12 = s32[2]{0:T(128)S(1)} copy-done((s32[2]{0:T(128)S(1)}, s32[2]{0:T(128)}, u32[]{:S(2)}) %copy-start.12) | copy-done | bytes 32
  6.8 0.6 %pack.1 = (f32[352,128]{1,0:T(8,128)S(1)}, f32[480,128]{1,0:T(8,128)S(1)}, f32[352,128]{1,0:T(8,128)S(1)}, f32[352,128]{1,0:T(8,128)S(1)}) custom-call(s32[2]{0:T(128)S(1)} %copy-done.12, f32[1920,128]{1,0:T(8,128)S(1)} %bitcast.13, f32[128,128]{1,0:T(8,128)S(1)} %copy-done.7), custom_call_target="tpu_custom_call" | custom-call | bytes 1835016 | tf_op jit(solution)/shard_map/pack/pallas_call | solution.py:359
  7.4 1.3 %collective-permute-start.1 = (f32[352,128]{1,0:T(8,128)S(1)}, f32[352,128]{1,0:T(8,128)S(1)}, u32[]{:S(2)}, u32[]{:S(2)}) collective-permute-start(f32[352,128]{1,0:T(8,128)S(1)} %get-tuple-element.39), channel_id=1, source_target_pairs={{0,2},{1,3},{2,0},{3,1},{4,6},{5,7},{6,4},{7,5},{8,10},{9,11},{10,... | collective-permute-start | bytes 540680 | tf_op jit(solution)/shard_map/ppermute | solution.py:385
  8.7 0.3 collective-permute-start.2
  9.0 0.4 collective-permute-start
  9.3 0.8 %pad_dynamic-slice_fusion.1 = f32[77]{0:T(128)S(1)} fusion(s32[]{:T(128)S(6)} %select_n.14, f32[479]{0:T(512)} %param.15), kind=kLoop, calls=%fused_computation.1 | loop fusion | bytes 2228 | tf_op jit(solution)/shard_map/dynamic_slice | solution.py:396
  10.1 0.7 %broadcast_multiply_fusion.1.couple_ref = f32[4,77]{1,0:T(4,128)S(1)} fusion(f32[77]{0:T(128)S(1)} %pad_dynamic-slice_fusion.1, f32[4]{0:T(128)} %param.16), kind=kLoop, calls=%fused_computation.3 | loop fusion | flops 308 | bytes 1556 | tf_op jit(solution)/shard_map/mul | solution.py:397
  10.8 0.8 %pad_dynamic-slice_fusion = f32[76]{0:T(128)S(1)} fusion(s32[]{:T(128)S(6)} %select_n.15, f32[480]{0:T(512)} %param.14), kind=kLoop, calls=%fused_computation | loop fusion | bytes 2228 | tf_op jit(solution)/shard_map/dynamic_slice | solution.py:395
  11.6 0.7 %broadcast_multiply_fusion.lon_ref = f32[4,76]{1,0:T(4,128)S(1)} fusion(f32[76]{0:T(128)S(1)} %pad_dynamic-slice_fusion, f32[4]{0:T(128)} %param.16), kind=kLoop, calls=%fused_computation.2 | loop fusion | flops 304 | bytes 1536 | tf_op jit(solution)/shard_map/mul | solution.py:397
  12.3 0.7 %copy-done.10 = f32[32,128]{1,0:T(8,128)S(1)} copy-done((f32[32,128]{1,0:T(8,128)S(1)}, f32[32,128]{1,0:T(8,128)}, u32[]{:S(2)}) %copy-start.10) | copy-done | bytes 16408
  13.0 0.6 %copy-done.13 = s32[2]{0:T(128)S(1)} copy-done((s32[2]{0:T(128)S(1)}, s32[2]{0:T(128)}, u32[]{:S(2)}) %copy-start.13) | copy-done | bytes 32
  13.6 0.7 %edge.1.refs_8_.refs_10_ = f32[512,128]{1,0:T(8,128)S(1)} custom-call(s32[2]{0:T(128)S(1)} %copy-done.13, f32[4,76]{1,0:T(4,128)S(1)} %broadcast_multiply_fusion.lon_ref, f32[4,77]{1,0:T(4,128)S(1)} %broadcast_multiply_fusion.1.couple_ref, f32[32,128]{1,0:T(8,128)S(1)} %copy-done.10), custom_call_target="tpu_custom_call" | custom-call | flops 1310720 | bytes 280984 | tf_op jit(solution)/shard_map/edge/pallas_call | solution.py:359
  14.4 0.8 %copy-done.8 = f32[128,128]{1,0:T(8,128)S(1)} copy-done((f32[128,128]{1,0:T(8,128)S(1)}, f32[128,128]{1,0:T(8,128)}, u32[]{:S(2)}) %copy-start.8) | copy-done | bytes 65560
  15.2 0.7 %copy-done.9 = f32[32,128]{1,0:T(8,128)S(1)} copy-done((f32[32,128]{1,0:T(8,128)S(1)}, f32[32,128]{1,0:T(8,128)}, u32[]{:S(2)}) %copy-start.9) | copy-done | bytes 16408
  15.9 1.2 %ends.1 = (f32[512,128]{1,0:T(8,128)S(1)}, f32[32,128]{1,0:T(8,128)S(1)}, f32[32,128]{1,0:T(8,128)S(1)}, f32[32,128]{1,0:T(8,128)S(1)}, f32[32,128]{1,0:T(8,128)S(1)}) custom-call(s32[2]{0:T(128)S(1)} %copy-done.13, f32[128,128]{1,0:T(8,128)S(1)} %copy-done.8, f32[480,128]{1,0:T(8,128)S(1)} %collective-permute-done.refs_1_, ...), custom_call_target="tpu_custom_call" | custom-call | flops 67108864 | bytes 1835016 | tf_op jit(solution)/shard_map/ends/pallas_call | solution.py:359
  17.1 1.3 %collective-permute-start.5 = (f32[32,128]{1,0:T(8,128)S(1)}, f32[32,128]{1,0:T(8,128)S(1)}, u32[]{:S(2)}, u32[]{:S(2)}) collective-permute-start(f32[32,128]{1,0:T(8,128)S(1)} %get-tuple-element.44), channel_id=1, source_target_pairs={{0,4},{4,0},{8,12},{12,8},{16,20},{20,16},{24,28},{28,24},{1,5},{5... | collective-permute-start | bytes 49160 | tf_op jit(solution)/shard_map/ppermute | solution.py:381
  18.5 2.0 %collective-permute-start.6 = (f32[32,128]{1,0:T(8,128)S(1)}, f32[32,128]{1,0:T(8,128)S(1)}, u32[]{:S(2)}, u32[]{:S(2)}) collective-permute-start(f32[32,128]{1,0:T(8,128)S(1)} %get-tuple-element.45), channel_id=1, source_target_pairs={{4,8},{8,4},{12,16},{16,12},{20,24},{24,20},{5,9},{9,5},{13,17},{1... | collective-permute-start | bytes 49160 | tf_op jit(solution)/shard_map/ppermute | solution.py:381
  20.5 0.0 copy-start.11
  20.5 0.7 %copy-done.11 = f32[32,128]{1,0:T(8,128)S(1)} copy-done((f32[32,128]{1,0:T(8,128)S(1)}, f32[32,128]{1,0:T(8,128)}, u32[]{:S(2)}) %copy-start.11) | copy-done | bytes 16408
  21.2 1.1 %own.1 = (f32[1920,128]{1,0:T(8,128)S(1)}, f32[1920,128]{1,0:T(8,128)S(1)}, f32[160,128]{1,0:T(8,128)S(1)}, f32[1024,128]{1,0:T(8,128)S(1)}, f32[1024,128]{1,0:T(8,128)S(1)}) custom-call(s32[2]{0:T(128)S(1)} %copy-done.13, f32[4,76]{1,0:T(4,128)S(1)} %broadcast_multiply_fusion.lon_ref, f32[4,77]{1,0:T(4,128)S(1)} %broadcast_multiply_fusion.1.couple_ref, ...), custom_call_target="tpu_custom_call" | custom-call | flops 4915200 | bytes 3115416 | tf_op jit(solution)/shard_map/own/pallas_call | solution.py:359
  22.3 1.5 %collective-permute-done.6.refs_13_.refs_3_ = f32[32,128]{1,0:T(8,128)S(1)} collective-permute-done((f32[32,128]{1,0:T(8,128)S(1)}, f32[32,128]{1,0:T(8,128)S(1)}, u32[]{:S(2)}, u32[]{:S(2)}) %collective-permute-start.6) | collective-permute-done | bytes 16416 | tf_op jit(solution)/shard_map/ppermute | solution.py:381
  23.8 3.1 %inner.1 = (f32[896,128]{1,0:T(8,128)S(1)}, f32[32,128]{1,0:T(8,128)S(1)}, f32[32,128]{1,0:T(8,128)S(1)}, f32[32,128]{1,0:T(8,128)S(1)}, f32[256,128]{1,0:T(8,12...) custom-call(s32[2]{0:T(128)S(1)} %copy-done.13, ...), custom_call_target="tpu_custom_call" | custom-call | flops 318767104 | bytes 5750792 | tf_op jit(solution)/shard_map/inner/pallas_call | solution.py:359
  26.9 1.7 %collective-permute-start.9 = (f32[256,128]{1,0:T(8,128)S(1)}, f32[256,128]{1,0:T(8,128)S(1)}, u32[]{:S(2)}, u32[]{:S(2)}) collective-permute-start(f32[256,128]{1,0:T(8,128)S(1)} %get-tuple-element.55), channel_id=1, source_target_pairs={{0,1},{1,0},{2,3},{3,2},{4,5},{5,4},{6,7},{7,6},{8,9},{9,8},{10,11... | collective-permute-start | bytes 393224 | tf_op jit(solution)/shard_map/ppermute | solution.py:385
  28.6 1.1 %collective-permute-start.10 = (f32[256,128]{1,0:T(8,128)S(1)}, f32[256,128]{1,0:T(8,128)S(1)}, u32[]{:S(2)}, u32[]{:S(2)}) collective-permute-start(f32[256,128]{1,0:T(8,128)S(1)} %get-tuple-element.56), channel_id=1, source_target_pairs={{0,2},{1,3},{2,0},{3,1},{4,6},{5,7},{6,4},{7,5},{8,10},{9,11},{10,... | collective-permute-start | bytes 393224 | tf_op jit(solution)/shard_map/ppermute | solution.py:385
  29.6 0.6 %collective-permute-start.11 = (f32[256,128]{1,0:T(8,128)S(1)}, f32[256,128]{1,0:T(8,128)S(1)}, u32[]{:S(2)}, u32[]{:S(2)}) collective-permute-start(f32[256,128]{1,0:T(8,128)S(1)} %get-tuple-element.57), channel_id=1, source_target_pairs={{0,3},{1,2},{2,1},{3,0},{4,7},{5,6},{6,5},{7,4},{8,11},{9,10},{10,... | collective-permute-start | bytes 393224 | tf_op jit(solution)/shard_map/ppermute | solution.py:385
  30.3 0.2 collective-permute-start.7
  30.5 3.0 %collective-permute-start.8 = (f32[32,128]{1,0:T(8,128)S(1)}, f32[32,128]{1,0:T(8,128)S(1)}, u32[]{:S(2)}, u32[]{:S(2)}) collective-permute-start(f32[32,128]{1,0:T(8,128)S(1)} %get-tuple-element.52), channel_id=1, source_target_pairs={{4,8},{8,4},{12,16},{16,12},{20,24},{24,20},{5,9},{9,5},{13,17},{1... | collective-permute-start | bytes 49160 | tf_op jit(solution)/shard_map/ppermute | solution.py:381
  33.6 2.3 %collective-permute-done.8.refs_5_ = f32[32,128]{1,0:T(8,128)S(1)} collective-permute-done((f32[32,128]{1,0:T(8,128)S(1)}, f32[32,128]{1,0:T(8,128)S(1)}, u32[]{:S(2)}, u32[]{:S(2)}) %collective-permute-start.8) | collective-permute-done | bytes 16416 | tf_op jit(solution)/shard_map/ppermute | solution.py:381
  35.9 1.0 %collective-permute-done.11.refs_13_.refs_3_ = f32[256,128]{1,0:T(8,128)S(1)} collective-permute-done((f32[256,128]{1,0:T(8,128)S(1)}, f32[256,128]{1,0:T(8,128)S(1)}, u32[]{:S(2)}, u32[]{:S(2)}) %collective-permute-start.11) | collective-permute-done | bytes 131104 | tf_op jit(solution)/shard_map/ppermute | solution.py:385
  36.9 0.6 %sigma.1.refs_0_.after_ref.refs_4_ = f32[64,128]{1,0:T(8,128)S(1)} custom-call(s32[2]{0:T(128)S(1)} %copy-done.13, f32[4,77]{1,0:T(4,128)S(1)} %broadcast_multiply_fusion.1.couple_ref, f32[896,128]{1,0:T(8,128)S(1)} %get-tuple-element.49.refs_0_.refs_1_, f32[32,128]{1,0:T(8,128)S(1)} %get-tuple-element.50.refs_1_, ...), custom_call_target="tpu_custom_call" | custom-call | flops 163840 | bytes 2327768 | tf_op jit(solution)/shard_map/sigma/pallas_call | solution.py:359
  37.5 0.0 copy-start.14
  37.5 1.6 %second.1 = (f32[224,128]{1,0:T(8,128)S(1)}, f32[288,128]{1,0:T(8,128)S(1)}, f32[224,128]{1,0:T(8,128)S(1)}, f32[224,128]{1,0:T(8,128)S(1)}) custom-call(s32[2]{0:T(128)S(1)} %copy-done.13, f32[64,128]{1,0:T(8,128)S(1)} %sigma.1.refs_0_.after_ref.refs_4_, f32[896,128]{1,0:T(8,128)S(1)} %get-tuple-element.49.refs_0_.refs_1_, ...), custom_call_target="tpu_custom_call" | custom-call | flops 117440512 | bytes 3833864 | tf_op jit(solution)/shard_map/second/pallas_call | solution.py:359
  39.2 0.6 %collective-permute-start.12 = (f32[288,128]{1,0:T(8,128)S(1)}, f32[288,128]{1,0:T(8,128)S(1)}, u32[]{:S(2)}, u32[]{:S(2)}) collective-permute-start(f32[288,128]{1,0:T(8,128)S(1)} %get-tuple-element.59), channel_id=1, source_target_pairs={{0,1},{1,0},{2,3},{3,2},{4,5},{5,4},{6,7},{7,6},{8,9},{9,8},{10,11... | collective-permute-start | bytes 442376 | tf_op jit(solution)/shard_map/ppermute | solution.py:385
  39.8 1.0 %collective-permute-start.16 = (f32[64,128]{1,0:T(8,128)S(1)}, f32[64,128]{1,0:T(8,128)S(1)}, u32[]{:S(2)}, u32[]{:S(2)}) collective-permute-start(f32[64,128]{1,0:T(8,128)S(1)} %sigma.1.refs_0_.after_ref.refs_4_), channel_id=1, source_target_pairs={{0,3},{1,2},{2,1},{3,0},{4,7},{5,6},{6,5},{7,4},{8,11},{9,10},{10,... | collective-permute-start | bytes 98312 | tf_op jit(solution)/shard_map/ppermute | solution.py:385
  40.8 0.4 collective-permute-start.15
  41.2 1.1 %collective-permute-start.13 = (f32[224,128]{1,0:T(8,128)S(1)}, f32[224,128]{1,0:T(8,128)S(1)}, u32[]{:S(2)}, u32[]{:S(2)}) collective-permute-start(f32[224,128]{1,0:T(8,128)S(1)} %get-tuple-element.60), channel_id=1, source_target_pairs={{0,2},{1,3},{2,0},{3,1},{4,6},{5,7},{6,4},{7,5},{8,10},{9,11},{10,... | collective-permute-start | bytes 344072 | tf_op jit(solution)/shard_map/ppermute | solution.py:385
  42.3 1.3 %collective-permute-start.14 = (f32[224,128]{1,0:T(8,128)S(1)}, f32[224,128]{1,0:T(8,128)S(1)}, u32[]{:S(2)}, u32[]{:S(2)}) collective-permute-start(f32[224,128]{1,0:T(8,128)S(1)} %get-tuple-element.61), channel_id=1, source_target_pairs={{0,3},{1,2},{2,1},{3,0},{4,7},{5,6},{6,5},{7,4},{8,11},{9,10},{10,... | collective-permute-start | bytes 344072 | tf_op jit(solution)/shard_map/ppermute | solution.py:385
  43.6 2.2 %partners.1 = (f32[3072,128]{1,0:T(8,128)S(1)}, f32[3072,128]{1,0:T(8,128)S(1)}) custom-call(s32[2]{0:T(128)S(1)} %copy-done.13, f32[4,76]{1,0:T(4,128)S(1)} %broadcast_multiply_fusion.lon_ref, f32[4,77]{1,0:T(4,128)S(1)} %broadcast_multiply_fusion.1.couple_ref, f32[32,128]{1,0:T(8,128)S(1)} %copy-done.11, f32[64,128]{1,0:T(8,128)S(1)} %sigma.1.refs_0_.after_ref.refs_4_), custom_call_target="tpu_custom_call" | custom-call | flops 14745600 | bytes 3197336 | tf_op jit(solution)/shard_map/partners/pallas_call | solution.py:359
  45.8 4.2 %correct.1.refs_4_ = f32[1920,128]{1,0:T(8,128)} custom-call(s32[2]{0:T(128)S(1)} %copy-done.13, f32[256,128]{1,0:T(8,128)S(1)} %get-tuple-element.62.refs_0_, f32[256,128]{1,0:T(8,128)S(1)} %collective-permute-done.9.refs_11_.refs_1_, f32[256,128]{1,0:T(8,128)S(1)} %collective-permute-done.10.refs_12_.refs_2_, ...), custom_call_target="tpu_custom_call" | custom-call | flops 5368709120 | bytes 6750216 | tf_op jit(solution)/shard_map/correct/pallas_call | solution.py:359
  50.1 1.3 %unpack.1 = f32[1920,128]{1,0:T(8,128)} custom-call(s32[2]{0:T(128)S(1)} %copy-done.13, f32[224,128]{1,0:T(8,128)S(1)} %get-tuple-element.58.refs_0_, f32[288,128]{1,0:T(8,128)S(1)} %collective-permute-done.12.refs_5_.refs_1_, f32[224,128]{1,0:T(8,128)S(1)} %collective-permute-done.13.refs_2_, ...), custom_call_target="tpu_custom_call", output_to_operand_aliasing={{}: (5, {})} | custom-call | bytes 2457608 | tf_op jit(solution)/shard_map/unpack/pallas_call | solution.py:359
  (32 shorter events, 0.1 us)
Async XLA Ops:
  0.0 5.3 %copy-start = (f32[60,4,1024]{2,1,0:T(4,128)S(1)}, f32[60,4,1024]{2,1,0:T(4,128)}, u32[]{:S(2)}) copy-start(f32[60,4,1024]{2,1,0:T(4,128)} %param.13) | copy-start | bytes 2949124
  0.0 14.3 %copy-start.1 = (bf16[512,256]{1,0:T(8,128)(2,1)S(1)}, bf16[512,256]{1,0:T(8,128)(2,1)}, u32[]{:S(2)}) copy-start(bf16[512,256]{1,0:T(8,128)(2,1)} %constant.54.clone.refs_7_) | copy-start | bytes 786436
  0.0 14.3 %copy-start.2 = (bf16[512,256]{1,0:T(8,128)(2,1)S(1)}, bf16[512,256]{1,0:T(8,128)(2,1)}, u32[]{:S(2)}) copy-start(bf16[512,256]{1,0:T(8,128)(2,1)} %constant.52.clone.refs_6_) | copy-start | bytes 786436
  0.0 14.3 %copy-start.3 = (bf16[512,256]{1,0:T(8,128)(2,1)S(1)}, bf16[512,256]{1,0:T(8,128)(2,1)}, u32[]{:S(2)}) copy-start(bf16[512,256]{1,0:T(8,128)(2,1)} %constant.50.clone.refs_4_) | copy-start | bytes 786436
  2.9 20.9 %copy-start.4 = (bf16[512,256]{1,0:T(8,128)(2,1)S(1)}, bf16[512,256]{1,0:T(8,128)(2,1)}, u32[]{:S(2)}) copy-start(bf16[512,256]{1,0:T(8,128)(2,1)} %constant.55.clone.refs_10_.refs_8_.refs_15_) | copy-start | bytes 786436
  2.9 20.9 %copy-start.5 = (bf16[512,256]{1,0:T(8,128)(2,1)S(1)}, bf16[512,256]{1,0:T(8,128)(2,1)}, u32[]{:S(2)}) copy-start(bf16[512,256]{1,0:T(8,128)(2,1)} %constant.53.clone.refs_9_.refs_7_.refs_14_) | copy-start | bytes 786436
  3.0 20.9 %copy-start.6 = (bf16[512,256]{1,0:T(8,128)(2,1)S(1)}, bf16[512,256]{1,0:T(8,128)(2,1)}, u32[]{:S(2)}) copy-start(bf16[512,256]{1,0:T(8,128)(2,1)} %constant.51.clone.refs_8_.refs_5_) | copy-start | bytes 786436
  3.0 11.3 %collective-permute-start.3 = (f32[128,128]{1,0:T(8,128)}, f32[128,128]{1,0:T(8,128)S(1)}, u32[]{:S(2)}, u32[]{:S(2)}) collective-permute-start(f32[128,128]{1,0:T(8,128)} %get-tuple-element.41), channel_id=1, source_target_pairs={{0,2},{1,3},{2,0},{3,1},{4,6},{5,7},{6,4},{7,5},{8,10},{9,11},{10,... | collective-permute-start | bytes 196616 | tf_op jit(solution)/shard_map/ppermute | solution.py:385
  4.2 10.1 %collective-permute-start.4 = (f32[128,128]{1,0:T(8,128)}, f32[128,128]{1,0:T(8,128)S(1)}, u32[]{:S(2)}, u32[]{:S(2)}) collective-permute-start(f32[128,128]{1,0:T(8,128)} %get-tuple-element.42), channel_id=1, source_target_pairs={{0,3},{1,2},{2,1},{3,0},{4,7},{5,6},{6,5},{7,4},{8,11},{9,10},{10,... | collective-permute-start | bytes 196616 | tf_op jit(solution)/shard_map/ppermute | solution.py:385
  5.3 0.8 %copy-start.7 = (f32[128,128]{1,0:T(8,128)S(1)}, f32[128,128]{1,0:T(8,128)}, u32[]{:S(2)}) copy-start(f32[128,128]{1,0:T(8,128)} %get-tuple-element.36.after_ref.refs_0_) | copy-start | bytes 196612
  6.2 0.6 %copy-start.12 = (s32[2]{0:T(128)S(1)}, s32[2]{0:T(128)}, u32[]{:S(2)}) copy-start(s32[2]{0:T(128)} %pad_add_fusion.place_ref.level_ref) | copy-start | bytes 28
  7.4 14.9 %collective-permute-start.1 = (f32[352,128]{1,0:T(8,128)S(1)}, f32[352,128]{1,0:T(8,128)S(1)}, u32[]{:S(2)}, u32[]{:S(2)}) collective-permute-start(f32[352,128]{1,0:T(8,128)S(1)} %get-tuple-element.39), channel_id=1, source_target_pairs={{0,2},{1,3},{2,0},{3,1},{4,6},{5,7},{6,4},{7,5},{8,10},{9,11},{10,... | collective-permute-start | bytes 540680 | tf_op jit(solution)/shard_map/ppermute | solution.py:385
  8.7 13.6 %collective-permute-start.2 = (f32[352,128]{1,0:T(8,128)S(1)}, f32[352,128]{1,0:T(8,128)S(1)}, u32[]{:S(2)}, u32[]{:S(2)}) collective-permute-start(f32[352,128]{1,0:T(8,128)S(1)} %get-tuple-element.40), channel_id=1, source_target_pairs={{0,3},{1,2},{2,1},{3,0},{4,7},{5,6},{6,5},{7,4},{8,11},{9,10},{10,... | collective-permute-start | bytes 540680 | tf_op jit(solution)/shard_map/ppermute | solution.py:385
  9.0 5.3 %collective-permute-start = (f32[480,128]{1,0:T(8,128)S(1)}, f32[480,128]{1,0:T(8,128)S(1)}, u32[]{:S(2)}, u32[]{:S(2)}) collective-permute-start(f32[480,128]{1,0:T(8,128)S(1)} %get-tuple-element.38), channel_id=1, source_target_pairs={{0,1},{1,0},{2,3},{3,2},{4,5},{5,4},{6,7},{7,6},{8,9},{9,8},{10,11... | collective-permute-start | bytes 737288 | tf_op jit(solution)/shard_map/ppermute | solution.py:385
  12.3 0.7 %copy-start.10 = (f32[32,128]{1,0:T(8,128)S(1)}, f32[32,128]{1,0:T(8,128)}, u32[]{:S(2)}) copy-start(f32[32,128]{1,0:T(8,128)} %constant.63.eigen_ref) | copy-start | bytes 49156
  13.0 0.6 %copy-start.13 = (s32[2]{0:T(128)S(1)}, s32[2]{0:T(128)}, u32[]{:S(2)}) copy-start(s32[2]{0:T(128)} %pad_add_fusion.place_ref.level_ref) | copy-start | bytes 28
  14.4 0.8 %copy-start.8 = (f32[128,128]{1,0:T(8,128)S(1)}, f32[128,128]{1,0:T(8,128)}, u32[]{:S(2)}) copy-start(f32[128,128]{1,0:T(8,128)} %get-tuple-element.36.after_ref.refs_0_) | copy-start | bytes 196612
  15.2 0.7 %copy-start.9 = (f32[32,128]{1,0:T(8,128)S(1)}, f32[32,128]{1,0:T(8,128)}, u32[]{:S(2)}) copy-start(f32[32,128]{1,0:T(8,128)} %constant.56.clone.refs_5_.refs_6_.refs_13_) | copy-start | bytes 49156
  17.1 5.2 %collective-permute-start.5 = (f32[32,128]{1,0:T(8,128)S(1)}, f32[32,128]{1,0:T(8,128)S(1)}, u32[]{:S(2)}, u32[]{:S(2)}) collective-permute-start(f32[32,128]{1,0:T(8,128)S(1)} %get-tuple-element.44), channel_id=1, source_target_pairs={{0,4},{4,0},{8,12},{12,8},{16,20},{20,16},{24,28},{28,24},{1,5},{5... | collective-permute-start | bytes 49160 | tf_op jit(solution)/shard_map/ppermute | solution.py:381
  18.5 5.4 %collective-permute-start.6 = (f32[32,128]{1,0:T(8,128)S(1)}, f32[32,128]{1,0:T(8,128)S(1)}, u32[]{:S(2)}, u32[]{:S(2)}) collective-permute-start(f32[32,128]{1,0:T(8,128)S(1)} %get-tuple-element.45), channel_id=1, source_target_pairs={{4,8},{8,4},{12,16},{16,12},{20,24},{24,20},{5,9},{9,5},{13,17},{1... | collective-permute-start | bytes 49160 | tf_op jit(solution)/shard_map/ppermute | solution.py:381
  20.5 0.7 %copy-start.11 = (f32[32,128]{1,0:T(8,128)S(1)}, f32[32,128]{1,0:T(8,128)}, u32[]{:S(2)}) copy-start(f32[32,128]{1,0:T(8,128)} %constant.63.eigen_ref) | copy-start | bytes 49156
  26.9 9.0 %collective-permute-start.9 = (f32[256,128]{1,0:T(8,128)S(1)}, f32[256,128]{1,0:T(8,128)S(1)}, u32[]{:S(2)}, u32[]{:S(2)}) collective-permute-start(f32[256,128]{1,0:T(8,128)S(1)} %get-tuple-element.55), channel_id=1, source_target_pairs={{0,1},{1,0},{2,3},{3,2},{4,5},{5,4},{6,7},{7,6},{8,9},{9,8},{10,11... | collective-permute-start | bytes 393224 | tf_op jit(solution)/shard_map/ppermute | solution.py:385
  28.6 7.3 %collective-permute-start.10 = (f32[256,128]{1,0:T(8,128)S(1)}, f32[256,128]{1,0:T(8,128)S(1)}, u32[]{:S(2)}, u32[]{:S(2)}) collective-permute-start(f32[256,128]{1,0:T(8,128)S(1)} %get-tuple-element.56), channel_id=1, source_target_pairs={{0,2},{1,3},{2,0},{3,1},{4,6},{5,7},{6,4},{7,5},{8,10},{9,11},{10,... | collective-permute-start | bytes 393224 | tf_op jit(solution)/shard_map/ppermute | solution.py:385
  29.6 7.3 %collective-permute-start.11 = (f32[256,128]{1,0:T(8,128)S(1)}, f32[256,128]{1,0:T(8,128)S(1)}, u32[]{:S(2)}, u32[]{:S(2)}) collective-permute-start(f32[256,128]{1,0:T(8,128)S(1)} %get-tuple-element.57), channel_id=1, source_target_pairs={{0,3},{1,2},{2,1},{3,0},{4,7},{5,6},{6,5},{7,4},{8,11},{9,10},{10,... | collective-permute-start | bytes 393224 | tf_op jit(solution)/shard_map/ppermute | solution.py:385
  30.3 3.3 %collective-permute-start.7 = (f32[32,128]{1,0:T(8,128)S(1)}, f32[32,128]{1,0:T(8,128)S(1)}, u32[]{:S(2)}, u32[]{:S(2)}) collective-permute-start(f32[32,128]{1,0:T(8,128)S(1)} %get-tuple-element.51), channel_id=1, source_target_pairs={{0,4},{4,0},{8,12},{12,8},{16,20},{20,16},{24,28},{28,24},{1,5},{5... | collective-permute-start | bytes 49160 | tf_op jit(solution)/shard_map/ppermute | solution.py:381
  30.5 5.4 %collective-permute-start.8 = (f32[32,128]{1,0:T(8,128)S(1)}, f32[32,128]{1,0:T(8,128)S(1)}, u32[]{:S(2)}, u32[]{:S(2)}) collective-permute-start(f32[32,128]{1,0:T(8,128)S(1)} %get-tuple-element.52), channel_id=1, source_target_pairs={{4,8},{8,4},{12,16},{16,12},{20,24},{24,20},{5,9},{9,5},{13,17},{1... | collective-permute-start | bytes 49160 | tf_op jit(solution)/shard_map/ppermute | solution.py:381
  37.5 8.3 %copy-start.14 = (bf16[512,256]{1,0:T(8,128)(2,1)S(1)}, bf16[512,256]{1,0:T(8,128)(2,1)}, u32[]{:S(2)}) copy-start(bf16[512,256]{1,0:T(8,128)(2,1)} %constant.49.clone.refs_12_) | copy-start | bytes 786436
  39.2 6.6 %collective-permute-start.12 = (f32[288,128]{1,0:T(8,128)S(1)}, f32[288,128]{1,0:T(8,128)S(1)}, u32[]{:S(2)}, u32[]{:S(2)}) collective-permute-start(f32[288,128]{1,0:T(8,128)S(1)} %get-tuple-element.59), channel_id=1, source_target_pairs={{0,1},{1,0},{2,3},{3,2},{4,5},{5,4},{6,7},{7,6},{8,9},{9,8},{10,11... | collective-permute-start | bytes 442376 | tf_op jit(solution)/shard_map/ppermute | solution.py:385
  39.8 6.0 %collective-permute-start.16 = (f32[64,128]{1,0:T(8,128)S(1)}, f32[64,128]{1,0:T(8,128)S(1)}, u32[]{:S(2)}, u32[]{:S(2)}) collective-permute-start(f32[64,128]{1,0:T(8,128)S(1)} %sigma.1.refs_0_.after_ref.refs_4_), channel_id=1, source_target_pairs={{0,3},{1,2},{2,1},{3,0},{4,7},{5,6},{6,5},{7,4},{8,11},{9,10},{10,... | collective-permute-start | bytes 98312 | tf_op jit(solution)/shard_map/ppermute | solution.py:385
  40.8 5.0 %collective-permute-start.15 = (f32[64,128]{1,0:T(8,128)S(1)}, f32[64,128]{1,0:T(8,128)S(1)}, u32[]{:S(2)}, u32[]{:S(2)}) collective-permute-start(f32[64,128]{1,0:T(8,128)S(1)} %sigma.1.refs_0_.after_ref.refs_4_), channel_id=1, source_target_pairs={{0,2},{1,3},{2,0},{3,1},{4,6},{5,7},{6,4},{7,5},{8,10},{9,11},{10,... | collective-permute-start | bytes 98312 | tf_op jit(solution)/shard_map/ppermute | solution.py:385
  41.2 8.8 %collective-permute-start.13 = (f32[224,128]{1,0:T(8,128)S(1)}, f32[224,128]{1,0:T(8,128)S(1)}, u32[]{:S(2)}, u32[]{:S(2)}) collective-permute-start(f32[224,128]{1,0:T(8,128)S(1)} %get-tuple-element.60), channel_id=1, source_target_pairs={{0,2},{1,3},{2,0},{3,1},{4,6},{5,7},{6,4},{7,5},{8,10},{9,11},{10,... | collective-permute-start | bytes 344072 | tf_op jit(solution)/shard_map/ppermute | solution.py:385
  42.3 7.8 %collective-permute-start.14 = (f32[224,128]{1,0:T(8,128)S(1)}, f32[224,128]{1,0:T(8,128)S(1)}, u32[]{:S(2)}, u32[]{:S(2)}) collective-permute-start(f32[224,128]{1,0:T(8,128)S(1)} %get-tuple-element.61), channel_id=1, source_target_pairs={{0,3},{1,2},{2,1},{3,0},{4,7},{5,6},{6,5},{7,4},{8,11},{9,10},{10,... | collective-permute-start | bytes 344072 | tf_op jit(solution)/shard_map/ppermute | solution.py:385

commit v4 on v3

--- a/solution.py
+++ b/solution.py
@@ -354,7 +354,7 @@
     meet(rows, groups, low, high, ratio_ref, inverse_ref, edge_ref, at, lambda i: at(mid_ref, i), put)
 
 
-def call(body, outs, ins, spaces, scratch, flops, name, out_spaces=None, aliases=None, limit=48):
+def call(body, outs, ins, spaces, scratch, flops, name, out_spaces=None, aliases=None):
     nbytes = sum(x.size * x.dtype.itemsize for x in ins) + sum(4 * math.prod(s) for s in outs)
     out = pl.pallas_call(
         body,
@@ -363,7 +363,7 @@
         out_specs=[pl.BlockSpec(memory_space=s) for s in out_spaces or [VMEM] * len(outs)],
         input_output_aliases=aliases or {},
         scratch_shapes=scratch,
-        compiler_params=pltpu.CompilerParams(vmem_limit_bytes=limit << 20),
+        compiler_params=pltpu.CompilerParams(vmem_limit_bytes=48 << 20),
         cost_estimate=pl.CostEstimate(flops=flops, bytes_accessed=nbytes, transcendentals=0),
         name=name,
     )(*ins)
@@ -378,7 +378,8 @@
     count = lax.axis_size("lat")
     even = [(i, i ^ 1) for i in range(count) if (i ^ 1) < count]
     odd = [(i, ((i + 1) ^ 1) - 1) for i in range(1, count) if ((i + 1) ^ 1) - 1 < count]
-    return lax.ppermute(value_even, "lat", even), lax.ppermute(value_odd, "lat", odd)
+    value_odd = lax.ppermute(value_odd, "lat", odd)
+    return lax.ppermute(value_even, "lat", even), value_odd
 
 
 def send_level(piece, mask, size):
@@ -427,6 +428,11 @@
 
 def early_rows(rows):
     return rows // 2 + 2
+
+
+def inverses(one, other):
+    inverse = 1.0 / (one * other)
+    return other * inverse, one * inverse
 
 
 def edge_kernel(rows, level_ref, lon_ref, couple_ref, eigen_ref, out_ref):
@@ -446,8 +452,7 @@
             out_ref[(OV + i - 1) * groups : (OV + i) * groups, :] = high_ratio
             low = 1.0 + lon_ref[level, e] * eigen + low_ratio * low
             high = 1.0 + lon_ref[level, f] * eigen + high_ratio * high
-        low_inverse = 1.0 / (couple_ref[level, e + 1] + low)
-        high_inverse = 1.0 / (couple_ref[level, f] + high)
+        low_inverse, high_inverse = inverses(couple_ref[level, e + 1] + low, couple_ref[level, f] + high)
     out_ref[(OV - 1) * groups : OV * groups, :] = low_inverse
     out_ref[(2 * OV - 1) * groups :, :] = high_inverse
 
@@ -474,8 +479,7 @@
             high = plain(f) + high_ratio * high
         low_divisor = couple_ref[level, e + 1] + low
         high_divisor = couple_ref[level, f] + high
-        low_inverse = 1.0 / low_divisor
-        high_inverse = 1.0 / high_divisor
+        low_inverse, high_inverse = inverses(low_divisor, high_divisor)
         if i == -1:
             keep(0, low_inverse)
             keep(1, high_inverse)
@@ -549,9 +553,9 @@
 
 
 def partners_kernel(
-    rows, early, levels, place_ref, lon_ref, couple_ref, eigen_ref, after_ref, phi_ref, psi_ref, kept_ref, value_ref
+    rows, early, levels, place_ref, lon_ref, couple_ref, eigen_ref, after_ref, phi_ref, psi_ref, token_ref, kept_ref, value_ref
 ):
-    del after_ref
+    token_ref[...] = after_ref[...]
     eigen = eigen_ref[...]
     groups = eigen.shape[0]
 
@@ -618,16 +622,7 @@
 
     far = list(range(2, levels))
 
-    def pack_ends(place_ref, in_ref, *refs):
-        out_refs, (low_ref, high_ref, sems) = refs[:-3], refs[-3:]
-        low = pltpu.make_async_copy(in_ref.at[pl.ds(0, levels * span), :], low_ref, sems.at[0])
-        high = pltpu.make_async_copy(
-            in_ref.at[pl.ds(levels * (rows - OV) * digits, levels * span), :], high_ref, sems.at[1]
-        )
-        low.start()
-        high.start()
-        low.wait()
-        high.wait()
+    def pack_ends(place_ref, low_ref, high_ref, *out_refs):
         for out_ref, mask in zip(out_refs, [0] + far):
             level = place_ref[0] ^ mask
             out_ref[:span, :] = low_ref[pl.ds(level, span, stride=levels), :]
@@ -636,12 +631,11 @@
     end_packed = call(
         pack_ends,
         [(ends * digits, N2)] * (1 + len(far)),
-        [place, by_row],
-        [SMEM, pltpu.HBM],
-        [vmem(levels * span, N2), vmem(levels * span, N2), pltpu.SemaphoreType.DMA((2,))],
+        [place, by_row[: levels * span], by_row[levels * (rows - OV) * digits :]],
+        [SMEM, VMEM, VMEM],
+        [],
         0,
         "pack_ends",
-        limit=58,
     )
 
     def pack(place_ref, in_ref, after_ref, *out_refs):
@@ -755,6 +749,16 @@
     early_pieces = swap_levels(early_pieces)
     even2, odd2 = swap(even2, odd2)
 
+    phi_others, psi_others, token = call(
+        functools.partial(partners_kernel, rows, early, levels),
+        [((levels - 1) * early * groups, N2)] * 2 + [row],
+        [place, lon_all, couple_all, eigen, own_top],
+        [SMEM, SMEM, SMEM, VMEM, VMEM],
+        [vmem(*early_block), vmem(*early_block)],
+        (levels - 1) * rows * groups * N2 * 20,
+        "partners",
+    )
+
     def sigma_body(place_ref, couple_ref, *refs):
         first_ref, own_top_ref, even_ref, odd_ref, even2_ref, odd2_ref, top_ref, bottom_ref = refs[:8]
         ratio_ref, edge_ref, around_ref = refs[8:11]
@@ -776,24 +780,14 @@
         [(2 * groups, N2)],
         [
             place, couple_all, late_first, own_top, even, odd, even2, odd2, sent_top, sent_bottom, ratio, edge, around,
-            *early_pieces[1:],
+            *early_pieces[1:], token,
         ],
-        [SMEM, SMEM] + [VMEM] * 11 + [pl.ANY] * (levels - 1),
+        [SMEM, SMEM] + [VMEM] * 11 + [pl.ANY] * levels,
         [],
         groups * N2 * 40,
         "sigma",
     )
     far_sigma = [send_level(sigma, mask, levels) for mask in far]
-    phi_others, psi_others = call(
-        functools.partial(partners_kernel, rows, early, levels),
-        [((levels - 1) * early * groups, N2)] * 2,
-        [place, lon_all, couple_all, eigen, sigma],
-        [SMEM, SMEM, SMEM, VMEM, pl.ANY],
-        [vmem(*early_block), vmem(*early_block)],
-        (levels - 1) * rows * groups * N2 * 20,
-        "partners",
-    )
-
     def second_body(place_ref, *refs):
         sigma_ref, first_ref, ratio_ref, inverse_ref, edge_ref = refs[:5]
         tables_in, refs = refs[5:9], refs[9:]

time: 52 us -> 44.2 us (0.85)
  local copies, waits for them, and re-layouts: 6.53 us -> 2.51 us
  other arithmetic: 2 us -> 0.22 us
  Pallas kernels: 19.1 us -> 17.7 us
  waiting for transfers between devices: 4.87 us -> 4.32 us
    unnamed x30 -> x26, local copies, waits for them, and re-layouts: 5.01 us -> 1.26 us
    ppermute x4, waiting for transfers between devices: 3.81 us -> 0.81 us  [the longest x2 0.81 us: swap(): value_odd = lax.ppermute(value_odd, 'lat', odd)]
    ppermute x13, waiting for transfers between devices: 1.06 us -> 3.51 us  [send_level(): return lax.ppermute(piece, 'lon', [(d, d ^ mask) for d in range(size)])]
    pallas_call x11, Pallas kernels: 19.1 us -> 17.7 us  [call(): pl.pallas_call(body, out_shape=[jax.ShapeDtypeStruct(s, jnp.float32) for...]
    slice x0 -> x1, local copies, waits for them, and re-layouts: none -> 1.1 us  [whole_levels(): by_row[levels * (rows - OV) * digits:]]
    dynamic_slice x1, local copies, waits for them, and re-layouts: 0.76 us -> 0.08 us  [operator_parts(): lax.dynamic_slice_in_dim(jnp.pad(lat_coef, (OV + 1, OV + 2)), row_first,...]
    dynamic_slice x1, local copies, waits for them, and re-layouts: 0.76 us -> 0.08 us  [operator_parts(): lax.dynamic_slice_in_dim(jnp.pad(lon_coef, (OV, OV)), row_first, extent)]
    mul x1, other arithmetic: 0.72 us -> 0.07 us  [operator_parts(): level_scale[:, None] * couple[None]]
  transfers between devices with their start and end apart: 17 -> 17, of which waited for: 3 -> 6; matrix products, arithmetic and copies ran while one was open for 6% -> 1% of each run, Pallas kernels for 20% -> 24%
where the time goes in v4:
time: 44.2 us; the launch traced here: 43.8 us
  starting transfers between devices  18.8 us (43%)
  Pallas kernels  17.7 us (40%)
  waiting for transfers between devices  4.32 us (10%)
  local copies, waits for them, and re-layouts  2.51 us (6%)
    pallas_call x11, Pallas kernels, call(): pl.pallas_call(body, out_shape=[jax.ShapeDtypeStruct(s, jnp.float32) for...  17.7 us
    ppermute x13, starting transfers between devices, send_level(): return lax.ppermute(piece, 'lon', [(d, d ^ mask) for d in range(size)])  12.3 us
    ppermute x2, starting transfers between devices, swap(): value_odd = lax.ppermute(value_odd, 'lat', odd)  5.04 us
    ppermute x13, waiting for transfers between devices, send_level(): return lax.ppermute(piece, 'lon', [(d, d ^ mask) for d in range(size)])  3.51 us
    ppermute x2, starting transfers between devices, swap(): return (lax.ppermute(value_even, 'lat', even), value_odd)  1.53 us
    unnamed x26, local copies, waits for them, and re-layouts  1.26 us
    slice x1, local copies, waits for them, and re-layouts, whole_levels(): by_row[levels * (rows - OV) * digits:]  1.1 us
  transfers between devices with their start and end apart: 17, of which 6 were waited for; matrix products, arithmetic and copies ran while one was open for 1% of the time, Pallas kernels for 24%

profile of v4, /device:TPU:17, one launch (start us, length us, event | category | flops | bytes accessed | tf_op | source)
XLA Modules:
  0.0 43.8 jit_solution(12584576089697112389)
XLA Ops:
  0.0 0.0 copy-start.2
  0.0 0.0 copy-start.3
  0.1 1.1 %fusion = (f32[8,8,4,128]{3,2,1,0:T(4,128)S(1)}, f32[8,8,4,128]{3,2,1,0:T(4,128)S(1)}) fusion(f32[60,8,4,128]{3,2,1,0:T(4,128)} %bitcast.14), kind=kLoop, calls=%fused_computation.5 | loop fusion | bytes 524288 | tf_op jit(solution)/shard_map/slice | solution.py:634
  1.2 0.1 pad_add_fusion.place_ref.level_ref
  1.3 0.6 %pack_ends.1 = (f32[128,128]{1,0:T(8,128)S(1)}, f32[128,128]{1,0:T(8,128)S(1)}, f32[128,128]{1,0:T(8,128)S(1)}) custom-call(s32[2]{0:T(128)S(1)} %pad_add_fusion.place_ref.level_ref, f32[256,128]{1,0:T(8,128)S(1)} %bitcast.17, f32[256,128]{1,0:T(8,128)S(1)} %bitcast.16), custom_call_target="tpu_custom_call" | custom-call | bytes 458760 | tf_op jit(solution)/shard_map/pack_ends/pallas_call | solution.py:359
  1.8 1.3 %collective-permute-start.3 = (f32[128,128]{1,0:T(8,128)S(1)}, f32[128,128]{1,0:T(8,128)S(1)}, u32[]{:S(2)}, u32[]{:S(2)}) collective-permute-start(f32[128,128]{1,0:T(8,128)S(1)} %get-tuple-element.42), channel_id=1, source_target_pairs={{0,2},{1,3},{2,0},{3,1},{4,6},{5,7},{6,4},{7,5},{8,10},{9,11},{10,... | collective-permute-start | bytes 196616 | tf_op jit(solution)/shard_map/ppermute | solution.py:386
  3.1 1.1 %collective-permute-start.4 = (f32[128,128]{1,0:T(8,128)S(1)}, f32[128,128]{1,0:T(8,128)S(1)}, u32[]{:S(2)}, u32[]{:S(2)}) collective-permute-start(f32[128,128]{1,0:T(8,128)S(1)} %get-tuple-element.43), channel_id=1, source_target_pairs={{0,3},{1,2},{2,1},{3,0},{4,7},{5,6},{6,5},{7,4},{8,11},{9,10},{10,... | collective-permute-start | bytes 196616 | tf_op jit(solution)/shard_map/ppermute | solution.py:386
  4.2 1.2 %copy-done = f32[60,4,1024]{2,1,0:T(4,128)S(1)} copy-done((f32[60,4,1024]{2,1,0:T(4,128)S(1)}, f32[60,4,1024]{2,1,0:T(4,128)}, u32[]{:S(2)}) %copy-start) | copy-done | bytes 983064
  5.4 0.6 %pack.1 = (f32[352,128]{1,0:T(8,128)S(1)}, f32[480,128]{1,0:T(8,128)S(1)}, f32[352,128]{1,0:T(8,128)S(1)}, f32[352,128]{1,0:T(8,128)S(1)}) custom-call(s32[2]{0:T(128)S(1)} %pad_add_fusion.place_ref.level_ref, f32[1920,128]{1,0:T(8,128)S(1)} %bitcast.15, f32[128,128]{1,0:T(8,128)S(1)} %get-tuple-element.37.after_ref.refs_0_), custom_call_target="tpu_custom_call" | custom-call | bytes 1835016 | tf_op jit(solution)/shard_map/pack/pallas_call | solution.py:359
  6.1 1.3 %collective-permute-start.1 = (f32[352,128]{1,0:T(8,128)S(1)}, f32[352,128]{1,0:T(8,128)S(1)}, u32[]{:S(2)}, u32[]{:S(2)}) collective-permute-start(f32[352,128]{1,0:T(8,128)S(1)} %get-tuple-element.40), channel_id=1, source_target_pairs={{0,2},{1,3},{2,0},{3,1},{4,6},{5,7},{6,4},{7,5},{8,10},{9,11},{10,... | collective-permute-start | bytes 540680 | tf_op jit(solution)/shard_map/ppermute | solution.py:386
  7.3 0.3 collective-permute-start.2
  7.6 0.4 collective-permute-start
  8.0 0.1 pad_dynamic-slice_fusion.1
  8.1 0.1 broadcast_multiply_fusion.1.couple_ref
  8.2 0.1 pad_dynamic-slice_fusion
  8.2 0.1 broadcast_multiply_fusion.lon_ref
  8.3 0.7 %edge.1.refs_8_.refs_10_ = f32[512,128]{1,0:T(8,128)S(1)} custom-call(s32[2]{0:T(128)S(1)} %pad_add_fusion.place_ref.level_ref, f32[4,76]{1,0:T(4,128)S(1)} %broadcast_multiply_fusion.lon_ref, f32[4,77]{1,0:T(4,128)S(1)} %broadcast_multiply_fusion.1.couple_ref, f32[32,128]{1,0:T(8,128)S(1)} %copy-done.8), custom_call_target="tpu_custom_call" | custom-call | flops 1310720 | bytes 280984 | tf_op jit(solution)/shard_map/edge/pallas_call | solution.py:359
  9.0 0.0 collective-permute-done.4.refs_3_
  9.0 0.1 collective-permute-done.refs_1_
  9.2 1.2 %ends.1 = (f32[512,128]{1,0:T(8,128)S(1)}, f32[32,128]{1,0:T(8,128)S(1)}, f32[32,128]{1,0:T(8,128)S(1)}, f32[32,128]{1,0:T(8,128)S(1)}, f32[32,128]{1,0:T(8,128)S(1)}) custom-call(s32[2]{0:T(128)S(1)} %pad_add_fusion.place_ref.level_ref, f32[128,128]{1,0:T(8,128)S(1)} %get-tuple-element.37.after_ref.refs_0_, f32[480,128]{1,0:T(8,128)S(1)} %collective-permute-done.refs_1_, ...), custom_call_target="tpu_custom_call" | custom-call | flops 67108864 | bytes 1835016 | tf_op jit(solution)/shard_map/ends/pallas_call | solution.py:359
  10.4 1.3 %collective-permute-start.5 = (f32[32,128]{1,0:T(8,128)S(1)}, f32[32,128]{1,0:T(8,128)S(1)}, u32[]{:S(2)}, u32[]{:S(2)}) collective-permute-start(f32[32,128]{1,0:T(8,128)S(1)} %get-tuple-element.45), channel_id=1, source_target_pairs={{0,4},{4,0},{8,12},{12,8},{16,20},{20,16},{24,28},{28,24},{1,5},{5... | collective-permute-start | bytes 49160 | tf_op jit(solution)/shard_map/ppermute | solution.py:382
  11.7 2.0 %collective-permute-start.6 = (f32[32,128]{1,0:T(8,128)S(1)}, f32[32,128]{1,0:T(8,128)S(1)}, u32[]{:S(2)}, u32[]{:S(2)}) collective-permute-start(f32[32,128]{1,0:T(8,128)S(1)} %get-tuple-element.46), channel_id=1, source_target_pairs={{4,8},{8,4},{12,16},{16,12},{20,24},{24,20},{5,9},{9,5},{13,17},{1... | collective-permute-start | bytes 49160 | tf_op jit(solution)/shard_map/ppermute | solution.py:381
  13.7 1.2 %own.1 = (f32[1920,128]{1,0:T(8,128)S(1)}, f32[1920,128]{1,0:T(8,128)S(1)}, f32[160,128]{1,0:T(8,128)S(1)}, f32[1024,128]{1,0:T(8,128)S(1)}, f32[1024,128]{1,0:T(8,128)S(1)}) custom-call(s32[2]{0:T(128)S(1)} %pad_add_fusion.place_ref.level_ref, f32[4,76]{1,0:T(4,128)S(1)} %broadcast_multiply_fusion.lon_ref, f32[4,77]{1,0:T(4,128)S(1)} %broadcast_multiply_fusion.1.couple_ref, ...), custom_call_target="tpu_custom_call" | custom-call | flops 4915200 | bytes 3115416 | tf_op jit(solution)/shard_map/own/pallas_call | solution.py:359
  15.0 0.0 collective-permute-done.1.refs_2_
  15.0 1.3 %collective-permute-done.2.refs_3_ = f32[352,128]{1,0:T(8,128)S(1)} collective-permute-done((f32[352,128]{1,0:T(8,128)S(1)}, f32[352,128]{1,0:T(8,128)S(1)}, u32[]{:S(2)}, u32[]{:S(2)}) %collective-permute-start.2) | collective-permute-done | bytes 180256 | tf_op jit(solution)/shard_map/ppermute | solution.py:386
  16.3 0.8 %collective-permute-done.6.refs_13_.refs_3_ = f32[32,128]{1,0:T(8,128)S(1)} collective-permute-done((f32[32,128]{1,0:T(8,128)S(1)}, f32[32,128]{1,0:T(8,128)S(1)}, u32[]{:S(2)}, u32[]{:S(2)}) %collective-permute-start.6) | collective-permute-done | bytes 16416 | tf_op jit(solution)/shard_map/ppermute | solution.py:381
  17.1 3.1 %inner.1 = (f32[896,128]{1,0:T(8,128)S(1)}, f32[32,128]{1,0:T(8,128)S(1)}, f32[32,128]{1,0:T(8,128)S(1)}, f32[32,128]{1,0:T(8,128)S(1)}, f32[256,128]{1,0:T(8,12...) custom-call(s32[2]{0:T(128)S(1)} %pad_add_fusion.place_ref.level_ref, ...), custom_call_target="tpu_custom_call" | custom-call | flops 318767104 | bytes 5750792 | tf_op jit(solution)/shard_map/inner/pallas_call | solution.py:359
  20.2 1.9 %collective-permute-start.9 = (f32[256,128]{1,0:T(8,128)S(1)}, f32[256,128]{1,0:T(8,128)S(1)}, u32[]{:S(2)}, u32[]{:S(2)}) collective-permute-start(f32[256,128]{1,0:T(8,128)S(1)} %get-tuple-element.56), channel_id=1, source_target_pairs={{0,1},{1,0},{2,3},{3,2},{4,5},{5,4},{6,7},{7,6},{8,9},{9,8},{10,11... | collective-permute-start | bytes 393224 | tf_op jit(solution)/shard_map/ppermute | solution.py:386
  22.0 1.2 %collective-permute-start.10 = (f32[256,128]{1,0:T(8,128)S(1)}, f32[256,128]{1,0:T(8,128)S(1)}, u32[]{:S(2)}, u32[]{:S(2)}) collective-permute-start(f32[256,128]{1,0:T(8,128)S(1)} %get-tuple-element.57), channel_id=1, source_target_pairs={{0,2},{1,3},{2,0},{3,1},{4,6},{5,7},{6,4},{7,5},{8,10},{9,11},{10,... | collective-permute-start | bytes 393224 | tf_op jit(solution)/shard_map/ppermute | solution.py:386
  23.3 0.5 %collective-permute-start.11 = (f32[256,128]{1,0:T(8,128)S(1)}, f32[256,128]{1,0:T(8,128)S(1)}, u32[]{:S(2)}, u32[]{:S(2)}) collective-permute-start(f32[256,128]{1,0:T(8,128)S(1)} %get-tuple-element.58), channel_id=1, source_target_pairs={{0,3},{1,2},{2,1},{3,0},{4,7},{5,6},{6,5},{7,4},{8,11},{9,10},{10,... | collective-permute-start | bytes 393224 | tf_op jit(solution)/shard_map/ppermute | solution.py:386
  23.7 0.2 collective-permute-start.7
  24.0 3.0 %collective-permute-start.8 = (f32[32,128]{1,0:T(8,128)S(1)}, f32[32,128]{1,0:T(8,128)S(1)}, u32[]{:S(2)}, u32[]{:S(2)}) collective-permute-start(f32[32,128]{1,0:T(8,128)S(1)} %get-tuple-element.53), channel_id=1, source_target_pairs={{4,8},{8,4},{12,16},{16,12},{20,24},{24,20},{5,9},{9,5},{13,17},{1... | collective-permute-start | bytes 49160 | tf_op jit(solution)/shard_map/ppermute | solution.py:381
  27.0 2.4 %partners.1 = (f32[3072,128]{1,0:T(8,128)S(1)}, f32[3072,128]{1,0:T(8,128)S(1)}, f32[32,128]{1,0:T(8,128)S(1)}) custom-call(s32[2]{0:T(128)S(1)} %pad_add_fusion.place_ref.level_ref, f32[4,76]{1,0:T(4,128)S(1)} %broadcast_multiply_fusion.lon_ref, f32[4,77]{1,0:T(4,128)S(1)} %broadcast_multiply_fusion.1.couple_ref, f32[32,128]{1,0:T(8,128)S(1)} %copy-done.8, ...), custom_call_target="tpu_custom_call" | custom-call | flops 14745600 | bytes 3197336 | tf_op jit(solution)/shard_map/partners/pallas_call | solution.py:359
  29.4 0.0 collective-permute-done.7.refs_4_
  29.4 0.0 collective-permute-done.8.refs_5_
  29.5 0.9 %collective-permute-done.11.refs_13_.refs_3_ = f32[256,128]{1,0:T(8,128)S(1)} collective-permute-done((f32[256,128]{1,0:T(8,128)S(1)}, f32[256,128]{1,0:T(8,128)S(1)}, u32[]{:S(2)}, u32[]{:S(2)}) %collective-permute-start.11) | collective-permute-done | bytes 131104 | tf_op jit(solution)/shard_map/ppermute | solution.py:386
  30.4 0.6 %sigma.1.refs_0_.refs_4_ = f32[64,128]{1,0:T(8,128)S(1)} custom-call(s32[2]{0:T(128)S(1)} %pad_add_fusion.place_ref.level_ref, f32[4,77]{1,0:T(4,128)S(1)} %broadcast_multiply_fusion.1.couple_ref, f32[896,128]{1,0:T(8,128)S(1)} %get-tuple-element.50.refs_0_.refs_1_, f32[32,128]{1,0:T(8,128)S(1)} %get-tuple-element.51.after_ref.refs_1_, ...), custom_call_target="tpu_custom_call" | custom-call | flops 163840 | bytes 2344152 | tf_op jit(solution)/shard_map/sigma/pallas_call | solution.py:359
  31.0 0.0 copy-start.9
  31.0 1.6 %second.1 = (f32[224,128]{1,0:T(8,128)S(1)}, f32[288,128]{1,0:T(8,128)S(1)}, f32[224,128]{1,0:T(8,128)S(1)}, f32[224,128]{1,0:T(8,128)S(1)}) custom-call(s32[2]{0:T(128)S(1)} %pad_add_fusion.place_ref.level_ref, f32[64,128]{1,0:T(8,128)S(1)} %sigma.1.refs_0_.refs_4_, f32[896,128]{1,0:T(8,128)S(1)} %get-tuple-element.50.refs_0_.refs_1_, ...), custom_call_target="tpu_custom_call" | custom-call | flops 117440512 | bytes 3833864 | tf_op jit(solution)/shard_map/second/pallas_call | solution.py:359
  32.6 0.6 %collective-permute-start.12 = (f32[288,128]{1,0:T(8,128)S(1)}, f32[288,128]{1,0:T(8,128)S(1)}, u32[]{:S(2)}, u32[]{:S(2)}) collective-permute-start(f32[288,128]{1,0:T(8,128)S(1)} %get-tuple-element.61), channel_id=1, source_target_pairs={{0,1},{1,0},{2,3},{3,2},{4,5},{5,4},{6,7},{7,6},{8,9},{9,8},{10,11... | collective-permute-start | bytes 442376 | tf_op jit(solution)/shard_map/ppermute | solution.py:386
  33.3 1.2 %collective-permute-start.16 = (f32[64,128]{1,0:T(8,128)S(1)}, f32[64,128]{1,0:T(8,128)S(1)}, u32[]{:S(2)}, u32[]{:S(2)}) collective-permute-start(f32[64,128]{1,0:T(8,128)S(1)} %sigma.1.refs_0_.refs_4_), channel_id=1, source_target_pairs={{0,3},{1,2},{2,1},{3,0},{4,7},{5,6},{6,5},{7,4},{8,11},{9,10},{10,... | collective-permute-start | bytes 98312 | tf_op jit(solution)/shard_map/ppermute | solution.py:386
  34.5 0.2 collective-permute-start.15
  34.7 1.2 %collective-permute-start.13 = (f32[224,128]{1,0:T(8,128)S(1)}, f32[224,128]{1,0:T(8,128)S(1)}, u32[]{:S(2)}, u32[]{:S(2)}) collective-permute-start(f32[224,128]{1,0:T(8,128)S(1)} %get-tuple-element.62), channel_id=1, source_target_pairs={{0,2},{1,3},{2,0},{3,1},{4,6},{5,7},{6,4},{7,5},{8,10},{9,11},{10,... | collective-permute-start | bytes 344072 | tf_op jit(solution)/shard_map/ppermute | solution.py:386
  35.9 1.1 %collective-permute-start.14 = (f32[224,128]{1,0:T(8,128)S(1)}, f32[224,128]{1,0:T(8,128)S(1)}, u32[]{:S(2)}, u32[]{:S(2)}) collective-permute-start(f32[224,128]{1,0:T(8,128)S(1)} %get-tuple-element.63), channel_id=1, source_target_pairs={{0,3},{1,2},{2,1},{3,0},{4,7},{5,6},{6,5},{7,4},{8,11},{9,10},{10,... | collective-permute-start | bytes 344072 | tf_op jit(solution)/shard_map/ppermute | solution.py:386
  37.1 0.2 collective-permute-done.15.refs_6_
  37.2 4.2 %correct.1.refs_4_ = f32[1920,128]{1,0:T(8,128)} custom-call(s32[2]{0:T(128)S(1)} %pad_add_fusion.place_ref.level_ref, f32[256,128]{1,0:T(8,128)S(1)} %get-tuple-element.64.refs_0_, f32[256,128]{1,0:T(8,128)S(1)} %collective-permute-done.9.refs_11_.refs_1_, f32[256,128]{1,0:T(8,128)S(1)} %collective-permute-done.10.refs_12_.refs_2_, ...), custom_call_target="tpu_custom_call" | custom-call | flops 5368709120 | bytes 6750216 | tf_op jit(solution)/shard_map/correct/pallas_call | solution.py:359
  41.4 1.0 %collective-permute-done.14.refs_3_ = f32[224,128]{1,0:T(8,128)S(1)} collective-permute-done((f32[224,128]{1,0:T(8,128)S(1)}, f32[224,128]{1,0:T(8,128)S(1)}, u32[]{:S(2)}, u32[]{:S(2)}) %collective-permute-start.14) | collective-permute-done | bytes 114720 | tf_op jit(solution)/shard_map/ppermute | solution.py:386
  42.5 1.3 %unpack.1 = f32[1920,128]{1,0:T(8,128)} custom-call(s32[2]{0:T(128)S(1)} %pad_add_fusion.place_ref.level_ref, f32[224,128]{1,0:T(8,128)S(1)} %get-tuple-element.60.refs_0_, f32[288,128]{1,0:T(8,128)S(1)} %collective-permute-done.12.refs_5_.refs_1_, f32[224,128]{1,0:T(8,128)S(1)} %collective-permute-done.13.refs_2_, ...), custom_call_target="tpu_custom_call", output_to_operand_aliasing={{}: (5, {})} | custom-call | bytes 2457608 | tf_op jit(solution)/shard_map/unpack/pallas_call | solution.py:359
  (29 shorter events, 0.1 us)
Async XLA Ops:
  0.0 8.3 %copy-start.8 = (f32[32,128]{1,0:T(8,128)S(1)}, f32[32,128]{1,0:T(8,128)}, u32[]{:S(2)}) copy-start(f32[32,128]{1,0:T(8,128)} %constant.63.eigen_ref) | copy-start | bytes 49156
  0.0 9.2 %copy-start.7 = (f32[32,128]{1,0:T(8,128)S(1)}, f32[32,128]{1,0:T(8,128)}, u32[]{:S(2)}) copy-start(f32[32,128]{1,0:T(8,128)} %constant.56.clone.refs_5_.refs_6_.refs_13_) | copy-start | bytes 49156
  0.0 9.2 %copy-start.1 = (bf16[512,256]{1,0:T(8,128)(2,1)S(1)}, bf16[512,256]{1,0:T(8,128)(2,1)}, u32[]{:S(2)}) copy-start(bf16[512,256]{1,0:T(8,128)(2,1)} %constant.54.clone.refs_7_) | copy-start | bytes 786436
  0.0 9.2 %copy-start.2 = (bf16[512,256]{1,0:T(8,128)(2,1)S(1)}, bf16[512,256]{1,0:T(8,128)(2,1)}, u32[]{:S(2)}) copy-start(bf16[512,256]{1,0:T(8,128)(2,1)} %constant.52.clone.refs_6_) | copy-start | bytes 786436
  0.0 9.1 %copy-start.3 = (bf16[512,256]{1,0:T(8,128)(2,1)S(1)}, bf16[512,256]{1,0:T(8,128)(2,1)}, u32[]{:S(2)}) copy-start(bf16[512,256]{1,0:T(8,128)(2,1)} %constant.50.clone.refs_4_) | copy-start | bytes 786436
  0.0 8.0 %copy-start.10 = (f32[479]{0:T(512)S(1)}, f32[479]{0:T(512)}, u32[]{:S(2)}) copy-start(f32[479]{0:T(512)} %param.15) | copy-start | bytes 5752
  0.0 8.0 %copy-start.12 = (f32[4]{0:T(128)S(1)}, f32[4]{0:T(128)}, u32[]{:S(2)}) copy-start(f32[4]{0:T(128)} %param.16) | copy-start | bytes 52
  0.1 8.1 %copy-start.11 = (f32[480]{0:T(512)S(1)}, f32[480]{0:T(512)}, u32[]{:S(2)}) copy-start(f32[480]{0:T(512)} %param.14) | copy-start | bytes 5764
  1.8 7.2 %collective-permute-start.3 = (f32[128,128]{1,0:T(8,128)S(1)}, f32[128,128]{1,0:T(8,128)S(1)}, u32[]{:S(2)}, u32[]{:S(2)}) collective-permute-start(f32[128,128]{1,0:T(8,128)S(1)} %get-tuple-element.42), channel_id=1, source_target_pairs={{0,2},{1,3},{2,0},{3,1},{4,6},{5,7},{6,4},{7,5},{8,10},{9,11},{10,... | collective-permute-start | bytes 196616 | tf_op jit(solution)/shard_map/ppermute | solution.py:386
  3.1 5.9 %collective-permute-start.4 = (f32[128,128]{1,0:T(8,128)S(1)}, f32[128,128]{1,0:T(8,128)S(1)}, u32[]{:S(2)}, u32[]{:S(2)}) collective-permute-start(f32[128,128]{1,0:T(8,128)S(1)} %get-tuple-element.43), channel_id=1, source_target_pairs={{0,3},{1,2},{2,1},{3,0},{4,7},{5,6},{6,5},{7,4},{8,11},{9,10},{10,... | collective-permute-start | bytes 196616 | tf_op jit(solution)/shard_map/ppermute | solution.py:386
  4.2 1.2 %copy-start = (f32[60,4,1024]{2,1,0:T(4,128)S(1)}, f32[60,4,1024]{2,1,0:T(4,128)}, u32[]{:S(2)}) copy-start(f32[60,4,1024]{2,1,0:T(4,128)} %param.13) | copy-start | bytes 2949124
  5.4 11.7 %copy-start.4 = (bf16[512,256]{1,0:T(8,128)(2,1)S(1)}, bf16[512,256]{1,0:T(8,128)(2,1)}, u32[]{:S(2)}) copy-start(bf16[512,256]{1,0:T(8,128)(2,1)} %constant.55.clone.refs_10_.refs_8_.refs_15_) | copy-start | bytes 786436
  5.4 11.7 %copy-start.5 = (bf16[512,256]{1,0:T(8,128)(2,1)S(1)}, bf16[512,256]{1,0:T(8,128)(2,1)}, u32[]{:S(2)}) copy-start(bf16[512,256]{1,0:T(8,128)(2,1)} %constant.53.clone.refs_9_.refs_7_.refs_14_) | copy-start | bytes 786436
  5.4 11.7 %copy-start.6 = (bf16[512,256]{1,0:T(8,128)(2,1)S(1)}, bf16[512,256]{1,0:T(8,128)(2,1)}, u32[]{:S(2)}) copy-start(bf16[512,256]{1,0:T(8,128)(2,1)} %constant.51.clone.refs_8_.refs_5_) | copy-start | bytes 786436
  6.1 8.9 %collective-permute-start.1 = (f32[352,128]{1,0:T(8,128)S(1)}, f32[352,128]{1,0:T(8,128)S(1)}, u32[]{:S(2)}, u32[]{:S(2)}) collective-permute-start(f32[352,128]{1,0:T(8,128)S(1)} %get-tuple-element.40), channel_id=1, source_target_pairs={{0,2},{1,3},{2,0},{3,1},{4,6},{5,7},{6,4},{7,5},{8,10},{9,11},{10,... | collective-permute-start | bytes 540680 | tf_op jit(solution)/shard_map/ppermute | solution.py:386
  7.3 8.9 %collective-permute-start.2 = (f32[352,128]{1,0:T(8,128)S(1)}, f32[352,128]{1,0:T(8,128)S(1)}, u32[]{:S(2)}, u32[]{:S(2)}) collective-permute-start(f32[352,128]{1,0:T(8,128)S(1)} %get-tuple-element.41), channel_id=1, source_target_pairs={{0,3},{1,2},{2,1},{3,0},{4,7},{5,6},{6,5},{7,4},{8,11},{9,10},{10,... | collective-permute-start | bytes 540680 | tf_op jit(solution)/shard_map/ppermute | solution.py:386
  7.6 1.5 %collective-permute-start = (f32[480,128]{1,0:T(8,128)S(1)}, f32[480,128]{1,0:T(8,128)S(1)}, u32[]{:S(2)}, u32[]{:S(2)}) collective-permute-start(f32[480,128]{1,0:T(8,128)S(1)} %get-tuple-element.39), channel_id=1, source_target_pairs={{0,1},{1,0},{2,3},{3,2},{4,5},{5,4},{6,7},{7,6},{8,9},{9,8},{10,11... | collective-permute-start | bytes 737288 | tf_op jit(solution)/shard_map/ppermute | solution.py:386
  10.4 5.9 %collective-permute-start.5 = (f32[32,128]{1,0:T(8,128)S(1)}, f32[32,128]{1,0:T(8,128)S(1)}, u32[]{:S(2)}, u32[]{:S(2)}) collective-permute-start(f32[32,128]{1,0:T(8,128)S(1)} %get-tuple-element.45), channel_id=1, source_target_pairs={{0,4},{4,0},{8,12},{12,8},{16,20},{20,16},{24,28},{28,24},{1,5},{5... | collective-permute-start | bytes 49160 | tf_op jit(solution)/shard_map/ppermute | solution.py:382
  11.7 5.4 %collective-permute-start.6 = (f32[32,128]{1,0:T(8,128)S(1)}, f32[32,128]{1,0:T(8,128)S(1)}, u32[]{:S(2)}, u32[]{:S(2)}) collective-permute-start(f32[32,128]{1,0:T(8,128)S(1)} %get-tuple-element.46), channel_id=1, source_target_pairs={{4,8},{8,4},{12,16},{16,12},{20,24},{24,20},{5,9},{9,5},{13,17},{1... | collective-permute-start | bytes 49160 | tf_op jit(solution)/shard_map/ppermute | solution.py:381
  20.2 9.3 %collective-permute-start.9 = (f32[256,128]{1,0:T(8,128)S(1)}, f32[256,128]{1,0:T(8,128)S(1)}, u32[]{:S(2)}, u32[]{:S(2)}) collective-permute-start(f32[256,128]{1,0:T(8,128)S(1)} %get-tuple-element.56), channel_id=1, source_target_pairs={{0,1},{1,0},{2,3},{3,2},{4,5},{5,4},{6,7},{7,6},{8,9},{9,8},{10,11... | collective-permute-start | bytes 393224 | tf_op jit(solution)/shard_map/ppermute | solution.py:386
  22.0 7.4 %collective-permute-start.10 = (f32[256,128]{1,0:T(8,128)S(1)}, f32[256,128]{1,0:T(8,128)S(1)}, u32[]{:S(2)}, u32[]{:S(2)}) collective-permute-start(f32[256,128]{1,0:T(8,128)S(1)} %get-tuple-element.57), channel_id=1, source_target_pairs={{0,2},{1,3},{2,0},{3,1},{4,6},{5,7},{6,4},{7,5},{8,10},{9,11},{10,... | collective-permute-start | bytes 393224 | tf_op jit(solution)/shard_map/ppermute | solution.py:386
  23.3 7.1 %collective-permute-start.11 = (f32[256,128]{1,0:T(8,128)S(1)}, f32[256,128]{1,0:T(8,128)S(1)}, u32[]{:S(2)}, u32[]{:S(2)}) collective-permute-start(f32[256,128]{1,0:T(8,128)S(1)} %get-tuple-element.58), channel_id=1, source_target_pairs={{0,3},{1,2},{2,1},{3,0},{4,7},{5,6},{6,5},{7,4},{8,11},{9,10},{10,... | collective-permute-start | bytes 393224 | tf_op jit(solution)/shard_map/ppermute | solution.py:386
  23.7 5.7 %collective-permute-start.7 = (f32[32,128]{1,0:T(8,128)S(1)}, f32[32,128]{1,0:T(8,128)S(1)}, u32[]{:S(2)}, u32[]{:S(2)}) collective-permute-start(f32[32,128]{1,0:T(8,128)S(1)} %get-tuple-element.52), channel_id=1, source_target_pairs={{0,4},{4,0},{8,12},{12,8},{16,20},{20,16},{24,28},{28,24},{1,5},{5... | collective-permute-start | bytes 49160 | tf_op jit(solution)/shard_map/ppermute | solution.py:382
  24.0 5.5 %collective-permute-start.8 = (f32[32,128]{1,0:T(8,128)S(1)}, f32[32,128]{1,0:T(8,128)S(1)}, u32[]{:S(2)}, u32[]{:S(2)}) collective-permute-start(f32[32,128]{1,0:T(8,128)S(1)} %get-tuple-element.53), channel_id=1, source_target_pairs={{4,8},{8,4},{12,16},{16,12},{20,24},{24,20},{5,9},{9,5},{13,17},{1... | collective-permute-start | bytes 49160 | tf_op jit(solution)/shard_map/ppermute | solution.py:381
  31.0 6.3 %copy-start.9 = (bf16[512,256]{1,0:T(8,128)(2,1)S(1)}, bf16[512,256]{1,0:T(8,128)(2,1)}, u32[]{:S(2)}) copy-start(bf16[512,256]{1,0:T(8,128)(2,1)} %constant.49.clone.refs_12_) | copy-start | bytes 786436
  32.6 4.6 %collective-permute-start.12 = (f32[288,128]{1,0:T(8,128)S(1)}, f32[288,128]{1,0:T(8,128)S(1)}, u32[]{:S(2)}, u32[]{:S(2)}) collective-permute-start(f32[288,128]{1,0:T(8,128)S(1)} %get-tuple-element.61), channel_id=1, source_target_pairs={{0,1},{1,0},{2,3},{3,2},{4,5},{5,4},{6,7},{7,6},{8,9},{9,8},{10,11... | collective-permute-start | bytes 442376 | tf_op jit(solution)/shard_map/ppermute | solution.py:386
  33.3 3.8 %collective-permute-start.16 = (f32[64,128]{1,0:T(8,128)S(1)}, f32[64,128]{1,0:T(8,128)S(1)}, u32[]{:S(2)}, u32[]{:S(2)}) collective-permute-start(f32[64,128]{1,0:T(8,128)S(1)} %sigma.1.refs_0_.refs_4_), channel_id=1, source_target_pairs={{0,3},{1,2},{2,1},{3,0},{4,7},{5,6},{6,5},{7,4},{8,11},{9,10},{10,... | collective-permute-start | bytes 98312 | tf_op jit(solution)/shard_map/ppermute | solution.py:386
  34.5 2.8 %collective-permute-start.15 = (f32[64,128]{1,0:T(8,128)S(1)}, f32[64,128]{1,0:T(8,128)S(1)}, u32[]{:S(2)}, u32[]{:S(2)}) collective-permute-start(f32[64,128]{1,0:T(8,128)S(1)} %sigma.1.refs_0_.refs_4_), channel_id=1, source_target_pairs={{0,2},{1,3},{2,0},{3,1},{4,6},{5,7},{6,4},{7,5},{8,10},{9,11},{10,... | collective-permute-start | bytes 98312 | tf_op jit(solution)/shard_map/ppermute | solution.py:386
  34.7 6.7 %collective-permute-start.13 = (f32[224,128]{1,0:T(8,128)S(1)}, f32[224,128]{1,0:T(8,128)S(1)}, u32[]{:S(2)}, u32[]{:S(2)}) collective-permute-start(f32[224,128]{1,0:T(8,128)S(1)} %get-tuple-element.62), channel_id=1, source_target_pairs={{0,2},{1,3},{2,0},{3,1},{4,6},{5,7},{6,4},{7,5},{8,10},{9,11},{10,... | collective-permute-start | bytes 344072 | tf_op jit(solution)/shard_map/ppermute | solution.py:386
  35.9 6.6 %collective-permute-start.14 = (f32[224,128]{1,0:T(8,128)S(1)}, f32[224,128]{1,0:T(8,128)S(1)}, u32[]{:S(2)}, u32[]{:S(2)}) collective-permute-start(f32[224,128]{1,0:T(8,128)S(1)} %get-tuple-element.63), channel_id=1, source_target_pairs={{0,3},{1,2},{2,1},{3,0},{4,7},{5,6},{6,5},{7,4},{8,11},{9,10},{10,... | collective-permute-start | bytes 344072 | tf_op jit(solution)/shard_map/ppermute | solution.py:386

commit v5 on v4

--- a/solution.py
+++ b/solution.py
@@ -430,11 +430,6 @@
     return rows // 2 + 2
 
 
-def inverses(one, other):
-    inverse = 1.0 / (one * other)
-    return other * inverse, one * inverse
-
-
 def edge_kernel(rows, level_ref, lon_ref, couple_ref, eigen_ref, out_ref):
     eigen = eigen_ref[...]
     groups = eigen.shape[0]
@@ -452,7 +447,8 @@
             out_ref[(OV + i - 1) * groups : (OV + i) * groups, :] = high_ratio
             low = 1.0 + lon_ref[level, e] * eigen + low_ratio * low
             high = 1.0 + lon_ref[level, f] * eigen + high_ratio * high
-        low_inverse, high_inverse = inverses(couple_ref[level, e + 1] + low, couple_ref[level, f] + high)
+        low_inverse = 1.0 / (couple_ref[level, e + 1] + low)
+        high_inverse = 1.0 / (couple_ref[level, f] + high)
     out_ref[(OV - 1) * groups : OV * groups, :] = low_inverse
     out_ref[(2 * OV - 1) * groups :, :] = high_inverse
 
@@ -479,7 +475,9 @@
             high = plain(f) + high_ratio * high
         low_divisor = couple_ref[level, e + 1] + low
         high_divisor = couple_ref[level, f] + high
-        low_inverse, high_inverse = inverses(low_divisor, high_divisor)
+        low_inverse = 1.0 / low_divisor
+        high_inverse = 1.0 / high_divisor
+        yield
         if i == -1:
             keep(0, low_inverse)
             keep(1, high_inverse)
@@ -511,6 +509,7 @@
     put_phi(half - 1, phi)
     put_psi(half - 1, psi)
     for i in range(half - 2, -1, -1):
+        yield
         ratio = ratio_at(i + 1)
         phi = value_at(i) + ratio * phi
         psi = ratio * psi
@@ -538,48 +537,72 @@
     return put
 
 
+def together(*steps):
+    steps = list(steps)
+    while steps:
+        steps = [step for step in steps if next(step, steps) is not steps]
+
+
+def partner_response(rows, early, place_ref, lon_ref, couple_ref, eigen, masks, phi_ref, psi_ref, kept_refs, value_refs):
+    groups = eigen.shape[0]
+
+    def nothing(index, value):
+        pass
+
+    def one(n, mask):
+        put_kept = putter(kept_refs[n], groups)
+
+        def put_ratio(index, value):
+            if index < early:
+                put_kept(index, value)
+
+        first = n * early * groups
+        return level_response(
+            rows, early, place_ref[0] ^ mask, lon_ref, couple_ref, eigen, put_ratio, nothing, nothing,
+            (
+                getter(kept_refs[n], groups), getter(value_refs[n], groups), putter(value_refs[n], groups),
+                putter(phi_ref, groups, first), putter(psi_ref, groups, first),
+            ),
+        )
+
+    return [one(n, mask) for n, mask in enumerate(masks)]
+
+
 def own_kernel(
-    rows, early, place_ref, lon_ref, couple_ref, eigen_ref, ratio_ref, inverse_ref, edge_ref, phi_ref, psi_ref, value_ref
+    rows, early, masks, place_ref, lon_ref, couple_ref, eigen_ref, ratio_ref, inverse_ref, edge_ref, phi_ref, psi_ref,
+    phi_near_ref, psi_near_ref, value_ref, *refs,
 ):
-    groups = eigen_ref.shape[0]
-    level_response(
-        rows, early, place_ref[0], lon_ref, couple_ref, eigen_ref[...], putter(ratio_ref, groups),
+    eigen = eigen_ref[...]
+    groups = eigen.shape[0]
+    own = level_response(
+        rows, early, place_ref[0], lon_ref, couple_ref, eigen, putter(ratio_ref, groups),
         putter(inverse_ref, groups), putter(edge_ref, groups),
         (
             getter(ratio_ref, groups), getter(value_ref, groups), putter(value_ref, groups),
             putter(phi_ref, groups), putter(psi_ref, groups),
         ),
     )
+    count = len(masks)
+    together(
+        own,
+        *partner_response(
+            rows, early, place_ref, lon_ref, couple_ref, eigen, masks, phi_near_ref, psi_near_ref,
+            refs[:count], refs[count:],
+        ),
+    )
 
 
 def partners_kernel(
-    rows, early, levels, place_ref, lon_ref, couple_ref, eigen_ref, after_ref, phi_ref, psi_ref, token_ref, kept_ref, value_ref
+    rows, early, masks, place_ref, lon_ref, couple_ref, eigen_ref, after_ref, phi_ref, psi_ref, token_ref, *refs
 ):
     token_ref[...] = after_ref[...]
-    eigen = eigen_ref[...]
-    groups = eigen.shape[0]
-
-    def partner(mask, carry):
-        def nothing(index, value):
-            pass
-
-        put_kept = putter(kept_ref, groups)
-
-        def put_ratio(index, value):
-            if index < early:
-                put_kept(index, value)
-
-        first = (mask - 1) * (early * groups)
-        level_response(
-            rows, early, place_ref[0] ^ mask, lon_ref, couple_ref, eigen, put_ratio, nothing, nothing,
-            (
-                getter(kept_ref, groups), getter(value_ref, groups), putter(value_ref, groups),
-                putter(phi_ref, groups, first), putter(psi_ref, groups, first),
-            ),
+    count = len(masks)
+    together(
+        *partner_response(
+            rows, early, place_ref, lon_ref, couple_ref, eigen_ref[...], masks, phi_ref, psi_ref,
+            refs[:count], refs[count:],
         )
-        return carry
-
-    lax.fori_loop(1, levels, partner, 0)
+    )
 
 
 def whole_levels(const, right_side, lon_coef, lat_coef, level_scale):
@@ -605,13 +628,15 @@
     )
     block = (rows * groups, N2)
     early_block = (early * groups, N2)
-    ratio, inverse, edge, phi, psi = call(
-        functools.partial(own_kernel, rows, early),
-        [block, block, (5 * groups, N2), early_block, early_block],
+    early_block = (early * groups, N2)
+    near_masks, far_masks = [1], list(range(2, levels))
+    ratio, inverse, edge, phi, psi, phi_near, psi_near = call(
+        functools.partial(own_kernel, rows, early, near_masks),
+        [block, block, (5 * groups, N2)] + [early_block] * 4,
         [place, lon_all, couple_all, eigen],
         [SMEM, SMEM, SMEM, VMEM],
-        [vmem(*early_block)],
-        rows * groups * N2 * 20,
+        [vmem(*early_block)] * 3,
+        2 * rows * groups * N2 * 20,
         "own",
     )
     row = (groups, N2)
@@ -622,28 +647,29 @@
 
     far = list(range(2, levels))
 
-    def pack_ends(place_ref, low_ref, high_ref, *out_refs):
-        for out_ref, mask in zip(out_refs, [0] + far):
+    def pack_ends(place_ref, in_ref, after_ref, *refs):
+        del after_ref
+        for end_ref, mask in zip(refs, [0] + far):
             level = place_ref[0] ^ mask
-            out_ref[:span, :] = low_ref[pl.ds(level, span, stride=levels), :]
-            out_ref[span:, :] = high_ref[pl.ds(level, span, stride=levels), :]
+            end_ref[:span, :] = in_ref[pl.ds(level, span, stride=levels), :]
+            end_ref[span:, :] = in_ref[pl.ds(level + levels * (rows - OV) * digits, span, stride=levels), :]
 
     end_packed = call(
         pack_ends,
-        [(ends * digits, N2)] * (1 + len(far)),
-        [place, by_row[: levels * span], by_row[levels * (rows - OV) * digits :]],
-        [SMEM, VMEM, VMEM],
+        [(ends * digits, N2)] * (levels - 1),
+        [place, by_row, around],
+        [SMEM, VMEM, pl.ANY],
         [],
         0,
         "pack_ends",
     )
 
-    def pack(place_ref, in_ref, after_ref, *out_refs):
+    def pack(place_ref, in_ref, after_ref, *refs):
         del after_ref
-        for mask, out_ref in enumerate(out_refs):
+        for mask, out_ref in enumerate(refs):
             level = place_ref[0] ^ mask
-            skip = 0 if mask == 1 else span
-            out_ref[...] = in_ref[pl.ds(level + levels * skip, out_ref.shape[0], stride=levels), :]
+            skip = 0 if mask == 1 else levels * span
+            out_ref[...] = in_ref[pl.ds(level + skip, out_ref.shape[0], stride=levels), :]
 
     packed = call(
         pack,
@@ -749,13 +775,13 @@
     early_pieces = swap_levels(early_pieces)
     even2, odd2 = swap(even2, odd2)
 
-    phi_others, psi_others, token = call(
-        functools.partial(partners_kernel, rows, early, levels),
-        [((levels - 1) * early * groups, N2)] * 2 + [row],
+    phi_far, psi_far, token = call(
+        functools.partial(partners_kernel, rows, early, far_masks),
+        [(len(far_masks) * early * groups, N2)] * 2 + [row],
         [place, lon_all, couple_all, eigen, own_top],
         [SMEM, SMEM, SMEM, VMEM, VMEM],
-        [vmem(*early_block), vmem(*early_block)],
-        (levels - 1) * rows * groups * N2 * 20,
+        [vmem(*early_block)] * (2 * len(far_masks)),
+        len(far_masks) * rows * groups * N2 * 20,
         "partners",
     )
 
@@ -789,8 +815,9 @@
     )
     far_sigma = [send_level(sigma, mask, levels) for mask in far]
     def second_body(place_ref, *refs):
-        sigma_ref, first_ref, ratio_ref, inverse_ref, edge_ref = refs[:5]
-        tables_in, refs = refs[5:9], refs[9:]
+        sigma_ref, after_ref, first_ref, ratio_ref, inverse_ref, edge_ref = refs[:6]
+        del after_ref
+        tables_in, refs = refs[6:10], refs[10:]
         late_refs = refs[:levels]
         sum_ref, mid_ref, full_ref = refs[levels:]
         low, high = sigma_ref[:groups, :], sigma_ref[groups:, :]
@@ -818,8 +845,8 @@
     late_pieces = call(
         second_body,
         [(late * digits + (2 * groups if mask == 1 else 0), N2) for mask in range(levels)],
-        [place, sigma, late_first, ratio, inverse, edge, *backward],
-        [SMEM] + [VMEM] * 9,
+        [place, sigma, far_sigma[0], late_first, ratio, inverse, edge, *backward],
+        [SMEM, VMEM, pl.ANY] + [VMEM] * 8,
         [vmem(late * groups, N2), vmem(max(pad_late, half) * N1, N2), vmem(pad_late, N1, N2)],
         late * NLON * 256 * 4,
         "second",
@@ -832,8 +859,9 @@
 
     def correct(place_ref, *refs):
         pieces, sigma_refs, refs = refs[:levels], refs[levels : 2 * levels], refs[2 * levels :]
-        phi_ref, psi_ref, phi_others_ref, psi_others_ref, part_ref, turn_ref, second_ref, special_ref = refs[:8]
-        out_ref, sum_ref, mid_ref, done_ref, sem = refs[8:]
+        responses, refs = refs[:6], refs[6:]
+        part_ref, turn_ref, second_ref, special_ref = refs[:4]
+        out_ref, sum_ref, mid_ref, done_ref, sem = refs[4:]
         part_rows = part_ref.shape[0] // levels
         mine = part_ref.at[pl.ds(pl.multiple_of(place_ref[0] * part_rows, part_rows), part_rows), :]
         size = early * groups
@@ -842,11 +870,10 @@
             last = sigma_refs[mask].shape[0]
             low = sigma_refs[mask][last - 2 * groups : last - groups, :]
             high = sigma_refs[mask][last - groups :, :]
-            first = (mask - 1) * size
-            phi_all = phi_others_ref[first : first + size, :] if mask else phi_ref[...]
-            psi_all = psi_others_ref[first : first + size, :] if mask else psi_ref[...]
-            phi_all = phi_all.reshape(early, groups, N2)
-            psi_all = psi_all.reshape(early, groups, N2)
+            phi_ref, psi_ref = responses[2 * min(mask, 2) : 2 * min(mask, 2) + 2]
+            first = max(mask - 2, 0) * size
+            phi_all = phi_ref[first : first + size, :].reshape(early, groups, N2)
+            psi_all = psi_ref[first : first + size, :].reshape(early, groups, N2)
             sum_ref[...] = (phi_all * low[None] + psi_all * high[None]).reshape(size, N2)
             spectral_back(sum_ref, early, pad_early, second_ref, special_ref, mid_ref)
             for pair in range(pad_early // (2 * BLOCK)):
@@ -868,8 +895,11 @@
     (out,) = call(
         correct,
         [(total, N2)],
-        [place, *early_pieces, *sigma_pieces, phi, psi, phi_others, psi_others, part, const["turn"], *backward[2:]],
-        [SMEM] + [VMEM] * (2 * levels + 8),
+        [
+            place, *early_pieces, *sigma_pieces, phi, psi, phi_near, psi_near, phi_far, psi_far,
+            part, const["turn"], *backward[2:],
+        ],
+        [SMEM] + [VMEM] * (2 * levels + 10),
         [
             vmem(early * groups, N2), vmem(pad_early * N1, N2), vmem(early_total, N2), pltpu.SemaphoreType.DMA,
         ],

time: 44.2 us -> 56.3 us (1.27)
  waiting for transfers between devices: 4.32 us -> 14.6 us
  starting transfers between devices: 18.8 us -> 21.8 us
  Pallas kernels: 17.7 us -> 17.1 us
    ppermute x13, waiting for transfers between devices: 3.51 us -> 12 us  [send_level(): return lax.ppermute(piece, 'lon', [(d, d ^ mask) for d in range(size)])]
    ppermute x13, starting transfers between devices: 12.3 us -> 15.2 us  [send_level(): return lax.ppermute(piece, 'lon', [(d, d ^ mask) for d in range(size)])]
    ppermute x2, waiting for transfers between devices: 0.81 us -> 2.6 us  [swap(): value_odd = lax.ppermute(value_odd, 'lat', odd)]
    slice x1 -> x0, local copies, waits for them, and re-layouts: 1.1 us -> none  [whole_levels(): by_row[levels * (rows - OV) * digits:]]
    unnamed x26, local copies, waits for them, and re-layouts: 1.26 us -> 1.92 us
  transfers between devices with their start and end apart: 17 -> 17, of which waited for: 6 -> 7; matrix products, arithmetic and copies ran while one was open for 1% -> 0% of each run, Pallas kernels for 24% -> 15%
where the time goes in v5:
time: 56.3 us; the launch traced here: 56.1 us
  starting transfers between devices  21.8 us (39%)
  Pallas kernels  17.1 us (30%)
  waiting for transfers between devices  14.6 us (26%)
  local copies, waits for them, and re-layouts  2.07 us (4%)
    pallas_call x11, Pallas kernels, call(): pl.pallas_call(body, out_shape=[jax.ShapeDtypeStruct(s, jnp.float32) for...  17.1 us
    ppermute x13, starting transfers between devices, send_level(): return lax.ppermute(piece, 'lon', [(d, d ^ mask) for d in range(size)])  15.2 us
    ppermute x13, waiting for transfers between devices, send_level(): return lax.ppermute(piece, 'lon', [(d, d ^ mask) for d in range(size)])  12 us
    ppermute x2, starting transfers between devices, swap(): value_odd = lax.ppermute(value_odd, 'lat', odd)  5 us
    ppermute x2, waiting for transfers between devices, swap(): value_odd = lax.ppermute(value_odd, 'lat', odd)  2.6 us
    unnamed x26, local copies, waits for them, and re-layouts  1.92 us
    ppermute x2, starting transfers between devices, swap(): return (lax.ppermute(value_even, 'lat', even), value_odd)  1.56 us
  transfers between devices with their start and end apart: 17, of which 7 were waited for; matrix products, arithmetic and copies ran while one was open for 0% of the time, Pallas kernels for 15%

profile of v5, /device:TPU:17, one launch (start us, length us, event | category | flops | bytes accessed | tf_op | source)
XLA Modules:
  0.0 56.1 jit_solution(15044463894561488923)
XLA Ops:
  0.0 0.0 copy-start.8
  0.0 0.7 %copy-done.10 = f32[479]{0:T(512)S(1)} copy-done((f32[479]{0:T(512)S(1)}, f32[479]{0:T(512)}, u32[]{:S(2)}) %copy-start.10) | copy-done | bytes 1940
  0.7 0.1 pad_dynamic-slice_fusion.1
  0.8 0.1 broadcast_multiply_fusion.1.couple_ref
  0.8 0.1 pad_dynamic-slice_fusion
  0.9 0.1 broadcast_multiply_fusion.lon_ref
  1.0 0.1 pad_add_fusion.level_ref.place_ref
  1.1 0.7 %edge.1.after_ref.refs_8_.refs_10_ = f32[512,128]{1,0:T(8,128)S(1)} custom-call(s32[2]{0:T(128)S(1)} %pad_add_fusion.level_ref.place_ref, f32[4,76]{1,0:T(4,128)S(1)} %broadcast_multiply_fusion.lon_ref, f32[4,77]{1,0:T(4,128)S(1)} %broadcast_multiply_fusion.1.couple_ref, f32[32,128]{1,0:T(8,128)S(1)} %copy-done.8), custom_call_target="tpu_custom_call" | custom-call | flops 1310720 | bytes 280984 | tf_op jit(solution)/shard_map/edge/pallas_call | solution.py:359
  1.8 0.0 copy-start
  1.8 1.2 %copy-done = f32[60,4,1024]{2,1,0:T(4,128)S(1)} copy-done((f32[60,4,1024]{2,1,0:T(4,128)S(1)}, f32[60,4,1024]{2,1,0:T(4,128)}, u32[]{:S(2)}) %copy-start) | copy-done | bytes 983064
  3.0 0.6 %pack_ends.1 = (f32[128,128]{1,0:T(8,128)S(1)}, f32[128,128]{1,0:T(8,128)S(1)}, f32[128,128]{1,0:T(8,128)S(1)}) custom-call(s32[2]{0:T(128)S(1)} %pad_add_fusion.level_ref.place_ref, f32[1920,128]{1,0:T(8,128)S(1)} %bitcast.12, f32[512,128]{1,0:T(8,128)S(1)} %edge.1.after_ref.refs_8_.refs_10_), custom_call_target="tpu_custom_call" | custom-call | bytes 1441800 | tf_op jit(solution)/shard_map/pack_ends/pallas_call | solution.py:359
  3.5 0.0 copy-start.1
  3.6 0.0 copy-start.2
  3.6 0.0 copy-start.3
  3.6 0.0 copy-start.7
  3.6 0.6 %pack.1 = (f32[352,128]{1,0:T(8,128)S(1)}, f32[480,128]{1,0:T(8,128)S(1)}, f32[352,128]{1,0:T(8,128)S(1)}, f32[352,128]{1,0:T(8,128)S(1)}) custom-call(s32[2]{0:T(128)S(1)} %pad_add_fusion.level_ref.place_ref, f32[1920,128]{1,0:T(8,128)S(1)} %bitcast.13, f32[128,128]{1,0:T(8,128)S(1)} %get-tuple-element.39.after_ref.refs_0_), custom_call_target="tpu_custom_call" | custom-call | bytes 1835016 | tf_op jit(solution)/shard_map/pack/pallas_call | solution.py:359
  4.3 0.7 %collective-permute-start = (f32[480,128]{1,0:T(8,128)S(1)}, f32[480,128]{1,0:T(8,128)S(1)}, u32[]{:S(2)}, u32[]{:S(2)}) collective-permute-start(f32[480,128]{1,0:T(8,128)S(1)} %get-tuple-element.41), channel_id=1, source_target_pairs={{0,1},{1,0},{2,3},{3,2},{4,5},{5,4},{6,7},{7,6},{8,9},{9,8},{10,11... | collective-permute-start | bytes 737288 | tf_op jit(solution)/shard_map/ppermute | solution.py:386
  5.0 1.2 %collective-permute-start.1 = (f32[352,128]{1,0:T(8,128)S(1)}, f32[352,128]{1,0:T(8,128)S(1)}, u32[]{:S(2)}, u32[]{:S(2)}) collective-permute-start(f32[352,128]{1,0:T(8,128)S(1)} %get-tuple-element.42), channel_id=1, source_target_pairs={{0,2},{1,3},{2,0},{3,1},{4,6},{5,7},{6,4},{7,5},{8,10},{9,11},{10,... | collective-permute-start | bytes 540680 | tf_op jit(solution)/shard_map/ppermute | solution.py:386
  6.2 0.5 collective-permute-start.2
  6.7 1.2 %collective-permute-start.3 = (f32[128,128]{1,0:T(8,128)S(1)}, f32[128,128]{1,0:T(8,128)S(1)}, u32[]{:S(2)}, u32[]{:S(2)}) collective-permute-start(f32[128,128]{1,0:T(8,128)S(1)} %get-tuple-element.44), channel_id=1, source_target_pairs={{0,2},{1,3},{2,0},{3,1},{4,6},{5,7},{6,4},{7,5},{8,10},{9,11},{10,... | collective-permute-start | bytes 196616 | tf_op jit(solution)/shard_map/ppermute | solution.py:386
  7.9 0.6 %collective-permute-start.4 = (f32[128,128]{1,0:T(8,128)S(1)}, f32[128,128]{1,0:T(8,128)S(1)}, u32[]{:S(2)}, u32[]{:S(2)}) collective-permute-start(f32[128,128]{1,0:T(8,128)S(1)} %get-tuple-element.45), channel_id=1, source_target_pairs={{0,3},{1,2},{2,1},{3,0},{4,7},{5,6},{6,5},{7,4},{8,11},{9,10},{10,... | collective-permute-start | bytes 196616 | tf_op jit(solution)/shard_map/ppermute | solution.py:386
  8.5 7.9 %collective-permute-done.3.refs_2_ = f32[128,128]{1,0:T(8,128)S(1)} collective-permute-done((f32[128,128]{1,0:T(8,128)S(1)}, f32[128,128]{1,0:T(8,128)S(1)}, u32[]{:S(2)}, u32[]{:S(2)}) %collective-permute-start.3) | collective-permute-done | bytes 65568 | tf_op jit(solution)/shard_map/ppermute | solution.py:386
  16.4 1.6 %collective-permute-done.4.refs_3_ = f32[128,128]{1,0:T(8,128)S(1)} collective-permute-done((f32[128,128]{1,0:T(8,128)S(1)}, f32[128,128]{1,0:T(8,128)S(1)}, u32[]{:S(2)}, u32[]{:S(2)}) %collective-permute-start.4) | collective-permute-done | bytes 65568 | tf_op jit(solution)/shard_map/ppermute | solution.py:386
  18.0 1.2 %ends.1 = (f32[512,128]{1,0:T(8,128)S(1)}, f32[32,128]{1,0:T(8,128)S(1)}, f32[32,128]{1,0:T(8,128)S(1)}, f32[32,128]{1,0:T(8,128)S(1)}, f32[32,128]{1,0:T(8,128)S(1)}) custom-call(s32[2]{0:T(128)S(1)} %pad_add_fusion.level_ref.place_ref, f32[128,128]{1,0:T(8,128)S(1)} %get-tuple-element.39.after_ref.refs_0_, f32[480,128]{1,0:T(8,128)S(1)} %collective-permute-done.refs_1_, ...), custom_call_target="tpu_custom_call" | custom-call | flops 67108864 | bytes 1835016 | tf_op jit(solution)/shard_map/ends/pallas_call | solution.py:359
  19.2 1.3 %collective-permute-start.5 = (f32[32,128]{1,0:T(8,128)S(1)}, f32[32,128]{1,0:T(8,128)S(1)}, u32[]{:S(2)}, u32[]{:S(2)}) collective-permute-start(f32[32,128]{1,0:T(8,128)S(1)} %get-tuple-element.47), channel_id=1, source_target_pairs={{0,4},{4,0},{8,12},{12,8},{16,20},{20,16},{24,28},{28,24},{1,5},{5... | collective-permute-start | bytes 49160 | tf_op jit(solution)/shard_map/ppermute | solution.py:382
  20.5 2.0 %collective-permute-start.6 = (f32[32,128]{1,0:T(8,128)S(1)}, f32[32,128]{1,0:T(8,128)S(1)}, u32[]{:S(2)}, u32[]{:S(2)}) collective-permute-start(f32[32,128]{1,0:T(8,128)S(1)} %get-tuple-element.48), channel_id=1, source_target_pairs={{4,8},{8,4},{12,16},{16,12},{20,24},{24,20},{5,9},{9,5},{13,17},{1... | collective-permute-start | bytes 49160 | tf_op jit(solution)/shard_map/ppermute | solution.py:381
  22.5 1.5 %own.1 = (f32[1920,128]{1,0:T(8,128)S(1)}, f32[1920,128]{1,0:T(8,128)S(1)}, f32[160,128]{1,0:T(8,128)S(1)}, f32[1024,128]{1,0:T(8,128)S(1)}, f32[1024,128]{1,0:T...) custom-call(s32[2]{0:T(128)S(1)} %pad_add_fusion.level_ref.place_ref, ...), custom_call_target="tpu_custom_call" | custom-call | flops 9830400 | bytes 4163992 | tf_op jit(solution)/shard_map/own/pallas_call | solution.py:359
  24.1 1.8 %collective-permute-done.6.refs_13_.refs_3_ = f32[32,128]{1,0:T(8,128)S(1)} collective-permute-done((f32[32,128]{1,0:T(8,128)S(1)}, f32[32,128]{1,0:T(8,128)S(1)}, u32[]{:S(2)}, u32[]{:S(2)}) %collective-permute-start.6) | collective-permute-done | bytes 16416 | tf_op jit(solution)/shard_map/ppermute | solution.py:381
  25.9 3.1 %inner.1 = (f32[896,128]{1,0:T(8,128)S(1)}, f32[32,128]{1,0:T(8,128)S(1)}, f32[32,128]{1,0:T(8,128)S(1)}, f32[32,128]{1,0:T(8,128)S(1)}, f32[256,128]{1,0:T(8,12...) custom-call(s32[2]{0:T(128)S(1)} %pad_add_fusion.level_ref.place_ref, ...), custom_call_target="tpu_custom_call" | custom-call | flops 318767104 | bytes 5750792 | tf_op jit(solution)/shard_map/inner/pallas_call | solution.py:359
  29.0 1.3 %collective-permute-start.10 = (f32[256,128]{1,0:T(8,128)S(1)}, f32[256,128]{1,0:T(8,128)S(1)}, u32[]{:S(2)}, u32[]{:S(2)}) collective-permute-start(f32[256,128]{1,0:T(8,128)S(1)} %get-tuple-element.59), channel_id=1, source_target_pairs={{0,2},{1,3},{2,0},{3,1},{4,6},{5,7},{6,4},{7,5},{8,10},{9,11},{10,... | collective-permute-start | bytes 393224 | tf_op jit(solution)/shard_map/ppermute | solution.py:386
  30.3 2.1 %collective-permute-start.11 = (f32[256,128]{1,0:T(8,128)S(1)}, f32[256,128]{1,0:T(8,128)S(1)}, u32[]{:S(2)}, u32[]{:S(2)}) collective-permute-start(f32[256,128]{1,0:T(8,128)S(1)} %get-tuple-element.60), channel_id=1, source_target_pairs={{0,3},{1,2},{2,1},{3,0},{4,7},{5,6},{6,5},{7,4},{8,11},{9,10},{10,... | collective-permute-start | bytes 393224 | tf_op jit(solution)/shard_map/ppermute | solution.py:386
  32.4 0.3 collective-permute-start.7
  32.6 3.0 %collective-permute-start.8 = (f32[32,128]{1,0:T(8,128)S(1)}, f32[32,128]{1,0:T(8,128)S(1)}, u32[]{:S(2)}, u32[]{:S(2)}) collective-permute-start(f32[32,128]{1,0:T(8,128)S(1)} %get-tuple-element.55), channel_id=1, source_target_pairs={{4,8},{8,4},{12,16},{16,12},{20,24},{24,20},{5,9},{9,5},{13,17},{1... | collective-permute-start | bytes 49160 | tf_op jit(solution)/shard_map/ppermute | solution.py:381
  35.6 1.6 %partners.1 = (f32[2048,128]{1,0:T(8,128)S(1)}, f32[2048,128]{1,0:T(8,128)S(1)}, f32[32,128]{1,0:T(8,128)S(1)}) custom-call(s32[2]{0:T(128)S(1)} %pad_add_fusion.level_ref.place_ref, f32[4,76]{1,0:T(4,128)S(1)} %broadcast_multiply_fusion.lon_ref, f32[4,77]{1,0:T(4,128)S(1)} %broadcast_multiply_fusion.1.couple_ref, f32[32,128]{1,0:T(8,128)S(1)} %copy-done.8, ...), custom_call_target="tpu_custom_call" | custom-call | flops 9830400 | bytes 2148760 | tf_op jit(solution)/shard_map/partners/pallas_call | solution.py:359
  37.2 0.8 %collective-permute-done.8.refs_5_ = f32[32,128]{1,0:T(8,128)S(1)} collective-permute-done((f32[32,128]{1,0:T(8,128)S(1)}, f32[32,128]{1,0:T(8,128)S(1)}, u32[]{:S(2)}, u32[]{:S(2)}) %collective-permute-start.8) | collective-permute-done | bytes 16416 | tf_op jit(solution)/shard_map/ppermute | solution.py:381
  38.0 0.6 %sigma.1.refs_0_.refs_4_ = f32[64,128]{1,0:T(8,128)S(1)} custom-call(s32[2]{0:T(128)S(1)} %pad_add_fusion.level_ref.place_ref, f32[4,77]{1,0:T(4,128)S(1)} %broadcast_multiply_fusion.1.couple_ref, f32[896,128]{1,0:T(8,128)S(1)} %get-tuple-element.52.refs_0_.refs_2_, f32[32,128]{1,0:T(8,128)S(1)} %get-tuple-element.53.after_ref.refs_1_, ...), custom_call_target="tpu_custom_call" | custom-call | flops 163840 | bytes 2344152 | tf_op jit(solution)/shard_map/sigma/pallas_call | solution.py:359
  38.6 0.0 copy-start.9
  38.6 1.2 %collective-permute-start.12 = (f32[64,128]{1,0:T(8,128)S(1)}, f32[64,128]{1,0:T(8,128)S(1)}, u32[]{:S(2)}, u32[]{:S(2)}) collective-permute-start(f32[64,128]{1,0:T(8,128)S(1)} %sigma.1.refs_0_.refs_4_), channel_id=1, source_target_pairs={{0,2},{1,3},{2,0},{3,1},{4,6},{5,7},{6,4},{7,5},{8,10},{9,11},{10,... | collective-permute-start | bytes 98312 | tf_op jit(solution)/shard_map/ppermute | solution.py:386
  39.9 1.6 %collective-permute-done.12.refs_1_.refs_6_ = f32[64,128]{1,0:T(8,128)S(1)} collective-permute-done((f32[64,128]{1,0:T(8,128)S(1)}, f32[64,128]{1,0:T(8,128)S(1)}, u32[]{:S(2)}, u32[]{:S(2)}) %collective-permute-start.12) | collective-permute-done | bytes 32800 | tf_op jit(solution)/shard_map/ppermute | solution.py:386
  41.5 1.6 %second.1 = (f32[224,128]{1,0:T(8,128)S(1)}, f32[288,128]{1,0:T(8,128)S(1)}, f32[224,128]{1,0:T(8,128)S(1)}, f32[224,128]{1,0:T(8,128)S(1)}) custom-call(s32[2]{0:T(128)S(1)} %pad_add_fusion.level_ref.place_ref, f32[64,128]{1,0:T(8,128)S(1)} %sigma.1.refs_0_.refs_4_, f32[64,128]{1,0:T(8,128)S(1)} %collective-permute-done.12.refs_1_.refs_6_, ...), custom_call_target="tpu_custom_call" | custom-call | flops 117440512 | bytes 3866632 | tf_op jit(solution)/shard_map/second/pallas_call | solution.py:359
  43.1 3.2 %collective-permute-start.13 = (f32[288,128]{1,0:T(8,128)S(1)}, f32[288,128]{1,0:T(8,128)S(1)}, u32[]{:S(2)}, u32[]{:S(2)}) collective-permute-start(f32[288,128]{1,0:T(8,128)S(1)} %get-tuple-element.63), channel_id=1, source_target_pairs={{0,1},{1,0},{2,3},{3,2},{4,5},{5,4},{6,7},{7,6},{8,9},{9,8},{10,11... | collective-permute-start | bytes 442376 | tf_op jit(solution)/shard_map/ppermute | solution.py:386
  46.3 1.1 %collective-permute-start.16 = (f32[64,128]{1,0:T(8,128)S(1)}, f32[64,128]{1,0:T(8,128)S(1)}, u32[]{:S(2)}, u32[]{:S(2)}) collective-permute-start(f32[64,128]{1,0:T(8,128)S(1)} %sigma.1.refs_0_.refs_4_), channel_id=1, source_target_pairs={{0,3},{1,2},{2,1},{3,0},{4,7},{5,6},{6,5},{7,4},{8,11},{9,10},{10,... | collective-permute-start | bytes 98312 | tf_op jit(solution)/shard_map/ppermute | solution.py:386
  47.4 0.3 collective-permute-start.14
  47.7 1.8 %collective-permute-start.15 = (f32[224,128]{1,0:T(8,128)S(1)}, f32[224,128]{1,0:T(8,128)S(1)}, u32[]{:S(2)}, u32[]{:S(2)}) collective-permute-start(f32[224,128]{1,0:T(8,128)S(1)} %get-tuple-element.65), channel_id=1, source_target_pairs={{0,3},{1,2},{2,1},{3,0},{4,7},{5,6},{6,5},{7,4},{8,11},{9,10},{10,... | collective-permute-start | bytes 344072 | tf_op jit(solution)/shard_map/ppermute | solution.py:386
  49.5 0.1 collective-permute-done.16.refs_7_
  49.6 4.3 %correct.1.refs_4_ = f32[1920,128]{1,0:T(8,128)} custom-call(s32[2]{0:T(128)S(1)} %pad_add_fusion.level_ref.place_ref, f32[256,128]{1,0:T(8,128)S(1)} %get-tuple-element.66.refs_0_, f32[256,128]{1,0:T(8,128)S(1)} %collective-permute-done.9.refs_11_.refs_1_, f32[256,128]{1,0:T(8,128)S(1)} %collective-permute-done.10.refs_12_.refs_2_, ...), custom_call_target="tpu_custom_call" | custom-call | flops 5368709120 | bytes 6750216 | tf_op jit(solution)/shard_map/correct/pallas_call | solution.py:359
  53.9 0.8 %collective-permute-done.15.refs_3_ = f32[224,128]{1,0:T(8,128)S(1)} collective-permute-done((f32[224,128]{1,0:T(8,128)S(1)}, f32[224,128]{1,0:T(8,128)S(1)}, u32[]{:S(2)}, u32[]{:S(2)}) %collective-permute-start.15) | collective-permute-done | bytes 114720 | tf_op jit(solution)/shard_map/ppermute | solution.py:386
  54.7 1.3 %unpack.1 = f32[1920,128]{1,0:T(8,128)} custom-call(s32[2]{0:T(128)S(1)} %pad_add_fusion.level_ref.place_ref, f32[224,128]{1,0:T(8,128)S(1)} %get-tuple-element.62.refs_0_, f32[288,128]{1,0:T(8,128)S(1)} %collective-permute-done.13.refs_5_.refs_1_, f32[224,128]{1,0:T(8,128)S(1)} %collective-permute-done.14.refs_2_, ...), custom_call_target="tpu_custom_call", output_to_operand_aliasing={{}: (5, {})} | custom-call | bytes 2457608 | tf_op jit(solution)/shard_map/unpack/pallas_call | solution.py:359
  (28 shorter events, 0.1 us)
Async XLA Ops:
  0.0 0.7 %copy-start.10 = (f32[479]{0:T(512)S(1)}, f32[479]{0:T(512)}, u32[]{:S(2)}) copy-start(f32[479]{0:T(512)} %param.15) | copy-start | bytes 5752
  0.0 0.8 %copy-start.12 = (f32[4]{0:T(128)S(1)}, f32[4]{0:T(128)}, u32[]{:S(2)}) copy-start(f32[4]{0:T(128)} %param.16) | copy-start | bytes 52
  0.0 0.8 %copy-start.11 = (f32[480]{0:T(512)S(1)}, f32[480]{0:T(512)}, u32[]{:S(2)}) copy-start(f32[480]{0:T(512)} %param.14) | copy-start | bytes 5764
  0.0 1.1 %copy-start.8 = (f32[32,128]{1,0:T(8,128)S(1)}, f32[32,128]{1,0:T(8,128)}, u32[]{:S(2)}) copy-start(f32[32,128]{1,0:T(8,128)} %constant.63.eigen_ref) | copy-start | bytes 49156
  1.8 1.2 %copy-start = (f32[60,4,1024]{2,1,0:T(4,128)S(1)}, f32[60,4,1024]{2,1,0:T(4,128)}, u32[]{:S(2)}) copy-start(f32[60,4,1024]{2,1,0:T(4,128)} %param.13) | copy-start | bytes 2949124
  3.5 14.4 %copy-start.1 = (bf16[512,256]{1,0:T(8,128)(2,1)S(1)}, bf16[512,256]{1,0:T(8,128)(2,1)}, u32[]{:S(2)}) copy-start(bf16[512,256]{1,0:T(8,128)(2,1)} %constant.50.clone.refs_4_) | copy-start | bytes 786436
  3.6 14.4 %copy-start.2 = (bf16[512,256]{1,0:T(8,128)(2,1)S(1)}, bf16[512,256]{1,0:T(8,128)(2,1)}, u32[]{:S(2)}) copy-start(bf16[512,256]{1,0:T(8,128)(2,1)} %constant.52.clone.refs_6_) | copy-start | bytes 786436
  3.6 14.4 %copy-start.3 = (bf16[512,256]{1,0:T(8,128)(2,1)S(1)}, bf16[512,256]{1,0:T(8,128)(2,1)}, u32[]{:S(2)}) copy-start(bf16[512,256]{1,0:T(8,128)(2,1)} %constant.54.clone.refs_7_) | copy-start | bytes 786436
  3.6 14.4 %copy-start.7 = (f32[32,128]{1,0:T(8,128)S(1)}, f32[32,128]{1,0:T(8,128)}, u32[]{:S(2)}) copy-start(f32[32,128]{1,0:T(8,128)} %constant.56.clone.refs_5_.refs_7_.refs_15_) | copy-start | bytes 49156
  4.3 13.7 %collective-permute-start = (f32[480,128]{1,0:T(8,128)S(1)}, f32[480,128]{1,0:T(8,128)S(1)}, u32[]{:S(2)}, u32[]{:S(2)}) collective-permute-start(f32[480,128]{1,0:T(8,128)S(1)} %get-tuple-element.41), channel_id=1, source_target_pairs={{0,1},{1,0},{2,3},{3,2},{4,5},{5,4},{6,7},{7,6},{8,9},{9,8},{10,11... | collective-permute-start | bytes 737288 | tf_op jit(solution)/shard_map/ppermute | solution.py:386
  5.0 19.0 %collective-permute-start.1 = (f32[352,128]{1,0:T(8,128)S(1)}, f32[352,128]{1,0:T(8,128)S(1)}, u32[]{:S(2)}, u32[]{:S(2)}) collective-permute-start(f32[352,128]{1,0:T(8,128)S(1)} %get-tuple-element.42), channel_id=1, source_target_pairs={{0,2},{1,3},{2,0},{3,1},{4,6},{5,7},{6,4},{7,5},{8,10},{9,11},{10,... | collective-permute-start | bytes 540680 | tf_op jit(solution)/shard_map/ppermute | solution.py:386
  6.2 17.8 %collective-permute-start.2 = (f32[352,128]{1,0:T(8,128)S(1)}, f32[352,128]{1,0:T(8,128)S(1)}, u32[]{:S(2)}, u32[]{:S(2)}) collective-permute-start(f32[352,128]{1,0:T(8,128)S(1)} %get-tuple-element.43), channel_id=1, source_target_pairs={{0,3},{1,2},{2,1},{3,0},{4,7},{5,6},{6,5},{7,4},{8,11},{9,10},{10,... | collective-permute-start | bytes 540680 | tf_op jit(solution)/shard_map/ppermute | solution.py:386
  6.7 9.7 %collective-permute-start.3 = (f32[128,128]{1,0:T(8,128)S(1)}, f32[128,128]{1,0:T(8,128)S(1)}, u32[]{:S(2)}, u32[]{:S(2)}) collective-permute-start(f32[128,128]{1,0:T(8,128)S(1)} %get-tuple-element.44), channel_id=1, source_target_pairs={{0,2},{1,3},{2,0},{3,1},{4,6},{5,7},{6,4},{7,5},{8,10},{9,11},{10,... | collective-permute-start | bytes 196616 | tf_op jit(solution)/shard_map/ppermute | solution.py:386
  7.9 18.0 %copy-start.4 = (bf16[512,256]{1,0:T(8,128)(2,1)S(1)}, bf16[512,256]{1,0:T(8,128)(2,1)}, u32[]{:S(2)}) copy-start(bf16[512,256]{1,0:T(8,128)(2,1)} %constant.53.clone.refs_9_.refs_8_.refs_16_) | copy-start | bytes 786436
  7.9 18.0 %copy-start.5 = (bf16[512,256]{1,0:T(8,128)(2,1)S(1)}, bf16[512,256]{1,0:T(8,128)(2,1)}, u32[]{:S(2)}) copy-start(bf16[512,256]{1,0:T(8,128)(2,1)} %constant.55.clone.refs_10_.refs_9_.refs_17_) | copy-start | bytes 786436
  7.9 18.0 %copy-start.6 = (bf16[512,256]{1,0:T(8,128)(2,1)S(1)}, bf16[512,256]{1,0:T(8,128)(2,1)}, u32[]{:S(2)}) copy-start(bf16[512,256]{1,0:T(8,128)(2,1)} %constant.51.clone.refs_8_.refs_6_) | copy-start | bytes 786436
  7.9 10.0 %collective-permute-start.4 = (f32[128,128]{1,0:T(8,128)S(1)}, f32[128,128]{1,0:T(8,128)S(1)}, u32[]{:S(2)}, u32[]{:S(2)}) collective-permute-start(f32[128,128]{1,0:T(8,128)S(1)} %get-tuple-element.45), channel_id=1, source_target_pairs={{0,3},{1,2},{2,1},{3,0},{4,7},{5,6},{6,5},{7,4},{8,11},{9,10},{10,... | collective-permute-start | bytes 196616 | tf_op jit(solution)/shard_map/ppermute | solution.py:386
  19.2 4.8 %collective-permute-start.5 = (f32[32,128]{1,0:T(8,128)S(1)}, f32[32,128]{1,0:T(8,128)S(1)}, u32[]{:S(2)}, u32[]{:S(2)}) collective-permute-start(f32[32,128]{1,0:T(8,128)S(1)} %get-tuple-element.47), channel_id=1, source_target_pairs={{0,4},{4,0},{8,12},{12,8},{16,20},{20,16},{24,28},{28,24},{1,5},{5... | collective-permute-start | bytes 49160 | tf_op jit(solution)/shard_map/ppermute | solution.py:382
  20.5 5.4 %collective-permute-start.6 = (f32[32,128]{1,0:T(8,128)S(1)}, f32[32,128]{1,0:T(8,128)S(1)}, u32[]{:S(2)}, u32[]{:S(2)}) collective-permute-start(f32[32,128]{1,0:T(8,128)S(1)} %get-tuple-element.48), channel_id=1, source_target_pairs={{4,8},{8,4},{12,16},{16,12},{20,24},{24,20},{5,9},{9,5},{13,17},{1... | collective-permute-start | bytes 49160 | tf_op jit(solution)/shard_map/ppermute | solution.py:381
  29.0 9.0 %collective-permute-start.10 = (f32[256,128]{1,0:T(8,128)S(1)}, f32[256,128]{1,0:T(8,128)S(1)}, u32[]{:S(2)}, u32[]{:S(2)}) collective-permute-start(f32[256,128]{1,0:T(8,128)S(1)} %get-tuple-element.59), channel_id=1, source_target_pairs={{0,2},{1,3},{2,0},{3,1},{4,6},{5,7},{6,4},{7,5},{8,10},{9,11},{10,... | collective-permute-start | bytes 393224 | tf_op jit(solution)/shard_map/ppermute | solution.py:386
  30.3 7.7 %collective-permute-start.11 = (f32[256,128]{1,0:T(8,128)S(1)}, f32[256,128]{1,0:T(8,128)S(1)}, u32[]{:S(2)}, u32[]{:S(2)}) collective-permute-start(f32[256,128]{1,0:T(8,128)S(1)} %get-tuple-element.60), channel_id=1, source_target_pairs={{0,3},{1,2},{2,1},{3,0},{4,7},{5,6},{6,5},{7,4},{8,11},{9,10},{10,... | collective-permute-start | bytes 393224 | tf_op jit(solution)/shard_map/ppermute | solution.py:386
  32.4 5.6 %collective-permute-start.9 = (f32[256,128]{1,0:T(8,128)S(1)}, f32[256,128]{1,0:T(8,128)S(1)}, u32[]{:S(2)}, u32[]{:S(2)}) collective-permute-start(f32[256,128]{1,0:T(8,128)S(1)} %get-tuple-element.58), channel_id=1, source_target_pairs={{0,1},{1,0},{2,3},{3,2},{4,5},{5,4},{6,7},{7,6},{8,9},{9,8},{10,11... | collective-permute-start | bytes 393224 | tf_op jit(solution)/shard_map/ppermute | solution.py:386
  32.4 4.8 %collective-permute-start.7 = (f32[32,128]{1,0:T(8,128)S(1)}, f32[32,128]{1,0:T(8,128)S(1)}, u32[]{:S(2)}, u32[]{:S(2)}) collective-permute-start(f32[32,128]{1,0:T(8,128)S(1)} %get-tuple-element.54), channel_id=1, source_target_pairs={{0,4},{4,0},{8,12},{12,8},{16,20},{20,16},{24,28},{28,24},{1,5},{5... | collective-permute-start | bytes 49160 | tf_op jit(solution)/shard_map/ppermute | solution.py:382
  32.6 5.4 %collective-permute-start.8 = (f32[32,128]{1,0:T(8,128)S(1)}, f32[32,128]{1,0:T(8,128)S(1)}, u32[]{:S(2)}, u32[]{:S(2)}) collective-permute-start(f32[32,128]{1,0:T(8,128)S(1)} %get-tuple-element.55), channel_id=1, source_target_pairs={{4,8},{8,4},{12,16},{16,12},{20,24},{24,20},{5,9},{9,5},{13,17},{1... | collective-permute-start | bytes 49160 | tf_op jit(solution)/shard_map/ppermute | solution.py:381
  38.6 11.0 %copy-start.9 = (bf16[512,256]{1,0:T(8,128)(2,1)S(1)}, bf16[512,256]{1,0:T(8,128)(2,1)}, u32[]{:S(2)}) copy-start(bf16[512,256]{1,0:T(8,128)(2,1)} %constant.49.clone.refs_14_) | copy-start | bytes 786436
  38.6 2.8 %collective-permute-start.12 = (f32[64,128]{1,0:T(8,128)S(1)}, f32[64,128]{1,0:T(8,128)S(1)}, u32[]{:S(2)}, u32[]{:S(2)}) collective-permute-start(f32[64,128]{1,0:T(8,128)S(1)} %sigma.1.refs_0_.refs_4_), channel_id=1, source_target_pairs={{0,2},{1,3},{2,0},{3,1},{4,6},{5,7},{6,4},{7,5},{8,10},{9,11},{10,... | collective-permute-start | bytes 98312 | tf_op jit(solution)/shard_map/ppermute | solution.py:386
  43.1 6.5 %collective-permute-start.13 = (f32[288,128]{1,0:T(8,128)S(1)}, f32[288,128]{1,0:T(8,128)S(1)}, u32[]{:S(2)}, u32[]{:S(2)}) collective-permute-start(f32[288,128]{1,0:T(8,128)S(1)} %get-tuple-element.63), channel_id=1, source_target_pairs={{0,1},{1,0},{2,3},{3,2},{4,5},{5,4},{6,7},{7,6},{8,9},{9,8},{10,11... | collective-permute-start | bytes 442376 | tf_op jit(solution)/shard_map/ppermute | solution.py:386
  46.3 3.4 %collective-permute-start.16 = (f32[64,128]{1,0:T(8,128)S(1)}, f32[64,128]{1,0:T(8,128)S(1)}, u32[]{:S(2)}, u32[]{:S(2)}) collective-permute-start(f32[64,128]{1,0:T(8,128)S(1)} %sigma.1.refs_0_.refs_4_), channel_id=1, source_target_pairs={{0,3},{1,2},{2,1},{3,0},{4,7},{5,6},{6,5},{7,4},{8,11},{9,10},{10,... | collective-permute-start | bytes 98312 | tf_op jit(solution)/shard_map/ppermute | solution.py:386
  47.4 6.5 %collective-permute-start.14 = (f32[224,128]{1,0:T(8,128)S(1)}, f32[224,128]{1,0:T(8,128)S(1)}, u32[]{:S(2)}, u32[]{:S(2)}) collective-permute-start(f32[224,128]{1,0:T(8,128)S(1)} %get-tuple-element.64), channel_id=1, source_target_pairs={{0,2},{1,3},{2,0},{3,1},{4,6},{5,7},{6,4},{7,5},{8,10},{9,11},{10,... | collective-permute-start | bytes 344072 | tf_op jit(solution)/shard_map/ppermute | solution.py:386
  47.7 7.0 %collective-permute-start.15 = (f32[224,128]{1,0:T(8,128)S(1)}, f32[224,128]{1,0:T(8,128)S(1)}, u32[]{:S(2)}, u32[]{:S(2)}) collective-permute-start(f32[224,128]{1,0:T(8,128)S(1)} %get-tuple-element.65), channel_id=1, source_target_pairs={{0,3},{1,2},{2,1},{3,0},{4,7},{5,6},{6,5},{7,4},{8,11},{9,10},{10,... | collective-permute-start | bytes 344072 | tf_op jit(solution)/shard_map/ppermute | solution.py:386

commit v6 on v5

--- a/solution.py
+++ b/solution.py
@@ -647,8 +647,7 @@
 
     far = list(range(2, levels))
 
-    def pack_ends(place_ref, in_ref, after_ref, *refs):
-        del after_ref
+    def pack_ends(place_ref, in_ref, *refs):
         for end_ref, mask in zip(refs, [0] + far):
             level = place_ref[0] ^ mask
             end_ref[:span, :] = in_ref[pl.ds(level, span, stride=levels), :]
@@ -657,8 +656,8 @@
     end_packed = call(
         pack_ends,
         [(ends * digits, N2)] * (levels - 1),
-        [place, by_row, around],
-        [SMEM, VMEM, pl.ANY],
+        [place, by_row],
+        [SMEM, VMEM],
         [],
         0,
         "pack_ends",
@@ -721,7 +720,7 @@
     def spread(place_ref, full_ref, count, out_refs):
         for mask, out_ref in enumerate(out_refs):
             at = pl.multiple_of((place_ref[0] ^ mask) * digits, digits)
-            out_ref[: count * digits, :] = full_ref[:count, pl.ds(at, digits), :].reshape(count * digits, N2)
+            out_ref[...] = full_ref[:count, pl.ds(at, digits), :].reshape(count * digits, N2)
 
     def inner_body(place_ref, *refs):
         pieces, refs = refs[:levels], refs[levels:]
@@ -813,11 +812,10 @@
         groups * N2 * 40,
         "sigma",
     )
-    far_sigma = [send_level(sigma, mask, levels) for mask in far]
+    sigma_pieces = swap_levels([sigma] * levels)
     def second_body(place_ref, *refs):
-        sigma_ref, after_ref, first_ref, ratio_ref, inverse_ref, edge_ref = refs[:6]
-        del after_ref
-        tables_in, refs = refs[6:10], refs[10:]
+        sigma_ref, first_ref, ratio_ref, inverse_ref, edge_ref = refs[:5]
+        tables_in, refs = refs[5:9], refs[9:]
         late_refs = refs[:levels]
         sum_ref, mid_ref, full_ref = refs[levels:]
         low, high = sigma_ref[:groups, :], sigma_ref[groups:, :]
@@ -840,19 +838,17 @@
                 sum_ref[here, :] = first_ref[here, :] + x_high
         backward_rows(sum_ref, late, *tables_in, mid_ref, full_ref)
         spread(place_ref, full_ref, late, late_refs)
-        late_refs[1][late * digits :, :] = sigma_ref[...]
 
     late_pieces = call(
         second_body,
-        [(late * digits + (2 * groups if mask == 1 else 0), N2) for mask in range(levels)],
-        [place, sigma, far_sigma[0], late_first, ratio, inverse, edge, *backward],
-        [SMEM, VMEM, pl.ANY] + [VMEM] * 8,
+        [(late * digits, N2)] * levels,
+        [place, sigma, late_first, ratio, inverse, edge, *backward],
+        [SMEM] + [VMEM] * 9,
         [vmem(late * groups, N2), vmem(max(pad_late, half) * N1, N2), vmem(pad_late, N1, N2)],
         late * NLON * 256 * 4,
         "second",
     )
     late_pieces = swap_levels(late_pieces)
-    sigma_pieces = [sigma, late_pieces[1], *far_sigma]
     total = rows * levels * digits
     early_total = early * levels * digits
     part = const["first_back_part"]
@@ -867,9 +863,7 @@
         size = early * groups
         for mask in range(levels):
             level = place_ref[0] ^ mask
-            last = sigma_refs[mask].shape[0]
-            low = sigma_refs[mask][last - 2 * groups : last - groups, :]
-            high = sigma_refs[mask][last - groups :, :]
+            low, high = sigma_refs[mask][:groups, :], sigma_refs[mask][groups:, :]
             phi_ref, psi_ref = responses[2 * min(mask, 2) : 2 * min(mask, 2) + 2]
             first = max(mask - 2, 0) * size
             phi_all = phi_ref[first : first + size, :].reshape(early, groups, N2)

time: 56.3 us -> 42.9 us (0.76)
  waiting for transfers between devices: 14.6 us -> 4.91 us
  starting transfers between devices: 21.8 us -> 18.8 us
  local copies, waits for them, and re-layouts: 2.07 us -> 1.42 us
    ppermute x13 -> x14, waiting for transfers between devices: 12 us -> 3.6 us  [send_level(): return lax.ppermute(piece, 'lon', [(d, d ^ mask) for d in range(size)])]
    ppermute x13 -> x14, starting transfers between devices: 15.2 us -> 12.3 us  [send_level(): return lax.ppermute(piece, 'lon', [(d, d ^ mask) for d in range(size)])]
    ppermute x2, waiting for transfers between devices: 2.6 us -> 1.31 us  [swap(): value_odd = lax.ppermute(value_odd, 'lat', odd)]
    unnamed x26, local copies, waits for them, and re-layouts: 1.92 us -> 1.27 us
  transfers between devices with their start and end apart: 17 -> 18, of which waited for: 7 -> 6; matrix products, arithmetic and copies ran while one was open for 0% -> 1% of each run, Pallas kernels for 15% -> 27%
where the time goes in v6:
time: 42.9 us; the launch traced here: 42.7 us
  starting transfers between devices  18.8 us (44%)
  Pallas kernels  17.1 us (40%)
  waiting for transfers between devices  4.91 us (11%)
  local copies, waits for them, and re-layouts  1.42 us (3%)
    pallas_call x11, Pallas kernels, call(): pl.pallas_call(body, out_shape=[jax.ShapeDtypeStruct(s, jnp.float32) for...  17.1 us
    ppermute x14, starting transfers between devices, send_level(): return lax.ppermute(piece, 'lon', [(d, d ^ mask) for d in range(size)])  12.3 us
    ppermute x2, starting transfers between devices, swap(): value_odd = lax.ppermute(value_odd, 'lat', odd)  5.03 us
    ppermute x14, waiting for transfers between devices, send_level(): return lax.ppermute(piece, 'lon', [(d, d ^ mask) for d in range(size)])  3.6 us
    ppermute x2, starting transfers between devices, swap(): return (lax.ppermute(value_even, 'lat', even), value_odd)  1.54 us
    ppermute x2, waiting for transfers between devices, swap(): value_odd = lax.ppermute(value_odd, 'lat', odd)  1.31 us
    unnamed x26, local copies, waits for them, and re-layouts  1.27 us
  transfers between devices with their start and end apart: 18, of which 6 were waited for; matrix products, arithmetic and copies ran while one was open for 1% of the time, Pallas kernels for 27%

profile of v6, /device:TPU:17, one launch (start us, length us, event | category | flops | bytes accessed | tf_op | source)
XLA Modules:
  0.0 42.7 jit_solution(9354170896019283620)
XLA Ops:
  0.0 0.1 pad_add_fusion.place_ref.level_ref
  0.1 1.2 %copy-done = f32[60,4,1024]{2,1,0:T(4,128)S(1)} copy-done((f32[60,4,1024]{2,1,0:T(4,128)S(1)}, f32[60,4,1024]{2,1,0:T(4,128)}, u32[]{:S(2)}) %copy-start) | copy-done | bytes 983064
  1.3 0.6 %pack_ends.1 = (f32[128,128]{1,0:T(8,128)S(1)}, f32[128,128]{1,0:T(8,128)S(1)}, f32[128,128]{1,0:T(8,128)S(1)}) custom-call(s32[2]{0:T(128)S(1)} %pad_add_fusion.place_ref.level_ref, f32[1920,128]{1,0:T(8,128)S(1)} %bitcast.12), custom_call_target="tpu_custom_call" | custom-call | bytes 1179656 | tf_op jit(solution)/shard_map/pack_ends/pallas_call | solution.py:359
  1.9 1.3 %collective-permute-start.3 = (f32[128,128]{1,0:T(8,128)S(1)}, f32[128,128]{1,0:T(8,128)S(1)}, u32[]{:S(2)}, u32[]{:S(2)}) collective-permute-start(f32[128,128]{1,0:T(8,128)S(1)} %get-tuple-element.44), channel_id=1, source_target_pairs={{0,2},{1,3},{2,0},{3,1},{4,6},{5,7},{6,4},{7,5},{8,10},{9,11},{10,... | collective-permute-start | bytes 196616 | tf_op jit(solution)/shard_map/ppermute | solution.py:386
  3.1 1.1 %collective-permute-start.4 = (f32[128,128]{1,0:T(8,128)S(1)}, f32[128,128]{1,0:T(8,128)S(1)}, u32[]{:S(2)}, u32[]{:S(2)}) collective-permute-start(f32[128,128]{1,0:T(8,128)S(1)} %get-tuple-element.45), channel_id=1, source_target_pairs={{0,3},{1,2},{2,1},{3,0},{4,7},{5,6},{6,5},{7,4},{8,11},{9,10},{10,... | collective-permute-start | bytes 196616 | tf_op jit(solution)/shard_map/ppermute | solution.py:386
  4.2 0.0 copy-start.2
  4.3 0.0 copy-start.3
  4.3 0.6 %pack.1 = (f32[352,128]{1,0:T(8,128)S(1)}, f32[480,128]{1,0:T(8,128)S(1)}, f32[352,128]{1,0:T(8,128)S(1)}, f32[352,128]{1,0:T(8,128)S(1)}) custom-call(s32[2]{0:T(128)S(1)} %pad_add_fusion.place_ref.level_ref, f32[1920,128]{1,0:T(8,128)S(1)} %bitcast.13, f32[128,128]{1,0:T(8,128)S(1)} %get-tuple-element.39.after_ref.refs_0_), custom_call_target="tpu_custom_call" | custom-call | bytes 1835016 | tf_op jit(solution)/shard_map/pack/pallas_call | solution.py:359
  4.9 0.0 copy-start.1
  4.9 1.3 %collective-permute-start.1 = (f32[352,128]{1,0:T(8,128)S(1)}, f32[352,128]{1,0:T(8,128)S(1)}, u32[]{:S(2)}, u32[]{:S(2)}) collective-permute-start(f32[352,128]{1,0:T(8,128)S(1)} %get-tuple-element.42), channel_id=1, source_target_pairs={{0,2},{1,3},{2,0},{3,1},{4,6},{5,7},{6,4},{7,5},{8,10},{9,11},{10,... | collective-permute-start | bytes 540680 | tf_op jit(solution)/shard_map/ppermute | solution.py:386
  6.2 0.3 collective-permute-start.2
  6.5 0.4 collective-permute-start
  6.9 0.1 pad_dynamic-slice_fusion.1
  6.9 0.1 broadcast_multiply_fusion.1.couple_ref
  7.0 0.1 pad_dynamic-slice_fusion
  7.1 0.1 broadcast_multiply_fusion.lon_ref
  7.2 0.7 %edge.1.refs_8_.refs_10_ = f32[512,128]{1,0:T(8,128)S(1)} custom-call(s32[2]{0:T(128)S(1)} %pad_add_fusion.place_ref.level_ref, f32[4,76]{1,0:T(4,128)S(1)} %broadcast_multiply_fusion.lon_ref, f32[4,77]{1,0:T(4,128)S(1)} %broadcast_multiply_fusion.1.couple_ref, f32[32,128]{1,0:T(8,128)S(1)} %copy-done.8), custom_call_target="tpu_custom_call" | custom-call | flops 1310720 | bytes 280984 | tf_op jit(solution)/shard_map/edge/pallas_call | solution.py:359
  7.9 0.0 copy-start.4
  7.9 0.0 copy-start.5
  7.9 0.0 copy-start.6
  7.9 0.1 collective-permute-done.refs_1_
  8.0 1.2 %ends.1 = (f32[512,128]{1,0:T(8,128)S(1)}, f32[32,128]{1,0:T(8,128)S(1)}, f32[32,128]{1,0:T(8,128)S(1)}, f32[32,128]{1,0:T(8,128)S(1)}, f32[32,128]{1,0:T(8,128)S(1)}) custom-call(s32[2]{0:T(128)S(1)} %pad_add_fusion.place_ref.level_ref, f32[128,128]{1,0:T(8,128)S(1)} %get-tuple-element.39.after_ref.refs_0_, f32[480,128]{1,0:T(8,128)S(1)} %collective-permute-done.refs_1_, ...), custom_call_target="tpu_custom_call" | custom-call | flops 67108864 | bytes 1835016 | tf_op jit(solution)/shard_map/ends/pallas_call | solution.py:359
  9.3 1.3 %collective-permute-start.5 = (f32[32,128]{1,0:T(8,128)S(1)}, f32[32,128]{1,0:T(8,128)S(1)}, u32[]{:S(2)}, u32[]{:S(2)}) collective-permute-start(f32[32,128]{1,0:T(8,128)S(1)} %get-tuple-element.47), channel_id=1, source_target_pairs={{0,4},{4,0},{8,12},{12,8},{16,20},{20,16},{24,28},{28,24},{1,5},{5... | collective-permute-start | bytes 49160 | tf_op jit(solution)/shard_map/ppermute | solution.py:382
  10.6 2.0 %collective-permute-start.6 = (f32[32,128]{1,0:T(8,128)S(1)}, f32[32,128]{1,0:T(8,128)S(1)}, u32[]{:S(2)}, u32[]{:S(2)}) collective-permute-start(f32[32,128]{1,0:T(8,128)S(1)} %get-tuple-element.48), channel_id=1, source_target_pairs={{4,8},{8,4},{12,16},{16,12},{20,24},{24,20},{5,9},{9,5},{13,17},{1... | collective-permute-start | bytes 49160 | tf_op jit(solution)/shard_map/ppermute | solution.py:381
  12.6 1.5 %own.1 = (f32[1920,128]{1,0:T(8,128)S(1)}, f32[1920,128]{1,0:T(8,128)S(1)}, f32[160,128]{1,0:T(8,128)S(1)}, f32[1024,128]{1,0:T(8,128)S(1)}, f32[1024,128]{1,0:T...) custom-call(s32[2]{0:T(128)S(1)} %pad_add_fusion.place_ref.level_ref, ...), custom_call_target="tpu_custom_call" | custom-call | flops 9830400 | bytes 4163992 | tf_op jit(solution)/shard_map/own/pallas_call | solution.py:359
  14.1 1.3 %collective-permute-done.2.refs_3_ = f32[352,128]{1,0:T(8,128)S(1)} collective-permute-done((f32[352,128]{1,0:T(8,128)S(1)}, f32[352,128]{1,0:T(8,128)S(1)}, u32[]{:S(2)}, u32[]{:S(2)}) %collective-permute-start.2) | collective-permute-done | bytes 180256 | tf_op jit(solution)/shard_map/ppermute | solution.py:386
  15.4 0.6 %collective-permute-done.6.refs_13_.refs_3_ = f32[32,128]{1,0:T(8,128)S(1)} collective-permute-done((f32[32,128]{1,0:T(8,128)S(1)}, f32[32,128]{1,0:T(8,128)S(1)}, u32[]{:S(2)}, u32[]{:S(2)}) %collective-permute-start.6) | collective-permute-done | bytes 16416 | tf_op jit(solution)/shard_map/ppermute | solution.py:381
  16.0 3.1 %inner.1 = (f32[896,128]{1,0:T(8,128)S(1)}, f32[32,128]{1,0:T(8,128)S(1)}, f32[32,128]{1,0:T(8,128)S(1)}, f32[32,128]{1,0:T(8,128)S(1)}, f32[256,128]{1,0:T(8,12...) custom-call(s32[2]{0:T(128)S(1)} %pad_add_fusion.place_ref.level_ref, ...), custom_call_target="tpu_custom_call" | custom-call | flops 318767104 | bytes 5750792 | tf_op jit(solution)/shard_map/inner/pallas_call | solution.py:359
  19.0 1.8 %collective-permute-start.9 = (f32[256,128]{1,0:T(8,128)S(1)}, f32[256,128]{1,0:T(8,128)S(1)}, u32[]{:S(2)}, u32[]{:S(2)}) collective-permute-start(f32[256,128]{1,0:T(8,128)S(1)} %get-tuple-element.58), channel_id=1, source_target_pairs={{0,1},{1,0},{2,3},{3,2},{4,5},{5,4},{6,7},{7,6},{8,9},{9,8},{10,11... | collective-permute-start | bytes 393224 | tf_op jit(solution)/shard_map/ppermute | solution.py:386
  20.9 1.2 %collective-permute-start.10 = (f32[256,128]{1,0:T(8,128)S(1)}, f32[256,128]{1,0:T(8,128)S(1)}, u32[]{:S(2)}, u32[]{:S(2)}) collective-permute-start(f32[256,128]{1,0:T(8,128)S(1)} %get-tuple-element.59), channel_id=1, source_target_pairs={{0,2},{1,3},{2,0},{3,1},{4,6},{5,7},{6,4},{7,5},{8,10},{9,11},{10,... | collective-permute-start | bytes 393224 | tf_op jit(solution)/shard_map/ppermute | solution.py:386
  22.1 0.5 %collective-permute-start.11 = (f32[256,128]{1,0:T(8,128)S(1)}, f32[256,128]{1,0:T(8,128)S(1)}, u32[]{:S(2)}, u32[]{:S(2)}) collective-permute-start(f32[256,128]{1,0:T(8,128)S(1)} %get-tuple-element.60), channel_id=1, source_target_pairs={{0,3},{1,2},{2,1},{3,0},{4,7},{5,6},{6,5},{7,4},{8,11},{9,10},{10,... | collective-permute-start | bytes 393224 | tf_op jit(solution)/shard_map/ppermute | solution.py:386
  22.6 0.2 collective-permute-start.7
  22.8 3.0 %collective-permute-start.8 = (f32[32,128]{1,0:T(8,128)S(1)}, f32[32,128]{1,0:T(8,128)S(1)}, u32[]{:S(2)}, u32[]{:S(2)}) collective-permute-start(f32[32,128]{1,0:T(8,128)S(1)} %get-tuple-element.55), channel_id=1, source_target_pairs={{4,8},{8,4},{12,16},{16,12},{20,24},{24,20},{5,9},{9,5},{13,17},{1... | collective-permute-start | bytes 49160 | tf_op jit(solution)/shard_map/ppermute | solution.py:381
  25.9 1.6 %partners.1 = (f32[2048,128]{1,0:T(8,128)S(1)}, f32[2048,128]{1,0:T(8,128)S(1)}, f32[32,128]{1,0:T(8,128)S(1)}) custom-call(s32[2]{0:T(128)S(1)} %pad_add_fusion.place_ref.level_ref, f32[4,76]{1,0:T(4,128)S(1)} %broadcast_multiply_fusion.lon_ref, f32[4,77]{1,0:T(4,128)S(1)} %broadcast_multiply_fusion.1.couple_ref, f32[32,128]{1,0:T(8,128)S(1)} %copy-done.8, ...), custom_call_target="tpu_custom_call" | custom-call | flops 9830400 | bytes 2148760 | tf_op jit(solution)/shard_map/partners/pallas_call | solution.py:359
  27.5 0.7 %collective-permute-done.8.refs_5_ = f32[32,128]{1,0:T(8,128)S(1)} collective-permute-done((f32[32,128]{1,0:T(8,128)S(1)}, f32[32,128]{1,0:T(8,128)S(1)}, u32[]{:S(2)}, u32[]{:S(2)}) %collective-permute-start.8) | collective-permute-done | bytes 16416 | tf_op jit(solution)/shard_map/ppermute | solution.py:381
  28.2 1.0 %collective-permute-done.11.refs_13_.refs_3_ = f32[256,128]{1,0:T(8,128)S(1)} collective-permute-done((f32[256,128]{1,0:T(8,128)S(1)}, f32[256,128]{1,0:T(8,128)S(1)}, u32[]{:S(2)}, u32[]{:S(2)}) %collective-permute-start.11) | collective-permute-done | bytes 131104 | tf_op jit(solution)/shard_map/ppermute | solution.py:386
  29.2 0.6 %sigma.1.refs_0_.refs_4_ = f32[64,128]{1,0:T(8,128)S(1)} custom-call(s32[2]{0:T(128)S(1)} %pad_add_fusion.place_ref.level_ref, f32[4,77]{1,0:T(4,128)S(1)} %broadcast_multiply_fusion.1.couple_ref, f32[896,128]{1,0:T(8,128)S(1)} %get-tuple-element.52.refs_0_.refs_1_, f32[32,128]{1,0:T(8,128)S(1)} %get-tuple-element.53.after_ref.refs_1_, ...), custom_call_target="tpu_custom_call" | custom-call | flops 163840 | bytes 2344152 | tf_op jit(solution)/shard_map/sigma/pallas_call | solution.py:359
  29.8 0.0 copy-start.9
  29.8 1.8 %collective-permute-start.17 = (f32[64,128]{1,0:T(8,128)S(1)}, f32[64,128]{1,0:T(8,128)S(1)}, u32[]{:S(2)}, u32[]{:S(2)}) collective-permute-start(f32[64,128]{1,0:T(8,128)S(1)} %sigma.1.refs_0_.refs_4_), channel_id=1, source_target_pairs={{0,3},{1,2},{2,1},{3,0},{4,7},{5,6},{6,5},{7,4},{8,11},{9,10},{10,... | collective-permute-start | bytes 98312 | tf_op jit(solution)/shard_map/ppermute | solution.py:386
  31.6 0.3 collective-permute-start.16
  31.8 0.2 collective-permute-start.15
  32.1 1.6 %second.1 = (f32[224,128]{1,0:T(8,128)S(1)}, f32[224,128]{1,0:T(8,128)S(1)}, f32[224,128]{1,0:T(8,128)S(1)}, f32[224,128]{1,0:T(8,128)S(1)}) custom-call(s32[2]{0:T(128)S(1)} %pad_add_fusion.place_ref.level_ref, f32[64,128]{1,0:T(8,128)S(1)} %sigma.1.refs_0_.refs_4_, f32[896,128]{1,0:T(8,128)S(1)} %get-tuple-element.52.refs_0_.refs_1_, ...), custom_call_target="tpu_custom_call" | custom-call | flops 117440512 | bytes 3801096 | tf_op jit(solution)/shard_map/second/pallas_call | solution.py:359
  33.7 0.4 collective-permute-start.12
  34.1 1.2 %collective-permute-start.13 = (f32[224,128]{1,0:T(8,128)S(1)}, f32[224,128]{1,0:T(8,128)S(1)}, u32[]{:S(2)}, u32[]{:S(2)}) collective-permute-start(f32[224,128]{1,0:T(8,128)S(1)} %get-tuple-element.64), channel_id=1, source_target_pairs={{0,2},{1,3},{2,0},{3,1},{4,6},{5,7},{6,4},{7,5},{8,10},{9,11},{10,... | collective-permute-start | bytes 344072 | tf_op jit(solution)/shard_map/ppermute | solution.py:386
  35.3 0.6 %collective-permute-start.14 = (f32[224,128]{1,0:T(8,128)S(1)}, f32[224,128]{1,0:T(8,128)S(1)}, u32[]{:S(2)}, u32[]{:S(2)}) collective-permute-start(f32[224,128]{1,0:T(8,128)S(1)} %get-tuple-element.65), channel_id=1, source_target_pairs={{0,3},{1,2},{2,1},{3,0},{4,7},{5,6},{6,5},{7,4},{8,11},{9,10},{10,... | collective-permute-start | bytes 344072 | tf_op jit(solution)/shard_map/ppermute | solution.py:386
  35.9 4.3 %correct.1.refs_4_ = f32[1920,128]{1,0:T(8,128)} custom-call(s32[2]{0:T(128)S(1)} %pad_add_fusion.place_ref.level_ref, f32[256,128]{1,0:T(8,128)S(1)} %get-tuple-element.66.refs_0_, f32[256,128]{1,0:T(8,128)S(1)} %collective-permute-done.9.refs_11_.refs_1_, f32[256,128]{1,0:T(8,128)S(1)} %collective-permute-done.10.refs_12_.refs_2_, ...), custom_call_target="tpu_custom_call" | custom-call | flops 5368709120 | bytes 6635528 | tf_op jit(solution)/shard_map/correct/pallas_call | solution.py:359
  40.2 1.2 %collective-permute-done.14.refs_3_ = f32[224,128]{1,0:T(8,128)S(1)} collective-permute-done((f32[224,128]{1,0:T(8,128)S(1)}, f32[224,128]{1,0:T(8,128)S(1)}, u32[]{:S(2)}, u32[]{:S(2)}) %collective-permute-start.14) | collective-permute-done | bytes 114720 | tf_op jit(solution)/shard_map/ppermute | solution.py:386
  41.4 1.3 %unpack.1 = f32[1920,128]{1,0:T(8,128)} custom-call(s32[2]{0:T(128)S(1)} %pad_add_fusion.place_ref.level_ref, f32[224,128]{1,0:T(8,128)S(1)} %get-tuple-element.62.refs_0_, f32[224,128]{1,0:T(8,128)S(1)} %collective-permute-done.12.refs_1_, f32[224,128]{1,0:T(8,128)S(1)} %collective-permute-done.13.refs_2_, ...), custom_call_target="tpu_custom_call", output_to_operand_aliasing={{}: (5, {})} | custom-call | bytes 2424840 | tf_op jit(solution)/shard_map/unpack/pallas_call | solution.py:359
  (30 shorter events, 0.1 us)
Async XLA Ops:
  0.1 1.2 %copy-start = (f32[60,4,1024]{2,1,0:T(4,128)S(1)}, f32[60,4,1024]{2,1,0:T(4,128)}, u32[]{:S(2)}) copy-start(f32[60,4,1024]{2,1,0:T(4,128)} %param.13) | copy-start | bytes 2949124
  1.9 6.1 %collective-permute-start.3 = (f32[128,128]{1,0:T(8,128)S(1)}, f32[128,128]{1,0:T(8,128)S(1)}, u32[]{:S(2)}, u32[]{:S(2)}) collective-permute-start(f32[128,128]{1,0:T(8,128)S(1)} %get-tuple-element.44), channel_id=1, source_target_pairs={{0,2},{1,3},{2,0},{3,1},{4,6},{5,7},{6,4},{7,5},{8,10},{9,11},{10,... | collective-permute-start | bytes 196616 | tf_op jit(solution)/shard_map/ppermute | solution.py:386
  3.1 4.8 %collective-permute-start.4 = (f32[128,128]{1,0:T(8,128)S(1)}, f32[128,128]{1,0:T(8,128)S(1)}, u32[]{:S(2)}, u32[]{:S(2)}) collective-permute-start(f32[128,128]{1,0:T(8,128)S(1)} %get-tuple-element.45), channel_id=1, source_target_pairs={{0,3},{1,2},{2,1},{3,0},{4,7},{5,6},{6,5},{7,4},{8,11},{9,10},{10,... | collective-permute-start | bytes 196616 | tf_op jit(solution)/shard_map/ppermute | solution.py:386
  4.2 2.6 %copy-start.10 = (f32[479]{0:T(512)S(1)}, f32[479]{0:T(512)}, u32[]{:S(2)}) copy-start(f32[479]{0:T(512)} %param.15) | copy-start | bytes 5752
  4.2 2.7 %copy-start.12 = (f32[4]{0:T(128)S(1)}, f32[4]{0:T(128)}, u32[]{:S(2)}) copy-start(f32[4]{0:T(128)} %param.16) | copy-start | bytes 52
  4.2 2.8 %copy-start.11 = (f32[480]{0:T(512)S(1)}, f32[480]{0:T(512)}, u32[]{:S(2)}) copy-start(f32[480]{0:T(512)} %param.14) | copy-start | bytes 5764
  4.2 2.9 %copy-start.8 = (f32[32,128]{1,0:T(8,128)S(1)}, f32[32,128]{1,0:T(8,128)}, u32[]{:S(2)}) copy-start(f32[32,128]{1,0:T(8,128)} %constant.63.eigen_ref) | copy-start | bytes 49156
  4.2 3.8 %copy-start.2 = (bf16[512,256]{1,0:T(8,128)(2,1)S(1)}, bf16[512,256]{1,0:T(8,128)(2,1)}, u32[]{:S(2)}) copy-start(bf16[512,256]{1,0:T(8,128)(2,1)} %constant.52.clone.refs_6_) | copy-start | bytes 786436
  4.3 3.8 %copy-start.3 = (bf16[512,256]{1,0:T(8,128)(2,1)S(1)}, bf16[512,256]{1,0:T(8,128)(2,1)}, u32[]{:S(2)}) copy-start(bf16[512,256]{1,0:T(8,128)(2,1)} %constant.50.clone.refs_4_) | copy-start | bytes 786436
  4.9 3.1 %copy-start.1 = (bf16[512,256]{1,0:T(8,128)(2,1)S(1)}, bf16[512,256]{1,0:T(8,128)(2,1)}, u32[]{:S(2)}) copy-start(bf16[512,256]{1,0:T(8,128)(2,1)} %constant.54.clone.refs_7_) | copy-start | bytes 786436
  4.9 9.1 %collective-permute-start.1 = (f32[352,128]{1,0:T(8,128)S(1)}, f32[352,128]{1,0:T(8,128)S(1)}, u32[]{:S(2)}, u32[]{:S(2)}) collective-permute-start(f32[352,128]{1,0:T(8,128)S(1)} %get-tuple-element.42), channel_id=1, source_target_pairs={{0,2},{1,3},{2,0},{3,1},{4,6},{5,7},{6,4},{7,5},{8,10},{9,11},{10,... | collective-permute-start | bytes 540680 | tf_op jit(solution)/shard_map/ppermute | solution.py:386
  6.2 9.2 %collective-permute-start.2 = (f32[352,128]{1,0:T(8,128)S(1)}, f32[352,128]{1,0:T(8,128)S(1)}, u32[]{:S(2)}, u32[]{:S(2)}) collective-permute-start(f32[352,128]{1,0:T(8,128)S(1)} %get-tuple-element.43), channel_id=1, source_target_pairs={{0,3},{1,2},{2,1},{3,0},{4,7},{5,6},{6,5},{7,4},{8,11},{9,10},{10,... | collective-permute-start | bytes 540680 | tf_op jit(solution)/shard_map/ppermute | solution.py:386
  6.5 1.5 %collective-permute-start = (f32[480,128]{1,0:T(8,128)S(1)}, f32[480,128]{1,0:T(8,128)S(1)}, u32[]{:S(2)}, u32[]{:S(2)}) collective-permute-start(f32[480,128]{1,0:T(8,128)S(1)} %get-tuple-element.41), channel_id=1, source_target_pairs={{0,1},{1,0},{2,3},{3,2},{4,5},{5,4},{6,7},{7,6},{8,9},{9,8},{10,11... | collective-permute-start | bytes 737288 | tf_op jit(solution)/shard_map/ppermute | solution.py:386
  7.2 0.9 %copy-start.7 = (f32[32,128]{1,0:T(8,128)S(1)}, f32[32,128]{1,0:T(8,128)}, u32[]{:S(2)}) copy-start(f32[32,128]{1,0:T(8,128)} %constant.56.clone.refs_5_.refs_6_.refs_15_) | copy-start | bytes 49156
  7.9 8.1 %copy-start.4 = (bf16[512,256]{1,0:T(8,128)(2,1)S(1)}, bf16[512,256]{1,0:T(8,128)(2,1)}, u32[]{:S(2)}) copy-start(bf16[512,256]{1,0:T(8,128)(2,1)} %constant.55.clone.refs_10_.refs_8_.refs_17_) | copy-start | bytes 786436
  7.9 8.1 %copy-start.5 = (bf16[512,256]{1,0:T(8,128)(2,1)S(1)}, bf16[512,256]{1,0:T(8,128)(2,1)}, u32[]{:S(2)}) copy-start(bf16[512,256]{1,0:T(8,128)(2,1)} %constant.53.clone.refs_9_.refs_7_.refs_16_) | copy-start | bytes 786436
  7.9 8.1 %copy-start.6 = (bf16[512,256]{1,0:T(8,128)(2,1)S(1)}, bf16[512,256]{1,0:T(8,128)(2,1)}, u32[]{:S(2)}) copy-start(bf16[512,256]{1,0:T(8,128)(2,1)} %constant.51.clone.refs_8_.refs_5_) | copy-start | bytes 786436
  9.3 6.1 %collective-permute-start.5 = (f32[32,128]{1,0:T(8,128)S(1)}, f32[32,128]{1,0:T(8,128)S(1)}, u32[]{:S(2)}, u32[]{:S(2)}) collective-permute-start(f32[32,128]{1,0:T(8,128)S(1)} %get-tuple-element.47), channel_id=1, source_target_pairs={{0,4},{4,0},{8,12},{12,8},{16,20},{20,16},{24,28},{28,24},{1,5},{5... | collective-permute-start | bytes 49160 | tf_op jit(solution)/shard_map/ppermute | solution.py:382
  10.6 5.4 %collective-permute-start.6 = (f32[32,128]{1,0:T(8,128)S(1)}, f32[32,128]{1,0:T(8,128)S(1)}, u32[]{:S(2)}, u32[]{:S(2)}) collective-permute-start(f32[32,128]{1,0:T(8,128)S(1)} %get-tuple-element.48), channel_id=1, source_target_pairs={{4,8},{8,4},{12,16},{16,12},{20,24},{24,20},{5,9},{9,5},{13,17},{1... | collective-permute-start | bytes 49160 | tf_op jit(solution)/shard_map/ppermute | solution.py:381
  19.0 9.2 %collective-permute-start.9 = (f32[256,128]{1,0:T(8,128)S(1)}, f32[256,128]{1,0:T(8,128)S(1)}, u32[]{:S(2)}, u32[]{:S(2)}) collective-permute-start(f32[256,128]{1,0:T(8,128)S(1)} %get-tuple-element.58), channel_id=1, source_target_pairs={{0,1},{1,0},{2,3},{3,2},{4,5},{5,4},{6,7},{7,6},{8,9},{9,8},{10,11... | collective-permute-start | bytes 393224 | tf_op jit(solution)/shard_map/ppermute | solution.py:386
  20.9 7.3 %collective-permute-start.10 = (f32[256,128]{1,0:T(8,128)S(1)}, f32[256,128]{1,0:T(8,128)S(1)}, u32[]{:S(2)}, u32[]{:S(2)}) collective-permute-start(f32[256,128]{1,0:T(8,128)S(1)} %get-tuple-element.59), channel_id=1, source_target_pairs={{0,2},{1,3},{2,0},{3,1},{4,6},{5,7},{6,4},{7,5},{8,10},{9,11},{10,... | collective-permute-start | bytes 393224 | tf_op jit(solution)/shard_map/ppermute | solution.py:386
  22.1 7.1 %collective-permute-start.11 = (f32[256,128]{1,0:T(8,128)S(1)}, f32[256,128]{1,0:T(8,128)S(1)}, u32[]{:S(2)}, u32[]{:S(2)}) collective-permute-start(f32[256,128]{1,0:T(8,128)S(1)} %get-tuple-element.60), channel_id=1, source_target_pairs={{0,3},{1,2},{2,1},{3,0},{4,7},{5,6},{6,5},{7,4},{8,11},{9,10},{10,... | collective-permute-start | bytes 393224 | tf_op jit(solution)/shard_map/ppermute | solution.py:386
  22.6 4.9 %collective-permute-start.7 = (f32[32,128]{1,0:T(8,128)S(1)}, f32[32,128]{1,0:T(8,128)S(1)}, u32[]{:S(2)}, u32[]{:S(2)}) collective-permute-start(f32[32,128]{1,0:T(8,128)S(1)} %get-tuple-element.54), channel_id=1, source_target_pairs={{0,4},{4,0},{8,12},{12,8},{16,20},{20,16},{24,28},{28,24},{1,5},{5... | collective-permute-start | bytes 49160 | tf_op jit(solution)/shard_map/ppermute | solution.py:382
  22.8 5.4 %collective-permute-start.8 = (f32[32,128]{1,0:T(8,128)S(1)}, f32[32,128]{1,0:T(8,128)S(1)}, u32[]{:S(2)}, u32[]{:S(2)}) collective-permute-start(f32[32,128]{1,0:T(8,128)S(1)} %get-tuple-element.55), channel_id=1, source_target_pairs={{4,8},{8,4},{12,16},{16,12},{20,24},{24,20},{5,9},{9,5},{13,17},{1... | collective-permute-start | bytes 49160 | tf_op jit(solution)/shard_map/ppermute | solution.py:381
  29.8 6.1 %copy-start.9 = (bf16[512,256]{1,0:T(8,128)(2,1)S(1)}, bf16[512,256]{1,0:T(8,128)(2,1)}, u32[]{:S(2)}) copy-start(bf16[512,256]{1,0:T(8,128)(2,1)} %constant.49.clone.refs_14_) | copy-start | bytes 786436
  29.8 5.4 %collective-permute-start.17 = (f32[64,128]{1,0:T(8,128)S(1)}, f32[64,128]{1,0:T(8,128)S(1)}, u32[]{:S(2)}, u32[]{:S(2)}) collective-permute-start(f32[64,128]{1,0:T(8,128)S(1)} %sigma.1.refs_0_.refs_4_), channel_id=1, source_target_pairs={{0,3},{1,2},{2,1},{3,0},{4,7},{5,6},{6,5},{7,4},{8,11},{9,10},{10,... | collective-permute-start | bytes 98312 | tf_op jit(solution)/shard_map/ppermute | solution.py:386
  31.6 4.3 %collective-permute-start.16 = (f32[64,128]{1,0:T(8,128)S(1)}, f32[64,128]{1,0:T(8,128)S(1)}, u32[]{:S(2)}, u32[]{:S(2)}) collective-permute-start(f32[64,128]{1,0:T(8,128)S(1)} %sigma.1.refs_0_.refs_4_), channel_id=1, source_target_pairs={{0,2},{1,3},{2,0},{3,1},{4,6},{5,7},{6,4},{7,5},{8,10},{9,11},{10,... | collective-permute-start | bytes 98312 | tf_op jit(solution)/shard_map/ppermute | solution.py:386
  31.8 4.1 %collective-permute-start.15 = (f32[64,128]{1,0:T(8,128)S(1)}, f32[64,128]{1,0:T(8,128)S(1)}, u32[]{:S(2)}, u32[]{:S(2)}) collective-permute-start(f32[64,128]{1,0:T(8,128)S(1)} %sigma.1.refs_0_.refs_4_), channel_id=1, source_target_pairs={{0,1},{1,0},{2,3},{3,2},{4,5},{5,4},{6,7},{7,6},{8,9},{9,8},{10,11... | collective-permute-start | bytes 98312 | tf_op jit(solution)/shard_map/ppermute | solution.py:386
  33.7 6.5 %collective-permute-start.12 = (f32[224,128]{1,0:T(8,128)S(1)}, f32[224,128]{1,0:T(8,128)S(1)}, u32[]{:S(2)}, u32[]{:S(2)}) collective-permute-start(f32[224,128]{1,0:T(8,128)S(1)} %get-tuple-element.63), channel_id=1, source_target_pairs={{0,1},{1,0},{2,3},{3,2},{4,5},{5,4},{6,7},{7,6},{8,9},{9,8},{10,11... | collective-permute-start | bytes 344072 | tf_op jit(solution)/shard_map/ppermute | solution.py:386
  34.1 6.1 %collective-permute-start.13 = (f32[224,128]{1,0:T(8,128)S(1)}, f32[224,128]{1,0:T(8,128)S(1)}, u32[]{:S(2)}, u32[]{:S(2)}) collective-permute-start(f32[224,128]{1,0:T(8,128)S(1)} %get-tuple-element.64), channel_id=1, source_target_pairs={{0,2},{1,3},{2,0},{3,1},{4,6},{5,7},{6,4},{7,5},{8,10},{9,11},{10,... | collective-permute-start | bytes 344072 | tf_op jit(solution)/shard_map/ppermute | solution.py:386
  35.3 6.1 %collective-permute-start.14 = (f32[224,128]{1,0:T(8,128)S(1)}, f32[224,128]{1,0:T(8,128)S(1)}, u32[]{:S(2)}, u32[]{:S(2)}) collective-permute-start(f32[224,128]{1,0:T(8,128)S(1)} %get-tuple-element.65), channel_id=1, source_target_pairs={{0,3},{1,2},{2,1},{3,0},{4,7},{5,6},{6,5},{7,4},{8,11},{9,10},{10,... | collective-permute-start | bytes 344072 | tf_op jit(solution)/shard_map/ppermute | solution.py:386

commit v7 on v6

--- a/solution.py
+++ b/solution.py
@@ -15,6 +15,7 @@
 N2 = 128
 GROUPS = 16
 BLOCK = 8
+WEIGHT = 256
 
 VMEM = pltpu.VMEM
 SMEM = pltpu.SMEM
@@ -364,7 +365,7 @@
         input_output_aliases=aliases or {},
         scratch_shapes=scratch,
         compiler_params=pltpu.CompilerParams(vmem_limit_bytes=48 << 20),
-        cost_estimate=pl.CostEstimate(flops=flops, bytes_accessed=nbytes, transcendentals=0),
+        cost_estimate=pl.CostEstimate(flops=WEIGHT * flops, bytes_accessed=WEIGHT * nbytes, transcendentals=0),
         name=name,
     )(*ins)
     return out
@@ -593,9 +594,9 @@
 
 
 def partners_kernel(
-    rows, early, masks, place_ref, lon_ref, couple_ref, eigen_ref, after_ref, phi_ref, psi_ref, token_ref, *refs
+    rows, early, masks, place_ref, lon_ref, couple_ref, eigen_ref, after_ref, phi_ref, psi_ref, *refs
 ):
-    token_ref[...] = after_ref[...]
+    del after_ref
     count = len(masks)
     together(
         *partner_response(
@@ -724,11 +725,10 @@
 
     def inner_body(place_ref, *refs):
         pieces, refs = refs[:levels], refs[levels:]
-        tables_in, back_in, refs = refs[:4], refs[4:7], refs[7:]
-        ends_ref, even_ref, odd_ref, ratio_ref, inverse_ref, edge_ref = refs[:6]
-        late_ref, top_ref, even_out, odd_out = refs[6:10]
-        early_refs, refs = refs[10 : 10 + levels], refs[10 + levels :]
-        full_ref, mid_ref, spec_ref, sum_ref, back_full_ref, back_mid_ref = refs
+        tables_in, refs = refs[:4], refs[4:]
+        ends_ref, odd_ref, even_ref, ratio_ref, inverse_ref, edge_ref = refs[:6]
+        early_ref, late_ref, top_ref, even_out, odd_out = refs[6:11]
+        full_ref, mid_ref, spec_ref, sum_ref = refs[11:]
         for mask, piece in enumerate(pieces):
             at = pl.multiple_of((place_ref[0] ^ mask) * digits, digits)
             skip = span if mask == 1 else 0
@@ -750,42 +750,40 @@
         solve_first(rows, groups, spec_row, low, high, ratio_ref, inverse_ref, edge_ref, sum_ref)
         top = sum_ref[:groups, :]
         top_ref[...] = top
+        early_ref[...] = sum_ref[: early * groups, :]
         late_ref[...] = sum_ref[early * groups :, :]
         swap_out(place_ref[1], sum_ref[(rows - 1) * groups :, :], top, even_out, odd_out)
-        early_sum = sum_ref.at[pl.ds(0, early * groups), :]
-        backward_rows(early_sum, early, back_in[0], tables_in[1], back_in[1], back_in[2], back_mid_ref, back_full_ref)
-        spread(place_ref, back_full_ref, early, early_refs)
-
-    late_first, own_top, even2, odd2, *early_pieces = call(
+
+    early_first, late_first, own_top, even2, odd2 = call(
         inner_body,
-        [(late * groups, N2), row, row, row] + [(early * digits, N2)] * levels,
-        [
-            place, *inner_pieces, *forward, backward[0], backward[2], backward[3],
-            end_spectral, even, odd, ratio, inverse, edge,
-        ],
-        [SMEM] + [VMEM] * (levels + 13),
-        [
-            vmem(pad_inner, N1, N2), vmem(pad_inner * N1, N2), vmem(inner * N1, N2), vmem(rows * groups, N2),
-            vmem(pad_early, N1, N2), vmem(pad_early * N1, N2),
-        ],
-        (inner + early) * NLON * 256 * 4,
+        [early_block, (late * groups, N2), row, row, row],
+        [place, *inner_pieces, *forward, end_spectral, odd, even, ratio, inverse, edge],
+        [SMEM] + [VMEM] * (levels + 10),
+        [vmem(pad_inner, N1, N2), vmem(pad_inner * N1, N2), vmem(inner * N1, N2), vmem(rows * groups, N2)],
+        inner * NLON * 256 * 4,
         "inner",
+    )
+
+    def early_body(place_ref, *refs):
+        first_ref, tables_in, out_refs = refs[0], refs[1:5], refs[5 : 5 + levels]
+        mid_ref, full_ref = refs[5 + levels :]
+        backward_rows(first_ref, early, *tables_in, mid_ref, full_ref)
+        spread(place_ref, full_ref, early, out_refs)
+
+    early_pieces = call(
+        early_body,
+        [(early * digits, N2)] * levels,
+        [place, early_first, *backward],
+        [SMEM] + [VMEM] * 5,
+        [vmem(pad_early * N1, N2), vmem(pad_early, N1, N2)],
+        early * NLON * 256 * 4,
+        "early",
     )
     early_pieces = swap_levels(early_pieces)
     even2, odd2 = swap(even2, odd2)
 
-    phi_far, psi_far, token = call(
-        functools.partial(partners_kernel, rows, early, far_masks),
-        [(len(far_masks) * early * groups, N2)] * 2 + [row],
-        [place, lon_all, couple_all, eigen, own_top],
-        [SMEM, SMEM, SMEM, VMEM, VMEM],
-        [vmem(*early_block)] * (2 * len(far_masks)),
-        len(far_masks) * rows * groups * N2 * 20,
-        "partners",
-    )
-
     def sigma_body(place_ref, couple_ref, *refs):
-        first_ref, own_top_ref, even_ref, odd_ref, even2_ref, odd2_ref, top_ref, bottom_ref = refs[:8]
+        first_ref, own_top_ref, odd_ref, even_ref, odd2_ref, even2_ref, top_ref, bottom_ref = refs[:8]
         ratio_ref, edge_ref, around_ref = refs[8:11]
         sigma_ref = refs[-1]
         level = place_ref[0]
@@ -804,19 +802,18 @@
         sigma_body,
         [(2 * groups, N2)],
         [
-            place, couple_all, late_first, own_top, even, odd, even2, odd2, sent_top, sent_bottom, ratio, edge, around,
-            *early_pieces[1:], token,
+            place, couple_all, late_first, own_top, odd, even, odd2, even2, sent_top, sent_bottom, ratio, edge, around,
         ],
-        [SMEM, SMEM] + [VMEM] * 11 + [pl.ANY] * levels,
+        [SMEM, SMEM] + [VMEM] * 11,
         [],
         groups * N2 * 40,
         "sigma",
     )
-    sigma_pieces = swap_levels([sigma] * levels)
+    far_sigma = [send_level(sigma, mask, levels) for mask in far]
     def second_body(place_ref, *refs):
         sigma_ref, first_ref, ratio_ref, inverse_ref, edge_ref = refs[:5]
-        tables_in, refs = refs[5:9], refs[9:]
-        late_refs = refs[:levels]
+        tables_in, refs = refs[5:9], refs[10:]
+        late_refs = list(refs[:levels])
         sum_ref, mid_ref, full_ref = refs[levels:]
         low, high = sigma_ref[:groups, :], sigma_ref[groups:, :]
 
@@ -837,18 +834,30 @@
                 here = slice((j - early) * groups, (j - early + 1) * groups)
                 sum_ref[here, :] = first_ref[here, :] + x_high
         backward_rows(sum_ref, late, *tables_in, mid_ref, full_ref)
+        late_refs[1][late * digits :, :] = sigma_ref[...]
+        late_refs[1] = late_refs[1].at[pl.ds(0, late * digits), :]
         spread(place_ref, full_ref, late, late_refs)
 
     late_pieces = call(
         second_body,
-        [(late * digits, N2)] * levels,
-        [place, sigma, late_first, ratio, inverse, edge, *backward],
-        [SMEM] + [VMEM] * 9,
+        [(late * digits + (2 * groups if mask == 1 else 0), N2) for mask in range(levels)],
+        [place, sigma, late_first, ratio, inverse, edge, *backward, early_pieces[1]],
+        [SMEM] + [VMEM] * 9 + [pl.ANY],
         [vmem(late * groups, N2), vmem(max(pad_late, half) * N1, N2), vmem(pad_late, N1, N2)],
         late * NLON * 256 * 4,
         "second",
     )
+    phi_far, psi_far = call(
+        functools.partial(partners_kernel, rows, early, far_masks),
+        [(len(far_masks) * early * groups, N2)] * 2,
+        [place, lon_all, couple_all, eigen, late_pieces[0]],
+        [SMEM, SMEM, SMEM, VMEM, pl.ANY],
+        [vmem(*early_block)] * (2 * len(far_masks)),
+        len(far_masks) * rows * groups * N2 * 20,
+        "partners",
+    )
     late_pieces = swap_levels(late_pieces)
+    sigma_pieces = [sigma, late_pieces[1], *far_sigma]
     total = rows * levels * digits
     early_total = early * levels * digits
     part = const["first_back_part"]
@@ -863,7 +872,9 @@
         size = early * groups
         for mask in range(levels):
             level = place_ref[0] ^ mask
-            low, high = sigma_refs[mask][:groups, :], sigma_refs[mask][groups:, :]
+            last = sigma_refs[mask].shape[0]
+            low = sigma_refs[mask][last - 2 * groups : last - groups, :]
+            high = sigma_refs[mask][last - groups :, :]
             phi_ref, psi_ref = responses[2 * min(mask, 2) : 2 * min(mask, 2) + 2]
             first = max(mask - 2, 0) * size
             phi_all = phi_ref[first : first + size, :].reshape(early, groups, N2)
@@ -912,7 +923,8 @@
         for chunk in range(chunks):
             for mask in range(levels):
                 first = (place_ref[0] ^ mask) + chunk * lines * levels
-                done_ref[pl.ds(first, lines, stride=levels), :] = pieces[mask][chunk * lines : (chunk + 1) * lines, :]
+                skip = chunk * lines
+                done_ref[pl.ds(first, lines, stride=levels), :] = pieces[mask][skip : skip + lines, :]
             here = pl.ds(chunk * lines * levels, lines * levels)
             there = pl.ds(early_total + chunk * lines * levels, lines * levels)
             copy = pltpu.make_async_copy(done_ref.at[here, :], out_ref.at[there, :], sems.at[chunk])

time: 42.9 us -> 46 us (1.072)
  the two profiles are of different devices: /device:TPU:17 before, /device:TPU:0 now
where the time goes in v7:
time: 46 us; the launch traced here: 45.8 us
  starting transfers between devices  21.1 us (46%)
  Pallas kernels  18.9 us (41%)
  local copies, waits for them, and re-layouts  2.94 us (6%)
  waiting for transfers between devices  2.41 us (5%)
    pallas_call x12, Pallas kernels, call(): pl.pallas_call(body, out_shape=[jax.ShapeDtypeStruct(s, jnp.float32) for...  18.9 us
    ppermute x13, starting transfers between devices, send_level(): return lax.ppermute(piece, 'lon', [(d, d ^ mask) for d in range(size)])  10.7 us
    ppermute x2, starting transfers between devices, swap(): return (lax.ppermute(value_even, 'lat', even), value_odd)  9.1 us
    unnamed x30, local copies, waits for them, and re-layouts  2.78 us
    ppermute x13, waiting for transfers between devices, send_level(): return lax.ppermute(piece, 'lon', [(d, d ^ mask) for d in range(size)])  1.82 us
    ppermute x2, starting transfers between devices, swap(): value_odd = lax.ppermute(value_odd, 'lat', odd)  1.32 us
  transfers between devices with their start and end apart: 17, of which 4 were waited for; matrix products, arithmetic and copies ran while one was open for 1% of the time, Pallas kernels for 28%

profile of v7, /device:TPU:0, one launch (start us, length us, event | category | flops | bytes accessed | tf_op | source)
XLA Modules:
  0.0 45.8 jit_solution(12315177786481161727)
XLA Ops:
  0.0 0.1 pad_add_fusion.place_ref.level_ref
  0.1 1.2 %copy-done = f32[60,4,1024]{2,1,0:T(4,128)S(1)} copy-done((f32[60,4,1024]{2,1,0:T(4,128)S(1)}, f32[60,4,1024]{2,1,0:T(4,128)}, u32[]{:S(2)}) %copy-start) | copy-done | bytes 983064
  1.3 0.6 %pack_ends.1 = (f32[128,128]{1,0:T(8,128)S(1)}, f32[128,128]{1,0:T(8,128)S(1)}, f32[128,128]{1,0:T(8,128)S(1)}) custom-call(s32[2]{0:T(128)S(1)} %pad_add_fusion.place_ref.level_ref, f32[1920,128]{1,0:T(8,128)S(1)} %bitcast.12), custom_call_target="tpu_custom_call" | custom-call | bytes 301991936 | tf_op jit(solution)/shard_map/pack_ends/pallas_call | solution.py:360
  1.9 3.0 %collective-permute-start.3 = (f32[128,128]{1,0:T(8,128)S(1)}, f32[128,128]{1,0:T(8,128)S(1)}, u32[]{:S(2)}, u32[]{:S(2)}) collective-permute-start(f32[128,128]{1,0:T(8,128)S(1)} %get-tuple-element.44), channel_id=1, source_target_pairs={{0,2},{1,3},{2,0},{3,1},{4,6},{5,7},{6,4},{7,5},{8,10},{9,11},{10,... | collective-permute-start | bytes 196616 | tf_op jit(solution)/shard_map/ppermute | solution.py:387
  4.9 0.0 collective-permute-start.4
  4.9 0.6 %pack.1 = (f32[352,128]{1,0:T(8,128)S(1)}, f32[480,128]{1,0:T(8,128)S(1)}, f32[352,128]{1,0:T(8,128)S(1)}, f32[352,128]{1,0:T(8,128)S(1)}) custom-call(s32[2]{0:T(128)S(1)} %pad_add_fusion.place_ref.level_ref, f32[1920,128]{1,0:T(8,128)S(1)} %bitcast.13, f32[128,128]{1,0:T(8,128)S(1)} %get-tuple-element.39.after_ref.refs_0_), custom_call_target="tpu_custom_call" | custom-call | bytes 469764096 | tf_op jit(solution)/shard_map/pack/pallas_call | solution.py:360
  5.5 0.0 copy-start.11
  5.5 1.2 %collective-permute-start.1 = (f32[352,128]{1,0:T(8,128)S(1)}, f32[352,128]{1,0:T(8,128)S(1)}, u32[]{:S(2)}, u32[]{:S(2)}) collective-permute-start(f32[352,128]{1,0:T(8,128)S(1)} %get-tuple-element.42), channel_id=1, source_target_pairs={{0,2},{1,3},{2,0},{3,1},{4,6},{5,7},{6,4},{7,5},{8,10},{9,11},{10,... | collective-permute-start | bytes 540680 | tf_op jit(solution)/shard_map/ppermute | solution.py:387
  6.8 0.6 %collective-permute-start.2 = (f32[352,128]{1,0:T(8,128)S(1)}, f32[352,128]{1,0:T(8,128)S(1)}, u32[]{:S(2)}, u32[]{:S(2)}) collective-permute-start(f32[352,128]{1,0:T(8,128)S(1)} %get-tuple-element.43), channel_id=1, source_target_pairs={{0,3},{1,2},{2,1},{3,0},{4,7},{5,6},{6,5},{7,4},{8,11},{9,10},{10,... | collective-permute-start | bytes 540680 | tf_op jit(solution)/shard_map/ppermute | solution.py:387
  7.4 0.3 collective-permute-start
  7.7 0.1 pad_dynamic-slice_fusion.1
  7.8 0.6 %copy-done.13 = f32[480]{0:T(512)S(1)} copy-done((f32[480]{0:T(512)S(1)}, f32[480]{0:T(512)}, u32[]{:S(2)}) %copy-start.13) | copy-done | bytes 1944
  8.4 0.1 pad_dynamic-slice_fusion
  8.5 0.6 %copy-done.14 = f32[4]{0:T(128)S(1)} copy-done((f32[4]{0:T(128)S(1)}, f32[4]{0:T(128)}, u32[]{:S(2)}) %copy-start.14) | copy-done | bytes 40
  9.1 0.1 broadcast_multiply_fusion.1.couple_ref
  9.1 0.1 broadcast_multiply_fusion.lon_ref
  9.2 0.0 copy-start.10
  9.2 0.7 %edge.1.refs_8_.refs_10_ = f32[512,128]{1,0:T(8,128)S(1)} custom-call(s32[2]{0:T(128)S(1)} %pad_add_fusion.place_ref.level_ref, f32[4,76]{1,0:T(4,128)S(1)} %broadcast_multiply_fusion.lon_ref, f32[4,77]{1,0:T(4,128)S(1)} %broadcast_multiply_fusion.1.couple_ref, f32[32,128]{1,0:T(8,128)S(1)} %copy-done.11), custom_call_target="tpu_custom_call" | custom-call | flops 335544320 | bytes 71931904 | tf_op jit(solution)/shard_map/edge/pallas_call | solution.py:360
  10.0 0.0 collective-permute-done.4.refs_3_
  10.0 0.0 collective-permute-done.refs_1_
  10.0 0.2 copy-done.7
  10.2 0.1 copy-done.8
  10.3 0.1 copy-done.9
  10.3 1.2 %ends.1 = (f32[512,128]{1,0:T(8,128)S(1)}, f32[32,128]{1,0:T(8,128)S(1)}, f32[32,128]{1,0:T(8,128)S(1)}, f32[32,128]{1,0:T(8,128)S(1)}, f32[32,128]{1,0:T(8,128)S(1)}) custom-call(s32[2]{0:T(128)S(1)} %pad_add_fusion.place_ref.level_ref, f32[128,128]{1,0:T(8,128)S(1)} %get-tuple-element.39.after_ref.refs_0_, f32[480,128]{1,0:T(8,128)S(1)} %collective-permute-done.refs_1_, ...), custom_call_target="tpu_custom_call" | custom-call | flops 17179869184 | bytes 469764096 | tf_op jit(solution)/shard_map/ends/pallas_call | solution.py:360
  11.6 0.7 %collective-permute-start.5 = (f32[32,128]{1,0:T(8,128)S(1)}, f32[32,128]{1,0:T(8,128)S(1)}, u32[]{:S(2)}, u32[]{:S(2)}) collective-permute-start(f32[32,128]{1,0:T(8,128)S(1)} %get-tuple-element.47), channel_id=1, source_target_pairs={{4,8},{8,4},{12,16},{16,12},{20,24},{24,20},{5,9},{9,5},{13,17},{1... | collective-permute-start | bytes 49160 | tf_op jit(solution)/shard_map/ppermute | solution.py:382
  12.2 4.4 %collective-permute-start.6 = (f32[32,128]{1,0:T(8,128)S(1)}, f32[32,128]{1,0:T(8,128)S(1)}, u32[]{:S(2)}, u32[]{:S(2)}) collective-permute-start(f32[32,128]{1,0:T(8,128)S(1)} %get-tuple-element.48), channel_id=1, source_target_pairs={{0,4},{4,0},{8,12},{12,8},{16,20},{20,16},{24,28},{28,24},{1,5},{5... | collective-permute-start | bytes 49160 | tf_op jit(solution)/shard_map/ppermute | solution.py:383
  16.6 1.5 %own.1 = (f32[1920,128]{1,0:T(8,128)S(1)}, f32[1920,128]{1,0:T(8,128)S(1)}, f32[160,128]{1,0:T(8,128)S(1)}, f32[1024,128]{1,0:T(8,128)S(1)}, f32[1024,128]{1,0:T...) custom-call(s32[2]{0:T(128)S(1)} %pad_add_fusion.place_ref.level_ref, ...), custom_call_target="tpu_custom_call" | custom-call | flops 2516582400 | bytes 1065981952 | tf_op jit(solution)/shard_map/own/pallas_call | solution.py:360
  18.1 0.0 collective-permute-done.1.refs_2_
  18.1 0.0 collective-permute-done.2.refs_3_
  18.1 0.2 collective-permute-done.6.refs_10_.refs_3_
  18.3 2.1 %inner.1 = (f32[1024,128]{1,0:T(8,128)S(1)}, f32[896,128]{1,0:T(8,128)S(1)}, f32[32,128]{1,0:T(8,128)S(1)}, f32[32,128]{1,0:T(8,128)S(1)}, f32[32,128]{1,0:T(8,128)S(1)}) custom-call(s32[2]{0:T(128)S(1)} %pad_add_fusion.place_ref.level_ref, f32[352,128]{1,0:T(8,128)S(1)} %get-tuple-element.40.refs_0_, f32[480,128]{1,0:T(8,128)S(1)} %collective-permute-done.refs_1_, ...), custom_call_target="tpu_custom_call" | custom-call | flops 47244640256 | bytes 1270876160 | tf_op jit(solution)/shard_map/inner/pallas_call | solution.py:360
  20.4 1.6 %early.1 = (f32[256,128]{1,0:T(8,128)S(1)}, f32[256,128]{1,0:T(8,128)S(1)}, f32[256,128]{1,0:T(8,128)S(1)}, f32[256,128]{1,0:T(8,128)S(1)}) custom-call(s32[2]{0:T(128)S(1)} %pad_add_fusion.place_ref.level_ref, f32[1024,128]{1,0:T(8,128)S(1)} %get-tuple-element.58.refs_0_, bf16[512,256]{1,0:T(8,128)(2,1)S(1)} %copy-done.6, f32[32,128]{1,0:T(8,128)S(1)} %copy-done.10, ...), custom_call_target="tpu_custom_call" | custom-call | flops 34359738368 | bytes 473958400 | tf_op jit(solution)/shard_map/early/pallas_call | solution.py:360
  22.1 0.1 collective-permute-start.9
  22.1 0.7 %collective-permute-start.7 = (f32[32,128]{1,0:T(8,128)S(1)}, f32[32,128]{1,0:T(8,128)S(1)}, u32[]{:S(2)}, u32[]{:S(2)}) collective-permute-start(f32[32,128]{1,0:T(8,128)S(1)} %get-tuple-element.54), channel_id=1, source_target_pairs={{4,8},{8,4},{12,16},{16,12},{20,24},{24,20},{5,9},{9,5},{13,17},{1... | collective-permute-start | bytes 49160 | tf_op jit(solution)/shard_map/ppermute | solution.py:382
  22.8 4.7 %collective-permute-start.8 = (f32[32,128]{1,0:T(8,128)S(1)}, f32[32,128]{1,0:T(8,128)S(1)}, u32[]{:S(2)}, u32[]{:S(2)}) collective-permute-start(f32[32,128]{1,0:T(8,128)S(1)} %get-tuple-element.55), channel_id=1, source_target_pairs={{0,4},{4,0},{8,12},{12,8},{16,20},{20,16},{24,28},{28,24},{1,5},{5... | collective-permute-start | bytes 49160 | tf_op jit(solution)/shard_map/ppermute | solution.py:383
  27.5 1.3 %collective-permute-start.13 = (f32[256,128]{1,0:T(8,128)S(1)}, f32[256,128]{1,0:T(8,128)S(1)}, u32[]{:S(2)}, u32[]{:S(2)}) collective-permute-start(f32[256,128]{1,0:T(8,128)S(1)} %get-tuple-element.65), channel_id=1, source_target_pairs={{0,2},{1,3},{2,0},{3,1},{4,6},{5,7},{6,4},{7,5},{8,10},{9,11},{10,... | collective-permute-start | bytes 393224 | tf_op jit(solution)/shard_map/ppermute | solution.py:387
  28.9 0.4 collective-permute-done.8.refs_5_
  29.3 0.6 %sigma.1.refs_0_.refs_4_ = f32[64,128]{1,0:T(8,128)S(1)} custom-call(s32[2]{0:T(128)S(1)} %pad_add_fusion.place_ref.level_ref, f32[4,77]{1,0:T(4,128)S(1)} %broadcast_multiply_fusion.1.couple_ref, f32[896,128]{1,0:T(8,128)S(1)} %get-tuple-element.52.refs_0_.refs_1_, f32[32,128]{1,0:T(8,128)S(1)} %get-tuple-element.53.refs_1_, ...), custom_call_target="tpu_custom_call" | custom-call | flops 41943040 | bytes 495245312 | tf_op jit(solution)/shard_map/sigma/pallas_call | solution.py:360
  29.9 1.5 %collective-permute-start.16 = (f32[64,128]{1,0:T(8,128)S(1)}, f32[64,128]{1,0:T(8,128)S(1)}, u32[]{:S(2)}, u32[]{:S(2)}) collective-permute-start(f32[64,128]{1,0:T(8,128)S(1)} %sigma.1.refs_0_.refs_4_), channel_id=1, source_target_pairs={{0,3},{1,2},{2,1},{3,0},{4,7},{5,6},{6,5},{7,4},{8,11},{9,10},{10,... | collective-permute-start | bytes 98312 | tf_op jit(solution)/shard_map/ppermute | solution.py:387
  31.3 0.7 %collective-permute-start.15 = (f32[64,128]{1,0:T(8,128)S(1)}, f32[64,128]{1,0:T(8,128)S(1)}, u32[]{:S(2)}, u32[]{:S(2)}) collective-permute-start(f32[64,128]{1,0:T(8,128)S(1)} %sigma.1.refs_0_.refs_4_), channel_id=1, source_target_pairs={{0,2},{1,3},{2,0},{3,1},{4,6},{5,7},{6,4},{7,5},{8,10},{9,11},{10,... | collective-permute-start | bytes 98312 | tf_op jit(solution)/shard_map/ppermute | solution.py:387
  32.0 2.3 %second.1 = (f32[224,128]{1,0:T(8,128)S(1)}, f32[288,128]{1,0:T(8,128)S(1)}, f32[224,128]{1,0:T(8,128)}, f32[224,128]{1,0:T(8,128)}) custom-call(s32[2]{0:T(128)S(1)} %pad_add_fusion.place_ref.level_ref, f32[64,128]{1,0:T(8,128)S(1)} %sigma.1.refs_0_.refs_4_, f32[896,128]{1,0:T(8,128)S(1)} %get-tuple-element.52.refs_0_.refs_1_, ...), custom_call_target="tpu_custom_call" | custom-call | flops 30064771072 | bytes 1015023616 | tf_op jit(solution)/shard_map/second/pallas_call | solution.py:360
  34.3 1.6 %partners.1 = (f32[2048,128]{1,0:T(8,128)S(1)}, f32[2048,128]{1,0:T(8,128)S(1)}) custom-call(s32[2]{0:T(128)S(1)} %pad_add_fusion.place_ref.level_ref, f32[4,76]{1,0:T(4,128)S(1)} %broadcast_multiply_fusion.lon_ref, f32[4,77]{1,0:T(4,128)S(1)} %broadcast_multiply_fusion.1.couple_ref, f32[32,128]{1,0:T(8,128)S(1)} %copy-done.11, ...), custom_call_target="tpu_custom_call" | custom-call | flops 2516582400 | bytes 571054080 | tf_op jit(solution)/shard_map/partners/pallas_call | solution.py:360
  36.0 1.4 %collective-permute-start.11 = (f32[224,128]{1,0:T(8,128)}, f32[224,128]{1,0:T(8,128)}, u32[]{:S(2)}, u32[]{:S(2)}) collective-permute-start(f32[224,128]{1,0:T(8,128)} %get-tuple-element.62), channel_id=1, source_target_pairs={{0,2},{1,3},{2,0},{3,1},{4,6},{5,7},{6,4},{7,5},{8,10},{9,11},{10,... | collective-permute-start | bytes 344072 | tf_op jit(solution)/shard_map/ppermute | solution.py:387
  37.4 0.5 %collective-permute-start.12 = (f32[224,128]{1,0:T(8,128)}, f32[224,128]{1,0:T(8,128)}, u32[]{:S(2)}, u32[]{:S(2)}) collective-permute-start(f32[224,128]{1,0:T(8,128)} %get-tuple-element.63), channel_id=1, source_target_pairs={{0,3},{1,2},{2,1},{3,0},{4,7},{5,6},{6,5},{7,4},{8,11},{9,10},{10,... | collective-permute-start | bytes 344072 | tf_op jit(solution)/shard_map/ppermute | solution.py:387
  37.9 4.3 %correct.1.refs_4_ = f32[1920,128]{1,0:T(8,128)} custom-call(s32[2]{0:T(128)S(1)} %pad_add_fusion.place_ref.level_ref, f32[256,128]{1,0:T(8,128)S(1)} %get-tuple-element.64.refs_0_, f32[256,128]{1,0:T(8,128)S(1)} %collective-permute-done.9.refs_9_.refs_1_, f32[256,128]{1,0:T(8,128)S(1)} %collective-permute-done.13.refs_2_, ...), custom_call_target="tpu_custom_call" | custom-call | flops 1374389534720 | bytes 1728055296 | tf_op jit(solution)/shard_map/correct/pallas_call | solution.py:360
  42.2 0.1 collective-permute-done.11.refs_2_
  42.3 1.7 %collective-permute-done.12.refs_3_ = f32[224,128]{1,0:T(8,128)} collective-permute-done((f32[224,128]{1,0:T(8,128)}, f32[224,128]{1,0:T(8,128)}, u32[]{:S(2)}, u32[]{:S(2)}) %collective-permute-start.12) | collective-permute-done | bytes 114720 | tf_op jit(solution)/shard_map/ppermute | solution.py:387
  44.0 1.8 %unpack.1 = f32[1920,128]{1,0:T(8,128)} custom-call(s32[2]{0:T(128)S(1)} %pad_add_fusion.place_ref.level_ref, f32[224,128]{1,0:T(8,128)S(1)} %copy-done.2, f32[288,128]{1,0:T(8,128)S(1)} %collective-permute-done.10.refs_5_.refs_1_, f32[224,128]{1,0:T(8,128)} %collective-permute-done.11.refs_2_, ...), custom_call_target="tpu_custom_call", output_to_operand_aliasing={{}: (5, {})} | custom-call | bytes 629147648 | tf_op jit(solution)/shard_map/unpack/pallas_call | solution.py:360
  (33 shorter events, 0.1 us)
Async XLA Ops:
  0.1 1.2 %copy-start = (f32[60,4,1024]{2,1,0:T(4,128)S(1)}, f32[60,4,1024]{2,1,0:T(4,128)}, u32[]{:S(2)}) copy-start(f32[60,4,1024]{2,1,0:T(4,128)} %param.13) | copy-start | bytes 2949124
  1.9 8.1 %collective-permute-start.3 = (f32[128,128]{1,0:T(8,128)S(1)}, f32[128,128]{1,0:T(8,128)S(1)}, u32[]{:S(2)}, u32[]{:S(2)}) collective-permute-start(f32[128,128]{1,0:T(8,128)S(1)} %get-tuple-element.44), channel_id=1, source_target_pairs={{0,2},{1,3},{2,0},{3,1},{4,6},{5,7},{6,4},{7,5},{8,10},{9,11},{10,... | collective-permute-start | bytes 196616 | tf_op jit(solution)/shard_map/ppermute | solution.py:387
  4.9 5.1 %collective-permute-start.4 = (f32[128,128]{1,0:T(8,128)S(1)}, f32[128,128]{1,0:T(8,128)S(1)}, u32[]{:S(2)}, u32[]{:S(2)}) collective-permute-start(f32[128,128]{1,0:T(8,128)S(1)} %get-tuple-element.45), channel_id=1, source_target_pairs={{0,3},{1,2},{2,1},{3,0},{4,7},{5,6},{6,5},{7,4},{8,11},{9,10},{10,... | collective-permute-start | bytes 196616 | tf_op jit(solution)/shard_map/ppermute | solution.py:387
  4.9 2.9 %copy-start.12 = (f32[479]{0:T(512)S(1)}, f32[479]{0:T(512)}, u32[]{:S(2)}) copy-start(f32[479]{0:T(512)} %param.15) | copy-start | bytes 5752
  5.5 3.7 %copy-start.11 = (f32[32,128]{1,0:T(8,128)S(1)}, f32[32,128]{1,0:T(8,128)}, u32[]{:S(2)}) copy-start(f32[32,128]{1,0:T(8,128)} %constant.63.eigen_ref) | copy-start | bytes 49156
  5.5 12.6 %collective-permute-start.1 = (f32[352,128]{1,0:T(8,128)S(1)}, f32[352,128]{1,0:T(8,128)S(1)}, u32[]{:S(2)}, u32[]{:S(2)}) collective-permute-start(f32[352,128]{1,0:T(8,128)S(1)} %get-tuple-element.42), channel_id=1, source_target_pairs={{0,2},{1,3},{2,0},{3,1},{4,6},{5,7},{6,4},{7,5},{8,10},{9,11},{10,... | collective-permute-start | bytes 540680 | tf_op jit(solution)/shard_map/ppermute | solution.py:387
  6.8 11.3 %collective-permute-start.2 = (f32[352,128]{1,0:T(8,128)S(1)}, f32[352,128]{1,0:T(8,128)S(1)}, u32[]{:S(2)}, u32[]{:S(2)}) collective-permute-start(f32[352,128]{1,0:T(8,128)S(1)} %get-tuple-element.43), channel_id=1, source_target_pairs={{0,3},{1,2},{2,1},{3,0},{4,7},{5,6},{6,5},{7,4},{8,11},{9,10},{10,... | collective-permute-start | bytes 540680 | tf_op jit(solution)/shard_map/ppermute | solution.py:387
  7.4 2.5 %collective-permute-start = (f32[480,128]{1,0:T(8,128)S(1)}, f32[480,128]{1,0:T(8,128)S(1)}, u32[]{:S(2)}, u32[]{:S(2)}) collective-permute-start(f32[480,128]{1,0:T(8,128)S(1)} %get-tuple-element.41), channel_id=1, source_target_pairs={{0,1},{1,0},{2,3},{3,2},{4,5},{5,4},{6,7},{7,6},{8,9},{9,8},{10,11... | collective-permute-start | bytes 737288 | tf_op jit(solution)/shard_map/ppermute | solution.py:387
  7.7 0.7 %copy-start.13 = (f32[480]{0:T(512)S(1)}, f32[480]{0:T(512)}, u32[]{:S(2)}) copy-start(f32[480]{0:T(512)} %param.14) | copy-start | bytes 5764
  8.4 0.7 %copy-start.14 = (f32[4]{0:T(128)S(1)}, f32[4]{0:T(128)}, u32[]{:S(2)}) copy-start(f32[4]{0:T(128)} %param.16) | copy-start | bytes 52
  9.2 1.0 %copy-start.7 = (bf16[512,256]{1,0:T(8,128)(2,1)S(1)}, bf16[512,256]{1,0:T(8,128)(2,1)}, u32[]{:S(2)}) copy-start(bf16[512,256]{1,0:T(8,128)(2,1)} %constant.54.clone.refs_7_) | copy-start | bytes 786436
  9.2 1.0 %copy-start.8 = (bf16[512,256]{1,0:T(8,128)(2,1)S(1)}, bf16[512,256]{1,0:T(8,128)(2,1)}, u32[]{:S(2)}) copy-start(bf16[512,256]{1,0:T(8,128)(2,1)} %constant.52.clone.refs_6_) | copy-start | bytes 786436
  9.2 1.1 %copy-start.9 = (bf16[512,256]{1,0:T(8,128)(2,1)S(1)}, bf16[512,256]{1,0:T(8,128)(2,1)}, u32[]{:S(2)}) copy-start(bf16[512,256]{1,0:T(8,128)(2,1)} %constant.50.clone.refs_4_) | copy-start | bytes 786436
  9.2 1.1 %copy-start.10 = (f32[32,128]{1,0:T(8,128)S(1)}, f32[32,128]{1,0:T(8,128)}, u32[]{:S(2)}) copy-start(f32[32,128]{1,0:T(8,128)} %constant.56.clone.refs_5_.refs_2_.refs_6_.refs_15_) | copy-start | bytes 49156
  11.6 6.5 %collective-permute-start.5 = (f32[32,128]{1,0:T(8,128)S(1)}, f32[32,128]{1,0:T(8,128)S(1)}, u32[]{:S(2)}, u32[]{:S(2)}) collective-permute-start(f32[32,128]{1,0:T(8,128)S(1)} %get-tuple-element.47), channel_id=1, source_target_pairs={{4,8},{8,4},{12,16},{16,12},{20,24},{24,20},{5,9},{9,5},{13,17},{1... | collective-permute-start | bytes 49160 | tf_op jit(solution)/shard_map/ppermute | solution.py:382
  12.2 6.1 %collective-permute-start.6 = (f32[32,128]{1,0:T(8,128)S(1)}, f32[32,128]{1,0:T(8,128)S(1)}, u32[]{:S(2)}, u32[]{:S(2)}) collective-permute-start(f32[32,128]{1,0:T(8,128)S(1)} %get-tuple-element.48), channel_id=1, source_target_pairs={{0,4},{4,0},{8,12},{12,8},{16,20},{20,16},{24,28},{28,24},{1,5},{5... | collective-permute-start | bytes 49160 | tf_op jit(solution)/shard_map/ppermute | solution.py:383
  18.3 2.1 %copy-start.3 = (bf16[512,256]{1,0:T(8,128)(2,1)S(1)}, bf16[512,256]{1,0:T(8,128)(2,1)}, u32[]{:S(2)}) copy-start(bf16[512,256]{1,0:T(8,128)(2,1)} %constant.55.clone.refs_4_.refs_8_.refs_17_) | copy-start | bytes 786436
  18.3 2.1 %copy-start.4 = (bf16[512,256]{1,0:T(8,128)(2,1)S(1)}, bf16[512,256]{1,0:T(8,128)(2,1)}, u32[]{:S(2)}) copy-start(bf16[512,256]{1,0:T(8,128)(2,1)} %constant.53.clone.refs_3_.refs_7_.refs_16_) | copy-start | bytes 786436
  18.3 2.1 %copy-start.6 = (bf16[512,256]{1,0:T(8,128)(2,1)S(1)}, bf16[512,256]{1,0:T(8,128)(2,1)}, u32[]{:S(2)}) copy-start(bf16[512,256]{1,0:T(8,128)(2,1)} %constant.51.clone.refs_1_.refs_5_) | copy-start | bytes 786436
  22.1 10.0 %collective-permute-start.9 = (f32[256,128]{1,0:T(8,128)S(1)}, f32[256,128]{1,0:T(8,128)S(1)}, u32[]{:S(2)}, u32[]{:S(2)}) collective-permute-start(f32[256,128]{1,0:T(8,128)S(1)} %get-tuple-element.59), channel_id=1, source_target_pairs={{0,1},{1,0},{2,3},{3,2},{4,5},{5,4},{6,7},{7,6},{8,9},{9,8},{10,11... | collective-permute-start | bytes 393224 | tf_op jit(solution)/shard_map/ppermute | solution.py:387
  22.1 6.8 %collective-permute-start.7 = (f32[32,128]{1,0:T(8,128)S(1)}, f32[32,128]{1,0:T(8,128)S(1)}, u32[]{:S(2)}, u32[]{:S(2)}) collective-permute-start(f32[32,128]{1,0:T(8,128)S(1)} %get-tuple-element.54), channel_id=1, source_target_pairs={{4,8},{8,4},{12,16},{16,12},{20,24},{24,20},{5,9},{9,5},{13,17},{1... | collective-permute-start | bytes 49160 | tf_op jit(solution)/shard_map/ppermute | solution.py:382
  22.8 6.5 %collective-permute-start.8 = (f32[32,128]{1,0:T(8,128)S(1)}, f32[32,128]{1,0:T(8,128)S(1)}, u32[]{:S(2)}, u32[]{:S(2)}) collective-permute-start(f32[32,128]{1,0:T(8,128)S(1)} %get-tuple-element.55), channel_id=1, source_target_pairs={{0,4},{4,0},{8,12},{12,8},{16,20},{20,16},{24,28},{28,24},{1,5},{5... | collective-permute-start | bytes 49160 | tf_op jit(solution)/shard_map/ppermute | solution.py:383
  27.5 10.4 %collective-permute-start.13 = (f32[256,128]{1,0:T(8,128)S(1)}, f32[256,128]{1,0:T(8,128)S(1)}, u32[]{:S(2)}, u32[]{:S(2)}) collective-permute-start(f32[256,128]{1,0:T(8,128)S(1)} %get-tuple-element.65), channel_id=1, source_target_pairs={{0,2},{1,3},{2,0},{3,1},{4,6},{5,7},{6,4},{7,5},{8,10},{9,11},{10,... | collective-permute-start | bytes 393224 | tf_op jit(solution)/shard_map/ppermute | solution.py:387
  28.9 9.0 %collective-permute-start.14 = (f32[256,128]{1,0:T(8,128)S(1)}, f32[256,128]{1,0:T(8,128)S(1)}, u32[]{:S(2)}, u32[]{:S(2)}) collective-permute-start(f32[256,128]{1,0:T(8,128)S(1)} %get-tuple-element.66), channel_id=1, source_target_pairs={{0,3},{1,2},{2,1},{3,0},{4,7},{5,6},{6,5},{7,4},{8,11},{9,10},{10,... | collective-permute-start | bytes 393224 | tf_op jit(solution)/shard_map/ppermute | solution.py:387
  29.9 6.1 %collective-permute-start.16 = (f32[64,128]{1,0:T(8,128)S(1)}, f32[64,128]{1,0:T(8,128)S(1)}, u32[]{:S(2)}, u32[]{:S(2)}) collective-permute-start(f32[64,128]{1,0:T(8,128)S(1)} %sigma.1.refs_0_.refs_4_), channel_id=1, source_target_pairs={{0,3},{1,2},{2,1},{3,0},{4,7},{5,6},{6,5},{7,4},{8,11},{9,10},{10,... | collective-permute-start | bytes 98312 | tf_op jit(solution)/shard_map/ppermute | solution.py:387
  31.3 6.1 %collective-permute-start.15 = (f32[64,128]{1,0:T(8,128)S(1)}, f32[64,128]{1,0:T(8,128)S(1)}, u32[]{:S(2)}, u32[]{:S(2)}) collective-permute-start(f32[64,128]{1,0:T(8,128)S(1)} %sigma.1.refs_0_.refs_4_), channel_id=1, source_target_pairs={{0,2},{1,3},{2,0},{3,1},{4,6},{5,7},{6,4},{7,5},{8,10},{9,11},{10,... | collective-permute-start | bytes 98312 | tf_op jit(solution)/shard_map/ppermute | solution.py:387
  34.3 1.6 %copy-start.1 = (f32[224,128]{1,0:T(8,128)}, f32[224,128]{1,0:T(8,128)S(1)}, u32[]{:S(2)}) copy-start(f32[224,128]{1,0:T(8,128)S(1)} %get-tuple-element.60.after_ref.refs_0_) | copy-start | bytes 344068
  34.3 3.6 %collective-permute-start.10 = (f32[288,128]{1,0:T(8,128)S(1)}, f32[288,128]{1,0:T(8,128)S(1)}, u32[]{:S(2)}, u32[]{:S(2)}) collective-permute-start(f32[288,128]{1,0:T(8,128)S(1)} %get-tuple-element.61), channel_id=1, source_target_pairs={{0,1},{1,0},{2,3},{3,2},{4,5},{5,4},{6,7},{7,6},{8,9},{9,8},{10,11... | collective-permute-start | bytes 442376 | tf_op jit(solution)/shard_map/ppermute | solution.py:387
  34.3 3.6 %copy-start.5 = (bf16[512,256]{1,0:T(8,128)(2,1)S(1)}, bf16[512,256]{1,0:T(8,128)(2,1)}, u32[]{:S(2)}) copy-start(bf16[512,256]{1,0:T(8,128)(2,1)} %constant.49.clone.refs_14_) | copy-start | bytes 786436
  36.0 6.3 %collective-permute-start.11 = (f32[224,128]{1,0:T(8,128)}, f32[224,128]{1,0:T(8,128)}, u32[]{:S(2)}, u32[]{:S(2)}) collective-permute-start(f32[224,128]{1,0:T(8,128)} %get-tuple-element.62), channel_id=1, source_target_pairs={{0,2},{1,3},{2,0},{3,1},{4,6},{5,7},{6,4},{7,5},{8,10},{9,11},{10,... | collective-permute-start | bytes 344072 | tf_op jit(solution)/shard_map/ppermute | solution.py:387
  37.4 6.6 %collective-permute-start.12 = (f32[224,128]{1,0:T(8,128)}, f32[224,128]{1,0:T(8,128)}, u32[]{:S(2)}, u32[]{:S(2)}) collective-permute-start(f32[224,128]{1,0:T(8,128)} %get-tuple-element.63), channel_id=1, source_target_pairs={{0,3},{1,2},{2,1},{3,0},{4,7},{5,6},{6,5},{7,4},{8,11},{9,10},{10,... | collective-permute-start | bytes 344072 | tf_op jit(solution)/shard_map/ppermute | solution.py:387
  37.9 6.1 %copy-start.2 = (f32[224,128]{1,0:T(8,128)S(1)}, f32[224,128]{1,0:T(8,128)}, u32[]{:S(2)}) copy-start(f32[224,128]{1,0:T(8,128)} %copy-done.1) | copy-start | bytes 344068

commit v8 on v7

--- a/solution.py
+++ b/solution.py
@@ -355,7 +355,7 @@
     meet(rows, groups, low, high, ratio_ref, inverse_ref, edge_ref, at, lambda i: at(mid_ref, i), put)
 
 
-def call(body, outs, ins, spaces, scratch, flops, name, out_spaces=None, aliases=None):
+def call(body, outs, ins, spaces, scratch, flops, name, out_spaces=None, aliases=None, weight=WEIGHT):
     nbytes = sum(x.size * x.dtype.itemsize for x in ins) + sum(4 * math.prod(s) for s in outs)
     out = pl.pallas_call(
         body,
@@ -365,7 +365,7 @@
         input_output_aliases=aliases or {},
         scratch_shapes=scratch,
         compiler_params=pltpu.CompilerParams(vmem_limit_bytes=48 << 20),
-        cost_estimate=pl.CostEstimate(flops=WEIGHT * flops, bytes_accessed=WEIGHT * nbytes, transcendentals=0),
+        cost_estimate=pl.CostEstimate(flops=weight * flops, bytes_accessed=weight * nbytes, transcendentals=0),
         name=name,
     )(*ins)
     return out
@@ -908,8 +908,9 @@
         [
             vmem(early * groups, N2), vmem(pad_early * N1, N2), vmem(early_total, N2), pltpu.SemaphoreType.DMA,
         ],
-        levels * early * NLON * 256 * 40,
+        levels * early * NLON * 256 * 3,
         "correct",
+        weight=1,
         out_spaces=[pl.ANY],
     )
 

time: 46 us -> 45.6 us (level)
  the two profiles are of different devices: /device:TPU:0 before, /device:TPU:1 now
where the time goes in v8:
time: 45.6 us; the launch traced here: 45.4 us
  starting transfers between devices  21.6 us (47%)
  Pallas kernels  17.7 us (39%)
  local copies, waits for them, and re-layouts  2.94 us (6%)
  waiting for transfers between devices  2.62 us (6%)
    pallas_call x12, Pallas kernels, call(): pl.pallas_call(body, out_shape=[jax.ShapeDtypeStruct(s, jnp.float32) for...  17.7 us
    ppermute x13, starting transfers between devices, send_level(): return lax.ppermute(piece, 'lon', [(d, d ^ mask) for d in range(size)])  12.2 us
    ppermute x2, starting transfers between devices, swap(): return (lax.ppermute(value_even, 'lat', even), value_odd)  8.15 us
    unnamed x26, local copies, waits for them, and re-layouts  2.79 us
    ppermute x13, waiting for transfers between devices, send_level(): return lax.ppermute(piece, 'lon', [(d, d ^ mask) for d in range(size)])  2.61 us
    ppermute x2, starting transfers between devices, swap(): value_odd = lax.ppermute(value_odd, 'lat', odd)  1.31 us
  transfers between devices with their start and end apart: 17, of which 1 were waited for; matrix products, arithmetic and copies ran while one was open for 1% of the time, Pallas kernels for 27%

profile of v8, /device:TPU:1, one launch (start us, length us, event | category | flops | bytes accessed | tf_op | source)
XLA Modules:
  0.0 45.4 jit_solution(12203443025666864944)
XLA Ops:
  0.0 0.1 pad_add_fusion.place_ref.level_ref
  0.1 1.2 %copy-done = f32[60,4,1024]{2,1,0:T(4,128)S(1)} copy-done((f32[60,4,1024]{2,1,0:T(4,128)S(1)}, f32[60,4,1024]{2,1,0:T(4,128)}, u32[]{:S(2)}) %copy-start) | copy-done | bytes 983064
  1.3 0.6 %pack_ends.1 = (f32[128,128]{1,0:T(8,128)S(1)}, f32[128,128]{1,0:T(8,128)S(1)}, f32[128,128]{1,0:T(8,128)S(1)}) custom-call(s32[2]{0:T(128)S(1)} %pad_add_fusion.place_ref.level_ref, f32[1920,128]{1,0:T(8,128)S(1)} %bitcast.12), custom_call_target="tpu_custom_call" | custom-call | bytes 301991936 | tf_op jit(solution)/shard_map/pack_ends/pallas_call | solution.py:360
  1.9 2.1 %collective-permute-start.3 = (f32[128,128]{1,0:T(8,128)S(1)}, f32[128,128]{1,0:T(8,128)S(1)}, u32[]{:S(2)}, u32[]{:S(2)}) collective-permute-start(f32[128,128]{1,0:T(8,128)S(1)} %get-tuple-element.44), channel_id=1, source_target_pairs={{0,2},{1,3},{2,0},{3,1},{4,6},{5,7},{6,4},{7,5},{8,10},{9,11},{10,... | collective-permute-start | bytes 196616 | tf_op jit(solution)/shard_map/ppermute | solution.py:387
  4.0 0.6 %collective-permute-start.4 = (f32[128,128]{1,0:T(8,128)S(1)}, f32[128,128]{1,0:T(8,128)S(1)}, u32[]{:S(2)}, u32[]{:S(2)}) collective-permute-start(f32[128,128]{1,0:T(8,128)S(1)} %get-tuple-element.45), channel_id=1, source_target_pairs={{0,3},{1,2},{2,1},{3,0},{4,7},{5,6},{6,5},{7,4},{8,11},{9,10},{10,... | collective-permute-start | bytes 196616 | tf_op jit(solution)/shard_map/ppermute | solution.py:387
  4.6 0.6 %pack.1 = (f32[352,128]{1,0:T(8,128)S(1)}, f32[480,128]{1,0:T(8,128)S(1)}, f32[352,128]{1,0:T(8,128)S(1)}, f32[352,128]{1,0:T(8,128)S(1)}) custom-call(s32[2]{0:T(128)S(1)} %pad_add_fusion.place_ref.level_ref, f32[1920,128]{1,0:T(8,128)S(1)} %bitcast.13, f32[128,128]{1,0:T(8,128)S(1)} %get-tuple-element.39.after_ref.refs_0_), custom_call_target="tpu_custom_call" | custom-call | bytes 469764096 | tf_op jit(solution)/shard_map/pack/pallas_call | solution.py:360
  5.3 0.0 copy-start.9
  5.3 1.7 %collective-permute-start.1 = (f32[352,128]{1,0:T(8,128)S(1)}, f32[352,128]{1,0:T(8,128)S(1)}, u32[]{:S(2)}, u32[]{:S(2)}) collective-permute-start(f32[352,128]{1,0:T(8,128)S(1)} %get-tuple-element.42), channel_id=1, source_target_pairs={{0,2},{1,3},{2,0},{3,1},{4,6},{5,7},{6,4},{7,5},{8,10},{9,11},{10,... | collective-permute-start | bytes 540680 | tf_op jit(solution)/shard_map/ppermute | solution.py:387
  7.0 0.3 collective-permute-start.2
  7.3 0.2 collective-permute-start
  7.5 0.1 pad_dynamic-slice_fusion.1
  7.6 0.6 %copy-done.11 = f32[480]{0:T(512)S(1)} copy-done((f32[480]{0:T(512)S(1)}, f32[480]{0:T(512)}, u32[]{:S(2)}) %copy-start.11) | copy-done | bytes 1944
  8.2 0.1 pad_dynamic-slice_fusion
  8.2 0.6 %copy-done.12 = f32[4]{0:T(128)S(1)} copy-done((f32[4]{0:T(128)S(1)}, f32[4]{0:T(128)}, u32[]{:S(2)}) %copy-start.12) | copy-done | bytes 40
  8.8 0.1 broadcast_multiply_fusion.1.couple_ref
  8.9 0.1 broadcast_multiply_fusion.lon_ref
  9.0 0.0 copy-start.8
  9.0 0.7 %edge.1.refs_8_.refs_10_ = f32[512,128]{1,0:T(8,128)S(1)} custom-call(s32[2]{0:T(128)S(1)} %pad_add_fusion.place_ref.level_ref, f32[4,76]{1,0:T(4,128)S(1)} %broadcast_multiply_fusion.lon_ref, f32[4,77]{1,0:T(4,128)S(1)} %broadcast_multiply_fusion.1.couple_ref, f32[32,128]{1,0:T(8,128)S(1)} %copy-done.9), custom_call_target="tpu_custom_call" | custom-call | flops 335544320 | bytes 71931904 | tf_op jit(solution)/shard_map/edge/pallas_call | solution.py:360
  9.7 0.0 collective-permute-done.4.refs_3_
  9.7 0.0 collective-permute-done.refs_1_
  9.7 0.2 copy-done.6
  9.9 0.1 copy-done.7
  10.0 0.1 copy-done.8
  10.1 1.2 %ends.1 = (f32[512,128]{1,0:T(8,128)S(1)}, f32[32,128]{1,0:T(8,128)S(1)}, f32[32,128]{1,0:T(8,128)S(1)}, f32[32,128]{1,0:T(8,128)S(1)}, f32[32,128]{1,0:T(8,128)S(1)}) custom-call(s32[2]{0:T(128)S(1)} %pad_add_fusion.place_ref.level_ref, f32[128,128]{1,0:T(8,128)S(1)} %get-tuple-element.39.after_ref.refs_0_, f32[480,128]{1,0:T(8,128)S(1)} %collective-permute-done.refs_1_, ...), custom_call_target="tpu_custom_call" | custom-call | flops 17179869184 | bytes 469764096 | tf_op jit(solution)/shard_map/ends/pallas_call | solution.py:360
  11.3 0.7 %collective-permute-start.5 = (f32[32,128]{1,0:T(8,128)S(1)}, f32[32,128]{1,0:T(8,128)S(1)}, u32[]{:S(2)}, u32[]{:S(2)}) collective-permute-start(f32[32,128]{1,0:T(8,128)S(1)} %get-tuple-element.47), channel_id=1, source_target_pairs={{4,8},{8,4},{12,16},{16,12},{20,24},{24,20},{5,9},{9,5},{13,17},{1... | collective-permute-start | bytes 49160 | tf_op jit(solution)/shard_map/ppermute | solution.py:382
  12.0 4.0 %collective-permute-start.6 = (f32[32,128]{1,0:T(8,128)S(1)}, f32[32,128]{1,0:T(8,128)S(1)}, u32[]{:S(2)}, u32[]{:S(2)}) collective-permute-start(f32[32,128]{1,0:T(8,128)S(1)} %get-tuple-element.48), channel_id=1, source_target_pairs={{0,4},{4,0},{8,12},{12,8},{16,20},{20,16},{24,28},{28,24},{1,5},{5... | collective-permute-start | bytes 49160 | tf_op jit(solution)/shard_map/ppermute | solution.py:383
  15.9 1.5 %own.1 = (f32[1920,128]{1,0:T(8,128)S(1)}, f32[1920,128]{1,0:T(8,128)S(1)}, f32[160,128]{1,0:T(8,128)S(1)}, f32[1024,128]{1,0:T(8,128)S(1)}, f32[1024,128]{1,0:T...) custom-call(s32[2]{0:T(128)S(1)} %pad_add_fusion.place_ref.level_ref, ...), custom_call_target="tpu_custom_call" | custom-call | flops 2516582400 | bytes 1065981952 | tf_op jit(solution)/shard_map/own/pallas_call | solution.py:360
  17.4 0.0 collective-permute-done.2.refs_3_
  17.5 0.0 copy-start.1
  17.5 0.0 copy-start.2
  17.5 0.0 copy-start.5
  17.5 2.1 %inner.1 = (f32[1024,128]{1,0:T(8,128)S(1)}, f32[896,128]{1,0:T(8,128)S(1)}, f32[32,128]{1,0:T(8,128)S(1)}, f32[32,128]{1,0:T(8,128)S(1)}, f32[32,128]{1,0:T(8,128)S(1)}) custom-call(s32[2]{0:T(128)S(1)} %pad_add_fusion.place_ref.level_ref, f32[352,128]{1,0:T(8,128)S(1)} %get-tuple-element.40.refs_0_, f32[480,128]{1,0:T(8,128)S(1)} %collective-permute-done.refs_1_, ...), custom_call_target="tpu_custom_call" | custom-call | flops 47244640256 | bytes 1270876160 | tf_op jit(solution)/shard_map/inner/pallas_call | solution.py:360
  19.6 1.6 %early.1 = (f32[256,128]{1,0:T(8,128)S(1)}, f32[256,128]{1,0:T(8,128)S(1)}, f32[256,128]{1,0:T(8,128)S(1)}, f32[256,128]{1,0:T(8,128)S(1)}) custom-call(s32[2]{0:T(128)S(1)} %pad_add_fusion.place_ref.level_ref, f32[1024,128]{1,0:T(8,128)S(1)} %get-tuple-element.58.refs_0_, bf16[512,256]{1,0:T(8,128)(2,1)S(1)} %copy-done.5, f32[32,128]{1,0:T(8,128)S(1)} %copy-done.4, ...), custom_call_target="tpu_custom_call" | custom-call | flops 34359738368 | bytes 473958400 | tf_op jit(solution)/shard_map/early/pallas_call | solution.py:360
  21.2 0.9 %collective-permute-start.9 = (f32[256,128]{1,0:T(8,128)S(1)}, f32[256,128]{1,0:T(8,128)S(1)}, u32[]{:S(2)}, u32[]{:S(2)}) collective-permute-start(f32[256,128]{1,0:T(8,128)S(1)} %get-tuple-element.59), channel_id=1, source_target_pairs={{0,1},{1,0},{2,3},{3,2},{4,5},{5,4},{6,7},{7,6},{8,9},{9,8},{10,11... | collective-permute-start | bytes 393224 | tf_op jit(solution)/shard_map/ppermute | solution.py:387
  22.2 0.7 %collective-permute-start.7 = (f32[32,128]{1,0:T(8,128)S(1)}, f32[32,128]{1,0:T(8,128)S(1)}, u32[]{:S(2)}, u32[]{:S(2)}) collective-permute-start(f32[32,128]{1,0:T(8,128)S(1)} %get-tuple-element.54), channel_id=1, source_target_pairs={{4,8},{8,4},{12,16},{16,12},{20,24},{24,20},{5,9},{9,5},{13,17},{1... | collective-permute-start | bytes 49160 | tf_op jit(solution)/shard_map/ppermute | solution.py:382
  22.8 4.2 %collective-permute-start.8 = (f32[32,128]{1,0:T(8,128)S(1)}, f32[32,128]{1,0:T(8,128)S(1)}, u32[]{:S(2)}, u32[]{:S(2)}) collective-permute-start(f32[32,128]{1,0:T(8,128)S(1)} %get-tuple-element.55), channel_id=1, source_target_pairs={{0,4},{4,0},{8,12},{12,8},{16,20},{20,16},{24,28},{28,24},{1,5},{5... | collective-permute-start | bytes 49160 | tf_op jit(solution)/shard_map/ppermute | solution.py:383
  27.0 1.0 %collective-permute-start.13 = (f32[256,128]{1,0:T(8,128)S(1)}, f32[256,128]{1,0:T(8,128)S(1)}, u32[]{:S(2)}, u32[]{:S(2)}) collective-permute-start(f32[256,128]{1,0:T(8,128)S(1)} %get-tuple-element.65), channel_id=1, source_target_pairs={{0,2},{1,3},{2,0},{3,1},{4,6},{5,7},{6,4},{7,5},{8,10},{9,11},{10,... | collective-permute-start | bytes 393224 | tf_op jit(solution)/shard_map/ppermute | solution.py:387
  28.1 1.2 %collective-permute-start.14 = (f32[256,128]{1,0:T(8,128)S(1)}, f32[256,128]{1,0:T(8,128)S(1)}, u32[]{:S(2)}, u32[]{:S(2)}) collective-permute-start(f32[256,128]{1,0:T(8,128)S(1)} %get-tuple-element.66), channel_id=1, source_target_pairs={{0,3},{1,2},{2,1},{3,0},{4,7},{5,6},{6,5},{7,4},{8,11},{9,10},{10,... | collective-permute-start | bytes 393224 | tf_op jit(solution)/shard_map/ppermute | solution.py:387
  29.2 0.6 %sigma.1.refs_0_.refs_4_ = f32[64,128]{1,0:T(8,128)S(1)} custom-call(s32[2]{0:T(128)S(1)} %pad_add_fusion.place_ref.level_ref, f32[4,77]{1,0:T(4,128)S(1)} %broadcast_multiply_fusion.1.couple_ref, f32[896,128]{1,0:T(8,128)S(1)} %get-tuple-element.52.refs_0_.refs_1_, f32[32,128]{1,0:T(8,128)S(1)} %get-tuple-element.53.refs_1_, ...), custom_call_target="tpu_custom_call" | custom-call | flops 41943040 | bytes 495245312 | tf_op jit(solution)/shard_map/sigma/pallas_call | solution.py:360
  29.8 1.1 %collective-permute-start.16 = (f32[64,128]{1,0:T(8,128)S(1)}, f32[64,128]{1,0:T(8,128)S(1)}, u32[]{:S(2)}, u32[]{:S(2)}) collective-permute-start(f32[64,128]{1,0:T(8,128)S(1)} %sigma.1.refs_0_.refs_4_), channel_id=1, source_target_pairs={{0,3},{1,2},{2,1},{3,0},{4,7},{5,6},{6,5},{7,4},{8,11},{9,10},{10,... | collective-permute-start | bytes 98312 | tf_op jit(solution)/shard_map/ppermute | solution.py:387
  30.9 0.4 collective-permute-start.15
  31.3 1.6 %second.1 = (f32[224,128]{1,0:T(8,128)S(1)}, f32[288,128]{1,0:T(8,128)S(1)}, f32[224,128]{1,0:T(8,128)S(1)}, f32[224,128]{1,0:T(8,128)S(1)}) custom-call(s32[2]{0:T(128)S(1)} %pad_add_fusion.place_ref.level_ref, f32[64,128]{1,0:T(8,128)S(1)} %sigma.1.refs_0_.refs_4_, f32[896,128]{1,0:T(8,128)S(1)} %get-tuple-element.52.refs_0_.refs_1_, ...), custom_call_target="tpu_custom_call" | custom-call | flops 30064771072 | bytes 1015023616 | tf_op jit(solution)/shard_map/second/pallas_call | solution.py:360
  33.0 1.1 %collective-permute-start.11 = (f32[224,128]{1,0:T(8,128)S(1)}, f32[224,128]{1,0:T(8,128)S(1)}, u32[]{:S(2)}, u32[]{:S(2)}) collective-permute-start(f32[224,128]{1,0:T(8,128)S(1)} %get-tuple-element.62), channel_id=1, source_target_pairs={{0,2},{1,3},{2,0},{3,1},{4,6},{5,7},{6,4},{7,5},{8,10},{9,11},{10,... | collective-permute-start | bytes 344072 | tf_op jit(solution)/shard_map/ppermute | solution.py:387
  34.1 2.6 %collective-permute-done.16.refs_7_ = f32[64,128]{1,0:T(8,128)S(1)} collective-permute-done((f32[64,128]{1,0:T(8,128)S(1)}, f32[64,128]{1,0:T(8,128)S(1)}, u32[]{:S(2)}, u32[]{:S(2)}) %collective-permute-start.16) | collective-permute-done | bytes 32800 | tf_op jit(solution)/shard_map/ppermute | solution.py:387
  36.7 1.4 %collective-permute-start.10 = (f32[288,128]{1,0:T(8,128)S(1)}, f32[288,128]{1,0:T(8,128)S(1)}, u32[]{:S(2)}, u32[]{:S(2)}) collective-permute-start(f32[288,128]{1,0:T(8,128)S(1)} %get-tuple-element.61), channel_id=1, source_target_pairs={{0,1},{1,0},{2,3},{3,2},{4,5},{5,4},{6,7},{7,6},{8,9},{9,8},{10,11... | collective-permute-start | bytes 442376 | tf_op jit(solution)/shard_map/ppermute | solution.py:387
  38.1 1.6 %partners.1 = (f32[2048,128]{1,0:T(8,128)S(1)}, f32[2048,128]{1,0:T(8,128)S(1)}) custom-call(s32[2]{0:T(128)S(1)} %pad_add_fusion.place_ref.level_ref, f32[4,76]{1,0:T(4,128)S(1)} %broadcast_multiply_fusion.lon_ref, f32[4,77]{1,0:T(4,128)S(1)} %broadcast_multiply_fusion.1.couple_ref, f32[32,128]{1,0:T(8,128)S(1)} %copy-done.9, ...), custom_call_target="tpu_custom_call" | custom-call | flops 2516582400 | bytes 571054080 | tf_op jit(solution)/shard_map/partners/pallas_call | solution.py:360
  39.7 4.2 %correct.1.refs_4_ = f32[1920,128]{1,0:T(8,128)} custom-call(s32[2]{0:T(128)S(1)} %pad_add_fusion.place_ref.level_ref, f32[256,128]{1,0:T(8,128)S(1)} %get-tuple-element.64.refs_0_, f32[256,128]{1,0:T(8,128)S(1)} %collective-permute-done.9.refs_9_.refs_1_, f32[256,128]{1,0:T(8,128)S(1)} %collective-permute-done.13.refs_2_, ...), custom_call_target="tpu_custom_call" | custom-call | flops 402653184 | bytes 6750216 | tf_op jit(solution)/shard_map/correct/pallas_call | solution.py:360
  44.0 1.4 %unpack.1 = f32[1920,128]{1,0:T(8,128)} custom-call(s32[2]{0:T(128)S(1)} %pad_add_fusion.place_ref.level_ref, f32[224,128]{1,0:T(8,128)S(1)} %get-tuple-element.60.after_ref.refs_0_, f32[288,128]{1,0:T(8,128)S(1)} %collective-permute-done.10.refs_5_.refs_1_, f32[224,128]{1,0:T(8,128)S(1)} %collective-permute-done.11.refs_2_, ...), custom_call_target="tpu_custom_call", output_to_operand_aliasing={{}: (5, {})} | custom-call | bytes 629147648 | tf_op jit(solution)/shard_map/unpack/pallas_call | solution.py:360
  (29 shorter events, 0.1 us)
Async XLA Ops:
  0.1 1.2 %copy-start = (f32[60,4,1024]{2,1,0:T(4,128)S(1)}, f32[60,4,1024]{2,1,0:T(4,128)}, u32[]{:S(2)}) copy-start(f32[60,4,1024]{2,1,0:T(4,128)} %param.13) | copy-start | bytes 2949124
  1.9 7.8 %collective-permute-start.3 = (f32[128,128]{1,0:T(8,128)S(1)}, f32[128,128]{1,0:T(8,128)S(1)}, u32[]{:S(2)}, u32[]{:S(2)}) collective-permute-start(f32[128,128]{1,0:T(8,128)S(1)} %get-tuple-element.44), channel_id=1, source_target_pairs={{0,2},{1,3},{2,0},{3,1},{4,6},{5,7},{6,4},{7,5},{8,10},{9,11},{10,... | collective-permute-start | bytes 196616 | tf_op jit(solution)/shard_map/ppermute | solution.py:387
  4.0 5.7 %collective-permute-start.4 = (f32[128,128]{1,0:T(8,128)S(1)}, f32[128,128]{1,0:T(8,128)S(1)}, u32[]{:S(2)}, u32[]{:S(2)}) collective-permute-start(f32[128,128]{1,0:T(8,128)S(1)} %get-tuple-element.45), channel_id=1, source_target_pairs={{0,3},{1,2},{2,1},{3,0},{4,7},{5,6},{6,5},{7,4},{8,11},{9,10},{10,... | collective-permute-start | bytes 196616 | tf_op jit(solution)/shard_map/ppermute | solution.py:387
  4.6 2.9 %copy-start.10 = (f32[479]{0:T(512)S(1)}, f32[479]{0:T(512)}, u32[]{:S(2)}) copy-start(f32[479]{0:T(512)} %param.15) | copy-start | bytes 5752
  5.3 3.7 %copy-start.9 = (f32[32,128]{1,0:T(8,128)S(1)}, f32[32,128]{1,0:T(8,128)}, u32[]{:S(2)}) copy-start(f32[32,128]{1,0:T(8,128)} %constant.63.eigen_ref) | copy-start | bytes 49156
  5.3 12.2 %collective-permute-start.1 = (f32[352,128]{1,0:T(8,128)S(1)}, f32[352,128]{1,0:T(8,128)S(1)}, u32[]{:S(2)}, u32[]{:S(2)}) collective-permute-start(f32[352,128]{1,0:T(8,128)S(1)} %get-tuple-element.42), channel_id=1, source_target_pairs={{0,2},{1,3},{2,0},{3,1},{4,6},{5,7},{6,4},{7,5},{8,10},{9,11},{10,... | collective-permute-start | bytes 540680 | tf_op jit(solution)/shard_map/ppermute | solution.py:387
  7.0 10.4 %collective-permute-start.2 = (f32[352,128]{1,0:T(8,128)S(1)}, f32[352,128]{1,0:T(8,128)S(1)}, u32[]{:S(2)}, u32[]{:S(2)}) collective-permute-start(f32[352,128]{1,0:T(8,128)S(1)} %get-tuple-element.43), channel_id=1, source_target_pairs={{0,3},{1,2},{2,1},{3,0},{4,7},{5,6},{6,5},{7,4},{8,11},{9,10},{10,... | collective-permute-start | bytes 540680 | tf_op jit(solution)/shard_map/ppermute | solution.py:387
  7.3 2.4 %collective-permute-start = (f32[480,128]{1,0:T(8,128)S(1)}, f32[480,128]{1,0:T(8,128)S(1)}, u32[]{:S(2)}, u32[]{:S(2)}) collective-permute-start(f32[480,128]{1,0:T(8,128)S(1)} %get-tuple-element.41), channel_id=1, source_target_pairs={{0,1},{1,0},{2,3},{3,2},{4,5},{5,4},{6,7},{7,6},{8,9},{9,8},{10,11... | collective-permute-start | bytes 737288 | tf_op jit(solution)/shard_map/ppermute | solution.py:387
  7.5 0.7 %copy-start.11 = (f32[480]{0:T(512)S(1)}, f32[480]{0:T(512)}, u32[]{:S(2)}) copy-start(f32[480]{0:T(512)} %param.14) | copy-start | bytes 5764
  8.2 0.7 %copy-start.12 = (f32[4]{0:T(128)S(1)}, f32[4]{0:T(128)}, u32[]{:S(2)}) copy-start(f32[4]{0:T(128)} %param.16) | copy-start | bytes 52
  9.0 0.8 %copy-start.4 = (f32[32,128]{1,0:T(8,128)S(1)}, f32[32,128]{1,0:T(8,128)}, u32[]{:S(2)}) copy-start(f32[32,128]{1,0:T(8,128)} %constant.56.clone.refs_5_.refs_2_.refs_6_.refs_15_) | copy-start | bytes 49156
  9.0 1.0 %copy-start.6 = (bf16[512,256]{1,0:T(8,128)(2,1)S(1)}, bf16[512,256]{1,0:T(8,128)(2,1)}, u32[]{:S(2)}) copy-start(bf16[512,256]{1,0:T(8,128)(2,1)} %constant.54.clone.refs_7_) | copy-start | bytes 786436
  9.0 1.0 %copy-start.7 = (bf16[512,256]{1,0:T(8,128)(2,1)S(1)}, bf16[512,256]{1,0:T(8,128)(2,1)}, u32[]{:S(2)}) copy-start(bf16[512,256]{1,0:T(8,128)(2,1)} %constant.52.clone.refs_6_) | copy-start | bytes 786436
  9.0 1.1 %copy-start.8 = (bf16[512,256]{1,0:T(8,128)(2,1)S(1)}, bf16[512,256]{1,0:T(8,128)(2,1)}, u32[]{:S(2)}) copy-start(bf16[512,256]{1,0:T(8,128)(2,1)} %constant.50.clone.refs_4_) | copy-start | bytes 786436
  11.3 6.1 %collective-permute-start.5 = (f32[32,128]{1,0:T(8,128)S(1)}, f32[32,128]{1,0:T(8,128)S(1)}, u32[]{:S(2)}, u32[]{:S(2)}) collective-permute-start(f32[32,128]{1,0:T(8,128)S(1)} %get-tuple-element.47), channel_id=1, source_target_pairs={{4,8},{8,4},{12,16},{16,12},{20,24},{24,20},{5,9},{9,5},{13,17},{1... | collective-permute-start | bytes 49160 | tf_op jit(solution)/shard_map/ppermute | solution.py:382
  12.0 5.5 %collective-permute-start.6 = (f32[32,128]{1,0:T(8,128)S(1)}, f32[32,128]{1,0:T(8,128)S(1)}, u32[]{:S(2)}, u32[]{:S(2)}) collective-permute-start(f32[32,128]{1,0:T(8,128)S(1)} %get-tuple-element.48), channel_id=1, source_target_pairs={{0,4},{4,0},{8,12},{12,8},{16,20},{20,16},{24,28},{28,24},{1,5},{5... | collective-permute-start | bytes 49160 | tf_op jit(solution)/shard_map/ppermute | solution.py:383
  17.5 2.1 %copy-start.1 = (bf16[512,256]{1,0:T(8,128)(2,1)S(1)}, bf16[512,256]{1,0:T(8,128)(2,1)}, u32[]{:S(2)}) copy-start(bf16[512,256]{1,0:T(8,128)(2,1)} %constant.55.clone.refs_4_.refs_8_.refs_17_) | copy-start | bytes 786436
  17.5 2.1 %copy-start.2 = (bf16[512,256]{1,0:T(8,128)(2,1)S(1)}, bf16[512,256]{1,0:T(8,128)(2,1)}, u32[]{:S(2)}) copy-start(bf16[512,256]{1,0:T(8,128)(2,1)} %constant.53.clone.refs_3_.refs_7_.refs_16_) | copy-start | bytes 786436
  17.5 2.1 %copy-start.5 = (bf16[512,256]{1,0:T(8,128)(2,1)S(1)}, bf16[512,256]{1,0:T(8,128)(2,1)}, u32[]{:S(2)}) copy-start(bf16[512,256]{1,0:T(8,128)(2,1)} %constant.51.clone.refs_1_.refs_5_) | copy-start | bytes 786436
  21.2 10.1 %collective-permute-start.9 = (f32[256,128]{1,0:T(8,128)S(1)}, f32[256,128]{1,0:T(8,128)S(1)}, u32[]{:S(2)}, u32[]{:S(2)}) collective-permute-start(f32[256,128]{1,0:T(8,128)S(1)} %get-tuple-element.59), channel_id=1, source_target_pairs={{0,1},{1,0},{2,3},{3,2},{4,5},{5,4},{6,7},{7,6},{8,9},{9,8},{10,11... | collective-permute-start | bytes 393224 | tf_op jit(solution)/shard_map/ppermute | solution.py:387
  22.2 7.1 %collective-permute-start.7 = (f32[32,128]{1,0:T(8,128)S(1)}, f32[32,128]{1,0:T(8,128)S(1)}, u32[]{:S(2)}, u32[]{:S(2)}) collective-permute-start(f32[32,128]{1,0:T(8,128)S(1)} %get-tuple-element.54), channel_id=1, source_target_pairs={{4,8},{8,4},{12,16},{16,12},{20,24},{24,20},{5,9},{9,5},{13,17},{1... | collective-permute-start | bytes 49160 | tf_op jit(solution)/shard_map/ppermute | solution.py:382
  22.8 6.4 %collective-permute-start.8 = (f32[32,128]{1,0:T(8,128)S(1)}, f32[32,128]{1,0:T(8,128)S(1)}, u32[]{:S(2)}, u32[]{:S(2)}) collective-permute-start(f32[32,128]{1,0:T(8,128)S(1)} %get-tuple-element.55), channel_id=1, source_target_pairs={{0,4},{4,0},{8,12},{12,8},{16,20},{20,16},{24,28},{28,24},{1,5},{5... | collective-permute-start | bytes 49160 | tf_op jit(solution)/shard_map/ppermute | solution.py:383
  27.0 12.7 %collective-permute-start.13 = (f32[256,128]{1,0:T(8,128)S(1)}, f32[256,128]{1,0:T(8,128)S(1)}, u32[]{:S(2)}, u32[]{:S(2)}) collective-permute-start(f32[256,128]{1,0:T(8,128)S(1)} %get-tuple-element.65), channel_id=1, source_target_pairs={{0,2},{1,3},{2,0},{3,1},{4,6},{5,7},{6,4},{7,5},{8,10},{9,11},{10,... | collective-permute-start | bytes 393224 | tf_op jit(solution)/shard_map/ppermute | solution.py:387
  28.1 11.7 %collective-permute-start.14 = (f32[256,128]{1,0:T(8,128)S(1)}, f32[256,128]{1,0:T(8,128)S(1)}, u32[]{:S(2)}, u32[]{:S(2)}) collective-permute-start(f32[256,128]{1,0:T(8,128)S(1)} %get-tuple-element.66), channel_id=1, source_target_pairs={{0,3},{1,2},{2,1},{3,0},{4,7},{5,6},{6,5},{7,4},{8,11},{9,10},{10,... | collective-permute-start | bytes 393224 | tf_op jit(solution)/shard_map/ppermute | solution.py:387
  29.8 6.8 %collective-permute-start.16 = (f32[64,128]{1,0:T(8,128)S(1)}, f32[64,128]{1,0:T(8,128)S(1)}, u32[]{:S(2)}, u32[]{:S(2)}) collective-permute-start(f32[64,128]{1,0:T(8,128)S(1)} %sigma.1.refs_0_.refs_4_), channel_id=1, source_target_pairs={{0,3},{1,2},{2,1},{3,0},{4,7},{5,6},{6,5},{7,4},{8,11},{9,10},{10,... | collective-permute-start | bytes 98312 | tf_op jit(solution)/shard_map/ppermute | solution.py:387
  30.9 5.8 %collective-permute-start.15 = (f32[64,128]{1,0:T(8,128)S(1)}, f32[64,128]{1,0:T(8,128)S(1)}, u32[]{:S(2)}, u32[]{:S(2)}) collective-permute-start(f32[64,128]{1,0:T(8,128)S(1)} %sigma.1.refs_0_.refs_4_), channel_id=1, source_target_pairs={{0,2},{1,3},{2,0},{3,1},{4,6},{5,7},{6,4},{7,5},{8,10},{9,11},{10,... | collective-permute-start | bytes 98312 | tf_op jit(solution)/shard_map/ppermute | solution.py:387
  33.0 11.0 %collective-permute-start.11 = (f32[224,128]{1,0:T(8,128)S(1)}, f32[224,128]{1,0:T(8,128)S(1)}, u32[]{:S(2)}, u32[]{:S(2)}) collective-permute-start(f32[224,128]{1,0:T(8,128)S(1)} %get-tuple-element.62), channel_id=1, source_target_pairs={{0,2},{1,3},{2,0},{3,1},{4,6},{5,7},{6,4},{7,5},{8,10},{9,11},{10,... | collective-permute-start | bytes 344072 | tf_op jit(solution)/shard_map/ppermute | solution.py:387
  36.7 7.3 %collective-permute-start.12 = (f32[224,128]{1,0:T(8,128)S(1)}, f32[224,128]{1,0:T(8,128)S(1)}, u32[]{:S(2)}, u32[]{:S(2)}) collective-permute-start(f32[224,128]{1,0:T(8,128)S(1)} %get-tuple-element.63), channel_id=1, source_target_pairs={{0,3},{1,2},{2,1},{3,0},{4,7},{5,6},{6,5},{7,4},{8,11},{9,10},{10,... | collective-permute-start | bytes 344072 | tf_op jit(solution)/shard_map/ppermute | solution.py:387
  36.7 3.1 %collective-permute-start.10 = (f32[288,128]{1,0:T(8,128)S(1)}, f32[288,128]{1,0:T(8,128)S(1)}, u32[]{:S(2)}, u32[]{:S(2)}) collective-permute-start(f32[288,128]{1,0:T(8,128)S(1)} %get-tuple-element.61), channel_id=1, source_target_pairs={{0,1},{1,0},{2,3},{3,2},{4,5},{5,4},{6,7},{7,6},{8,9},{9,8},{10,11... | collective-permute-start | bytes 442376 | tf_op jit(solution)/shard_map/ppermute | solution.py:387
  38.1 1.6 %copy-start.3 = (bf16[512,256]{1,0:T(8,128)(2,1)S(1)}, bf16[512,256]{1,0:T(8,128)(2,1)}, u32[]{:S(2)}) copy-start(bf16[512,256]{1,0:T(8,128)(2,1)} %constant.49.clone.refs_14_) | copy-start | bytes 786436

commit v9 on v6

--- a/solution.py
+++ b/solution.py
@@ -427,13 +427,21 @@
 
 
 def early_rows(rows):
-    return rows // 2 + 2
-
-
-def edge_kernel(rows, level_ref, lon_ref, couple_ref, eigen_ref, out_ref):
+    return rows // 2 + 4
+
+
+def lon_here():
+    return lax.axis_index("lon").astype(jnp.int32)
+
+
+def parity_here():
+    return lax.axis_index("lat").astype(jnp.int32) % 2
+
+
+def edge_kernel(rows, lon_ref, couple_ref, eigen_ref, out_ref):
     eigen = eigen_ref[...]
     groups = eigen.shape[0]
-    level = level_ref[0]
+    level = lon_here()
     low = high = low_inverse = high_inverse = None
     for i in range(OV):
         e, f = rows + i, 2 * OV - 1 - i
@@ -450,7 +458,9 @@
         low_inverse = 1.0 / (couple_ref[level, e + 1] + low)
         high_inverse = 1.0 / (couple_ref[level, f] + high)
     out_ref[(OV - 1) * groups : OV * groups, :] = low_inverse
-    out_ref[(2 * OV - 1) * groups :, :] = high_inverse
+    out_ref[(2 * OV - 1) * groups : 2 * OV * groups, :] = high_inverse
+    out_ref[2 * OV * groups : (2 * OV + 1) * groups, :] = jnp.full_like(eigen, couple_ref[level, OV])
+    out_ref[(2 * OV + 1) * groups :, :] = jnp.full_like(eigen, couple_ref[level, OV + rows])
 
 
 def level_response(rows, early, level, lon_ref, couple_ref, eigen, put_ratio, put_inverse, keep, tables):
@@ -543,7 +553,7 @@
         steps = [step for step in steps if next(step, steps) is not steps]
 
 
-def partner_response(rows, early, place_ref, lon_ref, couple_ref, eigen, masks, phi_ref, psi_ref, kept_refs, value_refs):
+def partner_response(rows, early, lon_ref, couple_ref, eigen, masks, phi_ref, psi_ref, kept_refs, value_refs):
     groups = eigen.shape[0]
 
     def nothing(index, value):
@@ -558,7 +568,7 @@
 
         first = n * early * groups
         return level_response(
-            rows, early, place_ref[0] ^ mask, lon_ref, couple_ref, eigen, put_ratio, nothing, nothing,
+            rows, early, lon_here() ^ mask, lon_ref, couple_ref, eigen, put_ratio, nothing, nothing,
             (
                 getter(kept_refs[n], groups), getter(value_refs[n], groups), putter(value_refs[n], groups),
                 putter(phi_ref, groups, first), putter(psi_ref, groups, first),
@@ -569,13 +579,13 @@
 
 
 def own_kernel(
-    rows, early, masks, place_ref, lon_ref, couple_ref, eigen_ref, ratio_ref, inverse_ref, edge_ref, phi_ref, psi_ref,
+    rows, early, masks, lon_ref, couple_ref, eigen_ref, ratio_ref, inverse_ref, edge_ref, phi_ref, psi_ref,
     phi_near_ref, psi_near_ref, value_ref, *refs,
 ):
     eigen = eigen_ref[...]
     groups = eigen.shape[0]
     own = level_response(
-        rows, early, place_ref[0], lon_ref, couple_ref, eigen, putter(ratio_ref, groups),
+        rows, early, lon_here(), lon_ref, couple_ref, eigen, putter(ratio_ref, groups),
         putter(inverse_ref, groups), putter(edge_ref, groups),
         (
             getter(ratio_ref, groups), getter(value_ref, groups), putter(value_ref, groups),
@@ -586,20 +596,20 @@
     together(
         own,
         *partner_response(
-            rows, early, place_ref, lon_ref, couple_ref, eigen, masks, phi_near_ref, psi_near_ref,
+            rows, early, lon_ref, couple_ref, eigen, masks, phi_near_ref, psi_near_ref,
             refs[:count], refs[count:],
         ),
     )
 
 
 def partners_kernel(
-    rows, early, masks, place_ref, lon_ref, couple_ref, eigen_ref, after_ref, phi_ref, psi_ref, token_ref, *refs
+    rows, early, masks, lon_ref, couple_ref, eigen_ref, after_ref, phi_ref, psi_ref, token_ref, *refs
 ):
     token_ref[...] = after_ref[...]
     count = len(masks)
     together(
         *partner_response(
-            rows, early, place_ref, lon_ref, couple_ref, eigen_ref[...], masks, phi_ref, psi_ref,
+            rows, early, lon_ref, couple_ref, eigen_ref[...], masks, phi_ref, psi_ref,
             refs[:count], refs[count:],
         )
     )
@@ -609,9 +619,6 @@
     rows, levels, lon_count = right_side.shape
     digits = N1 // levels
     groups = 2 * GROUPS
-    lon_at = lax.axis_index("lon").astype(jnp.int32)
-    parity = (lax.axis_index("lat") % 2).astype(jnp.int32)
-    place = jnp.stack([lon_at, parity])
     half = rows // 2
     early = early_rows(rows)
     late = rows - early
@@ -619,9 +626,9 @@
     lon_all, couple_all = operator_parts(rows, lon_coef, lat_coef, level_scale)
     (around,) = call(
         functools.partial(edge_kernel, rows),
-        [(2 * OV * groups, N2)],
-        [place, lon_all, couple_all, eigen],
-        [SMEM, SMEM, SMEM, VMEM],
+        [((2 * OV + 2) * groups, N2)],
+        [lon_all, couple_all, eigen],
+        [SMEM, SMEM, VMEM],
         [],
         16 * groups * N2 * 20,
         "edge",
@@ -633,8 +640,8 @@
     ratio, inverse, edge, phi, psi, phi_near, psi_near = call(
         functools.partial(own_kernel, rows, early, near_masks),
         [block, block, (5 * groups, N2)] + [early_block] * 4,
-        [place, lon_all, couple_all, eigen],
-        [SMEM, SMEM, SMEM, VMEM],
+        [lon_all, couple_all, eigen],
+        [SMEM, SMEM, VMEM],
         [vmem(*early_block)] * 3,
         2 * rows * groups * N2 * 20,
         "own",
@@ -647,34 +654,34 @@
 
     far = list(range(2, levels))
 
-    def pack_ends(place_ref, in_ref, *refs):
+    def pack_ends(in_ref, *refs):
         for end_ref, mask in zip(refs, [0] + far):
-            level = place_ref[0] ^ mask
+            level = lon_here() ^ mask
             end_ref[:span, :] = in_ref[pl.ds(level, span, stride=levels), :]
             end_ref[span:, :] = in_ref[pl.ds(level + levels * (rows - OV) * digits, span, stride=levels), :]
 
     end_packed = call(
         pack_ends,
         [(ends * digits, N2)] * (levels - 1),
-        [place, by_row],
-        [SMEM, VMEM],
+        [by_row],
+        [VMEM],
         [],
         0,
         "pack_ends",
     )
 
-    def pack(place_ref, in_ref, after_ref, *refs):
+    def pack(in_ref, after_ref, *refs):
         del after_ref
         for mask, out_ref in enumerate(refs):
-            level = place_ref[0] ^ mask
+            level = lon_here() ^ mask
             skip = 0 if mask == 1 else levels * span
             out_ref[...] = in_ref[pl.ds(level + skip, out_ref.shape[0], stride=levels), :]
 
     packed = call(
         pack,
         [((rows if mask == 1 else inner) * digits, N2) for mask in range(levels)],
-        [place, by_row, end_packed[0]],
-        [SMEM, VMEM, pl.ANY],
+        [by_row, end_packed[0]],
+        [VMEM, pl.ANY],
         [],
         0,
         "pack",
@@ -686,12 +693,12 @@
     forward = [const["first"], const["turn"], const["second"], const["special"]]
     pad_ends, pad_inner = pad_rows(ends), pad_rows(inner)
 
-    def ends_body(place_ref, *refs):
+    def ends_body(*refs):
         pieces, refs = refs[:levels], refs[levels:]
         tables_in, edge_ref = refs[:4], refs[4]
         spec_ref, top_ref, bottom_ref, even_ref, odd_ref, full_ref, mid_ref = refs[5:]
         for mask, piece in enumerate(pieces):
-            at = pl.multiple_of((place_ref[0] ^ mask) * digits, digits)
+            at = pl.multiple_of((lon_here() ^ mask) * digits, digits)
             last = piece.shape[0] - span
             full_ref[:OV, pl.ds(at, digits), :] = piece[:span, :].reshape(OV, digits, N2)
             full_ref[OV:ends, pl.ds(at, digits), :] = piece[last:, :].reshape(OV, digits, N2)
@@ -702,13 +709,13 @@
         )
         top_ref[...] = top
         bottom_ref[...] = bottom
-        swap_out(place_ref[1], top, bottom, even_ref, odd_ref)
+        swap_out(parity_here(), top, bottom, even_ref, odd_ref)
 
     end_spectral, sent_top, sent_bottom, even, odd = call(
         ends_body,
         [(ends * groups, N2)] + [row] * 4,
-        [place, *end_pieces, *forward, around],
-        [SMEM] + [VMEM] * (levels + 5),
+        [*end_pieces, *forward, around],
+        [VMEM] * (levels + 5),
         [vmem(pad_ends, N1, N2), vmem(pad_ends * N1, N2)],
         ends * NLON * 256 * 4,
         "ends",
@@ -717,12 +724,12 @@
     backward = [const["first_back"], const["turn"], const["second_back"], const["special_back"]]
     pad_early, pad_late = pad_rows(early), pad_rows(late)
 
-    def spread(place_ref, full_ref, count, out_refs):
+    def spread(full_ref, count, out_refs):
         for mask, out_ref in enumerate(out_refs):
-            at = pl.multiple_of((place_ref[0] ^ mask) * digits, digits)
+            at = pl.multiple_of((lon_here() ^ mask) * digits, digits)
             out_ref[...] = full_ref[:count, pl.ds(at, digits), :].reshape(count * digits, N2)
 
-    def inner_body(place_ref, *refs):
+    def inner_body(*refs):
         pieces, refs = refs[:levels], refs[levels:]
         tables_in, back_in, refs = refs[:4], refs[4:7], refs[7:]
         ends_ref, even_ref, odd_ref, ratio_ref, inverse_ref, edge_ref = refs[:6]
@@ -730,7 +737,7 @@
         early_refs, refs = refs[10 : 10 + levels], refs[10 + levels :]
         full_ref, mid_ref, spec_ref, sum_ref, back_full_ref, back_mid_ref = refs
         for mask, piece in enumerate(pieces):
-            at = pl.multiple_of((place_ref[0] ^ mask) * digits, digits)
+            at = pl.multiple_of((lon_here() ^ mask) * digits, digits)
             skip = span if mask == 1 else 0
             full_ref[:inner, pl.ds(at, digits), :] = piece[skip : skip + inner * digits, :].reshape(
                 inner, digits, N2
@@ -738,7 +745,7 @@
         if pad_inner > inner:
             full_ref[inner:] = jnp.zeros((pad_inner - inner, N1, N2), jnp.float32)
         forward_rows(full_ref, inner, *tables_in, mid_ref, spec_ref)
-        low, high = swap_in(place_ref[1], even_ref[...], odd_ref[...])
+        low, high = swap_in(parity_here(), even_ref[...], odd_ref[...])
 
         def spec_row(i):
             if i < OV:
@@ -751,19 +758,19 @@
         top = sum_ref[:groups, :]
         top_ref[...] = top
         late_ref[...] = sum_ref[early * groups :, :]
-        swap_out(place_ref[1], sum_ref[(rows - 1) * groups :, :], top, even_out, odd_out)
+        swap_out(parity_here(), sum_ref[(rows - 1) * groups :, :], top, even_out, odd_out)
         early_sum = sum_ref.at[pl.ds(0, early * groups), :]
         backward_rows(early_sum, early, back_in[0], tables_in[1], back_in[1], back_in[2], back_mid_ref, back_full_ref)
-        spread(place_ref, back_full_ref, early, early_refs)
+        spread(back_full_ref, early, early_refs)
 
     late_first, own_top, even2, odd2, *early_pieces = call(
         inner_body,
         [(late * groups, N2), row, row, row] + [(early * digits, N2)] * levels,
         [
-            place, *inner_pieces, *forward, backward[0], backward[2], backward[3],
+            *inner_pieces, *forward, backward[0], backward[2], backward[3],
             end_spectral, even, odd, ratio, inverse, edge,
         ],
-        [SMEM] + [VMEM] * (levels + 13),
+        [VMEM] * (levels + 13),
         [
             vmem(pad_inner, N1, N2), vmem(pad_inner * N1, N2), vmem(inner * N1, N2), vmem(rows * groups, N2),
             vmem(pad_early, N1, N2), vmem(pad_early * N1, N2),
@@ -777,25 +784,25 @@
     phi_far, psi_far, token = call(
         functools.partial(partners_kernel, rows, early, far_masks),
         [(len(far_masks) * early * groups, N2)] * 2 + [row],
-        [place, lon_all, couple_all, eigen, own_top],
-        [SMEM, SMEM, SMEM, VMEM, VMEM],
+        [lon_all, couple_all, eigen, own_top],
+        [SMEM, SMEM, VMEM, VMEM],
         [vmem(*early_block)] * (2 * len(far_masks)),
         len(far_masks) * rows * groups * N2 * 20,
         "partners",
     )
 
-    def sigma_body(place_ref, couple_ref, *refs):
+    def sigma_body(*refs):
         first_ref, own_top_ref, even_ref, odd_ref, even2_ref, odd2_ref, top_ref, bottom_ref = refs[:8]
         ratio_ref, edge_ref, around_ref = refs[8:11]
         sigma_ref = refs[-1]
-        level = place_ref[0]
-        got_top, got_bottom = swap_in(place_ref[1], even_ref[...], odd_ref[...])
-        from_low, from_high = swap_in(place_ref[1], even2_ref[...], odd2_ref[...])
+        got_top, got_bottom = swap_in(parity_here(), even_ref[...], odd_ref[...])
+        from_low, from_high = swap_in(parity_here(), even2_ref[...], odd2_ref[...])
         low, high = sigmas(
-            couple_ref[level, OV], couple_ref[level, OV + rows], own_top_ref[...], first_ref[(late - 1) * groups :, :],
+            around_ref[2 * OV * groups : (2 * OV + 1) * groups, :], around_ref[(2 * OV + 1) * groups :, :], own_top_ref[...], first_ref[(late - 1) * groups :, :],
             got_top, got_bottom, top_ref[...], bottom_ref[...], from_low, from_high,
             ratio_ref[:groups, :], ratio_ref[(rows - 1) * groups :, :], edge_ref,
-            around_ref[(OV - 1) * groups : OV * groups, :], around_ref[(2 * OV - 1) * groups :, :],
+            around_ref[(OV - 1) * groups : OV * groups, :],
+            around_ref[(2 * OV - 1) * groups : 2 * OV * groups, :],
         )
         sigma_ref[:groups, :] = low
         sigma_ref[groups:, :] = high
@@ -804,16 +811,16 @@
         sigma_body,
         [(2 * groups, N2)],
         [
-            place, couple_all, late_first, own_top, even, odd, even2, odd2, sent_top, sent_bottom, ratio, edge, around,
+            late_first, own_top, even, odd, even2, odd2, sent_top, sent_bottom, ratio, edge, around,
             *early_pieces[1:], token,
         ],
-        [SMEM, SMEM] + [VMEM] * 11 + [pl.ANY] * levels,
+        [VMEM] * 11 + [pl.ANY] * levels,
         [],
         groups * N2 * 40,
         "sigma",
     )
     sigma_pieces = swap_levels([sigma] * levels)
-    def second_body(place_ref, *refs):
+    def second_body(*refs):
         sigma_ref, first_ref, ratio_ref, inverse_ref, edge_ref = refs[:5]
         tables_in, refs = refs[5:9], refs[9:]
         late_refs = refs[:levels]
@@ -837,13 +844,13 @@
                 here = slice((j - early) * groups, (j - early + 1) * groups)
                 sum_ref[here, :] = first_ref[here, :] + x_high
         backward_rows(sum_ref, late, *tables_in, mid_ref, full_ref)
-        spread(place_ref, full_ref, late, late_refs)
+        spread(full_ref, late, late_refs)
 
     late_pieces = call(
         second_body,
         [(late * digits, N2)] * levels,
-        [place, sigma, late_first, ratio, inverse, edge, *backward],
-        [SMEM] + [VMEM] * 9,
+        [sigma, late_first, ratio, inverse, edge, *backward],
+        [VMEM] * 9,
         [vmem(late * groups, N2), vmem(max(pad_late, half) * N1, N2), vmem(pad_late, N1, N2)],
         late * NLON * 256 * 4,
         "second",
@@ -853,23 +860,33 @@
     early_total = early * levels * digits
     part = const["first_back_part"]
 
-    def correct(place_ref, *refs):
+    def correct(*refs):
         pieces, sigma_refs, refs = refs[:levels], refs[levels : 2 * levels], refs[2 * levels :]
         responses, refs = refs[:6], refs[6:]
         part_ref, turn_ref, second_ref, special_ref = refs[:4]
-        out_ref, sum_ref, mid_ref, done_ref, sem = refs[4:]
+        out_ref, done_ref, sems, *mid_refs = refs[4:]
         part_rows = part_ref.shape[0] // levels
-        mine = part_ref.at[pl.ds(pl.multiple_of(place_ref[0] * part_rows, part_rows), part_rows), :]
+        mine = part_ref.at[pl.ds(pl.multiple_of(lon_here() * part_rows, part_rows), part_rows), :]
         size = early * groups
+        copies = []
         for mask in range(levels):
-            level = place_ref[0] ^ mask
+            level = lon_here() ^ mask
+            mid_ref = mid_refs[mask % 2]
             low, high = sigma_refs[mask][:groups, :], sigma_refs[mask][groups:, :]
             phi_ref, psi_ref = responses[2 * min(mask, 2) : 2 * min(mask, 2) + 2]
             first = max(mask - 2, 0) * size
-            phi_all = phi_ref[first : first + size, :].reshape(early, groups, N2)
-            psi_all = psi_ref[first : first + size, :].reshape(early, groups, N2)
-            sum_ref[...] = (phi_all * low[None] + psi_all * high[None]).reshape(size, N2)
-            spectral_back(sum_ref, early, pad_early, second_ref, special_ref, mid_ref)
+            here = pl.ds(first, size)
+            phi_ref, psi_ref = phi_ref.at[here, :], psi_ref.at[here, :]
+            phi_all = phi_ref[...].reshape(early, groups, N2)
+            psi_all = psi_ref[...].reshape(early, groups, N2)
+            value = (phi_all * low[None] + psi_all * high[None]).reshape(size, N2)
+            mid_ref[:size, :] = lanes_apart(product_right(lanes_together(value, early), second_ref), early)
+            if pad_early > early:
+                mid_ref[size:, :] = jnp.zeros((pad_early * groups - size, N2), jnp.float32)
+            zeroth_low = jnp.concatenate([low[:1], low[GROUPS : GROUPS + 1]], axis=1)
+            zeroth_high = jnp.concatenate([high[:1], high[GROUPS : GROUPS + 1]], axis=1)
+            zeroth = load_zeroth(phi_ref, early) * zeroth_low + load_zeroth(psi_ref, early) * zeroth_high
+            store_zeroth(mid_ref, early, product_right(zeroth, special_ref))
             for pair in range(pad_early // (2 * BLOCK)):
                 value = digits_back(mid_ref, pair, turn_ref, mine)
                 for side in range(2):
@@ -882,20 +899,27 @@
                     done_ref[pl.ds(level + begin * digits * levels, lines, stride=levels), :] = (
                         whole + value[:lines, side * N2 : (side + 1) * N2]
                     )
-        copy = pltpu.make_async_copy(done_ref, out_ref.at[pl.ds(0, early_total), :], sem)
-        copy.start()
-        copy.wait()
+                if mask == levels - 1:
+                    begin = 2 * pair * BLOCK * digits * levels
+                    lines = min(2 * BLOCK * digits * levels, early_total - begin)
+                    there = pl.ds(begin, lines)
+                    copy = pltpu.make_async_copy(done_ref.at[there, :], out_ref.at[there, :], sems.at[pair])
+                    copy.start()
+                    copies.append(copy)
+        for copy in copies:
+            copy.wait()
 
     (out,) = call(
         correct,
         [(total, N2)],
         [
-            place, *early_pieces, *sigma_pieces, phi, psi, phi_near, psi_near, phi_far, psi_far,
+            *early_pieces, *sigma_pieces, phi, psi, phi_near, psi_near, phi_far, psi_far,
             part, const["turn"], *backward[2:],
         ],
-        [SMEM] + [VMEM] * (2 * levels + 10),
+        [VMEM] * (2 * levels + 10),
         [
-            vmem(early * groups, N2), vmem(pad_early * N1, N2), vmem(early_total, N2), pltpu.SemaphoreType.DMA,
+            vmem(early_total, N2), pltpu.SemaphoreType.DMA((pad_early // (2 * BLOCK),)),
+            vmem(pad_early * N1, N2), vmem(pad_early * N1, N2),
         ],
         levels * early * NLON * 256 * 40,
         "correct",
@@ -904,14 +928,14 @@
 
     chunks = 4
 
-    def unpack(place_ref, *refs):
+    def unpack(*refs):
         pieces = refs[:levels]
         out_ref, done_ref, sems = refs[levels + 1 :]
         lines = late * digits // chunks
         copies = []
         for chunk in range(chunks):
             for mask in range(levels):
-                first = (place_ref[0] ^ mask) + chunk * lines * levels
+                first = (lon_here() ^ mask) + chunk * lines * levels
                 done_ref[pl.ds(first, lines, stride=levels), :] = pieces[mask][chunk * lines : (chunk + 1) * lines, :]
             here = pl.ds(chunk * lines * levels, lines * levels)
             there = pl.ds(early_total + chunk * lines * levels, lines * levels)
@@ -924,13 +948,13 @@
     (out,) = call(
         unpack,
         [(total, N2)],
-        [place, *late_pieces, out],
-        [SMEM] + [VMEM] * levels + [pl.ANY],
+        [*late_pieces, out],
+        [VMEM] * levels + [pl.ANY],
         [vmem(total - early_total, N2), pltpu.SemaphoreType.DMA((chunks,))],
         0,
         "unpack",
         out_spaces=[pl.ANY],
-        aliases={levels + 1: 0},
+        aliases={levels: 0},
     )
     return out.reshape(rows, digits, levels, N2).transpose(0, 2, 1, 3).reshape(right_side.shape)
 

time: 42.9 us -> 39.4 us (0.918)
  Pallas kernels: 17.1 us -> 12.9 us
  waiting for transfers between devices: 4.91 us -> 5.64 us
    pallas_call x11, Pallas kernels: 17.1 us -> 12.9 us  [call(): pl.pallas_call(body, out_shape=[jax.ShapeDtypeStruct(s, jnp.float32) for...]
    ppermute x14, waiting for transfers between devices: 3.6 us -> 4.9 us  [send_level(): return lax.ppermute(piece, 'lon', [(d, d ^ mask) for d in range(size)])]
    ppermute x2, waiting for transfers between devices: 1.31 us -> 0.73 us  [swap(): value_odd = lax.ppermute(value_odd, 'lat', odd)]
  transfers between devices with their start and end apart: 18 -> 18, of which waited for: 6 -> 5; matrix products, arithmetic and copies ran while one was open for 1% -> 1% of each run, Pallas kernels for 27% -> 24%
where the time goes in v9:
time: 39.4 us; the launch traced here: 39.3 us
  starting transfers between devices  18.9 us (48%)
  Pallas kernels  12.9 us (33%)
  waiting for transfers between devices  5.64 us (14%)
  local copies, waits for them, and re-layouts  1.45 us (4%)
    pallas_call x11, Pallas kernels, call(): pl.pallas_call(body, out_shape=[jax.ShapeDtypeStruct(s, jnp.float32) for...  12.9 us
    ppermute x14, starting transfers between devices, send_level(): return lax.ppermute(piece, 'lon', [(d, d ^ mask) for d in range(size)])  12.4 us
    ppermute x2, starting transfers between devices, swap(): value_odd = lax.ppermute(value_odd, 'lat', odd)  5.03 us
    ppermute x14, waiting for transfers between devices, send_level(): return lax.ppermute(piece, 'lon', [(d, d ^ mask) for d in range(size)])  4.9 us
    ppermute x2, starting transfers between devices, swap(): return (lax.ppermute(value_even, 'lat', even), value_odd)  1.53 us
    unnamed x26, local copies, waits for them, and re-layouts  1.29 us
  transfers between devices with their start and end apart: 18, of which 5 were waited for; matrix products, arithmetic and copies ran while one was open for 1% of the time, Pallas kernels for 24%

profile of v9, /device:TPU:17, one launch (start us, length us, event | category | flops | bytes accessed | tf_op | source)
XLA Modules:
  0.0 39.3 jit_solution(12408960821709567909)
XLA Ops:
  0.0 1.2 %copy-done = f32[60,4,1024]{2,1,0:T(4,128)S(1)} copy-done((f32[60,4,1024]{2,1,0:T(4,128)S(1)}, f32[60,4,1024]{2,1,0:T(4,128)}, u32[]{:S(2)}) %copy-start) | copy-done | bytes 983064
  1.2 0.0 copy-start.6
  1.3 0.0 copy-start.7
  1.3 1.3 %collective-permute-start.3 = (f32[128,128]{1,0:T(8,128)S(1)}, f32[128,128]{1,0:T(8,128)S(1)}, u32[]{:S(2)}, u32[]{:S(2)}) collective-permute-start(f32[128,128]{1,0:T(8,128)S(1)} %get-tuple-element.44), channel_id=1, source_target_pairs={{0,2},{1,3},{2,0},{3,1},{4,6},{5,7},{6,4},{7,5},{8,10},{9,11},{10,... | collective-permute-start | bytes 196616 | tf_op jit(solution)/shard_map/ppermute | solution.py:386
  2.6 1.1 %collective-permute-start.4 = (f32[128,128]{1,0:T(8,128)S(1)}, f32[128,128]{1,0:T(8,128)S(1)}, u32[]{:S(2)}, u32[]{:S(2)}) collective-permute-start(f32[128,128]{1,0:T(8,128)S(1)} %get-tuple-element.45), channel_id=1, source_target_pairs={{0,3},{1,2},{2,1},{3,0},{4,7},{5,6},{6,5},{7,4},{8,11},{9,10},{10,... | collective-permute-start | bytes 196616 | tf_op jit(solution)/shard_map/ppermute | solution.py:386
  3.7 0.1 pack.1
  3.8 0.0 copy-start.1
  3.8 0.0 copy-start.2
  3.8 0.0 copy-start.3
  3.8 1.3 %collective-permute-start.1 = (f32[352,128]{1,0:T(8,128)S(1)}, f32[352,128]{1,0:T(8,128)S(1)}, u32[]{:S(2)}, u32[]{:S(2)}) collective-permute-start(f32[352,128]{1,0:T(8,128)S(1)} %get-tuple-element.42), channel_id=1, source_target_pairs={{0,2},{1,3},{2,0},{3,1},{4,6},{5,7},{6,4},{7,5},{8,10},{9,11},{10,... | collective-permute-start | bytes 540680 | tf_op jit(solution)/shard_map/ppermute | solution.py:386
  5.1 0.3 collective-permute-start.2
  5.4 0.4 collective-permute-start
  5.8 0.1 pad_dynamic-slice_fusion.1
  5.8 0.1 broadcast_multiply_fusion.1.lon_ref
  5.9 0.1 pad_dynamic-slice_fusion
  6.0 0.1 broadcast_multiply_fusion.couple_ref
  6.1 0.7 %edge.1.refs_8_.refs_10_ = f32[576,128]{1,0:T(8,128)S(1)} custom-call(f32[4,76]{1,0:T(4,128)S(1)} %broadcast_multiply_fusion.1.lon_ref, f32[4,77]{1,0:T(4,128)S(1)} %broadcast_multiply_fusion.couple_ref, f32[32,128]{1,0:T(8,128)S(1)} %copy-done.8), custom_call_target="tpu_custom_call" | custom-call | flops 1310720 | bytes 313744 | tf_op jit(solution)/shard_map/edge/pallas_call | solution.py:359
  6.8 0.0 collective-permute-done.3.refs_2_
  6.8 0.4 collective-permute-done.4.refs_3_
  7.1 0.0 collective-permute-done.refs_1_
  7.2 0.7 %ends.1 = (f32[512,128]{1,0:T(8,128)S(1)}, f32[32,128]{1,0:T(8,128)S(1)}, f32[32,128]{1,0:T(8,128)S(1)}, f32[32,128]{1,0:T(8,128)S(1)}, f32[32,128]{1,0:T(8,128)S(1)}) custom-call(f32[128,128]{1,0:T(8,128)S(1)} %get-tuple-element.39.after_ref.refs_0_, f32[480,128]{1,0:T(8,128)S(1)} %collective-permute-done.refs_1_, ...), custom_call_target="tpu_custom_call" | custom-call | flops 67108864 | bytes 1867776 | tf_op jit(solution)/shard_map/ends/pallas_call | solution.py:359
  7.9 1.3 %collective-permute-start.5 = (f32[32,128]{1,0:T(8,128)S(1)}, f32[32,128]{1,0:T(8,128)S(1)}, u32[]{:S(2)}, u32[]{:S(2)}) collective-permute-start(f32[32,128]{1,0:T(8,128)S(1)} %get-tuple-element.47), channel_id=1, source_target_pairs={{0,4},{4,0},{8,12},{12,8},{16,20},{20,16},{24,28},{28,24},{1,5},{5... | collective-permute-start | bytes 49160 | tf_op jit(solution)/shard_map/ppermute | solution.py:382
  9.2 2.0 %collective-permute-start.6 = (f32[32,128]{1,0:T(8,128)S(1)}, f32[32,128]{1,0:T(8,128)S(1)}, u32[]{:S(2)}, u32[]{:S(2)}) collective-permute-start(f32[32,128]{1,0:T(8,128)S(1)} %get-tuple-element.48), channel_id=1, source_target_pairs={{4,8},{8,4},{12,16},{16,12},{20,24},{24,20},{5,9},{9,5},{13,17},{1... | collective-permute-start | bytes 49160 | tf_op jit(solution)/shard_map/ppermute | solution.py:381
  11.2 1.5 %own.1 = (f32[1920,128]{1,0:T(8,128)S(1)}, f32[1920,128]{1,0:T(8,128)S(1)}, f32[160,128]{1,0:T(8,128)S(1)}, f32[1088,128]{1,0:T(8,128)S(1)}, f32[1088,128]{1,0:T...) custom-call(f32[4,76]{1,0:T(4,128)S(1)} %broadcast_multiply_fusion.1.lon_ref, ...), custom_call_target="tpu_custom_call" | custom-call | flops 9830400 | bytes 4295056 | tf_op jit(solution)/shard_map/own/pallas_call | solution.py:359
  12.7 2.2 %collective-permute-done.2.refs_3_ = f32[352,128]{1,0:T(8,128)S(1)} collective-permute-done((f32[352,128]{1,0:T(8,128)S(1)}, f32[352,128]{1,0:T(8,128)S(1)}, u32[]{:S(2)}, u32[]{:S(2)}) %collective-permute-start.2) | collective-permute-done | bytes 180256 | tf_op jit(solution)/shard_map/ppermute | solution.py:386
  14.9 0.0 collective-permute-done.5.refs_12_.refs_2_
  14.9 2.6 %inner.1 = (f32[832,128]{1,0:T(8,128)S(1)}, f32[32,128]{1,0:T(8,128)S(1)}, f32[32,128]{1,0:T(8,128)S(1)}, f32[32,128]{1,0:T(8,128)S(1)}, f32[272,128]{1,0:T(8,12...) custom-call(f32[352,128]{1,0:T(8,128)S(1)} %get-tuple-element.40.refs_0_, ...), custom_call_target="tpu_custom_call" | custom-call | flops 327155712 | bytes 5750784 | tf_op jit(solution)/shard_map/inner/pallas_call | solution.py:359
  17.5 1.9 %collective-permute-start.9 = (f32[272,128]{1,0:T(8,128)S(1)}, f32[272,128]{1,0:T(8,128)S(1)}, u32[]{:S(2)}, u32[]{:S(2)}) collective-permute-start(f32[272,128]{1,0:T(8,128)S(1)} %get-tuple-element.58), channel_id=1, source_target_pairs={{0,1},{1,0},{2,3},{3,2},{4,5},{5,4},{6,7},{7,6},{8,9},{9,8},{10,11... | collective-permute-start | bytes 417800 | tf_op jit(solution)/shard_map/ppermute | solution.py:386
  19.5 0.6 %collective-permute-start.10 = (f32[272,128]{1,0:T(8,128)S(1)}, f32[272,128]{1,0:T(8,128)S(1)}, u32[]{:S(2)}, u32[]{:S(2)}) collective-permute-start(f32[272,128]{1,0:T(8,128)S(1)} %get-tuple-element.59), channel_id=1, source_target_pairs={{0,2},{1,3},{2,0},{3,1},{4,6},{5,7},{6,4},{7,5},{8,10},{9,11},{10,... | collective-permute-start | bytes 417800 | tf_op jit(solution)/shard_map/ppermute | solution.py:386
  20.0 1.1 %collective-permute-start.11 = (f32[272,128]{1,0:T(8,128)S(1)}, f32[272,128]{1,0:T(8,128)S(1)}, u32[]{:S(2)}, u32[]{:S(2)}) collective-permute-start(f32[272,128]{1,0:T(8,128)S(1)} %get-tuple-element.60), channel_id=1, source_target_pairs={{0,3},{1,2},{2,1},{3,0},{4,7},{5,6},{6,5},{7,4},{8,11},{9,10},{10,... | collective-permute-start | bytes 417800 | tf_op jit(solution)/shard_map/ppermute | solution.py:386
  21.2 0.2 collective-permute-start.7
  21.4 3.0 %collective-permute-start.8 = (f32[32,128]{1,0:T(8,128)S(1)}, f32[32,128]{1,0:T(8,128)S(1)}, u32[]{:S(2)}, u32[]{:S(2)}) collective-permute-start(f32[32,128]{1,0:T(8,128)S(1)} %get-tuple-element.55), channel_id=1, source_target_pairs={{4,8},{8,4},{12,16},{16,12},{20,24},{24,20},{5,9},{9,5},{13,17},{1... | collective-permute-start | bytes 49160 | tf_op jit(solution)/shard_map/ppermute | solution.py:381
  24.4 1.6 %partners.1 = (f32[2176,128]{1,0:T(8,128)S(1)}, f32[2176,128]{1,0:T(8,128)S(1)}, f32[32,128]{1,0:T(8,128)S(1)}) custom-call(f32[4,76]{1,0:T(4,128)S(1)} %broadcast_multiply_fusion.1.lon_ref, f32[4,77]{1,0:T(4,128)S(1)} %broadcast_multiply_fusion.couple_ref, f32[32,128]{1,0:T(8,128)S(1)} %copy-done.8, f32[32,128]{1,0:T(8,128)S(1)} %get-tuple-element.53.after_ref.refs_1_), custom_call_target="tpu_custom_call" | custom-call | flops 9830400 | bytes 2279824 | tf_op jit(solution)/shard_map/partners/pallas_call | solution.py:359
  26.0 0.0 collective-permute-done.7.refs_4_
  26.1 0.7 %collective-permute-done.8.refs_5_ = f32[32,128]{1,0:T(8,128)S(1)} collective-permute-done((f32[32,128]{1,0:T(8,128)S(1)}, f32[32,128]{1,0:T(8,128)S(1)}, u32[]{:S(2)}, u32[]{:S(2)}) %collective-permute-start.8) | collective-permute-done | bytes 16416 | tf_op jit(solution)/shard_map/ppermute | solution.py:381
  26.8 0.0 collective-permute-done.9.refs_11_.refs_1_
  26.8 1.2 %collective-permute-done.11.refs_13_.refs_3_ = f32[272,128]{1,0:T(8,128)S(1)} collective-permute-done((f32[272,128]{1,0:T(8,128)S(1)}, f32[272,128]{1,0:T(8,128)S(1)}, u32[]{:S(2)}, u32[]{:S(2)}) %collective-permute-start.11) | collective-permute-done | bytes 139296 | tf_op jit(solution)/shard_map/ppermute | solution.py:386
  28.0 0.0 copy-start.9
  28.0 0.9 %collective-permute-start.17 = (f32[64,128]{1,0:T(8,128)S(1)}, f32[64,128]{1,0:T(8,128)S(1)}, u32[]{:S(2)}, u32[]{:S(2)}) collective-permute-start(f32[64,128]{1,0:T(8,128)S(1)} %sigma.1.refs_0_.refs_4_), channel_id=1, source_target_pairs={{0,3},{1,2},{2,1},{3,0},{4,7},{5,6},{6,5},{7,4},{8,11},{9,10},{10,... | collective-permute-start | bytes 98312 | tf_op jit(solution)/shard_map/ppermute | solution.py:386
  28.9 0.9 %collective-permute-start.16 = (f32[64,128]{1,0:T(8,128)S(1)}, f32[64,128]{1,0:T(8,128)S(1)}, u32[]{:S(2)}, u32[]{:S(2)}) collective-permute-start(f32[64,128]{1,0:T(8,128)S(1)} %sigma.1.refs_0_.refs_4_), channel_id=1, source_target_pairs={{0,2},{1,3},{2,0},{3,1},{4,6},{5,7},{6,4},{7,5},{8,10},{9,11},{10,... | collective-permute-start | bytes 98312 | tf_op jit(solution)/shard_map/ppermute | solution.py:386
  29.9 0.4 collective-permute-start.15
  30.2 1.0 %second.1 = (f32[208,128]{1,0:T(8,128)S(1)}, f32[208,128]{1,0:T(8,128)S(1)}, f32[208,128]{1,0:T(8,128)S(1)}, f32[208,128]{1,0:T(8,128)S(1)}) custom-call(f32[64,128]{1,0:T(8,128)S(1)} %sigma.1.refs_0_.refs_4_, f32[832,128]{1,0:T(8,128)S(1)} %get-tuple-element.52.refs_0_.refs_1_, f32[1920,128]{1,0:T(8,128)S(1)} %get-tuple-element.49.refs_14_.refs_8_.refs_2_, ...), custom_call_target="tpu_custom_call" | custom-call | flops 109051904 | bytes 3735552 | tf_op jit(solution)/shard_map/second/pallas_call | solution.py:359
  31.3 0.2 collective-permute-start.12
  31.5 0.5 %collective-permute-start.13 = (f32[208,128]{1,0:T(8,128)S(1)}, f32[208,128]{1,0:T(8,128)S(1)}, u32[]{:S(2)}, u32[]{:S(2)}) collective-permute-start(f32[208,128]{1,0:T(8,128)S(1)} %get-tuple-element.64), channel_id=1, source_target_pairs={{0,2},{1,3},{2,0},{3,1},{4,6},{5,7},{6,4},{7,5},{8,10},{9,11},{10,... | collective-permute-start | bytes 319496 | tf_op jit(solution)/shard_map/ppermute | solution.py:386
  32.0 1.4 %collective-permute-start.14 = (f32[208,128]{1,0:T(8,128)S(1)}, f32[208,128]{1,0:T(8,128)S(1)}, u32[]{:S(2)}, u32[]{:S(2)}) collective-permute-start(f32[208,128]{1,0:T(8,128)S(1)} %get-tuple-element.65), channel_id=1, source_target_pairs={{0,3},{1,2},{2,1},{3,0},{4,7},{5,6},{6,5},{7,4},{8,11},{9,10},{10,... | collective-permute-start | bytes 319496 | tf_op jit(solution)/shard_map/ppermute | solution.py:386
  33.5 3.8 %correct.1.refs_4_ = f32[1920,128]{1,0:T(8,128)} custom-call(f32[272,128]{1,0:T(8,128)S(1)} %get-tuple-element.66.refs_0_, f32[272,128]{1,0:T(8,128)S(1)} %collective-permute-done.9.refs_11_.refs_1_, f32[272,128]{1,0:T(8,128)S(1)} %collective-permute-done.10.refs_12_.refs_2_, f32[272,128]{1,0:T(8,128)S(1)} %collective-permute-done.11.refs_13_.refs_3_, ...), custom_call_target="tpu_custom_call" | custom-call | flops 5704253440 | bytes 6930432 | tf_op jit(solution)/shard_map/correct/pallas_call | solution.py:359
  37.3 1.1 %collective-permute-done.14.refs_3_ = f32[208,128]{1,0:T(8,128)S(1)} collective-permute-done((f32[208,128]{1,0:T(8,128)S(1)}, f32[208,128]{1,0:T(8,128)S(1)}, u32[]{:S(2)}, u32[]{:S(2)}) %collective-permute-start.14) | collective-permute-done | bytes 106528 | tf_op jit(solution)/shard_map/ppermute | solution.py:386
  38.5 0.8 %unpack.1 = f32[1920,128]{1,0:T(8,128)} custom-call(f32[208,128]{1,0:T(8,128)S(1)} %get-tuple-element.62.refs_0_, f32[208,128]{1,0:T(8,128)S(1)} %collective-permute-done.12.refs_1_, f32[208,128]{1,0:T(8,128)S(1)} %collective-permute-done.13.refs_2_, f32[208,128]{1,0:T(8,128)S(1)} %collective-permute-done.14.refs_3_, ...), custom_call_target="tpu_custom_call", output_to_operand_aliasing={{}: (4, {})} | custom-call | bytes 2392064 | tf_op jit(solution)/shard_map/unpack/pallas_call | solution.py:359
  (29 shorter events, 0.1 us)
Async XLA Ops:
  0.0 6.1 %copy-start.8 = (f32[32,128]{1,0:T(8,128)S(1)}, f32[32,128]{1,0:T(8,128)}, u32[]{:S(2)}) copy-start(f32[32,128]{1,0:T(8,128)} %constant.48.eigen_ref) | copy-start | bytes 49156
  0.0 5.8 %copy-start.12 = (f32[4]{0:T(128)S(1)}, f32[4]{0:T(128)}, u32[]{:S(2)}) copy-start(f32[4]{0:T(128)} %param.16) | copy-start | bytes 52
  0.0 1.2 %copy-start = (f32[60,4,1024]{2,1,0:T(4,128)S(1)}, f32[60,4,1024]{2,1,0:T(4,128)}, u32[]{:S(2)}) copy-start(f32[60,4,1024]{2,1,0:T(4,128)} %param.13) | copy-start | bytes 2949124
  1.2 4.5 %copy-start.10 = (f32[480]{0:T(512)S(1)}, f32[480]{0:T(512)}, u32[]{:S(2)}) copy-start(f32[480]{0:T(512)} %param.14) | copy-start | bytes 5764
  1.2 4.7 %copy-start.11 = (f32[479]{0:T(512)S(1)}, f32[479]{0:T(512)}, u32[]{:S(2)}) copy-start(f32[479]{0:T(512)} %param.15) | copy-start | bytes 5752
  1.2 5.9 %copy-start.4 = (bf16[512,256]{1,0:T(8,128)(2,1)S(1)}, bf16[512,256]{1,0:T(8,128)(2,1)}, u32[]{:S(2)}) copy-start(bf16[512,256]{1,0:T(8,128)(2,1)} %constant.39.clone.refs_7_) | copy-start | bytes 786436
  1.2 5.9 %copy-start.5 = (bf16[512,256]{1,0:T(8,128)(2,1)S(1)}, bf16[512,256]{1,0:T(8,128)(2,1)}, u32[]{:S(2)}) copy-start(bf16[512,256]{1,0:T(8,128)(2,1)} %constant.37.clone.refs_6_) | copy-start | bytes 786436
  1.2 5.9 %copy-start.6 = (bf16[512,256]{1,0:T(8,128)(2,1)S(1)}, bf16[512,256]{1,0:T(8,128)(2,1)}, u32[]{:S(2)}) copy-start(bf16[512,256]{1,0:T(8,128)(2,1)} %constant.35.clone.refs_4_) | copy-start | bytes 786436
  1.3 5.9 %copy-start.7 = (f32[32,128]{1,0:T(8,128)S(1)}, f32[32,128]{1,0:T(8,128)}, u32[]{:S(2)}) copy-start(f32[32,128]{1,0:T(8,128)} %constant.41.clone.refs_5_.refs_6_.refs_15_) | copy-start | bytes 49156
  1.3 5.5 %collective-permute-start.3 = (f32[128,128]{1,0:T(8,128)S(1)}, f32[128,128]{1,0:T(8,128)S(1)}, u32[]{:S(2)}, u32[]{:S(2)}) collective-permute-start(f32[128,128]{1,0:T(8,128)S(1)} %get-tuple-element.44), channel_id=1, source_target_pairs={{0,2},{1,3},{2,0},{3,1},{4,6},{5,7},{6,4},{7,5},{8,10},{9,11},{10,... | collective-permute-start | bytes 196616 | tf_op jit(solution)/shard_map/ppermute | solution.py:386
  2.6 4.5 %collective-permute-start.4 = (f32[128,128]{1,0:T(8,128)S(1)}, f32[128,128]{1,0:T(8,128)S(1)}, u32[]{:S(2)}, u32[]{:S(2)}) collective-permute-start(f32[128,128]{1,0:T(8,128)S(1)} %get-tuple-element.45), channel_id=1, source_target_pairs={{0,3},{1,2},{2,1},{3,0},{4,7},{5,6},{6,5},{7,4},{8,11},{9,10},{10,... | collective-permute-start | bytes 196616 | tf_op jit(solution)/shard_map/ppermute | solution.py:386
  3.8 11.1 %copy-start.1 = (bf16[512,256]{1,0:T(8,128)(2,1)S(1)}, bf16[512,256]{1,0:T(8,128)(2,1)}, u32[]{:S(2)}) copy-start(bf16[512,256]{1,0:T(8,128)(2,1)} %constant.40.clone.refs_10_.refs_8_.refs_17_) | copy-start | bytes 786436
  3.8 11.1 %copy-start.2 = (bf16[512,256]{1,0:T(8,128)(2,1)S(1)}, bf16[512,256]{1,0:T(8,128)(2,1)}, u32[]{:S(2)}) copy-start(bf16[512,256]{1,0:T(8,128)(2,1)} %constant.38.clone.refs_9_.refs_7_.refs_16_) | copy-start | bytes 786436
  3.8 11.1 %copy-start.3 = (bf16[512,256]{1,0:T(8,128)(2,1)S(1)}, bf16[512,256]{1,0:T(8,128)(2,1)}, u32[]{:S(2)}) copy-start(bf16[512,256]{1,0:T(8,128)(2,1)} %constant.36.clone.refs_8_.refs_5_) | copy-start | bytes 786436
  3.8 8.8 %collective-permute-start.1 = (f32[352,128]{1,0:T(8,128)S(1)}, f32[352,128]{1,0:T(8,128)S(1)}, u32[]{:S(2)}, u32[]{:S(2)}) collective-permute-start(f32[352,128]{1,0:T(8,128)S(1)} %get-tuple-element.42), channel_id=1, source_target_pairs={{0,2},{1,3},{2,0},{3,1},{4,6},{5,7},{6,4},{7,5},{8,10},{9,11},{10,... | collective-permute-start | bytes 540680 | tf_op jit(solution)/shard_map/ppermute | solution.py:386
  5.1 9.7 %collective-permute-start.2 = (f32[352,128]{1,0:T(8,128)S(1)}, f32[352,128]{1,0:T(8,128)S(1)}, u32[]{:S(2)}, u32[]{:S(2)}) collective-permute-start(f32[352,128]{1,0:T(8,128)S(1)} %get-tuple-element.43), channel_id=1, source_target_pairs={{0,3},{1,2},{2,1},{3,0},{4,7},{5,6},{6,5},{7,4},{8,11},{9,10},{10,... | collective-permute-start | bytes 540680 | tf_op jit(solution)/shard_map/ppermute | solution.py:386
  5.4 1.7 %collective-permute-start = (f32[480,128]{1,0:T(8,128)S(1)}, f32[480,128]{1,0:T(8,128)S(1)}, u32[]{:S(2)}, u32[]{:S(2)}) collective-permute-start(f32[480,128]{1,0:T(8,128)S(1)} %get-tuple-element.41), channel_id=1, source_target_pairs={{0,1},{1,0},{2,3},{3,2},{4,5},{5,4},{6,7},{7,6},{8,9},{9,8},{10,11... | collective-permute-start | bytes 737288 | tf_op jit(solution)/shard_map/ppermute | solution.py:386
  7.9 7.0 %collective-permute-start.5 = (f32[32,128]{1,0:T(8,128)S(1)}, f32[32,128]{1,0:T(8,128)S(1)}, u32[]{:S(2)}, u32[]{:S(2)}) collective-permute-start(f32[32,128]{1,0:T(8,128)S(1)} %get-tuple-element.47), channel_id=1, source_target_pairs={{0,4},{4,0},{8,12},{12,8},{16,20},{20,16},{24,28},{28,24},{1,5},{5... | collective-permute-start | bytes 49160 | tf_op jit(solution)/shard_map/ppermute | solution.py:382
  9.2 5.7 %collective-permute-start.6 = (f32[32,128]{1,0:T(8,128)S(1)}, f32[32,128]{1,0:T(8,128)S(1)}, u32[]{:S(2)}, u32[]{:S(2)}) collective-permute-start(f32[32,128]{1,0:T(8,128)S(1)} %get-tuple-element.48), channel_id=1, source_target_pairs={{4,8},{8,4},{12,16},{16,12},{20,24},{24,20},{5,9},{9,5},{13,17},{1... | collective-permute-start | bytes 49160 | tf_op jit(solution)/shard_map/ppermute | solution.py:381
  17.5 9.3 %collective-permute-start.9 = (f32[272,128]{1,0:T(8,128)S(1)}, f32[272,128]{1,0:T(8,128)S(1)}, u32[]{:S(2)}, u32[]{:S(2)}) collective-permute-start(f32[272,128]{1,0:T(8,128)S(1)} %get-tuple-element.58), channel_id=1, source_target_pairs={{0,1},{1,0},{2,3},{3,2},{4,5},{5,4},{6,7},{7,6},{8,9},{9,8},{10,11... | collective-permute-start | bytes 417800 | tf_op jit(solution)/shard_map/ppermute | solution.py:386
  19.5 7.3 %collective-permute-start.10 = (f32[272,128]{1,0:T(8,128)S(1)}, f32[272,128]{1,0:T(8,128)S(1)}, u32[]{:S(2)}, u32[]{:S(2)}) collective-permute-start(f32[272,128]{1,0:T(8,128)S(1)} %get-tuple-element.59), channel_id=1, source_target_pairs={{0,2},{1,3},{2,0},{3,1},{4,6},{5,7},{6,4},{7,5},{8,10},{9,11},{10,... | collective-permute-start | bytes 417800 | tf_op jit(solution)/shard_map/ppermute | solution.py:386
  20.0 7.9 %collective-permute-start.11 = (f32[272,128]{1,0:T(8,128)S(1)}, f32[272,128]{1,0:T(8,128)S(1)}, u32[]{:S(2)}, u32[]{:S(2)}) collective-permute-start(f32[272,128]{1,0:T(8,128)S(1)} %get-tuple-element.60), channel_id=1, source_target_pairs={{0,3},{1,2},{2,1},{3,0},{4,7},{5,6},{6,5},{7,4},{8,11},{9,10},{10,... | collective-permute-start | bytes 417800 | tf_op jit(solution)/shard_map/ppermute | solution.py:386
  21.2 4.9 %collective-permute-start.7 = (f32[32,128]{1,0:T(8,128)S(1)}, f32[32,128]{1,0:T(8,128)S(1)}, u32[]{:S(2)}, u32[]{:S(2)}) collective-permute-start(f32[32,128]{1,0:T(8,128)S(1)} %get-tuple-element.54), channel_id=1, source_target_pairs={{0,4},{4,0},{8,12},{12,8},{16,20},{20,16},{24,28},{28,24},{1,5},{5... | collective-permute-start | bytes 49160 | tf_op jit(solution)/shard_map/ppermute | solution.py:382
  21.4 5.4 %collective-permute-start.8 = (f32[32,128]{1,0:T(8,128)S(1)}, f32[32,128]{1,0:T(8,128)S(1)}, u32[]{:S(2)}, u32[]{:S(2)}) collective-permute-start(f32[32,128]{1,0:T(8,128)S(1)} %get-tuple-element.55), channel_id=1, source_target_pairs={{4,8},{8,4},{12,16},{16,12},{20,24},{24,20},{5,9},{9,5},{13,17},{1... | collective-permute-start | bytes 49160 | tf_op jit(solution)/shard_map/ppermute | solution.py:381
  28.0 5.5 %copy-start.9 = (bf16[512,256]{1,0:T(8,128)(2,1)S(1)}, bf16[512,256]{1,0:T(8,128)(2,1)}, u32[]{:S(2)}) copy-start(bf16[512,256]{1,0:T(8,128)(2,1)} %constant.34.clone.refs_14_) | copy-start | bytes 786436
  28.0 4.0 %collective-permute-start.17 = (f32[64,128]{1,0:T(8,128)S(1)}, f32[64,128]{1,0:T(8,128)S(1)}, u32[]{:S(2)}, u32[]{:S(2)}) collective-permute-start(f32[64,128]{1,0:T(8,128)S(1)} %sigma.1.refs_0_.refs_4_), channel_id=1, source_target_pairs={{0,3},{1,2},{2,1},{3,0},{4,7},{5,6},{6,5},{7,4},{8,11},{9,10},{10,... | collective-permute-start | bytes 98312 | tf_op jit(solution)/shard_map/ppermute | solution.py:386
  28.9 4.5 %collective-permute-start.16 = (f32[64,128]{1,0:T(8,128)S(1)}, f32[64,128]{1,0:T(8,128)S(1)}, u32[]{:S(2)}, u32[]{:S(2)}) collective-permute-start(f32[64,128]{1,0:T(8,128)S(1)} %sigma.1.refs_0_.refs_4_), channel_id=1, source_target_pairs={{0,2},{1,3},{2,0},{3,1},{4,6},{5,7},{6,4},{7,5},{8,10},{9,11},{10,... | collective-permute-start | bytes 98312 | tf_op jit(solution)/shard_map/ppermute | solution.py:386
  29.9 3.6 %collective-permute-start.15 = (f32[64,128]{1,0:T(8,128)S(1)}, f32[64,128]{1,0:T(8,128)S(1)}, u32[]{:S(2)}, u32[]{:S(2)}) collective-permute-start(f32[64,128]{1,0:T(8,128)S(1)} %sigma.1.refs_0_.refs_4_), channel_id=1, source_target_pairs={{0,1},{1,0},{2,3},{3,2},{4,5},{5,4},{6,7},{7,6},{8,9},{9,8},{10,11... | collective-permute-start | bytes 98312 | tf_op jit(solution)/shard_map/ppermute | solution.py:386
  31.3 6.0 %collective-permute-start.12 = (f32[208,128]{1,0:T(8,128)S(1)}, f32[208,128]{1,0:T(8,128)S(1)}, u32[]{:S(2)}, u32[]{:S(2)}) collective-permute-start(f32[208,128]{1,0:T(8,128)S(1)} %get-tuple-element.63), channel_id=1, source_target_pairs={{0,1},{1,0},{2,3},{3,2},{4,5},{5,4},{6,7},{7,6},{8,9},{9,8},{10,11... | collective-permute-start | bytes 319496 | tf_op jit(solution)/shard_map/ppermute | solution.py:386
  31.5 5.8 %collective-permute-start.13 = (f32[208,128]{1,0:T(8,128)S(1)}, f32[208,128]{1,0:T(8,128)S(1)}, u32[]{:S(2)}, u32[]{:S(2)}) collective-permute-start(f32[208,128]{1,0:T(8,128)S(1)} %get-tuple-element.64), channel_id=1, source_target_pairs={{0,2},{1,3},{2,0},{3,1},{4,6},{5,7},{6,4},{7,5},{8,10},{9,11},{10,... | collective-permute-start | bytes 319496 | tf_op jit(solution)/shard_map/ppermute | solution.py:386
  32.0 6.4 %collective-permute-start.14 = (f32[208,128]{1,0:T(8,128)S(1)}, f32[208,128]{1,0:T(8,128)S(1)}, u32[]{:S(2)}, u32[]{:S(2)}) collective-permute-start(f32[208,128]{1,0:T(8,128)S(1)} %get-tuple-element.65), channel_id=1, source_target_pairs={{0,3},{1,2},{2,1},{3,0},{4,7},{5,6},{6,5},{7,4},{8,11},{9,10},{10,... | collective-permute-start | bytes 319496 | tf_op jit(solution)/shard_map/ppermute | solution.py:386

commit v10 on v9

--- a/solution.py
+++ b/solution.py
@@ -363,7 +363,7 @@
         out_specs=[pl.BlockSpec(memory_space=s) for s in out_spaces or [VMEM] * len(outs)],
         input_output_aliases=aliases or {},
         scratch_shapes=scratch,
-        compiler_params=pltpu.CompilerParams(vmem_limit_bytes=48 << 20),
+        compiler_params=pltpu.CompilerParams(vmem_limit_bytes=32 << 20),
         cost_estimate=pl.CostEstimate(flops=flops, bytes_accessed=nbytes, transcendentals=0),
         name=name,
     )(*ins)
@@ -427,7 +427,7 @@
 
 
 def early_rows(rows):
-    return rows // 2 + 4
+    return rows // 2 + 6
 
 
 def lon_here():
@@ -446,21 +446,23 @@
     for i in range(OV):
         e, f = rows + i, 2 * OV - 1 - i
         if i == 0:
-            low = 1.0 + lon_ref[level, e] * eigen + couple_ref[level, e]
-            high = 1.0 + lon_ref[level, f] * eigen + couple_ref[level, f + 1]
+            low = 1.0 + lon_ref[level, e : e + 1, :] * eigen + couple_ref[level, e : e + 1, :]
+            high = 1.0 + lon_ref[level, f : f + 1, :] * eigen + couple_ref[level, f + 1 : f + 2, :]
         else:
-            low_ratio = couple_ref[level, e] * low_inverse
-            high_ratio = couple_ref[level, f + 1] * high_inverse
+            low_ratio = couple_ref[level, e : e + 1, :] * low_inverse
+            high_ratio = couple_ref[level, f + 1 : f + 2, :] * high_inverse
             out_ref[(i - 1) * groups : i * groups, :] = low_ratio
             out_ref[(OV + i - 1) * groups : (OV + i) * groups, :] = high_ratio
-            low = 1.0 + lon_ref[level, e] * eigen + low_ratio * low
-            high = 1.0 + lon_ref[level, f] * eigen + high_ratio * high
-        low_inverse = 1.0 / (couple_ref[level, e + 1] + low)
-        high_inverse = 1.0 / (couple_ref[level, f] + high)
+            low = 1.0 + lon_ref[level, e : e + 1, :] * eigen + low_ratio * low
+            high = 1.0 + lon_ref[level, f : f + 1, :] * eigen + high_ratio * high
+        low_inverse = 1.0 / (couple_ref[level, e + 1 : e + 2, :] + low)
+        high_inverse = 1.0 / (couple_ref[level, f : f + 1, :] + high)
     out_ref[(OV - 1) * groups : OV * groups, :] = low_inverse
     out_ref[(2 * OV - 1) * groups : 2 * OV * groups, :] = high_inverse
-    out_ref[2 * OV * groups : (2 * OV + 1) * groups, :] = jnp.full_like(eigen, couple_ref[level, OV])
-    out_ref[(2 * OV + 1) * groups :, :] = jnp.full_like(eigen, couple_ref[level, OV + rows])
+    out_ref[2 * OV * groups : (2 * OV + 1) * groups, :] = jnp.broadcast_to(couple_ref[level, OV : OV + 1, :], eigen.shape)
+    out_ref[(2 * OV + 1) * groups :, :] = jnp.broadcast_to(
+        couple_ref[level, OV + rows : OV + rows + 1, :], eigen.shape
+    )
 
 
 def level_response(rows, early, level, lon_ref, couple_ref, eigen, put_ratio, put_inverse, keep, tables):
@@ -468,7 +470,7 @@
     ratio_at, value_at, put_value, put_phi, put_psi = tables
 
     def plain(e):
-        return 1.0 + lon_ref[level, e] * eigen
+        return 1.0 + lon_ref[level, e : e + 1, :] * eigen
 
     low = high = None
     low_inverse = high_inverse = low_value = high_value = None
@@ -476,15 +478,15 @@
         j = rows - 1 - i
         e, f = i + OV, j + OV
         if low is None:
-            low = plain(e) + couple_ref[level, e]
-            high = plain(f) + couple_ref[level, f + 1]
+            low = plain(e) + couple_ref[level, e : e + 1, :]
+            high = plain(f) + couple_ref[level, f + 1 : f + 2, :]
         else:
-            low_ratio = couple_ref[level, e] * low_inverse
-            high_ratio = couple_ref[level, f + 1] * high_inverse
+            low_ratio = couple_ref[level, e : e + 1, :] * low_inverse
+            high_ratio = couple_ref[level, f + 1 : f + 2, :] * high_inverse
             low = plain(e) + low_ratio * low
             high = plain(f) + high_ratio * high
-        low_divisor = couple_ref[level, e + 1] + low
-        high_divisor = couple_ref[level, f] + high
+        low_divisor = couple_ref[level, e + 1 : e + 2, :] + low
+        high_divisor = couple_ref[level, f : f + 1, :] + high
         low_inverse = 1.0 / low_divisor
         high_inverse = 1.0 / high_divisor
         yield
@@ -504,7 +506,7 @@
             put_value(i, low_value * low_inverse)
             if j < early:
                 put_value(j, high_value * high_inverse)
-    between = couple_ref[level, OV + half]
+    between = couple_ref[level, OV + half : OV + half + 1, :]
     inverse = 1.0 / (between * (low + high) + low * high)
     across = between * inverse
     high_inverse = high_divisor * inverse
@@ -624,11 +626,13 @@
     late = rows - early
     eigen = const["eigen"].reshape(groups, N2)
     lon_all, couple_all = operator_parts(rows, lon_coef, lat_coef, level_scale)
+    lon_all = jnp.broadcast_to(lon_all[:, :, None], (*lon_all.shape, N2))
+    couple_all = jnp.broadcast_to(couple_all[:, :, None], (*couple_all.shape, N2))
     (around,) = call(
         functools.partial(edge_kernel, rows),
         [((2 * OV + 2) * groups, N2)],
         [lon_all, couple_all, eigen],
-        [SMEM, SMEM, VMEM],
+        [VMEM, VMEM, VMEM],
         [],
         16 * groups * N2 * 20,
         "edge",
@@ -641,7 +645,7 @@
         functools.partial(own_kernel, rows, early, near_masks),
         [block, block, (5 * groups, N2)] + [early_block] * 4,
         [lon_all, couple_all, eigen],
-        [SMEM, SMEM, VMEM],
+        [VMEM, VMEM, VMEM],
         [vmem(*early_block)] * 3,
         2 * rows * groups * N2 * 20,
         "own",
@@ -785,7 +789,7 @@
         functools.partial(partners_kernel, rows, early, far_masks),
         [(len(far_masks) * early * groups, N2)] * 2 + [row],
         [lon_all, couple_all, eigen, own_top],
-        [SMEM, SMEM, VMEM, VMEM],
+        [VMEM, VMEM, VMEM, VMEM],
         [vmem(*early_block)] * (2 * len(far_masks)),
         len(far_masks) * rows * groups * N2 * 20,
         "partners",

time: 39.4 us -> 39.1 us (level)
  Pallas kernels: 12.9 us -> 10.9 us
  waiting for transfers between devices: 5.64 us -> 7.06 us
    pallas_call x11, Pallas kernels: 12.9 us -> 10.9 us  [call(): pl.pallas_call(body, out_shape=[jax.ShapeDtypeStruct(s, jnp.float32) for...]
    ppermute x14, waiting for transfers between devices: 4.9 us -> 5.72 us  [send_level(): return lax.ppermute(piece, 'lon', [(d, d ^ mask) for d in range(size)])]
    ppermute x2, waiting for transfers between devices: 0.73 us -> 1.33 us  [swap(): value_odd = lax.ppermute(value_odd, 'lat', odd)]
  transfers between devices with their start and end apart: 18 -> 18, of which waited for: 5 -> 5; matrix products, arithmetic and copies ran while one was open for 1% -> 1% of each run, Pallas kernels for 24% -> 19%
where the time goes in v10:
time: 39.1 us; the launch traced here: 38.9 us
  starting transfers between devices  18.9 us (48%)
  Pallas kernels  10.9 us (28%)
  waiting for transfers between devices  7.06 us (18%)
  local copies, waits for them, and re-layouts  1.64 us (4%)
    ppermute x14, starting transfers between devices, send_level(): return lax.ppermute(piece, 'lon', [(d, d ^ mask) for d in range(size)])  12.4 us
    pallas_call x11, Pallas kernels, call(): pl.pallas_call(body, out_shape=[jax.ShapeDtypeStruct(s, jnp.float32) for...  10.9 us
    ppermute x14, waiting for transfers between devices, send_level(): return lax.ppermute(piece, 'lon', [(d, d ^ mask) for d in range(size)])  5.72 us
    ppermute x2, starting transfers between devices, swap(): value_odd = lax.ppermute(value_odd, 'lat', odd)  5.03 us
    ppermute x2, starting transfers between devices, swap(): return (lax.ppermute(value_even, 'lat', even), value_odd)  1.53 us
    ppermute x2, waiting for transfers between devices, swap(): value_odd = lax.ppermute(value_odd, 'lat', odd)  1.33 us
    unnamed x26, local copies, waits for them, and re-layouts  1.28 us
  transfers between devices with their start and end apart: 18, of which 5 were waited for; matrix products, arithmetic and copies ran while one was open for 1% of the time, Pallas kernels for 19%

profile of v10, /device:TPU:17, one launch (start us, length us, event | category | flops | bytes accessed | tf_op | source)
XLA Modules:
  0.0 38.9 jit_solution(12586952342073200478)
XLA Ops:
  0.0 1.2 %copy-done = f32[60,4,1024]{2,1,0:T(4,128)S(1)} copy-done((f32[60,4,1024]{2,1,0:T(4,128)S(1)}, f32[60,4,1024]{2,1,0:T(4,128)}, u32[]{:S(2)}) %copy-start) | copy-done | bytes 983064
  1.3 0.0 copy-start.4
  1.3 0.0 copy-start.5
  1.3 0.0 copy-start.6
  1.3 0.0 copy-start.7
  1.3 1.3 %collective-permute-start.3 = (f32[128,128]{1,0:T(8,128)S(1)}, f32[128,128]{1,0:T(8,128)S(1)}, u32[]{:S(2)}, u32[]{:S(2)}) collective-permute-start(f32[128,128]{1,0:T(8,128)S(1)} %get-tuple-element.44), channel_id=1, source_target_pairs={{0,2},{1,3},{2,0},{3,1},{4,6},{5,7},{6,4},{7,5},{8,10},{9,11},{10,... | collective-permute-start | bytes 196616 | tf_op jit(solution)/shard_map/ppermute | solution.py:386
  2.6 1.1 %collective-permute-start.4 = (f32[128,128]{1,0:T(8,128)S(1)}, f32[128,128]{1,0:T(8,128)S(1)}, u32[]{:S(2)}, u32[]{:S(2)}) collective-permute-start(f32[128,128]{1,0:T(8,128)S(1)} %get-tuple-element.45), channel_id=1, source_target_pairs={{0,3},{1,2},{2,1},{3,0},{4,7},{5,6},{6,5},{7,4},{8,11},{9,10},{10,... | collective-permute-start | bytes 196616 | tf_op jit(solution)/shard_map/ppermute | solution.py:386
  3.7 0.1 pack.1
  3.8 1.3 %collective-permute-start.1 = (f32[352,128]{1,0:T(8,128)S(1)}, f32[352,128]{1,0:T(8,128)S(1)}, u32[]{:S(2)}, u32[]{:S(2)}) collective-permute-start(f32[352,128]{1,0:T(8,128)S(1)} %get-tuple-element.42), channel_id=1, source_target_pairs={{0,2},{1,3},{2,0},{3,1},{4,6},{5,7},{6,4},{7,5},{8,10},{9,11},{10,... | collective-permute-start | bytes 540680 | tf_op jit(solution)/shard_map/ppermute | solution.py:386
  5.1 0.3 collective-permute-start.2
  5.4 0.4 collective-permute-start
  5.7 0.1 pad_dynamic-slice_fusion.1
  5.8 0.1 broadcast_multiply_fusion.1
  5.9 0.1 pad_dynamic-slice_fusion
  5.9 0.1 broadcast_multiply_fusion
  6.0 0.1 broadcast_in_dim.5.couple_ref
  6.1 0.1 broadcast_in_dim.4.lon_ref
  6.2 0.0 copy-start.1
  6.3 0.0 copy-start.2
  6.3 0.0 copy-start.3
  6.3 0.1 edge.1.refs_8_.refs_10_
  6.4 0.0 collective-permute-done.3.refs_2_
  6.4 0.7 %collective-permute-done.4.refs_3_ = f32[128,128]{1,0:T(8,128)S(1)} collective-permute-done((f32[128,128]{1,0:T(8,128)S(1)}, f32[128,128]{1,0:T(8,128)S(1)}, u32[]{:S(2)}, u32[]{:S(2)}) %collective-permute-start.4) | collective-permute-done | bytes 65568 | tf_op jit(solution)/shard_map/ppermute | solution.py:386
  7.1 0.7 %ends.1 = (f32[512,128]{1,0:T(8,128)S(1)}, f32[32,128]{1,0:T(8,128)S(1)}, f32[32,128]{1,0:T(8,128)S(1)}, f32[32,128]{1,0:T(8,128)S(1)}, f32[32,128]{1,0:T(8,128)S(1)}) custom-call(f32[128,128]{1,0:T(8,128)S(1)} %get-tuple-element.39.after_ref.refs_0_, f32[480,128]{1,0:T(8,128)S(1)} %collective-permute-done.refs_1_, ...), custom_call_target="tpu_custom_call" | custom-call | flops 67108864 | bytes 1867776 | tf_op jit(solution)/shard_map/ends/pallas_call | solution.py:359
  7.8 1.3 %collective-permute-start.5 = (f32[32,128]{1,0:T(8,128)S(1)}, f32[32,128]{1,0:T(8,128)S(1)}, u32[]{:S(2)}, u32[]{:S(2)}) collective-permute-start(f32[32,128]{1,0:T(8,128)S(1)} %get-tuple-element.47), channel_id=1, source_target_pairs={{0,4},{4,0},{8,12},{12,8},{16,20},{20,16},{24,28},{28,24},{1,5},{5... | collective-permute-start | bytes 49160 | tf_op jit(solution)/shard_map/ppermute | solution.py:382
  9.1 2.0 %collective-permute-start.6 = (f32[32,128]{1,0:T(8,128)S(1)}, f32[32,128]{1,0:T(8,128)S(1)}, u32[]{:S(2)}, u32[]{:S(2)}) collective-permute-start(f32[32,128]{1,0:T(8,128)S(1)} %get-tuple-element.48), channel_id=1, source_target_pairs={{4,8},{8,4},{12,16},{16,12},{20,24},{24,20},{5,9},{9,5},{13,17},{1... | collective-permute-start | bytes 49160 | tf_op jit(solution)/shard_map/ppermute | solution.py:381
  11.2 0.8 %own.1 = (f32[1920,128]{1,0:T(8,128)S(1)}, f32[1920,128]{1,0:T(8,128)S(1)}, f32[160,128]{1,0:T(8,128)S(1)}, f32[1152,128]{1,0:T(8,128)S(1)}, f32[1152,128]{1,0:T...) custom-call(f32[4,76,128]{2,1,0:T(8,128)S(1)} %broadcast_in_dim.4.lon_ref, ...), custom_call_target="tpu_custom_call" | custom-call | flops 9830400 | bytes 4737024 | tf_op jit(solution)/shard_map/own/pallas_call | solution.py:359
  12.0 2.8 %collective-permute-done.2.refs_3_ = f32[352,128]{1,0:T(8,128)S(1)} collective-permute-done((f32[352,128]{1,0:T(8,128)S(1)}, f32[352,128]{1,0:T(8,128)S(1)}, u32[]{:S(2)}, u32[]{:S(2)}) %collective-permute-start.2) | collective-permute-done | bytes 180256 | tf_op jit(solution)/shard_map/ppermute | solution.py:386
  14.9 2.7 %inner.1 = (f32[768,128]{1,0:T(8,128)S(1)}, f32[32,128]{1,0:T(8,128)S(1)}, f32[32,128]{1,0:T(8,128)S(1)}, f32[32,128]{1,0:T(8,128)S(1)}, f32[288,128]{1,0:T(8,12...) custom-call(f32[352,128]{1,0:T(8,128)S(1)} %get-tuple-element.40.refs_0_, ...), custom_call_target="tpu_custom_call" | custom-call | flops 335544320 | bytes 5750784 | tf_op jit(solution)/shard_map/inner/pallas_call | solution.py:359
  17.5 1.9 %collective-permute-start.9 = (f32[288,128]{1,0:T(8,128)S(1)}, f32[288,128]{1,0:T(8,128)S(1)}, u32[]{:S(2)}, u32[]{:S(2)}) collective-permute-start(f32[288,128]{1,0:T(8,128)S(1)} %get-tuple-element.58), channel_id=1, source_target_pairs={{0,1},{1,0},{2,3},{3,2},{4,5},{5,4},{6,7},{7,6},{8,9},{9,8},{10,11... | collective-permute-start | bytes 442376 | tf_op jit(solution)/shard_map/ppermute | solution.py:386
  19.5 0.5 %collective-permute-start.10 = (f32[288,128]{1,0:T(8,128)S(1)}, f32[288,128]{1,0:T(8,128)S(1)}, u32[]{:S(2)}, u32[]{:S(2)}) collective-permute-start(f32[288,128]{1,0:T(8,128)S(1)} %get-tuple-element.59), channel_id=1, source_target_pairs={{0,2},{1,3},{2,0},{3,1},{4,6},{5,7},{6,4},{7,5},{8,10},{9,11},{10,... | collective-permute-start | bytes 442376 | tf_op jit(solution)/shard_map/ppermute | solution.py:386
  20.0 1.2 %collective-permute-start.11 = (f32[288,128]{1,0:T(8,128)S(1)}, f32[288,128]{1,0:T(8,128)S(1)}, u32[]{:S(2)}, u32[]{:S(2)}) collective-permute-start(f32[288,128]{1,0:T(8,128)S(1)} %get-tuple-element.60), channel_id=1, source_target_pairs={{0,3},{1,2},{2,1},{3,0},{4,7},{5,6},{6,5},{7,4},{8,11},{9,10},{10,... | collective-permute-start | bytes 442376 | tf_op jit(solution)/shard_map/ppermute | solution.py:386
  21.2 0.2 collective-permute-start.7
  21.4 3.0 %collective-permute-start.8 = (f32[32,128]{1,0:T(8,128)S(1)}, f32[32,128]{1,0:T(8,128)S(1)}, u32[]{:S(2)}, u32[]{:S(2)}) collective-permute-start(f32[32,128]{1,0:T(8,128)S(1)} %get-tuple-element.55), channel_id=1, source_target_pairs={{4,8},{8,4},{12,16},{16,12},{20,24},{24,20},{5,9},{9,5},{13,17},{1... | collective-permute-start | bytes 49160 | tf_op jit(solution)/shard_map/ppermute | solution.py:381
  24.4 1.0 %partners.1 = (f32[2304,128]{1,0:T(8,128)S(1)}, f32[2304,128]{1,0:T(8,128)S(1)}, f32[32,128]{1,0:T(8,128)S(1)}) custom-call(f32[4,76,128]{2,1,0:T(8,128)S(1)} %broadcast_in_dim.4.lon_ref, f32[4,77,128]{2,1,0:T(8,128)S(1)} %broadcast_in_dim.5.couple_ref, f32[32,128]{1,0:T(8,128)S(1)} %copy-done.8, f32[32,128]{1,0:T(8,128)S(1)} %get-tuple-element.53.after_ref.refs_1_), custom_call_target="tpu_custom_call" | custom-call | flops 9830400 | bytes 2721792 | tf_op jit(solution)/shard_map/partners/pallas_call | solution.py:359
  25.5 1.3 %collective-permute-done.8.refs_5_ = f32[32,128]{1,0:T(8,128)S(1)} collective-permute-done((f32[32,128]{1,0:T(8,128)S(1)}, f32[32,128]{1,0:T(8,128)S(1)}, u32[]{:S(2)}, u32[]{:S(2)}) %collective-permute-start.8) | collective-permute-done | bytes 16416 | tf_op jit(solution)/shard_map/ppermute | solution.py:381
  26.8 1.4 %collective-permute-done.11.refs_13_.refs_3_ = f32[288,128]{1,0:T(8,128)S(1)} collective-permute-done((f32[288,128]{1,0:T(8,128)S(1)}, f32[288,128]{1,0:T(8,128)S(1)}, u32[]{:S(2)}, u32[]{:S(2)}) %collective-permute-start.11) | collective-permute-done | bytes 147488 | tf_op jit(solution)/shard_map/ppermute | solution.py:386
  28.3 0.0 copy-start.9
  28.3 0.7 %collective-permute-start.17 = (f32[64,128]{1,0:T(8,128)S(1)}, f32[64,128]{1,0:T(8,128)S(1)}, u32[]{:S(2)}, u32[]{:S(2)}) collective-permute-start(f32[64,128]{1,0:T(8,128)S(1)} %sigma.1.refs_0_.refs_4_), channel_id=1, source_target_pairs={{0,3},{1,2},{2,1},{3,0},{4,7},{5,6},{6,5},{7,4},{8,11},{9,10},{10,... | collective-permute-start | bytes 98312 | tf_op jit(solution)/shard_map/ppermute | solution.py:386
  29.0 1.0 %collective-permute-start.16 = (f32[64,128]{1,0:T(8,128)S(1)}, f32[64,128]{1,0:T(8,128)S(1)}, u32[]{:S(2)}, u32[]{:S(2)}) collective-permute-start(f32[64,128]{1,0:T(8,128)S(1)} %sigma.1.refs_0_.refs_4_), channel_id=1, source_target_pairs={{0,2},{1,3},{2,0},{3,1},{4,6},{5,7},{6,4},{7,5},{8,10},{9,11},{10,... | collective-permute-start | bytes 98312 | tf_op jit(solution)/shard_map/ppermute | solution.py:386
  29.9 0.6 %collective-permute-start.15 = (f32[64,128]{1,0:T(8,128)S(1)}, f32[64,128]{1,0:T(8,128)S(1)}, u32[]{:S(2)}, u32[]{:S(2)}) collective-permute-start(f32[64,128]{1,0:T(8,128)S(1)} %sigma.1.refs_0_.refs_4_), channel_id=1, source_target_pairs={{0,1},{1,0},{2,3},{3,2},{4,5},{5,4},{6,7},{7,6},{8,9},{9,8},{10,11... | collective-permute-start | bytes 98312 | tf_op jit(solution)/shard_map/ppermute | solution.py:386
  30.5 0.9 %second.1 = (f32[192,128]{1,0:T(8,128)S(1)}, f32[192,128]{1,0:T(8,128)S(1)}, f32[192,128]{1,0:T(8,128)S(1)}, f32[192,128]{1,0:T(8,128)S(1)}) custom-call(f32[64,128]{1,0:T(8,128)S(1)} %sigma.1.refs_0_.refs_4_, f32[768,128]{1,0:T(8,128)S(1)} %get-tuple-element.52.refs_0_.refs_1_, f32[1920,128]{1,0:T(8,128)S(1)} %get-tuple-element.49.refs_14_.refs_8_.refs_2_, ...), custom_call_target="tpu_custom_call" | custom-call | flops 100663296 | bytes 3670016 | tf_op jit(solution)/shard_map/second/pallas_call | solution.py:359
  31.4 0.1 collective-permute-start.12
  31.4 0.6 %collective-permute-start.13 = (f32[192,128]{1,0:T(8,128)S(1)}, f32[192,128]{1,0:T(8,128)S(1)}, u32[]{:S(2)}, u32[]{:S(2)}) collective-permute-start(f32[192,128]{1,0:T(8,128)S(1)} %get-tuple-element.64), channel_id=1, source_target_pairs={{0,2},{1,3},{2,0},{3,1},{4,6},{5,7},{6,4},{7,5},{8,10},{9,11},{10,... | collective-permute-start | bytes 294920 | tf_op jit(solution)/shard_map/ppermute | solution.py:386
  32.0 1.5 %collective-permute-start.14 = (f32[192,128]{1,0:T(8,128)S(1)}, f32[192,128]{1,0:T(8,128)S(1)}, u32[]{:S(2)}, u32[]{:S(2)}) collective-permute-start(f32[192,128]{1,0:T(8,128)S(1)} %get-tuple-element.65), channel_id=1, source_target_pairs={{0,3},{1,2},{2,1},{3,0},{4,7},{5,6},{6,5},{7,4},{8,11},{9,10},{10,... | collective-permute-start | bytes 294920 | tf_op jit(solution)/shard_map/ppermute | solution.py:386
  33.6 3.8 %correct.1.refs_4_ = f32[1920,128]{1,0:T(8,128)} custom-call(f32[288,128]{1,0:T(8,128)S(1)} %get-tuple-element.66.refs_0_, f32[288,128]{1,0:T(8,128)S(1)} %collective-permute-done.9.refs_11_.refs_1_, f32[288,128]{1,0:T(8,128)S(1)} %collective-permute-done.10.refs_12_.refs_2_, f32[288,128]{1,0:T(8,128)S(1)} %collective-permute-done.11.refs_13_.refs_3_, ...), custom_call_target="tpu_custom_call" | custom-call | flops 6039797760 | bytes 7225344 | tf_op jit(solution)/shard_map/correct/pallas_call | solution.py:359
  37.4 0.7 %collective-permute-done.14.refs_3_ = f32[192,128]{1,0:T(8,128)S(1)} collective-permute-done((f32[192,128]{1,0:T(8,128)S(1)}, f32[192,128]{1,0:T(8,128)S(1)}, u32[]{:S(2)}, u32[]{:S(2)}) %collective-permute-start.14) | collective-permute-done | bytes 98336 | tf_op jit(solution)/shard_map/ppermute | solution.py:386
  38.1 0.8 %unpack.1 = f32[1920,128]{1,0:T(8,128)} custom-call(f32[192,128]{1,0:T(8,128)S(1)} %get-tuple-element.62.refs_0_, f32[192,128]{1,0:T(8,128)S(1)} %collective-permute-done.12.refs_1_, f32[192,128]{1,0:T(8,128)S(1)} %collective-permute-done.13.refs_2_, f32[192,128]{1,0:T(8,128)S(1)} %collective-permute-done.14.refs_3_, ...), custom_call_target="tpu_custom_call", output_to_operand_aliasing={{}: (4, {})} | custom-call | bytes 2359296 | tf_op jit(solution)/shard_map/unpack/pallas_call | solution.py:359
  (31 shorter events, 0.1 us)
Async XLA Ops:
  0.0 5.8 %copy-start.12 = (f32[4]{0:T(128)S(1)}, f32[4]{0:T(128)}, u32[]{:S(2)}) copy-start(f32[4]{0:T(128)} %param.16) | copy-start | bytes 52
  0.0 1.2 %copy-start = (f32[60,4,1024]{2,1,0:T(4,128)S(1)}, f32[60,4,1024]{2,1,0:T(4,128)}, u32[]{:S(2)}) copy-start(f32[60,4,1024]{2,1,0:T(4,128)} %param.13) | copy-start | bytes 2949124
  1.2 4.5 %copy-start.10 = (f32[480]{0:T(512)S(1)}, f32[480]{0:T(512)}, u32[]{:S(2)}) copy-start(f32[480]{0:T(512)} %param.14) | copy-start | bytes 5764
  1.2 4.6 %copy-start.11 = (f32[479]{0:T(512)S(1)}, f32[479]{0:T(512)}, u32[]{:S(2)}) copy-start(f32[479]{0:T(512)} %param.15) | copy-start | bytes 5752
  1.2 5.0 %copy-start.8 = (f32[32,128]{1,0:T(8,128)S(1)}, f32[32,128]{1,0:T(8,128)}, u32[]{:S(2)}) copy-start(f32[32,128]{1,0:T(8,128)} %constant.48.eigen_ref) | copy-start | bytes 49156
  1.3 5.9 %copy-start.4 = (bf16[512,256]{1,0:T(8,128)(2,1)S(1)}, bf16[512,256]{1,0:T(8,128)(2,1)}, u32[]{:S(2)}) copy-start(bf16[512,256]{1,0:T(8,128)(2,1)} %constant.39.clone.refs_7_) | copy-start | bytes 786436
  1.3 5.9 %copy-start.5 = (bf16[512,256]{1,0:T(8,128)(2,1)S(1)}, bf16[512,256]{1,0:T(8,128)(2,1)}, u32[]{:S(2)}) copy-start(bf16[512,256]{1,0:T(8,128)(2,1)} %constant.37.clone.refs_6_) | copy-start | bytes 786436
  1.3 5.9 %copy-start.6 = (bf16[512,256]{1,0:T(8,128)(2,1)S(1)}, bf16[512,256]{1,0:T(8,128)(2,1)}, u32[]{:S(2)}) copy-start(bf16[512,256]{1,0:T(8,128)(2,1)} %constant.35.clone.refs_4_) | copy-start | bytes 786436
  1.3 5.8 %copy-start.7 = (f32[32,128]{1,0:T(8,128)S(1)}, f32[32,128]{1,0:T(8,128)}, u32[]{:S(2)}) copy-start(f32[32,128]{1,0:T(8,128)} %constant.41.clone.refs_5_.refs_6_.refs_15_) | copy-start | bytes 49156
  1.3 5.1 %collective-permute-start.3 = (f32[128,128]{1,0:T(8,128)S(1)}, f32[128,128]{1,0:T(8,128)S(1)}, u32[]{:S(2)}, u32[]{:S(2)}) collective-permute-start(f32[128,128]{1,0:T(8,128)S(1)} %get-tuple-element.44), channel_id=1, source_target_pairs={{0,2},{1,3},{2,0},{3,1},{4,6},{5,7},{6,4},{7,5},{8,10},{9,11},{10,... | collective-permute-start | bytes 196616 | tf_op jit(solution)/shard_map/ppermute | solution.py:386
  2.6 4.5 %collective-permute-start.4 = (f32[128,128]{1,0:T(8,128)S(1)}, f32[128,128]{1,0:T(8,128)S(1)}, u32[]{:S(2)}, u32[]{:S(2)}) collective-permute-start(f32[128,128]{1,0:T(8,128)S(1)} %get-tuple-element.45), channel_id=1, source_target_pairs={{0,3},{1,2},{2,1},{3,0},{4,7},{5,6},{6,5},{7,4},{8,11},{9,10},{10,... | collective-permute-start | bytes 196616 | tf_op jit(solution)/shard_map/ppermute | solution.py:386
  3.8 8.2 %collective-permute-start.1 = (f32[352,128]{1,0:T(8,128)S(1)}, f32[352,128]{1,0:T(8,128)S(1)}, u32[]{:S(2)}, u32[]{:S(2)}) collective-permute-start(f32[352,128]{1,0:T(8,128)S(1)} %get-tuple-element.42), channel_id=1, source_target_pairs={{0,2},{1,3},{2,0},{3,1},{4,6},{5,7},{6,4},{7,5},{8,10},{9,11},{10,... | collective-permute-start | bytes 540680 | tf_op jit(solution)/shard_map/ppermute | solution.py:386
  5.1 9.8 %collective-permute-start.2 = (f32[352,128]{1,0:T(8,128)S(1)}, f32[352,128]{1,0:T(8,128)S(1)}, u32[]{:S(2)}, u32[]{:S(2)}) collective-permute-start(f32[352,128]{1,0:T(8,128)S(1)} %get-tuple-element.43), channel_id=1, source_target_pairs={{0,3},{1,2},{2,1},{3,0},{4,7},{5,6},{6,5},{7,4},{8,11},{9,10},{10,... | collective-permute-start | bytes 540680 | tf_op jit(solution)/shard_map/ppermute | solution.py:386
  5.4 1.8 %collective-permute-start = (f32[480,128]{1,0:T(8,128)S(1)}, f32[480,128]{1,0:T(8,128)S(1)}, u32[]{:S(2)}, u32[]{:S(2)}) collective-permute-start(f32[480,128]{1,0:T(8,128)S(1)} %get-tuple-element.41), channel_id=1, source_target_pairs={{0,1},{1,0},{2,3},{3,2},{4,5},{5,4},{6,7},{7,6},{8,9},{9,8},{10,11... | collective-permute-start | bytes 737288 | tf_op jit(solution)/shard_map/ppermute | solution.py:386
  6.2 8.6 %copy-start.1 = (bf16[512,256]{1,0:T(8,128)(2,1)S(1)}, bf16[512,256]{1,0:T(8,128)(2,1)}, u32[]{:S(2)}) copy-start(bf16[512,256]{1,0:T(8,128)(2,1)} %constant.40.clone.refs_10_.refs_8_.refs_17_) | copy-start | bytes 786436
  6.3 8.6 %copy-start.2 = (bf16[512,256]{1,0:T(8,128)(2,1)S(1)}, bf16[512,256]{1,0:T(8,128)(2,1)}, u32[]{:S(2)}) copy-start(bf16[512,256]{1,0:T(8,128)(2,1)} %constant.38.clone.refs_9_.refs_7_.refs_16_) | copy-start | bytes 786436
  6.3 8.6 %copy-start.3 = (bf16[512,256]{1,0:T(8,128)(2,1)S(1)}, bf16[512,256]{1,0:T(8,128)(2,1)}, u32[]{:S(2)}) copy-start(bf16[512,256]{1,0:T(8,128)(2,1)} %constant.36.clone.refs_8_.refs_5_) | copy-start | bytes 786436
  7.8 7.0 %collective-permute-start.5 = (f32[32,128]{1,0:T(8,128)S(1)}, f32[32,128]{1,0:T(8,128)S(1)}, u32[]{:S(2)}, u32[]{:S(2)}) collective-permute-start(f32[32,128]{1,0:T(8,128)S(1)} %get-tuple-element.47), channel_id=1, source_target_pairs={{0,4},{4,0},{8,12},{12,8},{16,20},{20,16},{24,28},{28,24},{1,5},{5... | collective-permute-start | bytes 49160 | tf_op jit(solution)/shard_map/ppermute | solution.py:382
  9.1 5.7 %collective-permute-start.6 = (f32[32,128]{1,0:T(8,128)S(1)}, f32[32,128]{1,0:T(8,128)S(1)}, u32[]{:S(2)}, u32[]{:S(2)}) collective-permute-start(f32[32,128]{1,0:T(8,128)S(1)} %get-tuple-element.48), channel_id=1, source_target_pairs={{4,8},{8,4},{12,16},{16,12},{20,24},{24,20},{5,9},{9,5},{13,17},{1... | collective-permute-start | bytes 49160 | tf_op jit(solution)/shard_map/ppermute | solution.py:381
  17.5 9.3 %collective-permute-start.9 = (f32[288,128]{1,0:T(8,128)S(1)}, f32[288,128]{1,0:T(8,128)S(1)}, u32[]{:S(2)}, u32[]{:S(2)}) collective-permute-start(f32[288,128]{1,0:T(8,128)S(1)} %get-tuple-element.58), channel_id=1, source_target_pairs={{0,1},{1,0},{2,3},{3,2},{4,5},{5,4},{6,7},{7,6},{8,9},{9,8},{10,11... | collective-permute-start | bytes 442376 | tf_op jit(solution)/shard_map/ppermute | solution.py:386
  19.5 7.3 %collective-permute-start.10 = (f32[288,128]{1,0:T(8,128)S(1)}, f32[288,128]{1,0:T(8,128)S(1)}, u32[]{:S(2)}, u32[]{:S(2)}) collective-permute-start(f32[288,128]{1,0:T(8,128)S(1)} %get-tuple-element.59), channel_id=1, source_target_pairs={{0,2},{1,3},{2,0},{3,1},{4,6},{5,7},{6,4},{7,5},{8,10},{9,11},{10,... | collective-permute-start | bytes 442376 | tf_op jit(solution)/shard_map/ppermute | solution.py:386
  20.0 8.2 %collective-permute-start.11 = (f32[288,128]{1,0:T(8,128)S(1)}, f32[288,128]{1,0:T(8,128)S(1)}, u32[]{:S(2)}, u32[]{:S(2)}) collective-permute-start(f32[288,128]{1,0:T(8,128)S(1)} %get-tuple-element.60), channel_id=1, source_target_pairs={{0,3},{1,2},{2,1},{3,0},{4,7},{5,6},{6,5},{7,4},{8,11},{9,10},{10,... | collective-permute-start | bytes 442376 | tf_op jit(solution)/shard_map/ppermute | solution.py:386
  21.2 4.3 %collective-permute-start.7 = (f32[32,128]{1,0:T(8,128)S(1)}, f32[32,128]{1,0:T(8,128)S(1)}, u32[]{:S(2)}, u32[]{:S(2)}) collective-permute-start(f32[32,128]{1,0:T(8,128)S(1)} %get-tuple-element.54), channel_id=1, source_target_pairs={{0,4},{4,0},{8,12},{12,8},{16,20},{20,16},{24,28},{28,24},{1,5},{5... | collective-permute-start | bytes 49160 | tf_op jit(solution)/shard_map/ppermute | solution.py:382
  21.4 5.4 %collective-permute-start.8 = (f32[32,128]{1,0:T(8,128)S(1)}, f32[32,128]{1,0:T(8,128)S(1)}, u32[]{:S(2)}, u32[]{:S(2)}) collective-permute-start(f32[32,128]{1,0:T(8,128)S(1)} %get-tuple-element.55), channel_id=1, source_target_pairs={{4,8},{8,4},{12,16},{16,12},{20,24},{24,20},{5,9},{9,5},{13,17},{1... | collective-permute-start | bytes 49160 | tf_op jit(solution)/shard_map/ppermute | solution.py:381
  28.3 5.3 %copy-start.9 = (bf16[512,256]{1,0:T(8,128)(2,1)S(1)}, bf16[512,256]{1,0:T(8,128)(2,1)}, u32[]{:S(2)}) copy-start(bf16[512,256]{1,0:T(8,128)(2,1)} %constant.34.clone.refs_14_) | copy-start | bytes 786436
  28.3 3.8 %collective-permute-start.17 = (f32[64,128]{1,0:T(8,128)S(1)}, f32[64,128]{1,0:T(8,128)S(1)}, u32[]{:S(2)}, u32[]{:S(2)}) collective-permute-start(f32[64,128]{1,0:T(8,128)S(1)} %sigma.1.refs_0_.refs_4_), channel_id=1, source_target_pairs={{0,3},{1,2},{2,1},{3,0},{4,7},{5,6},{6,5},{7,4},{8,11},{9,10},{10,... | collective-permute-start | bytes 98312 | tf_op jit(solution)/shard_map/ppermute | solution.py:386
  29.0 4.6 %collective-permute-start.16 = (f32[64,128]{1,0:T(8,128)S(1)}, f32[64,128]{1,0:T(8,128)S(1)}, u32[]{:S(2)}, u32[]{:S(2)}) collective-permute-start(f32[64,128]{1,0:T(8,128)S(1)} %sigma.1.refs_0_.refs_4_), channel_id=1, source_target_pairs={{0,2},{1,3},{2,0},{3,1},{4,6},{5,7},{6,4},{7,5},{8,10},{9,11},{10,... | collective-permute-start | bytes 98312 | tf_op jit(solution)/shard_map/ppermute | solution.py:386
  29.9 3.6 %collective-permute-start.15 = (f32[64,128]{1,0:T(8,128)S(1)}, f32[64,128]{1,0:T(8,128)S(1)}, u32[]{:S(2)}, u32[]{:S(2)}) collective-permute-start(f32[64,128]{1,0:T(8,128)S(1)} %sigma.1.refs_0_.refs_4_), channel_id=1, source_target_pairs={{0,1},{1,0},{2,3},{3,2},{4,5},{5,4},{6,7},{7,6},{8,9},{9,8},{10,11... | collective-permute-start | bytes 98312 | tf_op jit(solution)/shard_map/ppermute | solution.py:386
  31.4 6.0 %collective-permute-start.12 = (f32[192,128]{1,0:T(8,128)S(1)}, f32[192,128]{1,0:T(8,128)S(1)}, u32[]{:S(2)}, u32[]{:S(2)}) collective-permute-start(f32[192,128]{1,0:T(8,128)S(1)} %get-tuple-element.63), channel_id=1, source_target_pairs={{0,1},{1,0},{2,3},{3,2},{4,5},{5,4},{6,7},{7,6},{8,9},{9,8},{10,11... | collective-permute-start | bytes 294920 | tf_op jit(solution)/shard_map/ppermute | solution.py:386
  31.4 6.0 %collective-permute-start.13 = (f32[192,128]{1,0:T(8,128)S(1)}, f32[192,128]{1,0:T(8,128)S(1)}, u32[]{:S(2)}, u32[]{:S(2)}) collective-permute-start(f32[192,128]{1,0:T(8,128)S(1)} %get-tuple-element.64), channel_id=1, source_target_pairs={{0,2},{1,3},{2,0},{3,1},{4,6},{5,7},{6,4},{7,5},{8,10},{9,11},{10,... | collective-permute-start | bytes 294920 | tf_op jit(solution)/shard_map/ppermute | solution.py:386
  32.0 6.1 %collective-permute-start.14 = (f32[192,128]{1,0:T(8,128)S(1)}, f32[192,128]{1,0:T(8,128)S(1)}, u32[]{:S(2)}, u32[]{:S(2)}) collective-permute-start(f32[192,128]{1,0:T(8,128)S(1)} %get-tuple-element.65), channel_id=1, source_target_pairs={{0,3},{1,2},{2,1},{3,0},{4,7},{5,6},{6,5},{7,4},{8,11},{9,10},{10,... | collective-permute-start | bytes 294920 | tf_op jit(solution)/shard_map/ppermute | solution.py:386

commit v11 on v10

--- a/solution.py
+++ b/solution.py
@@ -930,7 +930,7 @@
         out_spaces=[pl.ANY],
     )
 
-    chunks = 4
+    chunks = 2
 
     def unpack(*refs):
         pieces = refs[:levels]

time: 39.1 us -> 39.1 us (level)
  no operation moved by 1% of the time
where the time goes in v11:
time: 39.1 us; the launch traced here: 38.9 us
  starting transfers between devices  18.9 us (48%)
  Pallas kernels  10.9 us (28%)
  waiting for transfers between devices  7.06 us (18%)
  local copies, waits for them, and re-layouts  1.64 us (4%)
    ppermute x14, starting transfers between devices, send_level(): return lax.ppermute(piece, 'lon', [(d, d ^ mask) for d in range(size)])  12.4 us
    pallas_call x11, Pallas kernels, call(): pl.pallas_call(body, out_shape=[jax.ShapeDtypeStruct(s, jnp.float32) for...  10.9 us
    ppermute x14, waiting for transfers between devices, send_level(): return lax.ppermute(piece, 'lon', [(d, d ^ mask) for d in range(size)])  5.72 us
    ppermute x2, starting transfers between devices, swap(): value_odd = lax.ppermute(value_odd, 'lat', odd)  5.03 us
    ppermute x2, starting transfers between devices, swap(): return (lax.ppermute(value_even, 'lat', even), value_odd)  1.53 us
    ppermute x2, waiting for transfers between devices, swap(): value_odd = lax.ppermute(value_odd, 'lat', odd)  1.33 us
    unnamed x26, local copies, waits for them, and re-layouts  1.28 us
  transfers between devices with their start and end apart: 18, of which 5 were waited for; matrix products, arithmetic and copies ran while one was open for 1% of the time, Pallas kernels for 19%

profile of v11, /device:TPU:17, one launch (start us, length us, event | category | flops | bytes accessed | tf_op | source)
XLA Modules:
  0.0 38.9 jit_solution(2761382649087787660)
XLA Ops:
  0.0 1.2 %copy-done = f32[60,4,1024]{2,1,0:T(4,128)S(1)} copy-done((f32[60,4,1024]{2,1,0:T(4,128)S(1)}, f32[60,4,1024]{2,1,0:T(4,128)}, u32[]{:S(2)}) %copy-start) | copy-done | bytes 983064
  1.3 0.0 copy-start.4
  1.3 0.0 copy-start.5
  1.3 0.0 copy-start.6
  1.3 0.0 copy-start.7
  1.3 1.3 %collective-permute-start.3 = (f32[128,128]{1,0:T(8,128)S(1)}, f32[128,128]{1,0:T(8,128)S(1)}, u32[]{:S(2)}, u32[]{:S(2)}) collective-permute-start(f32[128,128]{1,0:T(8,128)S(1)} %get-tuple-element.44), channel_id=1, source_target_pairs={{0,2},{1,3},{2,0},{3,1},{4,6},{5,7},{6,4},{7,5},{8,10},{9,11},{10,... | collective-permute-start | bytes 196616 | tf_op jit(solution)/shard_map/ppermute | solution.py:386
  2.6 1.1 %collective-permute-start.4 = (f32[128,128]{1,0:T(8,128)S(1)}, f32[128,128]{1,0:T(8,128)S(1)}, u32[]{:S(2)}, u32[]{:S(2)}) collective-permute-start(f32[128,128]{1,0:T(8,128)S(1)} %get-tuple-element.45), channel_id=1, source_target_pairs={{0,3},{1,2},{2,1},{3,0},{4,7},{5,6},{6,5},{7,4},{8,11},{9,10},{10,... | collective-permute-start | bytes 196616 | tf_op jit(solution)/shard_map/ppermute | solution.py:386
  3.7 0.1 pack.1
  3.8 1.3 %collective-permute-start.1 = (f32[352,128]{1,0:T(8,128)S(1)}, f32[352,128]{1,0:T(8,128)S(1)}, u32[]{:S(2)}, u32[]{:S(2)}) collective-permute-start(f32[352,128]{1,0:T(8,128)S(1)} %get-tuple-element.42), channel_id=1, source_target_pairs={{0,2},{1,3},{2,0},{3,1},{4,6},{5,7},{6,4},{7,5},{8,10},{9,11},{10,... | collective-permute-start | bytes 540680 | tf_op jit(solution)/shard_map/ppermute | solution.py:386
  5.1 0.3 collective-permute-start.2
  5.4 0.4 collective-permute-start
  5.7 0.1 pad_dynamic-slice_fusion.1
  5.8 0.1 broadcast_multiply_fusion.1
  5.9 0.1 pad_dynamic-slice_fusion
  5.9 0.1 broadcast_multiply_fusion
  6.0 0.1 broadcast_in_dim.5.couple_ref
  6.1 0.1 broadcast_in_dim.4.lon_ref
  6.2 0.0 copy-start.1
  6.3 0.0 copy-start.2
  6.3 0.0 copy-start.3
  6.3 0.1 edge.1.refs_8_.refs_10_
  6.4 0.0 collective-permute-done.3.refs_2_
  6.4 0.7 %collective-permute-done.4.refs_3_ = f32[128,128]{1,0:T(8,128)S(1)} collective-permute-done((f32[128,128]{1,0:T(8,128)S(1)}, f32[128,128]{1,0:T(8,128)S(1)}, u32[]{:S(2)}, u32[]{:S(2)}) %collective-permute-start.4) | collective-permute-done | bytes 65568 | tf_op jit(solution)/shard_map/ppermute | solution.py:386
  7.1 0.7 %ends.1 = (f32[512,128]{1,0:T(8,128)S(1)}, f32[32,128]{1,0:T(8,128)S(1)}, f32[32,128]{1,0:T(8,128)S(1)}, f32[32,128]{1,0:T(8,128)S(1)}, f32[32,128]{1,0:T(8,128)S(1)}) custom-call(f32[128,128]{1,0:T(8,128)S(1)} %get-tuple-element.39.after_ref.refs_0_, f32[480,128]{1,0:T(8,128)S(1)} %collective-permute-done.refs_1_, ...), custom_call_target="tpu_custom_call" | custom-call | flops 67108864 | bytes 1867776 | tf_op jit(solution)/shard_map/ends/pallas_call | solution.py:359
  7.8 1.3 %collective-permute-start.5 = (f32[32,128]{1,0:T(8,128)S(1)}, f32[32,128]{1,0:T(8,128)S(1)}, u32[]{:S(2)}, u32[]{:S(2)}) collective-permute-start(f32[32,128]{1,0:T(8,128)S(1)} %get-tuple-element.47), channel_id=1, source_target_pairs={{0,4},{4,0},{8,12},{12,8},{16,20},{20,16},{24,28},{28,24},{1,5},{5... | collective-permute-start | bytes 49160 | tf_op jit(solution)/shard_map/ppermute | solution.py:382
  9.1 2.0 %collective-permute-start.6 = (f32[32,128]{1,0:T(8,128)S(1)}, f32[32,128]{1,0:T(8,128)S(1)}, u32[]{:S(2)}, u32[]{:S(2)}) collective-permute-start(f32[32,128]{1,0:T(8,128)S(1)} %get-tuple-element.48), channel_id=1, source_target_pairs={{4,8},{8,4},{12,16},{16,12},{20,24},{24,20},{5,9},{9,5},{13,17},{1... | collective-permute-start | bytes 49160 | tf_op jit(solution)/shard_map/ppermute | solution.py:381
  11.2 0.8 %own.1 = (f32[1920,128]{1,0:T(8,128)S(1)}, f32[1920,128]{1,0:T(8,128)S(1)}, f32[160,128]{1,0:T(8,128)S(1)}, f32[1152,128]{1,0:T(8,128)S(1)}, f32[1152,128]{1,0:T...) custom-call(f32[4,76,128]{2,1,0:T(8,128)S(1)} %broadcast_in_dim.4.lon_ref, ...), custom_call_target="tpu_custom_call" | custom-call | flops 9830400 | bytes 4737024 | tf_op jit(solution)/shard_map/own/pallas_call | solution.py:359
  12.0 2.8 %collective-permute-done.2.refs_3_ = f32[352,128]{1,0:T(8,128)S(1)} collective-permute-done((f32[352,128]{1,0:T(8,128)S(1)}, f32[352,128]{1,0:T(8,128)S(1)}, u32[]{:S(2)}, u32[]{:S(2)}) %collective-permute-start.2) | collective-permute-done | bytes 180256 | tf_op jit(solution)/shard_map/ppermute | solution.py:386
  14.9 2.7 %inner.1 = (f32[768,128]{1,0:T(8,128)S(1)}, f32[32,128]{1,0:T(8,128)S(1)}, f32[32,128]{1,0:T(8,128)S(1)}, f32[32,128]{1,0:T(8,128)S(1)}, f32[288,128]{1,0:T(8,12...) custom-call(f32[352,128]{1,0:T(8,128)S(1)} %get-tuple-element.40.refs_0_, ...), custom_call_target="tpu_custom_call" | custom-call | flops 335544320 | bytes 5750784 | tf_op jit(solution)/shard_map/inner/pallas_call | solution.py:359
  17.5 1.9 %collective-permute-start.9 = (f32[288,128]{1,0:T(8,128)S(1)}, f32[288,128]{1,0:T(8,128)S(1)}, u32[]{:S(2)}, u32[]{:S(2)}) collective-permute-start(f32[288,128]{1,0:T(8,128)S(1)} %get-tuple-element.58), channel_id=1, source_target_pairs={{0,1},{1,0},{2,3},{3,2},{4,5},{5,4},{6,7},{7,6},{8,9},{9,8},{10,11... | collective-permute-start | bytes 442376 | tf_op jit(solution)/shard_map/ppermute | solution.py:386
  19.5 0.5 %collective-permute-start.10 = (f32[288,128]{1,0:T(8,128)S(1)}, f32[288,128]{1,0:T(8,128)S(1)}, u32[]{:S(2)}, u32[]{:S(2)}) collective-permute-start(f32[288,128]{1,0:T(8,128)S(1)} %get-tuple-element.59), channel_id=1, source_target_pairs={{0,2},{1,3},{2,0},{3,1},{4,6},{5,7},{6,4},{7,5},{8,10},{9,11},{10,... | collective-permute-start | bytes 442376 | tf_op jit(solution)/shard_map/ppermute | solution.py:386
  20.0 1.2 %collective-permute-start.11 = (f32[288,128]{1,0:T(8,128)S(1)}, f32[288,128]{1,0:T(8,128)S(1)}, u32[]{:S(2)}, u32[]{:S(2)}) collective-permute-start(f32[288,128]{1,0:T(8,128)S(1)} %get-tuple-element.60), channel_id=1, source_target_pairs={{0,3},{1,2},{2,1},{3,0},{4,7},{5,6},{6,5},{7,4},{8,11},{9,10},{10,... | collective-permute-start | bytes 442376 | tf_op jit(solution)/shard_map/ppermute | solution.py:386
  21.2 0.2 collective-permute-start.7
  21.4 3.0 %collective-permute-start.8 = (f32[32,128]{1,0:T(8,128)S(1)}, f32[32,128]{1,0:T(8,128)S(1)}, u32[]{:S(2)}, u32[]{:S(2)}) collective-permute-start(f32[32,128]{1,0:T(8,128)S(1)} %get-tuple-element.55), channel_id=1, source_target_pairs={{4,8},{8,4},{12,16},{16,12},{20,24},{24,20},{5,9},{9,5},{13,17},{1... | collective-permute-start | bytes 49160 | tf_op jit(solution)/shard_map/ppermute | solution.py:381
  24.4 1.0 %partners.1 = (f32[2304,128]{1,0:T(8,128)S(1)}, f32[2304,128]{1,0:T(8,128)S(1)}, f32[32,128]{1,0:T(8,128)S(1)}) custom-call(f32[4,76,128]{2,1,0:T(8,128)S(1)} %broadcast_in_dim.4.lon_ref, f32[4,77,128]{2,1,0:T(8,128)S(1)} %broadcast_in_dim.5.couple_ref, f32[32,128]{1,0:T(8,128)S(1)} %copy-done.8, f32[32,128]{1,0:T(8,128)S(1)} %get-tuple-element.53.after_ref.refs_1_), custom_call_target="tpu_custom_call" | custom-call | flops 9830400 | bytes 2721792 | tf_op jit(solution)/shard_map/partners/pallas_call | solution.py:359
  25.5 1.3 %collective-permute-done.8.refs_5_ = f32[32,128]{1,0:T(8,128)S(1)} collective-permute-done((f32[32,128]{1,0:T(8,128)S(1)}, f32[32,128]{1,0:T(8,128)S(1)}, u32[]{:S(2)}, u32[]{:S(2)}) %collective-permute-start.8) | collective-permute-done | bytes 16416 | tf_op jit(solution)/shard_map/ppermute | solution.py:381
  26.8 1.4 %collective-permute-done.11.refs_13_.refs_3_ = f32[288,128]{1,0:T(8,128)S(1)} collective-permute-done((f32[288,128]{1,0:T(8,128)S(1)}, f32[288,128]{1,0:T(8,128)S(1)}, u32[]{:S(2)}, u32[]{:S(2)}) %collective-permute-start.11) | collective-permute-done | bytes 147488 | tf_op jit(solution)/shard_map/ppermute | solution.py:386
  28.3 0.0 copy-start.9
  28.3 0.7 %collective-permute-start.17 = (f32[64,128]{1,0:T(8,128)S(1)}, f32[64,128]{1,0:T(8,128)S(1)}, u32[]{:S(2)}, u32[]{:S(2)}) collective-permute-start(f32[64,128]{1,0:T(8,128)S(1)} %sigma.1.refs_0_.refs_4_), channel_id=1, source_target_pairs={{0,3},{1,2},{2,1},{3,0},{4,7},{5,6},{6,5},{7,4},{8,11},{9,10},{10,... | collective-permute-start | bytes 98312 | tf_op jit(solution)/shard_map/ppermute | solution.py:386
  29.0 1.0 %collective-permute-start.16 = (f32[64,128]{1,0:T(8,128)S(1)}, f32[64,128]{1,0:T(8,128)S(1)}, u32[]{:S(2)}, u32[]{:S(2)}) collective-permute-start(f32[64,128]{1,0:T(8,128)S(1)} %sigma.1.refs_0_.refs_4_), channel_id=1, source_target_pairs={{0,2},{1,3},{2,0},{3,1},{4,6},{5,7},{6,4},{7,5},{8,10},{9,11},{10,... | collective-permute-start | bytes 98312 | tf_op jit(solution)/shard_map/ppermute | solution.py:386
  29.9 0.6 %collective-permute-start.15 = (f32[64,128]{1,0:T(8,128)S(1)}, f32[64,128]{1,0:T(8,128)S(1)}, u32[]{:S(2)}, u32[]{:S(2)}) collective-permute-start(f32[64,128]{1,0:T(8,128)S(1)} %sigma.1.refs_0_.refs_4_), channel_id=1, source_target_pairs={{0,1},{1,0},{2,3},{3,2},{4,5},{5,4},{6,7},{7,6},{8,9},{9,8},{10,11... | collective-permute-start | bytes 98312 | tf_op jit(solution)/shard_map/ppermute | solution.py:386
  30.5 0.9 %second.1 = (f32[192,128]{1,0:T(8,128)S(1)}, f32[192,128]{1,0:T(8,128)S(1)}, f32[192,128]{1,0:T(8,128)S(1)}, f32[192,128]{1,0:T(8,128)S(1)}) custom-call(f32[64,128]{1,0:T(8,128)S(1)} %sigma.1.refs_0_.refs_4_, f32[768,128]{1,0:T(8,128)S(1)} %get-tuple-element.52.refs_0_.refs_1_, f32[1920,128]{1,0:T(8,128)S(1)} %get-tuple-element.49.refs_14_.refs_8_.refs_2_, ...), custom_call_target="tpu_custom_call" | custom-call | flops 100663296 | bytes 3670016 | tf_op jit(solution)/shard_map/second/pallas_call | solution.py:359
  31.4 0.1 collective-permute-start.12
  31.4 0.6 %collective-permute-start.13 = (f32[192,128]{1,0:T(8,128)S(1)}, f32[192,128]{1,0:T(8,128)S(1)}, u32[]{:S(2)}, u32[]{:S(2)}) collective-permute-start(f32[192,128]{1,0:T(8,128)S(1)} %get-tuple-element.64), channel_id=1, source_target_pairs={{0,2},{1,3},{2,0},{3,1},{4,6},{5,7},{6,4},{7,5},{8,10},{9,11},{10,... | collective-permute-start | bytes 294920 | tf_op jit(solution)/shard_map/ppermute | solution.py:386
  32.0 1.5 %collective-permute-start.14 = (f32[192,128]{1,0:T(8,128)S(1)}, f32[192,128]{1,0:T(8,128)S(1)}, u32[]{:S(2)}, u32[]{:S(2)}) collective-permute-start(f32[192,128]{1,0:T(8,128)S(1)} %get-tuple-element.65), channel_id=1, source_target_pairs={{0,3},{1,2},{2,1},{3,0},{4,7},{5,6},{6,5},{7,4},{8,11},{9,10},{10,... | collective-permute-start | bytes 294920 | tf_op jit(solution)/shard_map/ppermute | solution.py:386
  33.6 3.8 %correct.1.refs_4_ = f32[1920,128]{1,0:T(8,128)} custom-call(f32[288,128]{1,0:T(8,128)S(1)} %get-tuple-element.66.refs_0_, f32[288,128]{1,0:T(8,128)S(1)} %collective-permute-done.9.refs_11_.refs_1_, f32[288,128]{1,0:T(8,128)S(1)} %collective-permute-done.10.refs_12_.refs_2_, f32[288,128]{1,0:T(8,128)S(1)} %collective-permute-done.11.refs_13_.refs_3_, ...), custom_call_target="tpu_custom_call" | custom-call | flops 6039797760 | bytes 7225344 | tf_op jit(solution)/shard_map/correct/pallas_call | solution.py:359
  37.4 0.7 %collective-permute-done.14.refs_3_ = f32[192,128]{1,0:T(8,128)S(1)} collective-permute-done((f32[192,128]{1,0:T(8,128)S(1)}, f32[192,128]{1,0:T(8,128)S(1)}, u32[]{:S(2)}, u32[]{:S(2)}) %collective-permute-start.14) | collective-permute-done | bytes 98336 | tf_op jit(solution)/shard_map/ppermute | solution.py:386
  38.1 0.8 %unpack.1 = f32[1920,128]{1,0:T(8,128)} custom-call(f32[192,128]{1,0:T(8,128)S(1)} %get-tuple-element.62.refs_0_, f32[192,128]{1,0:T(8,128)S(1)} %collective-permute-done.12.refs_1_, f32[192,128]{1,0:T(8,128)S(1)} %collective-permute-done.13.refs_2_, f32[192,128]{1,0:T(8,128)S(1)} %collective-permute-done.14.refs_3_, ...), custom_call_target="tpu_custom_call", output_to_operand_aliasing={{}: (4, {})} | custom-call | bytes 2359296 | tf_op jit(solution)/shard_map/unpack/pallas_call | solution.py:359
  (31 shorter events, 0.1 us)
Async XLA Ops:
  0.0 5.8 %copy-start.12 = (f32[4]{0:T(128)S(1)}, f32[4]{0:T(128)}, u32[]{:S(2)}) copy-start(f32[4]{0:T(128)} %param.16) | copy-start | bytes 52
  0.0 1.2 %copy-start = (f32[60,4,1024]{2,1,0:T(4,128)S(1)}, f32[60,4,1024]{2,1,0:T(4,128)}, u32[]{:S(2)}) copy-start(f32[60,4,1024]{2,1,0:T(4,128)} %param.13) | copy-start | bytes 2949124
  1.2 4.5 %copy-start.10 = (f32[480]{0:T(512)S(1)}, f32[480]{0:T(512)}, u32[]{:S(2)}) copy-start(f32[480]{0:T(512)} %param.14) | copy-start | bytes 5764
  1.2 4.6 %copy-start.11 = (f32[479]{0:T(512)S(1)}, f32[479]{0:T(512)}, u32[]{:S(2)}) copy-start(f32[479]{0:T(512)} %param.15) | copy-start | bytes 5752
  1.2 5.0 %copy-start.8 = (f32[32,128]{1,0:T(8,128)S(1)}, f32[32,128]{1,0:T(8,128)}, u32[]{:S(2)}) copy-start(f32[32,128]{1,0:T(8,128)} %constant.48.eigen_ref) | copy-start | bytes 49156
  1.3 5.9 %copy-start.4 = (bf16[512,256]{1,0:T(8,128)(2,1)S(1)}, bf16[512,256]{1,0:T(8,128)(2,1)}, u32[]{:S(2)}) copy-start(bf16[512,256]{1,0:T(8,128)(2,1)} %constant.39.clone.refs_7_) | copy-start | bytes 786436
  1.3 5.9 %copy-start.5 = (bf16[512,256]{1,0:T(8,128)(2,1)S(1)}, bf16[512,256]{1,0:T(8,128)(2,1)}, u32[]{:S(2)}) copy-start(bf16[512,256]{1,0:T(8,128)(2,1)} %constant.37.clone.refs_6_) | copy-start | bytes 786436
  1.3 5.9 %copy-start.6 = (bf16[512,256]{1,0:T(8,128)(2,1)S(1)}, bf16[512,256]{1,0:T(8,128)(2,1)}, u32[]{:S(2)}) copy-start(bf16[512,256]{1,0:T(8,128)(2,1)} %constant.35.clone.refs_4_) | copy-start | bytes 786436
  1.3 5.8 %copy-start.7 = (f32[32,128]{1,0:T(8,128)S(1)}, f32[32,128]{1,0:T(8,128)}, u32[]{:S(2)}) copy-start(f32[32,128]{1,0:T(8,128)} %constant.41.clone.refs_5_.refs_6_.refs_15_) | copy-start | bytes 49156
  1.3 5.1 %collective-permute-start.3 = (f32[128,128]{1,0:T(8,128)S(1)}, f32[128,128]{1,0:T(8,128)S(1)}, u32[]{:S(2)}, u32[]{:S(2)}) collective-permute-start(f32[128,128]{1,0:T(8,128)S(1)} %get-tuple-element.44), channel_id=1, source_target_pairs={{0,2},{1,3},{2,0},{3,1},{4,6},{5,7},{6,4},{7,5},{8,10},{9,11},{10,... | collective-permute-start | bytes 196616 | tf_op jit(solution)/shard_map/ppermute | solution.py:386
  2.6 4.5 %collective-permute-start.4 = (f32[128,128]{1,0:T(8,128)S(1)}, f32[128,128]{1,0:T(8,128)S(1)}, u32[]{:S(2)}, u32[]{:S(2)}) collective-permute-start(f32[128,128]{1,0:T(8,128)S(1)} %get-tuple-element.45), channel_id=1, source_target_pairs={{0,3},{1,2},{2,1},{3,0},{4,7},{5,6},{6,5},{7,4},{8,11},{9,10},{10,... | collective-permute-start | bytes 196616 | tf_op jit(solution)/shard_map/ppermute | solution.py:386
  3.8 8.2 %collective-permute-start.1 = (f32[352,128]{1,0:T(8,128)S(1)}, f32[352,128]{1,0:T(8,128)S(1)}, u32[]{:S(2)}, u32[]{:S(2)}) collective-permute-start(f32[352,128]{1,0:T(8,128)S(1)} %get-tuple-element.42), channel_id=1, source_target_pairs={{0,2},{1,3},{2,0},{3,1},{4,6},{5,7},{6,4},{7,5},{8,10},{9,11},{10,... | collective-permute-start | bytes 540680 | tf_op jit(solution)/shard_map/ppermute | solution.py:386
  5.1 9.8 %collective-permute-start.2 = (f32[352,128]{1,0:T(8,128)S(1)}, f32[352,128]{1,0:T(8,128)S(1)}, u32[]{:S(2)}, u32[]{:S(2)}) collective-permute-start(f32[352,128]{1,0:T(8,128)S(1)} %get-tuple-element.43), channel_id=1, source_target_pairs={{0,3},{1,2},{2,1},{3,0},{4,7},{5,6},{6,5},{7,4},{8,11},{9,10},{10,... | collective-permute-start | bytes 540680 | tf_op jit(solution)/shard_map/ppermute | solution.py:386
  5.4 1.8 %collective-permute-start = (f32[480,128]{1,0:T(8,128)S(1)}, f32[480,128]{1,0:T(8,128)S(1)}, u32[]{:S(2)}, u32[]{:S(2)}) collective-permute-start(f32[480,128]{1,0:T(8,128)S(1)} %get-tuple-element.41), channel_id=1, source_target_pairs={{0,1},{1,0},{2,3},{3,2},{4,5},{5,4},{6,7},{7,6},{8,9},{9,8},{10,11... | collective-permute-start | bytes 737288 | tf_op jit(solution)/shard_map/ppermute | solution.py:386
  6.2 8.6 %copy-start.1 = (bf16[512,256]{1,0:T(8,128)(2,1)S(1)}, bf16[512,256]{1,0:T(8,128)(2,1)}, u32[]{:S(2)}) copy-start(bf16[512,256]{1,0:T(8,128)(2,1)} %constant.40.clone.refs_10_.refs_8_.refs_17_) | copy-start | bytes 786436
  6.3 8.6 %copy-start.2 = (bf16[512,256]{1,0:T(8,128)(2,1)S(1)}, bf16[512,256]{1,0:T(8,128)(2,1)}, u32[]{:S(2)}) copy-start(bf16[512,256]{1,0:T(8,128)(2,1)} %constant.38.clone.refs_9_.refs_7_.refs_16_) | copy-start | bytes 786436
  6.3 8.6 %copy-start.3 = (bf16[512,256]{1,0:T(8,128)(2,1)S(1)}, bf16[512,256]{1,0:T(8,128)(2,1)}, u32[]{:S(2)}) copy-start(bf16[512,256]{1,0:T(8,128)(2,1)} %constant.36.clone.refs_8_.refs_5_) | copy-start | bytes 786436
  7.8 7.0 %collective-permute-start.5 = (f32[32,128]{1,0:T(8,128)S(1)}, f32[32,128]{1,0:T(8,128)S(1)}, u32[]{:S(2)}, u32[]{:S(2)}) collective-permute-start(f32[32,128]{1,0:T(8,128)S(1)} %get-tuple-element.47), channel_id=1, source_target_pairs={{0,4},{4,0},{8,12},{12,8},{16,20},{20,16},{24,28},{28,24},{1,5},{5... | collective-permute-start | bytes 49160 | tf_op jit(solution)/shard_map/ppermute | solution.py:382
  9.1 5.7 %collective-permute-start.6 = (f32[32,128]{1,0:T(8,128)S(1)}, f32[32,128]{1,0:T(8,128)S(1)}, u32[]{:S(2)}, u32[]{:S(2)}) collective-permute-start(f32[32,128]{1,0:T(8,128)S(1)} %get-tuple-element.48), channel_id=1, source_target_pairs={{4,8},{8,4},{12,16},{16,12},{20,24},{24,20},{5,9},{9,5},{13,17},{1... | collective-permute-start | bytes 49160 | tf_op jit(solution)/shard_map/ppermute | solution.py:381
  17.5 9.3 %collective-permute-start.9 = (f32[288,128]{1,0:T(8,128)S(1)}, f32[288,128]{1,0:T(8,128)S(1)}, u32[]{:S(2)}, u32[]{:S(2)}) collective-permute-start(f32[288,128]{1,0:T(8,128)S(1)} %get-tuple-element.58), channel_id=1, source_target_pairs={{0,1},{1,0},{2,3},{3,2},{4,5},{5,4},{6,7},{7,6},{8,9},{9,8},{10,11... | collective-permute-start | bytes 442376 | tf_op jit(solution)/shard_map/ppermute | solution.py:386
  19.5 7.3 %collective-permute-start.10 = (f32[288,128]{1,0:T(8,128)S(1)}, f32[288,128]{1,0:T(8,128)S(1)}, u32[]{:S(2)}, u32[]{:S(2)}) collective-permute-start(f32[288,128]{1,0:T(8,128)S(1)} %get-tuple-element.59), channel_id=1, source_target_pairs={{0,2},{1,3},{2,0},{3,1},{4,6},{5,7},{6,4},{7,5},{8,10},{9,11},{10,... | collective-permute-start | bytes 442376 | tf_op jit(solution)/shard_map/ppermute | solution.py:386
  20.0 8.2 %collective-permute-start.11 = (f32[288,128]{1,0:T(8,128)S(1)}, f32[288,128]{1,0:T(8,128)S(1)}, u32[]{:S(2)}, u32[]{:S(2)}) collective-permute-start(f32[288,128]{1,0:T(8,128)S(1)} %get-tuple-element.60), channel_id=1, source_target_pairs={{0,3},{1,2},{2,1},{3,0},{4,7},{5,6},{6,5},{7,4},{8,11},{9,10},{10,... | collective-permute-start | bytes 442376 | tf_op jit(solution)/shard_map/ppermute | solution.py:386
  21.2 4.3 %collective-permute-start.7 = (f32[32,128]{1,0:T(8,128)S(1)}, f32[32,128]{1,0:T(8,128)S(1)}, u32[]{:S(2)}, u32[]{:S(2)}) collective-permute-start(f32[32,128]{1,0:T(8,128)S(1)} %get-tuple-element.54), channel_id=1, source_target_pairs={{0,4},{4,0},{8,12},{12,8},{16,20},{20,16},{24,28},{28,24},{1,5},{5... | collective-permute-start | bytes 49160 | tf_op jit(solution)/shard_map/ppermute | solution.py:382
  21.4 5.4 %collective-permute-start.8 = (f32[32,128]{1,0:T(8,128)S(1)}, f32[32,128]{1,0:T(8,128)S(1)}, u32[]{:S(2)}, u32[]{:S(2)}) collective-permute-start(f32[32,128]{1,0:T(8,128)S(1)} %get-tuple-element.55), channel_id=1, source_target_pairs={{4,8},{8,4},{12,16},{16,12},{20,24},{24,20},{5,9},{9,5},{13,17},{1... | collective-permute-start | bytes 49160 | tf_op jit(solution)/shard_map/ppermute | solution.py:381
  28.3 5.3 %copy-start.9 = (bf16[512,256]{1,0:T(8,128)(2,1)S(1)}, bf16[512,256]{1,0:T(8,128)(2,1)}, u32[]{:S(2)}) copy-start(bf16[512,256]{1,0:T(8,128)(2,1)} %constant.34.clone.refs_14_) | copy-start | bytes 786436
  28.3 3.8 %collective-permute-start.17 = (f32[64,128]{1,0:T(8,128)S(1)}, f32[64,128]{1,0:T(8,128)S(1)}, u32[]{:S(2)}, u32[]{:S(2)}) collective-permute-start(f32[64,128]{1,0:T(8,128)S(1)} %sigma.1.refs_0_.refs_4_), channel_id=1, source_target_pairs={{0,3},{1,2},{2,1},{3,0},{4,7},{5,6},{6,5},{7,4},{8,11},{9,10},{10,... | collective-permute-start | bytes 98312 | tf_op jit(solution)/shard_map/ppermute | solution.py:386
  29.0 4.6 %collective-permute-start.16 = (f32[64,128]{1,0:T(8,128)S(1)}, f32[64,128]{1,0:T(8,128)S(1)}, u32[]{:S(2)}, u32[]{:S(2)}) collective-permute-start(f32[64,128]{1,0:T(8,128)S(1)} %sigma.1.refs_0_.refs_4_), channel_id=1, source_target_pairs={{0,2},{1,3},{2,0},{3,1},{4,6},{5,7},{6,4},{7,5},{8,10},{9,11},{10,... | collective-permute-start | bytes 98312 | tf_op jit(solution)/shard_map/ppermute | solution.py:386
  29.9 3.6 %collective-permute-start.15 = (f32[64,128]{1,0:T(8,128)S(1)}, f32[64,128]{1,0:T(8,128)S(1)}, u32[]{:S(2)}, u32[]{:S(2)}) collective-permute-start(f32[64,128]{1,0:T(8,128)S(1)} %sigma.1.refs_0_.refs_4_), channel_id=1, source_target_pairs={{0,1},{1,0},{2,3},{3,2},{4,5},{5,4},{6,7},{7,6},{8,9},{9,8},{10,11... | collective-permute-start | bytes 98312 | tf_op jit(solution)/shard_map/ppermute | solution.py:386
  31.4 6.0 %collective-permute-start.12 = (f32[192,128]{1,0:T(8,128)S(1)}, f32[192,128]{1,0:T(8,128)S(1)}, u32[]{:S(2)}, u32[]{:S(2)}) collective-permute-start(f32[192,128]{1,0:T(8,128)S(1)} %get-tuple-element.63), channel_id=1, source_target_pairs={{0,1},{1,0},{2,3},{3,2},{4,5},{5,4},{6,7},{7,6},{8,9},{9,8},{10,11... | collective-permute-start | bytes 294920 | tf_op jit(solution)/shard_map/ppermute | solution.py:386
  31.4 6.0 %collective-permute-start.13 = (f32[192,128]{1,0:T(8,128)S(1)}, f32[192,128]{1,0:T(8,128)S(1)}, u32[]{:S(2)}, u32[]{:S(2)}) collective-permute-start(f32[192,128]{1,0:T(8,128)S(1)} %get-tuple-element.64), channel_id=1, source_target_pairs={{0,2},{1,3},{2,0},{3,1},{4,6},{5,7},{6,4},{7,5},{8,10},{9,11},{10,... | collective-permute-start | bytes 294920 | tf_op jit(solution)/shard_map/ppermute | solution.py:386
  32.0 6.1 %collective-permute-start.14 = (f32[192,128]{1,0:T(8,128)S(1)}, f32[192,128]{1,0:T(8,128)S(1)}, u32[]{:S(2)}, u32[]{:S(2)}) collective-permute-start(f32[192,128]{1,0:T(8,128)S(1)} %get-tuple-element.65), channel_id=1, source_target_pairs={{0,3},{1,2},{2,1},{3,0},{4,7},{5,6},{6,5},{7,4},{8,11},{9,10},{10,... | collective-permute-start | bytes 294920 | tf_op jit(solution)/shard_map/ppermute | solution.py:386
